TPU v7x, 256 devices: a whole 4x4x8 slice. The times are simulated.
256 devices in a mesh: section: 16 (over y_hi, x, core), tensor: 16 (over y_lo, z).
Axes of the slice: x: 4, y: 4 (y_hi: 2, y_lo: 2; y = y_hi * 2 + y_lo), z: 8, core: 2. Of those that a mesh axis runs over, the one named last changes fastest.
Arguments:
- state: bfloat16 [16, 256, 6144], P('section', None, 'tensor'), may hold values from -6 to 6
- ln_gain: float32 [16, 6144], P('section'), may hold values from 0.1 to 1.9
- w_qkv: bfloat16 [16, 6144, 3, 4096], P('section', None, None, 'tensor'), may hold values from -0.078125 to 0.078125
- qk_gain: float32 [16, 2, 128], P('section'), may hold values from 0.5 to 1.5
- w_out: bfloat16 [16, 4096, 6144], P('section', 'tensor'), may hold values from -1 to 1
Outputs:
- advanced: bfloat16 [16, 256, 6144], P('section', None, 'tensor')
All inputs are finite; a program needn't handle non-finite values.
Results may differ from a plain program's by a relative error of at most 0.03.
Values may be sent and summed in bfloat16 or wider, within the bound.
No kernel may reach another device: no remote copies, remote signals or barrier semaphores. Data moves between devices by JAX's collectives and lax.ppermute only.
A program may use at most 128 MiB of HBM per device.

v0:
```python
import functools

import jax
import jax.numpy as jnp
from jax import lax
from jax.experimental import pallas as pl
from jax.experimental.pallas import tpu as pltpu
from jax.sharding import Mesh, PartitionSpec as P

HD = 128
STEPS = 2
EPS = 1e-06
SECTION = ("yh", "x", "core")
PAIR = "yl"
RING = "z"
EXTRA = 16
VMEM = pl.BlockSpec(memory_space=pltpu.VMEM)
SMEM = pl.BlockSpec(memory_space=pltpu.SMEM)
ROWS = 64
GROUP = 4
LATE = 4


def fetches(rows_ref, w_hbm, w_ref, w_sem, count, width):
    def fetch(at):
        start = pl.multiple_of(rows_ref[at] * width, width)
        return pltpu.make_async_copy(
            w_hbm.at[:, pl.ds(start, width), :], w_ref.at[:, pl.ds(at * width, width), :], w_sem.at[at]
        )

    return [fetch(at) for at in range(count)]


def scale_blocks(first, rows_ref, gain_ref, x_refs, before_ref, sums_ref, shift_ref, scaled_ref):
    patches, width = x_refs[0].shape
    for at in range(len(x_refs)):
        gain = gain_ref[rows_ref[at]]
        high = gain.astype(jnp.bfloat16).astype(jnp.float32)
        row = lax.broadcasted_iota(jnp.int32, (EXTRA, width), 0)
        both = jnp.where(row == 0, high, jnp.where(row == 1, gain - high, 0.0))
        scaled_ref[patches : patches + EXTRA, at * width : (at + 1) * width] = both.astype(jnp.bfloat16)

    @pl.loop(0, patches // ROWS)
    def _(block):
        part = pl.ds(pl.multiple_of(block * ROWS, ROWS), ROWS)
        if first:
            shift = jnp.sum(x_refs[0][part, :].astype(jnp.float32), axis=-1, keepdims=True) / width
            shift_ref[part, :] = jnp.broadcast_to(shift, (ROWS, 128))
            total = squares = jnp.zeros((ROWS, 128), jnp.float32)
        else:
            shift = shift_ref[part, 0:1]
            total, squares = before_ref[0, part, :], before_ref[1, part, :]
        for at, x_ref in enumerate(x_refs):
            values = x_ref[part, :].astype(jnp.float32)
            for lane in range(0, width, 128):
                piece = values[:, lane : lane + 128]
                total += piece
                squares += piece * piece
            scaled = (values - shift) * gain_ref[rows_ref[at]]
            scaled_ref[part, at * width : (at + 1) * width] = scaled.astype(jnp.bfloat16)
        sums_ref[0, part, :] = total
        sums_ref[1, part, :] = squares


def partial_block(blocks, rows_ref, late_rows_ref, gain_ref, w_hbm, *refs):
    x_refs, (acc_ref, sums_ref, shift_ref, w_late_ref, scaled_ref, w_ref, w_sem, late_sem) = refs[:blocks], refs[blocks:]
    width = x_refs[0].shape[1]
    now = fetches(rows_ref, w_hbm, w_ref, w_sem, blocks, width)
    late = fetches(late_rows_ref, w_hbm, w_late_ref, late_sem, LATE, width)
    for copy in now + late:
        copy.start()
    scale_blocks(True, rows_ref, gain_ref, x_refs, None, sums_ref, shift_ref, scaled_ref)
    for copy in now:
        copy.wait()
    depth = GROUP * width

    @pl.loop(0, 3)
    def _(plane):
        for group in range(blocks // GROUP):
            span = slice(group * depth, (group + 1) * depth)
            out = jnp.dot(scaled_ref[:, span], w_ref[plane, span, :], preferred_element_type=jnp.float32)
            if group == 0:
                acc_ref[plane] = out
            else:
                acc_ref[plane] += out

    for copy in late:
        copy.wait()


def final_block(blocks, pieces, rows_ref, gain_ref, *refs):
    x_refs, (acc_ref, before_ref, shift_ref, w_ref, qk_gain_ref, out_ref, sums_ref, scaled_ref) = (
        refs[:blocks],
        refs[blocks:],
    )
    patches, width = x_refs[0].shape
    full_width = pieces * width
    scale_blocks(False, rows_ref, gain_ref, x_refs, before_ref, sums_ref, shift_ref, scaled_ref)
    mean = jnp.sum(sums_ref[0], axis=-1, keepdims=True) / full_width
    spread = jnp.sum(sums_ref[1], axis=-1, keepdims=True) / full_width - mean * mean
    scale = lax.rsqrt(spread + EPS)
    offset = mean - shift_ref[:, 0:1]

    def projected(plane):
        out = acc_ref[plane] + jnp.dot(scaled_ref[...], w_ref[plane], preferred_element_type=jnp.float32)
        weighed = out[patches : patches + 1] + out[patches + 1 : patches + 2]
        return (out[:patches] - offset * weighed) * scale

    def head_norm(values, gain):
        mean = jnp.mean(values, axis=-1, keepdims=True)
        squares = jnp.mean(values * values, axis=-1, keepdims=True)
        return ((values - mean) * lax.rsqrt(squares - mean * mean + EPS) * gain).astype(jnp.bfloat16)

    all_query, all_keys, all_value = (projected(plane) for plane in range(3))
    for head in range(out_ref.shape[1] // HD):
        cols = slice(head * HD, (head + 1) * HD)
        query = head_norm(all_query[:, cols], qk_gain_ref[0:1, :])
        keys = head_norm(all_keys[:, cols], qk_gain_ref[1:2, :])
        value = all_value[:, cols].astype(jnp.bfloat16)
        scores = lax.dot_general(query, keys, (((1,), (1,)), ((), ())), preferred_element_type=jnp.float32)
        expo = jnp.exp(scores * HD**-0.5)
        attend = (expo * (1.0 / jnp.sum(expo, axis=-1, keepdims=True))).astype(jnp.bfloat16)
        out_ref[:, cols] = jnp.dot(attend, value, preferred_element_type=jnp.float32).astype(jnp.bfloat16)


def partial(rows, late_rows, gain, w_planes, blocks):
    patches, width = blocks[0].shape
    planes, _, cols = w_planes.shape
    count = len(blocks)
    return pl.pallas_call(
        functools.partial(partial_block, count),
        out_shape=[
            jax.ShapeDtypeStruct((planes, patches + EXTRA, cols), jnp.float32),
            jax.ShapeDtypeStruct((2, patches, 128), jnp.float32),
            jax.ShapeDtypeStruct((patches, 128), jnp.float32),
            jax.ShapeDtypeStruct((planes, LATE * width, cols), jnp.bfloat16),
        ],
        in_specs=[SMEM, SMEM, VMEM, pl.BlockSpec(memory_space=pltpu.HBM)] + [VMEM] * count,
        out_specs=[VMEM] * 4,
        scratch_shapes=[
            pltpu.VMEM((patches + EXTRA, count * width), jnp.bfloat16),
            pltpu.VMEM((planes, count * width, cols), jnp.bfloat16),
            pltpu.SemaphoreType.DMA((count,)),
            pltpu.SemaphoreType.DMA((LATE,)),
        ],
        compiler_params=pltpu.CompilerParams(vmem_limit_bytes=28 << 20),
        name="qkv_partial",
    )(rows, late_rows, gain, w_planes, *blocks)


def attention(rows, gain, blocks, carried, qk_gain, pieces):
    patches, width = blocks[0].shape
    cols = carried[0].shape[2]
    count = len(blocks)
    return pl.pallas_call(
        functools.partial(final_block, count, pieces),
        out_shape=jax.ShapeDtypeStruct((patches, cols), jnp.bfloat16),
        in_specs=[SMEM] + [VMEM] * (count + 6),
        out_specs=VMEM,
        scratch_shapes=[
            pltpu.VMEM((2, patches, 128), jnp.float32),
            pltpu.VMEM((patches + EXTRA, count * width), jnp.bfloat16),
        ],
        compiler_params=pltpu.CompilerParams(vmem_limit_bytes=20 << 20),
        name="attention_block",
    )(rows, gain, *blocks, *carried, qk_gain)


def projection_block(places, order_ref, own_ref, other_ref, w_own_ref, w_other_ref, *out_refs):
    width = out_refs[0].shape[1]
    for at, out_ref in zip(places, out_refs):
        in_own = pl.ds(pl.multiple_of((order_ref[0] + order_ref[1 + at]) * width, width), width)
        in_other = pl.ds(pl.multiple_of(order_ref[1 + at] * width, width), width)
        out = jnp.dot(own_ref[...], w_own_ref[:, in_own], preferred_element_type=jnp.float32)
        out += jnp.dot(other_ref[...], w_other_ref[:, in_other], preferred_element_type=jnp.float32)
        out_ref[...] = out.astype(out_ref.dtype)


def projection(order, own, other, w_own, w_other, ring, places):
    shape = (own.shape[0], w_other.shape[1] // ring)
    out = pl.pallas_call(
        functools.partial(projection_block, places),
        out_shape=[jax.ShapeDtypeStruct(shape, jnp.bfloat16)] * len(places),
        in_specs=[SMEM] + [VMEM] * 4,
        out_specs=[VMEM] * len(places),
        compiler_params=pltpu.CompilerParams(vmem_limit_bytes=24 << 20),
        name="projection_block",
    )(order, own, other, w_own, w_other)
    return dict(zip(places, out))


def shifted(block, axis, by):
    peers = lax.axis_size(axis)
    return lax.ppermute(block, axis, [(i, (i + by) % peers) for i in range(peers)])


def across(block, by):
    ring = lax.axis_size(RING)
    pairs = [(y * ring + z, (1 - y) * ring + (z + by) % ring) for y in range(2) for z in range(ring)]
    return lax.ppermute(block, (PAIR, RING), pairs)


def to_next_section(block, by):
    sections, ring = lax.axis_size(SECTION), lax.axis_size(RING)

    def place(s, y, z):
        return ((s % sections) * 2 + y) * ring + z % ring

    pairs = [
        (place(s, y, z), place(s + 1, y, z + by)) for s in range(sections) for y in range(2) for z in range(ring)
    ]
    return lax.ppermute(block, SECTION + (PAIR, RING), pairs)


def added(*blocks):
    return functools.reduce(jnp.add, (b.astype(jnp.float32) for b in blocks)).astype(jnp.bfloat16)


def on_device(state, ln_gain, w_qkv, qk_gain, w_out):
    ring = lax.axis_size(RING)
    assert ring == 8
    here, side = lax.axis_index(RING), lax.axis_index(PAIR)
    own = state[0]
    width = own.shape[1]
    w_planes = pltpu.with_memory_space_constraint(jnp.transpose(w_qkv[0], (1, 0, 2)), pltpu.HBM)
    gain = ln_gain[0].reshape(2 * ring, 1, width)
    w_own = w_out[0]

    def rows(*places):
        return jnp.stack([(side ^ y) * ring + (here + o) % ring for y, o in places]).astype(jnp.int32)

    early_rows = rows(
        (0, 0), (1, 0), (0, -1), (0, 1), (0, -2), (0, 2), (1, -1), (1, 1), (0, -3), (0, 3), (1, -2), (1, 2)
    )
    late_rows = rows((0, -4), (1, -3), (1, 3), (1, 4))
    order = jnp.concatenate([side[None] * ring, (here + jnp.arange(ring)) % ring]).astype(jnp.int32)

    half = w_own.shape[1] // 2

    def step(_, own):
        a_up, a_down = shifted(own, RING, 1), shifted(own, RING, -1)
        other = shifted(own, PAIR, 1)
        a_up, a_down, other = lax.optimization_barrier((a_up, a_down, other))
        w_give = lax.dynamic_slice_in_dim(lax.optimization_barrier((w_own, own))[0], (1 - side) * half, half, 1)
        w_other = shifted(lax.optimization_barrier((w_give, other))[0], PAIR, 1)
        blocks = [own, other, a_up, a_down]
        b_up = b_down = other
        for _ in range(2):
            a_up, a_down = shifted(a_up, RING, 1), shifted(a_down, RING, -1)
            b_up, b_down = shifted(b_up, RING, 1), shifted(b_down, RING, -1)
            blocks += [a_up, a_down, b_up, b_down]
        late = [shifted(a_up, RING, 1), shifted(b_up, RING, 1), shifted(b_down, RING, -1), across(a_down, -1)]

        sums = partial(early_rows, late_rows, gain, w_planes, blocks)
        mixed = attention(late_rows, gain, late, sums, qk_gain[0], 2 * ring)
        mixed_other = shifted(mixed, PAIR, 1)
        parts = projection(order, mixed, mixed_other, w_own, w_other, ring, (4, 5))
        up, down = shifted(parts[4], RING, 1), shifted(parts[5], RING, -1)
        parts |= projection(order, mixed, mixed_other, w_own, w_other, ring, (3, 6, 0, 7, 2, 1))

        kept = to_next_section(added(own, parts[0]), 0)
        down = to_next_section(added(shifted(added(down, parts[6]), RING, -1), parts[7]), -1)
        for k in (3, 2):
            up = shifted(added(up, parts[k]), RING, 1)
        up = to_next_section(added(up, parts[1]), 1)
        return added(kept, down, up)

    return lax.fori_loop(0, STEPS, step, own)[None]


def solution(mesh):
    assert dict(mesh.shape) == {"section": 16, "tensor": 16}
    devices = mesh.devices.reshape(2, 4, 2, 2, 8)
    fine = Mesh(devices, SECTION + (PAIR, RING))
    tensor = (PAIR, RING)
    return jax.shard_map(
        on_device,
        mesh=fine,
        in_specs=(
            P(SECTION, None, tensor),
            P(SECTION, None),
            P(SECTION, None, None, tensor),
            P(SECTION, None, None),
            P(SECTION, tensor, None),
        ),
        out_specs=P(SECTION, None, tensor),
        check_vma=False,
    )
```

profile of v0, /device:TPU:0, one launch (start us, length us, event | category | flops | bytes accessed | tf_op | source)
XLA Modules:
  0.0 175.9 jit_solution(9827993730595557984)
XLA Ops:
  0.0 0.9 copy.14
  1.2 174.0 %while.12 = (s32[]{:T(128)}, bf16[256,384]{1,0:T(8,128)(2,1)S(1)}, s32[12]{0:T(128)S(1)}, s32[4]{0:T(128)S(1)}, f32[16,1,384]{2,1,0:T(1,128)}, /*index=5*/bf16[3...) while((s32[]{:T(128)}, bf16[256,384]{1,0:T(8,128)(2,1)S(1)}, ...), condition=%wide.region_1.2_spmd, body=%wide.region_0.1_spmd.sunk | while | flops 2949122 | bytes 45061292 | solution.py:268
  1.4 4.0 %collective-permute-start.1 = (bf16[256,384]{1,0:T(8,128)(2,1)S(1)}, bf16[256,384]{1,0:T(8,128)(2,1)S(1)}, u32[]{:S(2)}, u32[]{:S(2)}) collective-permute-start(bf16[256,384]{1,0:T(8,128)(2,1)S(1)} %get-tuple-element.263.refs_0_), channel_id=1, source_target_pairs={{0,7},{1,0},{2,1},{3,2},{4,3},{5,4},{6,5},{7,6},{8,15},{9,8},{10,9... | collective-permute-start | bytes 589832 | tf_op jit(solution)/shard_map/while/body/eval_jaxpr/ppermute | solution.py:194
  5.5 1.6 collective-permute-start.2
  7.0 1.5 constant_dynamic-slice_fusion.2
  8.6 1.7 collective-permute-done.refs_2_
  10.3 1.5 collective-permute-done.2.refs_1_
  11.8 1.6 collective-permute-start.16
  13.4 1.7 collective-permute-start.9
  15.1 0.4 collective-permute-start.6
  15.4 2.9 %collective-permute-start.12 = (bf16[256,384]{1,0:T(8,128)(2,1)S(1)}, bf16[256,384]{1,0:T(8,128)(2,1)S(1)}, u32[]{:S(2)}, u32[]{:S(2)}) collective-permute-start(bf16[256,384]{1,0:T(8,128)(2,1)S(1)} %collective-permute-done.1.refs_3_), channel_id=1, source_target_pairs={{0,7},{1,0},{2,1},{3,2},{4,3},{5,4},{6,5},{7,6},{8,15},{9,8},{10,9... | collective-permute-start | bytes 589832 | tf_op jit(solution)/shard_map/while/body/eval_jaxpr/ppermute | solution.py:194
  18.3 2.9 %collective-permute-done.9.refs_7_ = bf16[256,384]{1,0:T(8,128)(2,1)S(1)} collective-permute-done((bf16[256,384]{1,0:T(8,128)(2,1)S(1)}, bf16[256,384]{1,0:T(8,128)(2,1)S(1)}, u32[]{:S(2)}, u32[]{:S(2)}) %collective-permute-start.9) | collective-permute-done | bytes 196640 | tf_op jit(solution)/shard_map/while/body/eval_jaxpr/ppermute | solution.py:194
  21.2 2.6 %collective-permute-start.10 = (bf16[256,384]{1,0:T(8,128)(2,1)S(1)}, bf16[256,384]{1,0:T(8,128)(2,1)S(1)}, u32[]{:S(2)}, u32[]{:S(2)}) collective-permute-start(bf16[256,384]{1,0:T(8,128)(2,1)S(1)} %collective-permute-done.9.refs_7_), channel_id=1, source_target_pairs={{0,7},{1,0},{2,1},{3,2},{4,3},{5,4},{6,5},{7,6},{8,15},{9,8},{10,9... | collective-permute-start | bytes 589832 | tf_op jit(solution)/shard_map/while/body/eval_jaxpr/ppermute | solution.py:194
  23.8 0.2 collective-permute-done.6.refs_6_
  24.1 1.4 collective-permute-done.12.refs_5_
  25.5 2.6 %collective-permute-start.13 = (bf16[256,384]{1,0:T(8,128)(2,1)S(1)}, bf16[256,384]{1,0:T(8,128)(2,1)S(1)}, u32[]{:S(2)}, u32[]{:S(2)}) collective-permute-start(bf16[256,384]{1,0:T(8,128)(2,1)S(1)} %collective-permute-done.12.refs_5_), channel_id=1, source_target_pairs={{0,7},{1,0},{2,1},{3,2},{4,3},{5,4},{6,5},{7,6},{8,15},{9,8},{10,9... | collective-permute-start | bytes 589832 | tf_op jit(solution)/shard_map/while/body/eval_jaxpr/ppermute | solution.py:194
  28.3 1.4 collective-permute-done.10.refs_11_
  29.7 3.2 %collective-permute-start.11 = (bf16[256,384]{1,0:T(8,128)(2,1)S(1)}, bf16[256,384]{1,0:T(8,128)(2,1)S(1)}, u32[]{:S(2)}, u32[]{:S(2)}) collective-permute-start(bf16[256,384]{1,0:T(8,128)(2,1)S(1)} %collective-permute-done.10.refs_11_), channel_id=1, source_target_pairs={{0,7},{1,0},{2,1},{3,2},{4,3},{5,4},{6,5},{7,6},{8,15},{9,8},{10,9... | collective-permute-start | bytes 589832 | tf_op jit(solution)/shard_map/while/body/eval_jaxpr/ppermute | solution.py:194
  32.9 1.0 collective-permute-done.13.refs_9_
  33.9 2.7 %collective-permute-start.14 = (bf16[256,384]{1,0:T(8,128)(2,1)S(1)}, bf16[256,384]{1,0:T(8,128)(2,1)S(1)}, u32[]{:S(2)}, u32[]{:S(2)}) collective-permute-start(bf16[256,384]{1,0:T(8,128)(2,1)S(1)} %collective-permute-done.13.refs_9_), channel_id=1, source_target_pairs={{0,15},{1,8},{2,9},{3,10},{4,11},{5,12},{6,13},{7,14},{8,7},{9,0},... | collective-permute-start | bytes 589832 | tf_op jit(solution)/shard_map/while/body/eval_jaxpr/ppermute | solution.py:200
  36.6 0.7 collective-permute-done.4.refs_8_
  37.3 6.7 %qkv_partial.3 = (f32[3,272,256]{2,1,0:T(8,128)S(1)}, f32[2,256,128]{2,1,0:T(8,128)S(1)}, f32[256,128]{1,0:T(8,128)S(1)}, bf16[3,1536,256]{2,1,0:T(8,128)(2,1)S(1)}) custom-call(s32[12]{0:T(128)S(1)} %get-tuple-element.275.rows_ref, s32[4]{0:T(128)S(1)} %get-tuple-element.276.late_rows_ref.rows_ref, f32[16,1,384]{2,1,0:T(1,128)S(1)} %copy-done.2, ...), custom_call_target="tpu_custom_call" | custom-call | tf_op jit(solution)/shard_map/while/body/eval_jaxpr/qkv_partial/pallas_call | solution.py:130
  44.1 2.6 %attention_block.1.own_ref = bf16[256,256]{1,0:T(8,128)(2,1)S(1)} custom-call(s32[4]{0:T(128)S(1)} %get-tuple-element.276.late_rows_ref.rows_ref, f32[16,1,384]{2,1,0:T(1,128)S(1)} %copy-done.2, bf16[256,384]{1,0:T(8,128)(2,1)S(1)} %collective-permute-done.5.refs_0_, bf16[256,384]{1,0:T(8,128)(2,1)S(1)} %collective-permute-done.8.refs_1_, ...), custom_call_target="tpu_custom_call" | custom-call | tf_op jit(solution)/shard_map/while/body/eval_jaxpr/attention_block/pallas_call | solution.py:155
  46.8 1.4 collective-permute-start.15
  48.2 5.6 %collective-permute-done.15.other_ref = bf16[256,256]{1,0:T(8,128)(2,1)S(1)} collective-permute-done((bf16[256,256]{1,0:T(8,128)(2,1)S(1)}, bf16[256,256]{1,0:T(8,128)(2,1)S(1)}, u32[]{:S(2)}, u32[]{:S(2)}) %collective-permute-start.15) | collective-permute-done | bytes 131104 | tf_op jit(solution)/shard_map/while/body/eval_jaxpr/ppermute | solution.py:194
  53.8 1.0 projection_block.7
  54.8 1.9 %collective-permute-start.21 = (bf16[256,384]{1,0:T(8,128)(2,1)S(1)}, bf16[256,384]{1,0:T(8,128)(2,1)S(1)}, u32[]{:S(2)}, u32[]{:S(2)}) collective-permute-start(bf16[256,384]{1,0:T(8,128)(2,1)S(1)} %get-tuple-element.249), channel_id=1, source_target_pairs={{0,7},{1,0},{2,1},{3,2},{4,3},{5,4},{6,5},{7,6},{8,15},{9,8},{10,9... | collective-permute-start | bytes 589832 | tf_op jit(solution)/shard_map/while/body/eval_jaxpr/ppermute | solution.py:194
  56.9 1.5 projection_block.6
  58.6 5.0 %collective-permute-done.17 = bf16[256,384]{1,0:T(8,128)(2,1)S(1)} collective-permute-done((bf16[256,384]{1,0:T(8,128)(2,1)S(1)}, bf16[256,384]{1,0:T(8,128)(2,1)S(1)}, u32[]{:S(2)}, u32[]{:S(2)}) %collective-permute-start.17) | collective-permute-done | bytes 196640 | tf_op jit(solution)/shard_map/while/body/eval_jaxpr/ppermute | solution.py:194
  63.8 3.3 %collective-permute-start.22 = (bf16[256,384]{1,0:T(8,128)(2,1)S(1)}, bf16[256,384]{1,0:T(8,128)(2,1)S(1)}, u32[]{:S(2)}, u32[]{:S(2)}) collective-permute-start(bf16[256,384]{1,0:T(8,128)(2,1)S(1)} %add_convert_fusion.17), channel_id=1, source_target_pairs={{0,7},{1,0},{2,1},{3,2},{4,3},{5,4},{6,5},{7,6},{8,15},{9,8},{10,9... | collective-permute-start | bytes 589832 | tf_op jit(solution)/shard_map/while/body/eval_jaxpr/ppermute | solution.py:194
  67.1 3.6 %collective-permute-done.18 = bf16[256,384]{1,0:T(8,128)(2,1)S(1)} collective-permute-done((bf16[256,384]{1,0:T(8,128)(2,1)S(1)}, bf16[256,384]{1,0:T(8,128)(2,1)S(1)}, u32[]{:S(2)}, u32[]{:S(2)}) %collective-permute-start.18) | collective-permute-done | bytes 196640 | tf_op jit(solution)/shard_map/while/body/eval_jaxpr/ppermute | solution.py:194
  71.0 6.7 %collective-permute-done.19 = bf16[256,384]{1,0:T(8,128)(2,1)S(1)} collective-permute-done((bf16[256,384]{1,0:T(8,128)(2,1)S(1)}, bf16[256,384]{1,0:T(8,128)(2,1)S(1)}, u32[]{:S(2)}, u32[]{:S(2)}) %collective-permute-start.19) | collective-permute-done | bytes 196640 | tf_op jit(solution)/shard_map/while/body/eval_jaxpr/ppermute | solution.py:194
  77.9 2.8 %collective-permute-done.23 = bf16[256,384]{1,0:T(8,128)(2,1)S(1)} collective-permute-done((bf16[256,384]{1,0:T(8,128)(2,1)S(1)}, bf16[256,384]{1,0:T(8,128)(2,1)S(1)}, u32[]{:S(2)}, u32[]{:S(2)}) %collective-permute-start.23) | collective-permute-done | bytes 196640 | tf_op jit(solution)/shard_map/while/body/eval_jaxpr/ppermute | solution.py:212
  80.7 8.0 %collective-permute-done.20 = bf16[256,384]{1,0:T(8,128)(2,1)S(1)} collective-permute-done((bf16[256,384]{1,0:T(8,128)(2,1)S(1)}, bf16[256,384]{1,0:T(8,128)(2,1)S(1)}, u32[]{:S(2)}, u32[]{:S(2)}) %collective-permute-start.20) | collective-permute-done | bytes 196640 | tf_op jit(solution)/shard_map/while/body/eval_jaxpr/ppermute | solution.py:212
  88.9 3.2 %collective-permute-start.1 = (bf16[256,384]{1,0:T(8,128)(2,1)S(1)}, bf16[256,384]{1,0:T(8,128)(2,1)S(1)}, u32[]{:S(2)}, u32[]{:S(2)}) collective-permute-start(bf16[256,384]{1,0:T(8,128)(2,1)S(1)} %get-tuple-element.263.refs_0_), channel_id=1, source_target_pairs={{0,7},{1,0},{2,1},{3,2},{4,3},{5,4},{6,5},{7,6},{8,15},{9,8},{10,9... | collective-permute-start | bytes 589832 | tf_op jit(solution)/shard_map/while/body/eval_jaxpr/ppermute | solution.py:194
  92.1 1.6 collective-permute-start.2
  93.7 1.5 constant_dynamic-slice_fusion.2
  95.2 0.5 collective-permute-done.refs_2_
  95.7 1.6 collective-permute-done.1.refs_3_
  97.3 2.6 %collective-permute-done.2.refs_1_ = bf16[256,384]{1,0:T(8,128)(2,1)S(1)} collective-permute-done((bf16[256,384]{1,0:T(8,128)(2,1)S(1)}, bf16[256,384]{1,0:T(8,128)(2,1)S(1)}, u32[]{:S(2)}, u32[]{:S(2)}) %collective-permute-start.2) | collective-permute-done | bytes 196640 | tf_op jit(solution)/shard_map/while/body/eval_jaxpr/ppermute | solution.py:194
  99.9 1.6 collective-permute-start.16
  101.5 1.0 collective-permute-start.9
  102.5 1.0 collective-permute-start.6
  103.6 2.2 %collective-permute-start.12 = (bf16[256,384]{1,0:T(8,128)(2,1)S(1)}, bf16[256,384]{1,0:T(8,128)(2,1)S(1)}, u32[]{:S(2)}, u32[]{:S(2)}) collective-permute-start(bf16[256,384]{1,0:T(8,128)(2,1)S(1)} %collective-permute-done.1.refs_3_), channel_id=1, source_target_pairs={{0,7},{1,0},{2,1},{3,2},{4,3},{5,4},{6,5},{7,6},{8,15},{9,8},{10,9... | collective-permute-start | bytes 589832 | tf_op jit(solution)/shard_map/while/body/eval_jaxpr/ppermute | solution.py:194
  105.8 3.4 %collective-permute-done.9.refs_7_ = bf16[256,384]{1,0:T(8,128)(2,1)S(1)} collective-permute-done((bf16[256,384]{1,0:T(8,128)(2,1)S(1)}, bf16[256,384]{1,0:T(8,128)(2,1)S(1)}, u32[]{:S(2)}, u32[]{:S(2)}) %collective-permute-start.9) | collective-permute-done | bytes 196640 | tf_op jit(solution)/shard_map/while/body/eval_jaxpr/ppermute | solution.py:194
  109.1 2.3 %collective-permute-start.10 = (bf16[256,384]{1,0:T(8,128)(2,1)S(1)}, bf16[256,384]{1,0:T(8,128)(2,1)S(1)}, u32[]{:S(2)}, u32[]{:S(2)}) collective-permute-start(bf16[256,384]{1,0:T(8,128)(2,1)S(1)} %collective-permute-done.9.refs_7_), channel_id=1, source_target_pairs={{0,7},{1,0},{2,1},{3,2},{4,3},{5,4},{6,5},{7,6},{8,15},{9,8},{10,9... | collective-permute-start | bytes 589832 | tf_op jit(solution)/shard_map/while/body/eval_jaxpr/ppermute | solution.py:194
  111.5 1.8 %collective-permute-done.12.refs_5_ = bf16[256,384]{1,0:T(8,128)(2,1)S(1)} collective-permute-done((bf16[256,384]{1,0:T(8,128)(2,1)S(1)}, bf16[256,384]{1,0:T(8,128)(2,1)S(1)}, u32[]{:S(2)}, u32[]{:S(2)}) %collective-permute-start.12) | collective-permute-done | bytes 196640 | tf_op jit(solution)/shard_map/while/body/eval_jaxpr/ppermute | solution.py:194
  113.3 2.3 %collective-permute-start.13 = (bf16[256,384]{1,0:T(8,128)(2,1)S(1)}, bf16[256,384]{1,0:T(8,128)(2,1)S(1)}, u32[]{:S(2)}, u32[]{:S(2)}) collective-permute-start(bf16[256,384]{1,0:T(8,128)(2,1)S(1)} %collective-permute-done.12.refs_5_), channel_id=1, source_target_pairs={{0,7},{1,0},{2,1},{3,2},{4,3},{5,4},{6,5},{7,6},{8,15},{9,8},{10,9... | collective-permute-start | bytes 589832 | tf_op jit(solution)/shard_map/while/body/eval_jaxpr/ppermute | solution.py:194
  115.7 3.6 %collective-permute-start.11 = (bf16[256,384]{1,0:T(8,128)(2,1)S(1)}, bf16[256,384]{1,0:T(8,128)(2,1)S(1)}, u32[]{:S(2)}, u32[]{:S(2)}) collective-permute-start(bf16[256,384]{1,0:T(8,128)(2,1)S(1)} %collective-permute-done.10.refs_11_), channel_id=1, source_target_pairs={{0,7},{1,0},{2,1},{3,2},{4,3},{5,4},{6,5},{7,6},{8,15},{9,8},{10,9... | collective-permute-start | bytes 589832 | tf_op jit(solution)/shard_map/while/body/eval_jaxpr/ppermute | solution.py:194
  119.3 3.3 %collective-permute-start.14 = (bf16[256,384]{1,0:T(8,128)(2,1)S(1)}, bf16[256,384]{1,0:T(8,128)(2,1)S(1)}, u32[]{:S(2)}, u32[]{:S(2)}) collective-permute-start(bf16[256,384]{1,0:T(8,128)(2,1)S(1)} %collective-permute-done.13.refs_9_), channel_id=1, source_target_pairs={{0,15},{1,8},{2,9},{3,10},{4,11},{5,12},{6,13},{7,14},{8,7},{9,0},... | collective-permute-start | bytes 589832 | tf_op jit(solution)/shard_map/while/body/eval_jaxpr/ppermute | solution.py:200
  122.6 6.7 %qkv_partial.3 = (f32[3,272,256]{2,1,0:T(8,128)S(1)}, f32[2,256,128]{2,1,0:T(8,128)S(1)}, f32[256,128]{1,0:T(8,128)S(1)}, bf16[3,1536,256]{2,1,0:T(8,128)(2,1)S(1)}) custom-call(s32[12]{0:T(128)S(1)} %get-tuple-element.275.rows_ref, s32[4]{0:T(128)S(1)} %get-tuple-element.276.late_rows_ref.rows_ref, f32[16,1,384]{2,1,0:T(1,128)S(1)} %copy-done.2, ...), custom_call_target="tpu_custom_call" | custom-call | tf_op jit(solution)/shard_map/while/body/eval_jaxpr/qkv_partial/pallas_call | solution.py:130
  129.5 2.6 %attention_block.1.own_ref = bf16[256,256]{1,0:T(8,128)(2,1)S(1)} custom-call(s32[4]{0:T(128)S(1)} %get-tuple-element.276.late_rows_ref.rows_ref, f32[16,1,384]{2,1,0:T(1,128)S(1)} %copy-done.2, bf16[256,384]{1,0:T(8,128)(2,1)S(1)} %collective-permute-done.5.refs_0_, bf16[256,384]{1,0:T(8,128)(2,1)S(1)} %collective-permute-done.8.refs_1_, ...), custom_call_target="tpu_custom_call" | custom-call | tf_op jit(solution)/shard_map/while/body/eval_jaxpr/attention_block/pallas_call | solution.py:155
  132.1 1.5 collective-permute-start.15
  133.6 3.5 %collective-permute-done.15.other_ref = bf16[256,256]{1,0:T(8,128)(2,1)S(1)} collective-permute-done((bf16[256,256]{1,0:T(8,128)(2,1)S(1)}, bf16[256,256]{1,0:T(8,128)(2,1)S(1)}, u32[]{:S(2)}, u32[]{:S(2)}) %collective-permute-start.15) | collective-permute-done | bytes 131104 | tf_op jit(solution)/shard_map/while/body/eval_jaxpr/ppermute | solution.py:194
  137.2 1.0 projection_block.7
  138.1 3.2 %collective-permute-start.21 = (bf16[256,384]{1,0:T(8,128)(2,1)S(1)}, bf16[256,384]{1,0:T(8,128)(2,1)S(1)}, u32[]{:S(2)}, u32[]{:S(2)}) collective-permute-start(bf16[256,384]{1,0:T(8,128)(2,1)S(1)} %get-tuple-element.249), channel_id=1, source_target_pairs={{0,7},{1,0},{2,1},{3,2},{4,3},{5,4},{6,5},{7,6},{8,15},{9,8},{10,9... | collective-permute-start | bytes 589832 | tf_op jit(solution)/shard_map/while/body/eval_jaxpr/ppermute | solution.py:194
  141.3 1.5 projection_block.6
  143.0 6.4 %collective-permute-done.17 = bf16[256,384]{1,0:T(8,128)(2,1)S(1)} collective-permute-done((bf16[256,384]{1,0:T(8,128)(2,1)S(1)}, bf16[256,384]{1,0:T(8,128)(2,1)S(1)}, u32[]{:S(2)}, u32[]{:S(2)}) %collective-permute-start.17) | collective-permute-done | bytes 196640 | tf_op jit(solution)/shard_map/while/body/eval_jaxpr/ppermute | solution.py:194
  149.6 3.3 %collective-permute-start.22 = (bf16[256,384]{1,0:T(8,128)(2,1)S(1)}, bf16[256,384]{1,0:T(8,128)(2,1)S(1)}, u32[]{:S(2)}, u32[]{:S(2)}) collective-permute-start(bf16[256,384]{1,0:T(8,128)(2,1)S(1)} %add_convert_fusion.17), channel_id=1, source_target_pairs={{0,7},{1,0},{2,1},{3,2},{4,3},{5,4},{6,5},{7,6},{8,15},{9,8},{10,9... | collective-permute-start | bytes 589832 | tf_op jit(solution)/shard_map/while/body/eval_jaxpr/ppermute | solution.py:194
  152.9 3.9 %collective-permute-done.18 = bf16[256,384]{1,0:T(8,128)(2,1)S(1)} collective-permute-done((bf16[256,384]{1,0:T(8,128)(2,1)S(1)}, bf16[256,384]{1,0:T(8,128)(2,1)S(1)}, u32[]{:S(2)}, u32[]{:S(2)}) %collective-permute-start.18) | collective-permute-done | bytes 196640 | tf_op jit(solution)/shard_map/while/body/eval_jaxpr/ppermute | solution.py:194
  157.1 7.1 %collective-permute-done.19 = bf16[256,384]{1,0:T(8,128)(2,1)S(1)} collective-permute-done((bf16[256,384]{1,0:T(8,128)(2,1)S(1)}, bf16[256,384]{1,0:T(8,128)(2,1)S(1)}, u32[]{:S(2)}, u32[]{:S(2)}) %collective-permute-start.19) | collective-permute-done | bytes 196640 | tf_op jit(solution)/shard_map/while/body/eval_jaxpr/ppermute | solution.py:194
  164.4 2.3 %collective-permute-done.23 = bf16[256,384]{1,0:T(8,128)(2,1)S(1)} collective-permute-done((bf16[256,384]{1,0:T(8,128)(2,1)S(1)}, bf16[256,384]{1,0:T(8,128)(2,1)S(1)}, u32[]{:S(2)}, u32[]{:S(2)}) %collective-permute-start.23) | collective-permute-done | bytes 196640 | tf_op jit(solution)/shard_map/while/body/eval_jaxpr/ppermute | solution.py:212
  166.7 8.5 %collective-permute-done.20 = bf16[256,384]{1,0:T(8,128)(2,1)S(1)} collective-permute-done((bf16[256,384]{1,0:T(8,128)(2,1)S(1)}, bf16[256,384]{1,0:T(8,128)(2,1)S(1)}, u32[]{:S(2)}, u32[]{:S(2)}) %collective-permute-start.20) | collective-permute-done | bytes 196640 | tf_op jit(solution)/shard_map/while/body/eval_jaxpr/ppermute | solution.py:212
  175.3 0.7 copy-done.1
  (80 shorter events, 3.1 us)
Async XLA Ops:
  1.2 36.0 %copy-start.2 = (f32[16,1,384]{2,1,0:T(1,128)S(1)}, f32[16,1,384]{2,1,0:T(1,128)}, u32[]{:S(2)}) copy-start(f32[16,1,384]{2,1,0:T(1,128)} %get-tuple-element.277.gain_ref) | copy-start | bytes 73732 | tf_op jit(solution)/shard_map/while
  1.2 9.1 %collective-permute-start = (bf16[256,384]{1,0:T(8,128)(2,1)S(1)}, bf16[256,384]{1,0:T(8,128)(2,1)S(1)}, u32[]{:S(2)}, u32[]{:S(2)}) collective-permute-start(bf16[256,384]{1,0:T(8,128)(2,1)S(1)} %get-tuple-element.263.refs_0_), channel_id=1, source_target_pairs={{0,1},{1,2},{2,3},{3,4},{4,5},{5,6},{6,7},{7,0},{8,9},{9,10},{10,1... | collective-permute-start | bytes 589832 | tf_op jit(solution)/shard_map/while/body/eval_jaxpr/ppermute | solution.py:194
  1.4 8.8 %collective-permute-start.1 = (bf16[256,384]{1,0:T(8,128)(2,1)S(1)}, bf16[256,384]{1,0:T(8,128)(2,1)S(1)}, u32[]{:S(2)}, u32[]{:S(2)}) collective-permute-start(bf16[256,384]{1,0:T(8,128)(2,1)S(1)} %get-tuple-element.263.refs_0_), channel_id=1, source_target_pairs={{0,7},{1,0},{2,1},{3,2},{4,3},{5,4},{6,5},{7,6},{8,15},{9,8},{10,9... | collective-permute-start | bytes 589832 | tf_op jit(solution)/shard_map/while/body/eval_jaxpr/ppermute | solution.py:194
  5.5 6.4 %collective-permute-start.2 = (bf16[256,384]{1,0:T(8,128)(2,1)S(1)}, bf16[256,384]{1,0:T(8,128)(2,1)S(1)}, u32[]{:S(2)}, u32[]{:S(2)}) collective-permute-start(bf16[256,384]{1,0:T(8,128)(2,1)S(1)} %get-tuple-element.263.refs_0_), channel_id=1, source_target_pairs={{0,8},{8,0},{1,9},{9,1},{2,10},{10,2},{3,11},{11,3},{4,12},{12,4},... | collective-permute-start | bytes 589832 | tf_op jit(solution)/shard_map/while/body/eval_jaxpr/ppermute | solution.py:194
  11.8 42.0 %collective-permute-start.16 = (bf16[256,3072]{1,0:T(8,128)(2,1)S(1)}, bf16[256,3072]{1,0:T(8,128)(2,1)S(1)}, u32[]{:S(2)}, u32[]{:S(2)}) collective-permute-start(bf16[256,3072]{1,0:T(8,128)(2,1)S(1)} %constant_dynamic-slice_fusion.2), channel_id=1, source_target_pairs={{0,8},{8,0},{1,9},{9,1},{2,10},{10,2},{3,11},{11,3},{4,12},{12,4},... | collective-permute-start | bytes 4718600 | tf_op jit(solution)/shard_map/while/body/eval_jaxpr/ppermute | solution.py:194
  13.4 7.8 %collective-permute-start.9 = (bf16[256,384]{1,0:T(8,128)(2,1)S(1)}, bf16[256,384]{1,0:T(8,128)(2,1)S(1)}, u32[]{:S(2)}, u32[]{:S(2)}) collective-permute-start(bf16[256,384]{1,0:T(8,128)(2,1)S(1)} %collective-permute-done.2.refs_1_), channel_id=1, source_target_pairs={{0,7},{1,0},{2,1},{3,2},{4,3},{5,4},{6,5},{7,6},{8,15},{9,8},{10,9... | collective-permute-start | bytes 589832 | tf_op jit(solution)/shard_map/while/body/eval_jaxpr/ppermute | solution.py:194
  15.1 9.0 %collective-permute-start.6 = (bf16[256,384]{1,0:T(8,128)(2,1)S(1)}, bf16[256,384]{1,0:T(8,128)(2,1)S(1)}, u32[]{:S(2)}, u32[]{:S(2)}) collective-permute-start(bf16[256,384]{1,0:T(8,128)(2,1)S(1)} %collective-permute-done.2.refs_1_), channel_id=1, source_target_pairs={{0,1},{1,2},{2,3},{3,4},{4,5},{5,6},{6,7},{7,0},{8,9},{9,10},{10,1... | collective-permute-start | bytes 589832 | tf_op jit(solution)/shard_map/while/body/eval_jaxpr/ppermute | solution.py:194
  15.4 10.0 %collective-permute-start.12 = (bf16[256,384]{1,0:T(8,128)(2,1)S(1)}, bf16[256,384]{1,0:T(8,128)(2,1)S(1)}, u32[]{:S(2)}, u32[]{:S(2)}) collective-permute-start(bf16[256,384]{1,0:T(8,128)(2,1)S(1)} %collective-permute-done.1.refs_3_), channel_id=1, source_target_pairs={{0,7},{1,0},{2,1},{3,2},{4,3},{5,4},{6,5},{7,6},{8,15},{9,8},{10,9... | collective-permute-start | bytes 589832 | tf_op jit(solution)/shard_map/while/body/eval_jaxpr/ppermute | solution.py:194
  18.3 10.0 %collective-permute-start.3 = (bf16[256,384]{1,0:T(8,128)(2,1)S(1)}, bf16[256,384]{1,0:T(8,128)(2,1)S(1)}, u32[]{:S(2)}, u32[]{:S(2)}) collective-permute-start(bf16[256,384]{1,0:T(8,128)(2,1)S(1)} %collective-permute-done.refs_2_), channel_id=1, source_target_pairs={{0,1},{1,2},{2,3},{3,4},{4,5},{5,6},{6,7},{7,0},{8,9},{9,10},{10,1... | collective-permute-start | bytes 589832 | tf_op jit(solution)/shard_map/while/body/eval_jaxpr/ppermute | solution.py:194
  21.2 8.4 %collective-permute-start.10 = (bf16[256,384]{1,0:T(8,128)(2,1)S(1)}, bf16[256,384]{1,0:T(8,128)(2,1)S(1)}, u32[]{:S(2)}, u32[]{:S(2)}) collective-permute-start(bf16[256,384]{1,0:T(8,128)(2,1)S(1)} %collective-permute-done.9.refs_7_), channel_id=1, source_target_pairs={{0,7},{1,0},{2,1},{3,2},{4,3},{5,4},{6,5},{7,6},{8,15},{9,8},{10,9... | collective-permute-start | bytes 589832 | tf_op jit(solution)/shard_map/while/body/eval_jaxpr/ppermute | solution.py:194
  24.1 8.8 %collective-permute-start.7 = (bf16[256,384]{1,0:T(8,128)(2,1)S(1)}, bf16[256,384]{1,0:T(8,128)(2,1)S(1)}, u32[]{:S(2)}, u32[]{:S(2)}) collective-permute-start(bf16[256,384]{1,0:T(8,128)(2,1)S(1)} %collective-permute-done.6.refs_6_), channel_id=1, source_target_pairs={{0,1},{1,2},{2,3},{3,4},{4,5},{5,6},{6,7},{7,0},{8,9},{9,10},{10,1... | collective-permute-start | bytes 589832 | tf_op jit(solution)/shard_map/while/body/eval_jaxpr/ppermute | solution.py:194
  25.5 8.4 %collective-permute-start.13 = (bf16[256,384]{1,0:T(8,128)(2,1)S(1)}, bf16[256,384]{1,0:T(8,128)(2,1)S(1)}, u32[]{:S(2)}, u32[]{:S(2)}) collective-permute-start(bf16[256,384]{1,0:T(8,128)(2,1)S(1)} %collective-permute-done.12.refs_5_), channel_id=1, source_target_pairs={{0,7},{1,0},{2,1},{3,2},{4,3},{5,4},{6,5},{7,6},{8,15},{9,8},{10,9... | collective-permute-start | bytes 589832 | tf_op jit(solution)/shard_map/while/body/eval_jaxpr/ppermute | solution.py:194
  28.3 9.0 %collective-permute-start.4 = (bf16[256,384]{1,0:T(8,128)(2,1)S(1)}, bf16[256,384]{1,0:T(8,128)(2,1)S(1)}, u32[]{:S(2)}, u32[]{:S(2)}) collective-permute-start(bf16[256,384]{1,0:T(8,128)(2,1)S(1)} %collective-permute-done.3.refs_4_), channel_id=1, source_target_pairs={{0,1},{1,2},{2,3},{3,4},{4,5},{5,6},{6,7},{7,0},{8,9},{9,10},{10,1... | collective-permute-start | bytes 589832 | tf_op jit(solution)/shard_map/while/body/eval_jaxpr/ppermute | solution.py:194
  29.7 14.3 %collective-permute-start.11 = (bf16[256,384]{1,0:T(8,128)(2,1)S(1)}, bf16[256,384]{1,0:T(8,128)(2,1)S(1)}, u32[]{:S(2)}, u32[]{:S(2)}) collective-permute-start(bf16[256,384]{1,0:T(8,128)(2,1)S(1)} %collective-permute-done.10.refs_11_), channel_id=1, source_target_pairs={{0,7},{1,0},{2,1},{3,2},{4,3},{5,4},{6,5},{7,6},{8,15},{9,8},{10,9... | collective-permute-start | bytes 589832 | tf_op jit(solution)/shard_map/while/body/eval_jaxpr/ppermute | solution.py:194
  32.9 11.1 %collective-permute-start.8 = (bf16[256,384]{1,0:T(8,128)(2,1)S(1)}, bf16[256,384]{1,0:T(8,128)(2,1)S(1)}, u32[]{:S(2)}, u32[]{:S(2)}) collective-permute-start(bf16[256,384]{1,0:T(8,128)(2,1)S(1)} %collective-permute-done.7.refs_10_), channel_id=1, source_target_pairs={{0,1},{1,2},{2,3},{3,4},{4,5},{5,6},{6,7},{7,0},{8,9},{9,10},{10,1... | collective-permute-start | bytes 589832 | tf_op jit(solution)/shard_map/while/body/eval_jaxpr/ppermute | solution.py:194
  33.9 10.1 %collective-permute-start.14 = (bf16[256,384]{1,0:T(8,128)(2,1)S(1)}, bf16[256,384]{1,0:T(8,128)(2,1)S(1)}, u32[]{:S(2)}, u32[]{:S(2)}) collective-permute-start(bf16[256,384]{1,0:T(8,128)(2,1)S(1)} %collective-permute-done.13.refs_9_), channel_id=1, source_target_pairs={{0,15},{1,8},{2,9},{3,10},{4,11},{5,12},{6,13},{7,14},{8,7},{9,0},... | collective-permute-start | bytes 589832 | tf_op jit(solution)/shard_map/while/body/eval_jaxpr/ppermute | solution.py:200
  37.2 6.9 %collective-permute-start.5 = (bf16[256,384]{1,0:T(8,128)(2,1)S(1)}, bf16[256,384]{1,0:T(8,128)(2,1)S(1)}, u32[]{:S(2)}, u32[]{:S(2)}) collective-permute-start(bf16[256,384]{1,0:T(8,128)(2,1)S(1)} %collective-permute-done.4.refs_8_), channel_id=1, source_target_pairs={{0,1},{1,2},{2,3},{3,4},{4,5},{5,6},{6,7},{7,0},{8,9},{9,10},{10,1... | collective-permute-start | bytes 589832 | tf_op jit(solution)/shard_map/while/body/eval_jaxpr/ppermute | solution.py:194
  37.3 6.9 %copy-start.3 = (f32[1,2,128]{2,1,0:T(2,128)S(1)}, f32[1,2,128]{2,1,0:T(2,128)}, u32[]{:S(2)}) copy-start(f32[1,2,128]{2,1,0:T(2,128)} %get-tuple-element.279) | copy-start | bytes 3076 | tf_op jit(solution)/shard_map/while
  43.9 9.9 %copy-start = (bf16[256,6144]{1,0:T(8,128)(2,1)S(1)}, bf16[256,6144]{1,0:T(8,128)(2,1)}, u32[]{:S(2)}) copy-start(bf16[256,6144]{1,0:T(8,128)(2,1)} %get-tuple-element.241.w_own_ref) | copy-start | bytes 9437188 | tf_op jit(solution)/shard_map/while
  46.8 7.0 %collective-permute-start.15 = (bf16[256,256]{1,0:T(8,128)(2,1)S(1)}, bf16[256,256]{1,0:T(8,128)(2,1)S(1)}, u32[]{:S(2)}, u32[]{:S(2)}) collective-permute-start(bf16[256,256]{1,0:T(8,128)(2,1)S(1)} %attention_block.1.own_ref), channel_id=1, source_target_pairs={{0,8},{8,0},{1,9},{9,1},{2,10},{10,2},{3,11},{11,3},{4,12},{12,4},... | collective-permute-start | bytes 393224 | tf_op jit(solution)/shard_map/while/body/eval_jaxpr/ppermute | solution.py:194
  54.8 8.9 %collective-permute-start.21 = (bf16[256,384]{1,0:T(8,128)(2,1)S(1)}, bf16[256,384]{1,0:T(8,128)(2,1)S(1)}, u32[]{:S(2)}, u32[]{:S(2)}) collective-permute-start(bf16[256,384]{1,0:T(8,128)(2,1)S(1)} %get-tuple-element.249), channel_id=1, source_target_pairs={{0,7},{1,0},{2,1},{3,2},{4,3},{5,4},{6,5},{7,6},{8,15},{9,8},{10,9... | collective-permute-start | bytes 589832 | tf_op jit(solution)/shard_map/while/body/eval_jaxpr/ppermute | solution.py:194
  56.7 6.9 %collective-permute-start.17 = (bf16[256,384]{1,0:T(8,128)(2,1)S(1)}, bf16[256,384]{1,0:T(8,128)(2,1)S(1)}, u32[]{:S(2)}, u32[]{:S(2)}) collective-permute-start(bf16[256,384]{1,0:T(8,128)(2,1)S(1)} %get-tuple-element.246), channel_id=1, source_target_pairs={{0,1},{1,2},{2,3},{3,4},{4,5},{5,6},{6,7},{7,0},{8,9},{9,10},{10,1... | collective-permute-start | bytes 589832 | tf_op jit(solution)/shard_map/while/body/eval_jaxpr/ppermute | solution.py:194
  58.5 19.4 %collective-permute-start.24 = (bf16[256,384]{1,0:T(8,128)(2,1)S(1)}, bf16[256,384]{1,0:T(8,128)(2,1)S(1)}, u32[]{:S(2)}, u32[]{:S(2)}) collective-permute-start(bf16[256,384]{1,0:T(8,128)(2,1)S(1)} %add_convert_fusion.19), channel_id=1, source_target_pairs={{0,16},{1,17},{2,18},{3,19},{4,20},{5,21},{6,22},{7,23},{8,24},{9,... | collective-permute-start | bytes 589832 | tf_op jit(solution)/shard_map/while/body/eval_jaxpr/ppermute | solution.py:212
  63.6 7.1 %collective-permute-start.18 = (bf16[256,384]{1,0:T(8,128)(2,1)S(1)}, bf16[256,384]{1,0:T(8,128)(2,1)S(1)}, u32[]{:S(2)}, u32[]{:S(2)}) collective-permute-start(bf16[256,384]{1,0:T(8,128)(2,1)S(1)} %add_convert_fusion.14), channel_id=1, source_target_pairs={{0,1},{1,2},{2,3},{3,4},{4,5},{5,6},{6,7},{7,0},{8,9},{9,10},{10,1... | collective-permute-start | bytes 589832 | tf_op jit(solution)/shard_map/while/body/eval_jaxpr/ppermute | solution.py:194
  63.8 7.1 %collective-permute-start.22 = (bf16[256,384]{1,0:T(8,128)(2,1)S(1)}, bf16[256,384]{1,0:T(8,128)(2,1)S(1)}, u32[]{:S(2)}, u32[]{:S(2)}) collective-permute-start(bf16[256,384]{1,0:T(8,128)(2,1)S(1)} %add_convert_fusion.17), channel_id=1, source_target_pairs={{0,7},{1,0},{2,1},{3,2},{4,3},{5,4},{6,5},{7,6},{8,15},{9,8},{10,9... | collective-permute-start | bytes 589832 | tf_op jit(solution)/shard_map/while/body/eval_jaxpr/ppermute | solution.py:194
  70.8 7.0 %collective-permute-start.19 = (bf16[256,384]{1,0:T(8,128)(2,1)S(1)}, bf16[256,384]{1,0:T(8,128)(2,1)S(1)}, u32[]{:S(2)}, u32[]{:S(2)}) collective-permute-start(bf16[256,384]{1,0:T(8,128)(2,1)S(1)} %add_convert_fusion.15), channel_id=1, source_target_pairs={{0,1},{1,2},{2,3},{3,4},{4,5},{5,6},{6,7},{7,0},{8,9},{9,10},{10,1... | collective-permute-start | bytes 589832 | tf_op jit(solution)/shard_map/while/body/eval_jaxpr/ppermute | solution.py:194
  70.9 9.7 %collective-permute-start.23 = (bf16[256,384]{1,0:T(8,128)(2,1)S(1)}, bf16[256,384]{1,0:T(8,128)(2,1)S(1)}, u32[]{:S(2)}, u32[]{:S(2)}) collective-permute-start(bf16[256,384]{1,0:T(8,128)(2,1)S(1)} %add_convert_fusion.18), channel_id=1, source_target_pairs={{0,23},{1,16},{2,17},{3,18},{4,19},{5,20},{6,21},{7,22},{8,31},{9,... | collective-permute-start | bytes 589832 | tf_op jit(solution)/shard_map/while/body/eval_jaxpr/ppermute | solution.py:212
  77.8 10.9 %collective-permute-start.20 = (bf16[256,384]{1,0:T(8,128)(2,1)S(1)}, bf16[256,384]{1,0:T(8,128)(2,1)S(1)}, u32[]{:S(2)}, u32[]{:S(2)}) collective-permute-start(bf16[256,384]{1,0:T(8,128)(2,1)S(1)} %add_convert_fusion.16), channel_id=1, source_target_pairs={{0,17},{1,18},{2,19},{3,20},{4,21},{5,22},{6,23},{7,16},{8,25},{9,... | collective-permute-start | bytes 589832 | tf_op jit(solution)/shard_map/while/body/eval_jaxpr/ppermute | solution.py:212
  88.8 33.8 %copy-start.2 = (f32[16,1,384]{2,1,0:T(1,128)S(1)}, f32[16,1,384]{2,1,0:T(1,128)}, u32[]{:S(2)}) copy-start(f32[16,1,384]{2,1,0:T(1,128)} %get-tuple-element.277.gain_ref) | copy-start | bytes 73732 | tf_op jit(solution)/shard_map/while
  88.8 7.0 %collective-permute-start = (bf16[256,384]{1,0:T(8,128)(2,1)S(1)}, bf16[256,384]{1,0:T(8,128)(2,1)S(1)}, u32[]{:S(2)}, u32[]{:S(2)}) collective-permute-start(bf16[256,384]{1,0:T(8,128)(2,1)S(1)} %get-tuple-element.263.refs_0_), channel_id=1, source_target_pairs={{0,1},{1,2},{2,3},{3,4},{4,5},{5,6},{6,7},{7,0},{8,9},{9,10},{10,1... | collective-permute-start | bytes 589832 | tf_op jit(solution)/shard_map/while/body/eval_jaxpr/ppermute | solution.py:194
  88.9 8.4 %collective-permute-start.1 = (bf16[256,384]{1,0:T(8,128)(2,1)S(1)}, bf16[256,384]{1,0:T(8,128)(2,1)S(1)}, u32[]{:S(2)}, u32[]{:S(2)}) collective-permute-start(bf16[256,384]{1,0:T(8,128)(2,1)S(1)} %get-tuple-element.263.refs_0_), channel_id=1, source_target_pairs={{0,7},{1,0},{2,1},{3,2},{4,3},{5,4},{6,5},{7,6},{8,15},{9,8},{10,9... | collective-permute-start | bytes 589832 | tf_op jit(solution)/shard_map/while/body/eval_jaxpr/ppermute | solution.py:194
  92.1 7.8 %collective-permute-start.2 = (bf16[256,384]{1,0:T(8,128)(2,1)S(1)}, bf16[256,384]{1,0:T(8,128)(2,1)S(1)}, u32[]{:S(2)}, u32[]{:S(2)}) collective-permute-start(bf16[256,384]{1,0:T(8,128)(2,1)S(1)} %get-tuple-element.263.refs_0_), channel_id=1, source_target_pairs={{0,8},{8,0},{1,9},{9,1},{2,10},{10,2},{3,11},{11,3},{4,12},{12,4},... | collective-permute-start | bytes 589832 | tf_op jit(solution)/shard_map/while/body/eval_jaxpr/ppermute | solution.py:194
  99.9 37.2 %collective-permute-start.16 = (bf16[256,3072]{1,0:T(8,128)(2,1)S(1)}, bf16[256,3072]{1,0:T(8,128)(2,1)S(1)}, u32[]{:S(2)}, u32[]{:S(2)}) collective-permute-start(bf16[256,3072]{1,0:T(8,128)(2,1)S(1)} %constant_dynamic-slice_fusion.2), channel_id=1, source_target_pairs={{0,8},{8,0},{1,9},{9,1},{2,10},{10,2},{3,11},{11,3},{4,12},{12,4},... | collective-permute-start | bytes 4718600 | tf_op jit(solution)/shard_map/while/body/eval_jaxpr/ppermute | solution.py:194
  101.5 7.6 %collective-permute-start.9 = (bf16[256,384]{1,0:T(8,128)(2,1)S(1)}, bf16[256,384]{1,0:T(8,128)(2,1)S(1)}, u32[]{:S(2)}, u32[]{:S(2)}) collective-permute-start(bf16[256,384]{1,0:T(8,128)(2,1)S(1)} %collective-permute-done.2.refs_1_), channel_id=1, source_target_pairs={{0,7},{1,0},{2,1},{3,2},{4,3},{5,4},{6,5},{7,6},{8,15},{9,8},{10,9... | collective-permute-start | bytes 589832 | tf_op jit(solution)/shard_map/while/body/eval_jaxpr/ppermute | solution.py:194
  102.5 9.0 %collective-permute-start.6 = (bf16[256,384]{1,0:T(8,128)(2,1)S(1)}, bf16[256,384]{1,0:T(8,128)(2,1)S(1)}, u32[]{:S(2)}, u32[]{:S(2)}) collective-permute-start(bf16[256,384]{1,0:T(8,128)(2,1)S(1)} %collective-permute-done.2.refs_1_), channel_id=1, source_target_pairs={{0,1},{1,2},{2,3},{3,4},{4,5},{5,6},{6,7},{7,0},{8,9},{9,10},{10,1... | collective-permute-start | bytes 589832 | tf_op jit(solution)/shard_map/while/body/eval_jaxpr/ppermute | solution.py:194
  103.6 9.8 %collective-permute-start.12 = (bf16[256,384]{1,0:T(8,128)(2,1)S(1)}, bf16[256,384]{1,0:T(8,128)(2,1)S(1)}, u32[]{:S(2)}, u32[]{:S(2)}) collective-permute-start(bf16[256,384]{1,0:T(8,128)(2,1)S(1)} %collective-permute-done.1.refs_3_), channel_id=1, source_target_pairs={{0,7},{1,0},{2,1},{3,2},{4,3},{5,4},{6,5},{7,6},{8,15},{9,8},{10,9... | collective-permute-start | bytes 589832 | tf_op jit(solution)/shard_map/while/body/eval_jaxpr/ppermute | solution.py:194
  105.8 9.9 %collective-permute-start.3 = (bf16[256,384]{1,0:T(8,128)(2,1)S(1)}, bf16[256,384]{1,0:T(8,128)(2,1)S(1)}, u32[]{:S(2)}, u32[]{:S(2)}) collective-permute-start(bf16[256,384]{1,0:T(8,128)(2,1)S(1)} %collective-permute-done.refs_2_), channel_id=1, source_target_pairs={{0,1},{1,2},{2,3},{3,4},{4,5},{5,6},{6,7},{7,0},{8,9},{9,10},{10,1... | collective-permute-start | bytes 589832 | tf_op jit(solution)/shard_map/while/body/eval_jaxpr/ppermute | solution.py:194
  109.1 6.6 %collective-permute-start.10 = (bf16[256,384]{1,0:T(8,128)(2,1)S(1)}, bf16[256,384]{1,0:T(8,128)(2,1)S(1)}, u32[]{:S(2)}, u32[]{:S(2)}) collective-permute-start(bf16[256,384]{1,0:T(8,128)(2,1)S(1)} %collective-permute-done.9.refs_7_), channel_id=1, source_target_pairs={{0,7},{1,0},{2,1},{3,2},{4,3},{5,4},{6,5},{7,6},{8,15},{9,8},{10,9... | collective-permute-start | bytes 589832 | tf_op jit(solution)/shard_map/while/body/eval_jaxpr/ppermute | solution.py:194
  111.5 7.8 %collective-permute-start.7 = (bf16[256,384]{1,0:T(8,128)(2,1)S(1)}, bf16[256,384]{1,0:T(8,128)(2,1)S(1)}, u32[]{:S(2)}, u32[]{:S(2)}) collective-permute-start(bf16[256,384]{1,0:T(8,128)(2,1)S(1)} %collective-permute-done.6.refs_6_), channel_id=1, source_target_pairs={{0,1},{1,2},{2,3},{3,4},{4,5},{5,6},{6,7},{7,0},{8,9},{9,10},{10,1... | collective-permute-start | bytes 589832 | tf_op jit(solution)/shard_map/while/body/eval_jaxpr/ppermute | solution.py:194
  113.3 6.0 %collective-permute-start.13 = (bf16[256,384]{1,0:T(8,128)(2,1)S(1)}, bf16[256,384]{1,0:T(8,128)(2,1)S(1)}, u32[]{:S(2)}, u32[]{:S(2)}) collective-permute-start(bf16[256,384]{1,0:T(8,128)(2,1)S(1)} %collective-permute-done.12.refs_5_), channel_id=1, source_target_pairs={{0,7},{1,0},{2,1},{3,2},{4,3},{5,4},{6,5},{7,6},{8,15},{9,8},{10,9... | collective-permute-start | bytes 589832 | tf_op jit(solution)/shard_map/while/body/eval_jaxpr/ppermute | solution.py:194
  115.7 6.9 %collective-permute-start.4 = (bf16[256,384]{1,0:T(8,128)(2,1)S(1)}, bf16[256,384]{1,0:T(8,128)(2,1)S(1)}, u32[]{:S(2)}, u32[]{:S(2)}) collective-permute-start(bf16[256,384]{1,0:T(8,128)(2,1)S(1)} %collective-permute-done.3.refs_4_), channel_id=1, source_target_pairs={{0,1},{1,2},{2,3},{3,4},{4,5},{5,6},{6,7},{7,0},{8,9},{9,10},{10,1... | collective-permute-start | bytes 589832 | tf_op jit(solution)/shard_map/while/body/eval_jaxpr/ppermute | solution.py:194
  115.7 13.6 %collective-permute-start.11 = (bf16[256,384]{1,0:T(8,128)(2,1)S(1)}, bf16[256,384]{1,0:T(8,128)(2,1)S(1)}, u32[]{:S(2)}, u32[]{:S(2)}) collective-permute-start(bf16[256,384]{1,0:T(8,128)(2,1)S(1)} %collective-permute-done.10.refs_11_), channel_id=1, source_target_pairs={{0,7},{1,0},{2,1},{3,2},{4,3},{5,4},{6,5},{7,6},{8,15},{9,8},{10,9... | collective-permute-start | bytes 589832 | tf_op jit(solution)/shard_map/while/body/eval_jaxpr/ppermute | solution.py:194
  119.3 10.0 %collective-permute-start.8 = (bf16[256,384]{1,0:T(8,128)(2,1)S(1)}, bf16[256,384]{1,0:T(8,128)(2,1)S(1)}, u32[]{:S(2)}, u32[]{:S(2)}) collective-permute-start(bf16[256,384]{1,0:T(8,128)(2,1)S(1)} %collective-permute-done.7.refs_10_), channel_id=1, source_target_pairs={{0,1},{1,2},{2,3},{3,4},{4,5},{5,6},{6,7},{7,0},{8,9},{9,10},{10,1... | collective-permute-start | bytes 589832 | tf_op jit(solution)/shard_map/while/body/eval_jaxpr/ppermute | solution.py:194
  119.3 10.0 %collective-permute-start.14 = (bf16[256,384]{1,0:T(8,128)(2,1)S(1)}, bf16[256,384]{1,0:T(8,128)(2,1)S(1)}, u32[]{:S(2)}, u32[]{:S(2)}) collective-permute-start(bf16[256,384]{1,0:T(8,128)(2,1)S(1)} %collective-permute-done.13.refs_9_), channel_id=1, source_target_pairs={{0,15},{1,8},{2,9},{3,10},{4,11},{5,12},{6,13},{7,14},{8,7},{9,0},... | collective-permute-start | bytes 589832 | tf_op jit(solution)/shard_map/while/body/eval_jaxpr/ppermute | solution.py:200
  122.6 6.9 %collective-permute-start.5 = (bf16[256,384]{1,0:T(8,128)(2,1)S(1)}, bf16[256,384]{1,0:T(8,128)(2,1)S(1)}, u32[]{:S(2)}, u32[]{:S(2)}) collective-permute-start(bf16[256,384]{1,0:T(8,128)(2,1)S(1)} %collective-permute-done.4.refs_8_), channel_id=1, source_target_pairs={{0,1},{1,2},{2,3},{3,4},{4,5},{5,6},{6,7},{7,0},{8,9},{9,10},{10,1... | collective-permute-start | bytes 589832 | tf_op jit(solution)/shard_map/while/body/eval_jaxpr/ppermute | solution.py:194
  122.6 6.9 %copy-start.3 = (f32[1,2,128]{2,1,0:T(2,128)S(1)}, f32[1,2,128]{2,1,0:T(2,128)}, u32[]{:S(2)}) copy-start(f32[1,2,128]{2,1,0:T(2,128)} %get-tuple-element.279) | copy-start | bytes 3076 | tf_op jit(solution)/shard_map/while
  129.3 7.9 %copy-start = (bf16[256,6144]{1,0:T(8,128)(2,1)S(1)}, bf16[256,6144]{1,0:T(8,128)(2,1)}, u32[]{:S(2)}) copy-start(bf16[256,6144]{1,0:T(8,128)(2,1)} %get-tuple-element.241.w_own_ref) | copy-start | bytes 9437188 | tf_op jit(solution)/shard_map/while
  132.1 5.1 %collective-permute-start.15 = (bf16[256,256]{1,0:T(8,128)(2,1)S(1)}, bf16[256,256]{1,0:T(8,128)(2,1)S(1)}, u32[]{:S(2)}, u32[]{:S(2)}) collective-permute-start(bf16[256,256]{1,0:T(8,128)(2,1)S(1)} %attention_block.1.own_ref), channel_id=1, source_target_pairs={{0,8},{8,0},{1,9},{9,1},{2,10},{10,2},{3,11},{11,3},{4,12},{12,4},... | collective-permute-start | bytes 393224 | tf_op jit(solution)/shard_map/while/body/eval_jaxpr/ppermute | solution.py:194
  138.1 11.4 %collective-permute-start.21 = (bf16[256,384]{1,0:T(8,128)(2,1)S(1)}, bf16[256,384]{1,0:T(8,128)(2,1)S(1)}, u32[]{:S(2)}, u32[]{:S(2)}) collective-permute-start(bf16[256,384]{1,0:T(8,128)(2,1)S(1)} %get-tuple-element.249), channel_id=1, source_target_pairs={{0,7},{1,0},{2,1},{3,2},{4,3},{5,4},{6,5},{7,6},{8,15},{9,8},{10,9... | collective-permute-start | bytes 589832 | tf_op jit(solution)/shard_map/while/body/eval_jaxpr/ppermute | solution.py:194
  141.3 8.1 %collective-permute-start.17 = (bf16[256,384]{1,0:T(8,128)(2,1)S(1)}, bf16[256,384]{1,0:T(8,128)(2,1)S(1)}, u32[]{:S(2)}, u32[]{:S(2)}) collective-permute-start(bf16[256,384]{1,0:T(8,128)(2,1)S(1)} %get-tuple-element.246), channel_id=1, source_target_pairs={{0,1},{1,2},{2,3},{3,4},{4,5},{5,6},{6,7},{7,0},{8,9},{9,10},{10,1... | collective-permute-start | bytes 589832 | tf_op jit(solution)/shard_map/while/body/eval_jaxpr/ppermute | solution.py:194
  142.9 21.5 %collective-permute-start.24 = (bf16[256,384]{1,0:T(8,128)(2,1)S(1)}, bf16[256,384]{1,0:T(8,128)(2,1)S(1)}, u32[]{:S(2)}, u32[]{:S(2)}) collective-permute-start(bf16[256,384]{1,0:T(8,128)(2,1)S(1)} %add_convert_fusion.19), channel_id=1, source_target_pairs={{0,16},{1,17},{2,18},{3,19},{4,20},{5,21},{6,22},{7,23},{8,24},{9,... | collective-permute-start | bytes 589832 | tf_op jit(solution)/shard_map/while/body/eval_jaxpr/ppermute | solution.py:212
  149.4 7.3 %collective-permute-start.18 = (bf16[256,384]{1,0:T(8,128)(2,1)S(1)}, bf16[256,384]{1,0:T(8,128)(2,1)S(1)}, u32[]{:S(2)}, u32[]{:S(2)}) collective-permute-start(bf16[256,384]{1,0:T(8,128)(2,1)S(1)} %add_convert_fusion.14), channel_id=1, source_target_pairs={{0,1},{1,2},{2,3},{3,4},{4,5},{5,6},{6,7},{7,0},{8,9},{9,10},{10,1... | collective-permute-start | bytes 589832 | tf_op jit(solution)/shard_map/while/body/eval_jaxpr/ppermute | solution.py:194
  149.6 7.3 %collective-permute-start.22 = (bf16[256,384]{1,0:T(8,128)(2,1)S(1)}, bf16[256,384]{1,0:T(8,128)(2,1)S(1)}, u32[]{:S(2)}, u32[]{:S(2)}) collective-permute-start(bf16[256,384]{1,0:T(8,128)(2,1)S(1)} %add_convert_fusion.17), channel_id=1, source_target_pairs={{0,7},{1,0},{2,1},{3,2},{4,3},{5,4},{6,5},{7,6},{8,15},{9,8},{10,9... | collective-permute-start | bytes 589832 | tf_op jit(solution)/shard_map/while/body/eval_jaxpr/ppermute | solution.py:194
  156.8 7.4 %collective-permute-start.19 = (bf16[256,384]{1,0:T(8,128)(2,1)S(1)}, bf16[256,384]{1,0:T(8,128)(2,1)S(1)}, u32[]{:S(2)}, u32[]{:S(2)}) collective-permute-start(bf16[256,384]{1,0:T(8,128)(2,1)S(1)} %add_convert_fusion.15), channel_id=1, source_target_pairs={{0,1},{1,2},{2,3},{3,4},{4,5},{5,6},{6,7},{7,0},{8,9},{9,10},{10,1... | collective-permute-start | bytes 589832 | tf_op jit(solution)/shard_map/while/body/eval_jaxpr/ppermute | solution.py:194
  157.0 9.7 %collective-permute-start.23 = (bf16[256,384]{1,0:T(8,128)(2,1)S(1)}, bf16[256,384]{1,0:T(8,128)(2,1)S(1)}, u32[]{:S(2)}, u32[]{:S(2)}) collective-permute-start(bf16[256,384]{1,0:T(8,128)(2,1)S(1)} %add_convert_fusion.18), channel_id=1, source_target_pairs={{0,23},{1,16},{2,17},{3,18},{4,19},{5,20},{6,21},{7,22},{8,31},{9,... | collective-permute-start | bytes 589832 | tf_op jit(solution)/shard_map/while/body/eval_jaxpr/ppermute | solution.py:212
  164.3 10.9 %collective-permute-start.20 = (bf16[256,384]{1,0:T(8,128)(2,1)S(1)}, bf16[256,384]{1,0:T(8,128)(2,1)S(1)}, u32[]{:S(2)}, u32[]{:S(2)}) collective-permute-start(bf16[256,384]{1,0:T(8,128)(2,1)S(1)} %add_convert_fusion.16), channel_id=1, source_target_pairs={{0,17},{1,18},{2,19},{3,20},{4,21},{5,22},{6,23},{7,16},{8,25},{9,... | collective-permute-start | bytes 589832 | tf_op jit(solution)/shard_map/while/body/eval_jaxpr/ppermute | solution.py:212
  175.3 0.7 copy-start.1
where the time goes:
time: 178 us; the launch traced here: 176 us
  waiting for transfers between devices  85 us (48%)
  starting transfers between devices  61.2 us (34%)
  Pallas kernels  23.6 us (13%)
  local copies, waits for them, and re-layouts  4.73 us (3%)
    ppermute x42, waiting for transfers between devices, shifted(): lax.ppermute(block, axis, [(i, (i + by) % peers) for i in range(peers)])  63.4 us
    ppermute x42, starting transfers between devices, shifted(): lax.ppermute(block, axis, [(i, (i + by) % peers) for i in range(peers)])  54.7 us
    ppermute x6, waiting for transfers between devices, to_next_section(): return lax.ppermute(block, SECTION + (PAIR, RING), pairs)  21.6 us
    pallas_call x2, Pallas kernels, partial(): pl.pallas_call(functools.partial(partial_block, count), out_shape=[jax.Sh...  13.3 us
    ppermute x2, starting transfers between devices, across(): return lax.ppermute(block, (PAIR, RING), pairs)  5.95 us
    pallas_call x2, Pallas kernels, attention(): pl.pallas_call(functools.partial(final_block, count, pieces), out_shape=j...  5.24 us
    pallas_call x4, Pallas kernels, projection(): pl.pallas_call(functools.partial(projection_block, places), out_shape=[ja...  4.98 us
  transfers between devices with their start and end apart: 50, of which 28 were waited for; matrix products, arithmetic and copies ran while one was open for 2% of the time, Pallas kernels for 12%

commit v1 on v0

--- a/solution.py
+++ b/solution.py
@@ -200,6 +200,10 @@
     return lax.ppermute(block, (PAIR, RING), pairs)
 
 
+def turns(section):
+    return section % 8 == 7
+
+
 def to_next_section(block, by):
     sections, ring = lax.axis_size(SECTION), lax.axis_size(RING)
 
@@ -207,7 +211,10 @@
         return ((s % sections) * 2 + y) * ring + z % ring
 
     pairs = [
-        (place(s, y, z), place(s + 1, y, z + by)) for s in range(sections) for y in range(2) for z in range(ring)
+        (place(s, y, z), place(s + 1, 1 - y if turns(s) else y, z + by))
+        for s in range(sections)
+        for y in range(2)
+        for z in range(ring)
     ]
     return lax.ppermute(block, SECTION + (PAIR, RING), pairs)
 
@@ -222,6 +229,8 @@
     here, side = lax.axis_index(RING), lax.axis_index(PAIR)
     own = state[0]
     width = own.shape[1]
+    flip = turns(lax.axis_index(SECTION))
+    kept_side = side ^ flip.astype(side.dtype)
     w_planes = pltpu.with_memory_space_constraint(jnp.transpose(w_qkv[0], (1, 0, 2)), pltpu.HBM)
     gain = ln_gain[0].reshape(2 * ring, 1, width)
     w_own = w_out[0]
@@ -233,7 +242,7 @@
         (0, 0), (1, 0), (0, -1), (0, 1), (0, -2), (0, 2), (1, -1), (1, 1), (0, -3), (0, 3), (1, -2), (1, 2)
     )
     late_rows = rows((0, -4), (1, -3), (1, 3), (1, 4))
-    order = jnp.concatenate([side[None] * ring, (here + jnp.arange(ring)) % ring]).astype(jnp.int32)
+    order = jnp.concatenate([kept_side[None] * ring, (here + jnp.arange(ring)) % ring]).astype(jnp.int32)
 
     half = w_own.shape[1] // 2
 
@@ -241,7 +250,7 @@
         a_up, a_down = shifted(own, RING, 1), shifted(own, RING, -1)
         other = shifted(own, PAIR, 1)
         a_up, a_down, other = lax.optimization_barrier((a_up, a_down, other))
-        w_give = lax.dynamic_slice_in_dim(lax.optimization_barrier((w_own, own))[0], (1 - side) * half, half, 1)
+        w_give = lax.dynamic_slice_in_dim(lax.optimization_barrier((w_own, own))[0], (1 - kept_side) * half, half, 1)
         w_other = shifted(lax.optimization_barrier((w_give, other))[0], PAIR, 1)
         blocks = [own, other, a_up, a_down]
         b_up = b_down = other
@@ -254,11 +263,13 @@
         sums = partial(early_rows, late_rows, gain, w_planes, blocks)
         mixed = attention(late_rows, gain, late, sums, qk_gain[0], 2 * ring)
         mixed_other = shifted(mixed, PAIR, 1)
-        parts = projection(order, mixed, mixed_other, w_own, w_other, ring, (4, 5))
-        up, down = shifted(parts[4], RING, 1), shifted(parts[5], RING, -1)
-        parts |= projection(order, mixed, mixed_other, w_own, w_other, ring, (3, 6, 0, 7, 2, 1))
-
-        kept = to_next_section(added(own, parts[0]), 0)
+        parts = projection(order, mixed, mixed_other, w_own, w_other, ring, (4,))
+        up = shifted(parts[4], RING, 1)
+        mixed_other = lax.optimization_barrier((mixed_other, parts[4]))[0]
+        parts |= projection(order, mixed, mixed_other, w_own, w_other, ring, (5, 3, 6, 0, 7, 2, 1))
+        down = shifted(parts[5], RING, -1)
+
+        kept = to_next_section(added(jnp.where(flip, other, own), parts[0]), 0)
         down = to_next_section(added(shifted(added(down, parts[6]), RING, -1), parts[7]), -1)
         for k in (3, 2):
             up = shifted(added(up, parts[k]), RING, 1)

time: 178 us -> 172 us (0.966); the launches traced: 176 us -> 172 us
  waiting for transfers between devices: 85 us -> 79.5 us
    ppermute x42, waiting for transfers between devices: 63.4 us -> 57.8 us  [shifted(): lax.ppermute(block, axis, [(i, (i + by) % peers) for i in range(peers)])]
  transfers between devices with their start and end apart: 50 -> 50, of which waited for: 28 -> 33; matrix products, arithmetic and copies ran while one was open for 2% -> 2% of each run, Pallas kernels for 12% -> 13%
where the time goes in v1:
time: 172 us
  waiting for transfers between devices  79.5 us (46%)
  starting transfers between devices  62.7 us (36%)
  Pallas kernels  23.6 us (14%)
  local copies, waits for them, and re-layouts  4.74 us (3%)
    ppermute x42, waiting for transfers between devices, shifted(): lax.ppermute(block, axis, [(i, (i + by) % peers) for i in range(peers)])  57.8 us
    ppermute x42, starting transfers between devices, shifted(): lax.ppermute(block, axis, [(i, (i + by) % peers) for i in range(peers)])  53.6 us
    ppermute x6, waiting for transfers between devices, to_next_section(): return lax.ppermute(block, SECTION + (PAIR, RING), pairs)  21.6 us
    pallas_call x2, Pallas kernels, partial(): pl.pallas_call(functools.partial(partial_block, count), out_shape=[jax.Sh...  13.3 us
    ppermute x2, starting transfers between devices, across(): return lax.ppermute(block, (PAIR, RING), pairs)  7.14 us
    pallas_call x2, Pallas kernels, attention(): pl.pallas_call(functools.partial(final_block, count, pieces), out_shape=j...  5.24 us
    pallas_call x4, Pallas kernels, projection(): pl.pallas_call(functools.partial(projection_block, places), out_shape=[ja...  5 us
  transfers between devices with their start and end apart: 50, of which 33 were waited for; matrix products, arithmetic and copies ran while one was open for 2% of the time, Pallas kernels for 13%

profile of v1, /device:TPU:0, one launch (start us, length us, event | category | flops | bytes accessed | tf_op | source)
XLA Modules:
  0.0 171.8 jit_solution(13242810058557313993)
XLA Ops:
  0.0 0.9 copy.14
  1.2 170.0 %while.12 = (s32[]{:T(128)}, bf16[256,384]{1,0:T(8,128)(2,1)S(1)}, pred[]{:T(512)}, s32[12]{0:T(128)S(1)}, s32[4]{0:T(128)S(1)}, /*index=5*/f32[16,1,384]{2,1,0:...) while((s32[]{:T(128)}, bf16[256,384]{1,0:T(8,128)(2,1)S(1)}, ...), condition=%wide.region_1.2_spmd, body=%wide.region_0.1_spmd.sunk | while | flops 3047426 | bytes 45257908 | solution.py:279
  1.4 4.0 %collective-permute-start.1 = (bf16[256,384]{1,0:T(8,128)(2,1)S(1)}, bf16[256,384]{1,0:T(8,128)(2,1)S(1)}, u32[]{:S(2)}, u32[]{:S(2)}) collective-permute-start(bf16[256,384]{1,0:T(8,128)(2,1)S(1)} %get-tuple-element.283.refs_0_), channel_id=1, source_target_pairs={{0,7},{1,0},{2,1},{3,2},{4,3},{5,4},{6,5},{7,6},{8,15},{9,8},{10,9... | collective-permute-start | bytes 589832 | tf_op jit(solution)/shard_map/while/body/eval_jaxpr/ppermute | solution.py:194
  5.5 1.6 collective-permute-start.2
  7.0 1.5 constant_dynamic-slice_fusion.2
  8.6 1.7 %collective-permute-done.refs_2_ = bf16[256,384]{1,0:T(8,128)(2,1)S(1)} collective-permute-done((bf16[256,384]{1,0:T(8,128)(2,1)S(1)}, bf16[256,384]{1,0:T(8,128)(2,1)S(1)}, u32[]{:S(2)}, u32[]{:S(2)}) %collective-permute-start) | collective-permute-done | bytes 196640 | tf_op jit(solution)/shard_map/while/body/eval_jaxpr/ppermute | solution.py:194
  10.3 1.5 collective-permute-done.2.refs_1_
  11.8 1.6 collective-permute-start.16
  13.4 1.7 collective-permute-start.9
  15.4 2.9 %collective-permute-start.12 = (bf16[256,384]{1,0:T(8,128)(2,1)S(1)}, bf16[256,384]{1,0:T(8,128)(2,1)S(1)}, u32[]{:S(2)}, u32[]{:S(2)}) collective-permute-start(bf16[256,384]{1,0:T(8,128)(2,1)S(1)} %collective-permute-done.1.refs_3_), channel_id=1, source_target_pairs={{0,7},{1,0},{2,1},{3,2},{4,3},{5,4},{6,5},{7,6},{8,15},{9,8},{10,9... | collective-permute-start | bytes 589832 | tf_op jit(solution)/shard_map/while/body/eval_jaxpr/ppermute | solution.py:194
  18.3 2.9 %collective-permute-done.9.refs_7_ = bf16[256,384]{1,0:T(8,128)(2,1)S(1)} collective-permute-done((bf16[256,384]{1,0:T(8,128)(2,1)S(1)}, bf16[256,384]{1,0:T(8,128)(2,1)S(1)}, u32[]{:S(2)}, u32[]{:S(2)}) %collective-permute-start.9) | collective-permute-done | bytes 196640 | tf_op jit(solution)/shard_map/while/body/eval_jaxpr/ppermute | solution.py:194
  21.2 2.6 %collective-permute-start.10 = (bf16[256,384]{1,0:T(8,128)(2,1)S(1)}, bf16[256,384]{1,0:T(8,128)(2,1)S(1)}, u32[]{:S(2)}, u32[]{:S(2)}) collective-permute-start(bf16[256,384]{1,0:T(8,128)(2,1)S(1)} %collective-permute-done.9.refs_7_), channel_id=1, source_target_pairs={{0,7},{1,0},{2,1},{3,2},{4,3},{5,4},{6,5},{7,6},{8,15},{9,8},{10,9... | collective-permute-start | bytes 589832 | tf_op jit(solution)/shard_map/while/body/eval_jaxpr/ppermute | solution.py:194
  24.0 1.4 collective-permute-done.12.refs_5_
  25.4 2.6 %collective-permute-start.13 = (bf16[256,384]{1,0:T(8,128)(2,1)S(1)}, bf16[256,384]{1,0:T(8,128)(2,1)S(1)}, u32[]{:S(2)}, u32[]{:S(2)}) collective-permute-start(bf16[256,384]{1,0:T(8,128)(2,1)S(1)} %collective-permute-done.12.refs_5_), channel_id=1, source_target_pairs={{0,7},{1,0},{2,1},{3,2},{4,3},{5,4},{6,5},{7,6},{8,15},{9,8},{10,9... | collective-permute-start | bytes 589832 | tf_op jit(solution)/shard_map/while/body/eval_jaxpr/ppermute | solution.py:194
  28.3 1.4 collective-permute-done.10.refs_11_
  29.7 3.2 %collective-permute-start.11 = (bf16[256,384]{1,0:T(8,128)(2,1)S(1)}, bf16[256,384]{1,0:T(8,128)(2,1)S(1)}, u32[]{:S(2)}, u32[]{:S(2)}) collective-permute-start(bf16[256,384]{1,0:T(8,128)(2,1)S(1)} %collective-permute-done.10.refs_11_), channel_id=1, source_target_pairs={{0,7},{1,0},{2,1},{3,2},{4,3},{5,4},{6,5},{7,6},{8,15},{9,8},{10,9... | collective-permute-start | bytes 589832 | tf_op jit(solution)/shard_map/while/body/eval_jaxpr/ppermute | solution.py:194
  32.9 1.0 collective-permute-done.13.refs_9_
  33.9 2.7 %collective-permute-start.14 = (bf16[256,384]{1,0:T(8,128)(2,1)S(1)}, bf16[256,384]{1,0:T(8,128)(2,1)S(1)}, u32[]{:S(2)}, u32[]{:S(2)}) collective-permute-start(bf16[256,384]{1,0:T(8,128)(2,1)S(1)} %collective-permute-done.13.refs_9_), channel_id=1, source_target_pairs={{0,15},{1,8},{2,9},{3,10},{4,11},{5,12},{6,13},{7,14},{8,7},{9,0},... | collective-permute-start | bytes 589832 | tf_op jit(solution)/shard_map/while/body/eval_jaxpr/ppermute | solution.py:200
  36.6 0.7 collective-permute-done.4.refs_8_
  37.2 6.7 %qkv_partial.3 = (f32[3,272,256]{2,1,0:T(8,128)S(1)}, f32[2,256,128]{2,1,0:T(8,128)S(1)}, f32[256,128]{1,0:T(8,128)S(1)}, bf16[3,1536,256]{2,1,0:T(8,128)(2,1)S(1)}) custom-call(s32[12]{0:T(128)S(1)} %get-tuple-element.297.rows_ref, s32[4]{0:T(128)S(1)} %get-tuple-element.298.late_rows_ref.rows_ref, f32[16,1,384]{2,1,0:T(1,128)S(1)} %copy-done.2, ...), custom_call_target="tpu_custom_call" | custom-call | tf_op jit(solution)/shard_map/while/body/eval_jaxpr/qkv_partial/pallas_call | solution.py:130
  44.1 2.6 %attention_block.1.own_ref = bf16[256,256]{1,0:T(8,128)(2,1)S(1)} custom-call(s32[4]{0:T(128)S(1)} %get-tuple-element.298.late_rows_ref.rows_ref, f32[16,1,384]{2,1,0:T(1,128)S(1)} %copy-done.2, bf16[256,384]{1,0:T(8,128)(2,1)S(1)} %collective-permute-done.5.refs_0_, bf16[256,384]{1,0:T(8,128)(2,1)S(1)} %collective-permute-done.8.refs_1_, ...), custom_call_target="tpu_custom_call" | custom-call | tf_op jit(solution)/shard_map/while/body/eval_jaxpr/attention_block/pallas_call | solution.py:155
  46.7 1.4 collective-permute-start.15
  48.1 5.6 %collective-permute-done.15.other_ref = bf16[256,256]{1,0:T(8,128)(2,1)S(1)} collective-permute-done((bf16[256,256]{1,0:T(8,128)(2,1)S(1)}, bf16[256,256]{1,0:T(8,128)(2,1)S(1)}, u32[]{:S(2)}, u32[]{:S(2)}) %collective-permute-start.15) | collective-permute-done | bytes 131104 | tf_op jit(solution)/shard_map/while/body/eval_jaxpr/ppermute | solution.py:194
  53.8 0.8 projection_block.6
  54.7 1.7 projection_block.7
  56.4 3.3 %collective-permute-start.21 = (bf16[256,384]{1,0:T(8,128)(2,1)S(1)}, bf16[256,384]{1,0:T(8,128)(2,1)S(1)}, u32[]{:S(2)}, u32[]{:S(2)}) collective-permute-start(bf16[256,384]{1,0:T(8,128)(2,1)S(1)} %get-tuple-element.268), channel_id=1, source_target_pairs={{0,7},{1,0},{2,1},{3,2},{4,3},{5,4},{6,5},{7,6},{8,15},{9,8},{10,9... | collective-permute-start | bytes 589832 | tf_op jit(solution)/shard_map/while/body/eval_jaxpr/ppermute | solution.py:194
  59.9 1.7 %collective-permute-done.17 = bf16[256,384]{1,0:T(8,128)(2,1)S(1)} collective-permute-done((bf16[256,384]{1,0:T(8,128)(2,1)S(1)}, bf16[256,384]{1,0:T(8,128)(2,1)S(1)}, u32[]{:S(2)}, u32[]{:S(2)}) %collective-permute-start.17) | collective-permute-done | bytes 196640 | tf_op jit(solution)/shard_map/while/body/eval_jaxpr/ppermute | solution.py:194
  61.7 1.1 collective-permute-done.21
  62.9 3.8 %collective-permute-start.22 = (bf16[256,384]{1,0:T(8,128)(2,1)S(1)}, bf16[256,384]{1,0:T(8,128)(2,1)S(1)}, u32[]{:S(2)}, u32[]{:S(2)}) collective-permute-start(bf16[256,384]{1,0:T(8,128)(2,1)S(1)} %add_convert_fusion.17), channel_id=1, source_target_pairs={{0,7},{1,0},{2,1},{3,2},{4,3},{5,4},{6,5},{7,6},{8,15},{9,8},{10,9... | collective-permute-start | bytes 589832 | tf_op jit(solution)/shard_map/while/body/eval_jaxpr/ppermute | solution.py:194
  66.7 2.9 %collective-permute-done.18 = bf16[256,384]{1,0:T(8,128)(2,1)S(1)} collective-permute-done((bf16[256,384]{1,0:T(8,128)(2,1)S(1)}, bf16[256,384]{1,0:T(8,128)(2,1)S(1)}, u32[]{:S(2)}, u32[]{:S(2)}) %collective-permute-start.18) | collective-permute-done | bytes 196640 | tf_op jit(solution)/shard_map/while/body/eval_jaxpr/ppermute | solution.py:194
  70.0 1.5 collective-permute-start.23
  71.4 5.3 %collective-permute-done.19 = bf16[256,384]{1,0:T(8,128)(2,1)S(1)} collective-permute-done((bf16[256,384]{1,0:T(8,128)(2,1)S(1)}, bf16[256,384]{1,0:T(8,128)(2,1)S(1)}, u32[]{:S(2)}, u32[]{:S(2)}) %collective-permute-start.19) | collective-permute-done | bytes 196640 | tf_op jit(solution)/shard_map/while/body/eval_jaxpr/ppermute | solution.py:194
  76.9 4.0 %collective-permute-done.23 = bf16[256,384]{1,0:T(8,128)(2,1)S(1)} collective-permute-done((bf16[256,384]{1,0:T(8,128)(2,1)S(1)}, bf16[256,384]{1,0:T(8,128)(2,1)S(1)}, u32[]{:S(2)}, u32[]{:S(2)}) %collective-permute-start.23) | collective-permute-done | bytes 196640 | tf_op jit(solution)/shard_map/while/body/eval_jaxpr/ppermute | solution.py:219
  80.9 6.5 %collective-permute-done.20 = bf16[256,384]{1,0:T(8,128)(2,1)S(1)} collective-permute-done((bf16[256,384]{1,0:T(8,128)(2,1)S(1)}, bf16[256,384]{1,0:T(8,128)(2,1)S(1)}, u32[]{:S(2)}, u32[]{:S(2)}) %collective-permute-start.20) | collective-permute-done | bytes 196640 | tf_op jit(solution)/shard_map/while/body/eval_jaxpr/ppermute | solution.py:219
  87.6 3.2 %collective-permute-start.1 = (bf16[256,384]{1,0:T(8,128)(2,1)S(1)}, bf16[256,384]{1,0:T(8,128)(2,1)S(1)}, u32[]{:S(2)}, u32[]{:S(2)}) collective-permute-start(bf16[256,384]{1,0:T(8,128)(2,1)S(1)} %get-tuple-element.283.refs_0_), channel_id=1, source_target_pairs={{0,7},{1,0},{2,1},{3,2},{4,3},{5,4},{6,5},{7,6},{8,15},{9,8},{10,9... | collective-permute-start | bytes 589832 | tf_op jit(solution)/shard_map/while/body/eval_jaxpr/ppermute | solution.py:194
  91.2 1.5 constant_dynamic-slice_fusion.2
  92.7 1.8 %collective-permute-done.refs_2_ = bf16[256,384]{1,0:T(8,128)(2,1)S(1)} collective-permute-done((bf16[256,384]{1,0:T(8,128)(2,1)S(1)}, bf16[256,384]{1,0:T(8,128)(2,1)S(1)}, u32[]{:S(2)}, u32[]{:S(2)}) %collective-permute-start) | collective-permute-done | bytes 196640 | tf_op jit(solution)/shard_map/while/body/eval_jaxpr/ppermute | solution.py:194
  94.5 1.6 collective-permute-done.1.refs_3_
  96.1 2.5 %collective-permute-done.2.refs_1_ = bf16[256,384]{1,0:T(8,128)(2,1)S(1)} collective-permute-done((bf16[256,384]{1,0:T(8,128)(2,1)S(1)}, bf16[256,384]{1,0:T(8,128)(2,1)S(1)}, u32[]{:S(2)}, u32[]{:S(2)}) %collective-permute-start.2) | collective-permute-done | bytes 196640 | tf_op jit(solution)/shard_map/while/body/eval_jaxpr/ppermute | solution.py:194
  99.0 1.1 collective-permute-start.9
  100.2 0.9 collective-permute-start.6
  101.1 2.4 %collective-permute-start.12 = (bf16[256,384]{1,0:T(8,128)(2,1)S(1)}, bf16[256,384]{1,0:T(8,128)(2,1)S(1)}, u32[]{:S(2)}, u32[]{:S(2)}) collective-permute-start(bf16[256,384]{1,0:T(8,128)(2,1)S(1)} %collective-permute-done.1.refs_3_), channel_id=1, source_target_pairs={{0,7},{1,0},{2,1},{3,2},{4,3},{5,4},{6,5},{7,6},{8,15},{9,8},{10,9... | collective-permute-start | bytes 589832 | tf_op jit(solution)/shard_map/while/body/eval_jaxpr/ppermute | solution.py:194
  103.4 3.4 %collective-permute-done.9.refs_7_ = bf16[256,384]{1,0:T(8,128)(2,1)S(1)} collective-permute-done((bf16[256,384]{1,0:T(8,128)(2,1)S(1)}, bf16[256,384]{1,0:T(8,128)(2,1)S(1)}, u32[]{:S(2)}, u32[]{:S(2)}) %collective-permute-start.9) | collective-permute-done | bytes 196640 | tf_op jit(solution)/shard_map/while/body/eval_jaxpr/ppermute | solution.py:194
  106.8 2.2 %collective-permute-start.10 = (bf16[256,384]{1,0:T(8,128)(2,1)S(1)}, bf16[256,384]{1,0:T(8,128)(2,1)S(1)}, u32[]{:S(2)}, u32[]{:S(2)}) collective-permute-start(bf16[256,384]{1,0:T(8,128)(2,1)S(1)} %collective-permute-done.9.refs_7_), channel_id=1, source_target_pairs={{0,7},{1,0},{2,1},{3,2},{4,3},{5,4},{6,5},{7,6},{8,15},{9,8},{10,9... | collective-permute-start | bytes 589832 | tf_op jit(solution)/shard_map/while/body/eval_jaxpr/ppermute | solution.py:194
  109.0 2.0 %collective-permute-done.12.refs_5_ = bf16[256,384]{1,0:T(8,128)(2,1)S(1)} collective-permute-done((bf16[256,384]{1,0:T(8,128)(2,1)S(1)}, bf16[256,384]{1,0:T(8,128)(2,1)S(1)}, u32[]{:S(2)}, u32[]{:S(2)}) %collective-permute-start.12) | collective-permute-done | bytes 196640 | tf_op jit(solution)/shard_map/while/body/eval_jaxpr/ppermute | solution.py:194
  111.0 2.2 %collective-permute-start.13 = (bf16[256,384]{1,0:T(8,128)(2,1)S(1)}, bf16[256,384]{1,0:T(8,128)(2,1)S(1)}, u32[]{:S(2)}, u32[]{:S(2)}) collective-permute-start(bf16[256,384]{1,0:T(8,128)(2,1)S(1)} %collective-permute-done.12.refs_5_), channel_id=1, source_target_pairs={{0,7},{1,0},{2,1},{3,2},{4,3},{5,4},{6,5},{7,6},{8,15},{9,8},{10,9... | collective-permute-start | bytes 589832 | tf_op jit(solution)/shard_map/while/body/eval_jaxpr/ppermute | solution.py:194
  113.2 1.3 collective-permute-done.10.refs_11_
  114.5 3.4 %collective-permute-start.11 = (bf16[256,384]{1,0:T(8,128)(2,1)S(1)}, bf16[256,384]{1,0:T(8,128)(2,1)S(1)}, u32[]{:S(2)}, u32[]{:S(2)}) collective-permute-start(bf16[256,384]{1,0:T(8,128)(2,1)S(1)} %collective-permute-done.10.refs_11_), channel_id=1, source_target_pairs={{0,7},{1,0},{2,1},{3,2},{4,3},{5,4},{6,5},{7,6},{8,15},{9,8},{10,9... | collective-permute-start | bytes 589832 | tf_op jit(solution)/shard_map/while/body/eval_jaxpr/ppermute | solution.py:194
  117.9 4.5 %collective-permute-start.14 = (bf16[256,384]{1,0:T(8,128)(2,1)S(1)}, bf16[256,384]{1,0:T(8,128)(2,1)S(1)}, u32[]{:S(2)}, u32[]{:S(2)}) collective-permute-start(bf16[256,384]{1,0:T(8,128)(2,1)S(1)} %collective-permute-done.13.refs_9_), channel_id=1, source_target_pairs={{0,15},{1,8},{2,9},{3,10},{4,11},{5,12},{6,13},{7,14},{8,7},{9,0},... | collective-permute-start | bytes 589832 | tf_op jit(solution)/shard_map/while/body/eval_jaxpr/ppermute | solution.py:200
  122.4 6.7 %qkv_partial.3 = (f32[3,272,256]{2,1,0:T(8,128)S(1)}, f32[2,256,128]{2,1,0:T(8,128)S(1)}, f32[256,128]{1,0:T(8,128)S(1)}, bf16[3,1536,256]{2,1,0:T(8,128)(2,1)S(1)}) custom-call(s32[12]{0:T(128)S(1)} %get-tuple-element.297.rows_ref, s32[4]{0:T(128)S(1)} %get-tuple-element.298.late_rows_ref.rows_ref, f32[16,1,384]{2,1,0:T(1,128)S(1)} %copy-done.2, ...), custom_call_target="tpu_custom_call" | custom-call | tf_op jit(solution)/shard_map/while/body/eval_jaxpr/qkv_partial/pallas_call | solution.py:130
  129.3 2.6 %attention_block.1.own_ref = bf16[256,256]{1,0:T(8,128)(2,1)S(1)} custom-call(s32[4]{0:T(128)S(1)} %get-tuple-element.298.late_rows_ref.rows_ref, f32[16,1,384]{2,1,0:T(1,128)S(1)} %copy-done.2, bf16[256,384]{1,0:T(8,128)(2,1)S(1)} %collective-permute-done.5.refs_0_, bf16[256,384]{1,0:T(8,128)(2,1)S(1)} %collective-permute-done.8.refs_1_, ...), custom_call_target="tpu_custom_call" | custom-call | tf_op jit(solution)/shard_map/while/body/eval_jaxpr/attention_block/pallas_call | solution.py:155
  132.2 4.7 %collective-permute-done.15.other_ref = bf16[256,256]{1,0:T(8,128)(2,1)S(1)} collective-permute-done((bf16[256,256]{1,0:T(8,128)(2,1)S(1)}, bf16[256,256]{1,0:T(8,128)(2,1)S(1)}, u32[]{:S(2)}, u32[]{:S(2)}) %collective-permute-start.15) | collective-permute-done | bytes 131104 | tf_op jit(solution)/shard_map/while/body/eval_jaxpr/ppermute | solution.py:194
  137.0 0.8 projection_block.6
  137.9 1.7 projection_block.7
  139.6 3.3 %collective-permute-start.21 = (bf16[256,384]{1,0:T(8,128)(2,1)S(1)}, bf16[256,384]{1,0:T(8,128)(2,1)S(1)}, u32[]{:S(2)}, u32[]{:S(2)}) collective-permute-start(bf16[256,384]{1,0:T(8,128)(2,1)S(1)} %get-tuple-element.268), channel_id=1, source_target_pairs={{0,7},{1,0},{2,1},{3,2},{4,3},{5,4},{6,5},{7,6},{8,15},{9,8},{10,9... | collective-permute-start | bytes 589832 | tf_op jit(solution)/shard_map/while/body/eval_jaxpr/ppermute | solution.py:194
  143.0 1.7 %collective-permute-done.17 = bf16[256,384]{1,0:T(8,128)(2,1)S(1)} collective-permute-done((bf16[256,384]{1,0:T(8,128)(2,1)S(1)}, bf16[256,384]{1,0:T(8,128)(2,1)S(1)}, u32[]{:S(2)}, u32[]{:S(2)}) %collective-permute-start.17) | collective-permute-done | bytes 196640 | tf_op jit(solution)/shard_map/while/body/eval_jaxpr/ppermute | solution.py:194
  144.9 2.3 %collective-permute-done.21 = bf16[256,384]{1,0:T(8,128)(2,1)S(1)} collective-permute-done((bf16[256,384]{1,0:T(8,128)(2,1)S(1)}, bf16[256,384]{1,0:T(8,128)(2,1)S(1)}, u32[]{:S(2)}, u32[]{:S(2)}) %collective-permute-start.21) | collective-permute-done | bytes 196640 | tf_op jit(solution)/shard_map/while/body/eval_jaxpr/ppermute | solution.py:194
  147.2 3.8 %collective-permute-start.22 = (bf16[256,384]{1,0:T(8,128)(2,1)S(1)}, bf16[256,384]{1,0:T(8,128)(2,1)S(1)}, u32[]{:S(2)}, u32[]{:S(2)}) collective-permute-start(bf16[256,384]{1,0:T(8,128)(2,1)S(1)} %add_convert_fusion.17), channel_id=1, source_target_pairs={{0,7},{1,0},{2,1},{3,2},{4,3},{5,4},{6,5},{7,6},{8,15},{9,8},{10,9... | collective-permute-start | bytes 589832 | tf_op jit(solution)/shard_map/while/body/eval_jaxpr/ppermute | solution.py:194
  151.0 1.8 %collective-permute-done.18 = bf16[256,384]{1,0:T(8,128)(2,1)S(1)} collective-permute-done((bf16[256,384]{1,0:T(8,128)(2,1)S(1)}, bf16[256,384]{1,0:T(8,128)(2,1)S(1)}, u32[]{:S(2)}, u32[]{:S(2)}) %collective-permute-start.18) | collective-permute-done | bytes 196640 | tf_op jit(solution)/shard_map/while/body/eval_jaxpr/ppermute | solution.py:194
  153.3 0.9 collective-permute-done.22
  154.3 5.5 %collective-permute-done.19 = bf16[256,384]{1,0:T(8,128)(2,1)S(1)} collective-permute-done((bf16[256,384]{1,0:T(8,128)(2,1)S(1)}, bf16[256,384]{1,0:T(8,128)(2,1)S(1)}, u32[]{:S(2)}, u32[]{:S(2)}) %collective-permute-start.19) | collective-permute-done | bytes 196640 | tf_op jit(solution)/shard_map/while/body/eval_jaxpr/ppermute | solution.py:194
  160.0 3.7 %collective-permute-done.23 = bf16[256,384]{1,0:T(8,128)(2,1)S(1)} collective-permute-done((bf16[256,384]{1,0:T(8,128)(2,1)S(1)}, bf16[256,384]{1,0:T(8,128)(2,1)S(1)}, u32[]{:S(2)}, u32[]{:S(2)}) %collective-permute-start.23) | collective-permute-done | bytes 196640 | tf_op jit(solution)/shard_map/while/body/eval_jaxpr/ppermute | solution.py:219
  163.6 7.4 %collective-permute-done.20 = bf16[256,384]{1,0:T(8,128)(2,1)S(1)} collective-permute-done((bf16[256,384]{1,0:T(8,128)(2,1)S(1)}, bf16[256,384]{1,0:T(8,128)(2,1)S(1)}, u32[]{:S(2)}, u32[]{:S(2)}) %collective-permute-start.20) | collective-permute-done | bytes 196640 | tf_op jit(solution)/shard_map/while/body/eval_jaxpr/ppermute | solution.py:219
  171.2 0.7 copy-done.1
  (80 shorter events, 5.1 us)
Async XLA Ops:
  1.2 36.0 %copy-start.2 = (f32[16,1,384]{2,1,0:T(1,128)S(1)}, f32[16,1,384]{2,1,0:T(1,128)}, u32[]{:S(2)}) copy-start(f32[16,1,384]{2,1,0:T(1,128)} %get-tuple-element.299.gain_ref) | copy-start | bytes 73732 | tf_op jit(solution)/shard_map/while
  1.2 9.1 %collective-permute-start = (bf16[256,384]{1,0:T(8,128)(2,1)S(1)}, bf16[256,384]{1,0:T(8,128)(2,1)S(1)}, u32[]{:S(2)}, u32[]{:S(2)}) collective-permute-start(bf16[256,384]{1,0:T(8,128)(2,1)S(1)} %get-tuple-element.283.refs_0_), channel_id=1, source_target_pairs={{0,1},{1,2},{2,3},{3,4},{4,5},{5,6},{6,7},{7,0},{8,9},{9,10},{10,1... | collective-permute-start | bytes 589832 | tf_op jit(solution)/shard_map/while/body/eval_jaxpr/ppermute | solution.py:194
  1.4 8.8 %collective-permute-start.1 = (bf16[256,384]{1,0:T(8,128)(2,1)S(1)}, bf16[256,384]{1,0:T(8,128)(2,1)S(1)}, u32[]{:S(2)}, u32[]{:S(2)}) collective-permute-start(bf16[256,384]{1,0:T(8,128)(2,1)S(1)} %get-tuple-element.283.refs_0_), channel_id=1, source_target_pairs={{0,7},{1,0},{2,1},{3,2},{4,3},{5,4},{6,5},{7,6},{8,15},{9,8},{10,9... | collective-permute-start | bytes 589832 | tf_op jit(solution)/shard_map/while/body/eval_jaxpr/ppermute | solution.py:194
  5.5 6.4 %collective-permute-start.2 = (bf16[256,384]{1,0:T(8,128)(2,1)S(1)}, bf16[256,384]{1,0:T(8,128)(2,1)S(1)}, u32[]{:S(2)}, u32[]{:S(2)}) collective-permute-start(bf16[256,384]{1,0:T(8,128)(2,1)S(1)} %get-tuple-element.283.refs_0_), channel_id=1, source_target_pairs={{0,8},{8,0},{1,9},{9,1},{2,10},{10,2},{3,11},{11,3},{4,12},{12,4},... | collective-permute-start | bytes 589832 | tf_op jit(solution)/shard_map/while/body/eval_jaxpr/ppermute | solution.py:194
  11.8 42.0 %collective-permute-start.16 = (bf16[256,3072]{1,0:T(8,128)(2,1)S(1)}, bf16[256,3072]{1,0:T(8,128)(2,1)S(1)}, u32[]{:S(2)}, u32[]{:S(2)}) collective-permute-start(bf16[256,3072]{1,0:T(8,128)(2,1)S(1)} %constant_dynamic-slice_fusion.2), channel_id=1, source_target_pairs={{0,8},{8,0},{1,9},{9,1},{2,10},{10,2},{3,11},{11,3},{4,12},{12,4},... | collective-permute-start | bytes 4718600 | tf_op jit(solution)/shard_map/while/body/eval_jaxpr/ppermute | solution.py:194
  13.4 7.8 %collective-permute-start.9 = (bf16[256,384]{1,0:T(8,128)(2,1)S(1)}, bf16[256,384]{1,0:T(8,128)(2,1)S(1)}, u32[]{:S(2)}, u32[]{:S(2)}) collective-permute-start(bf16[256,384]{1,0:T(8,128)(2,1)S(1)} %collective-permute-done.2.refs_1_), channel_id=1, source_target_pairs={{0,7},{1,0},{2,1},{3,2},{4,3},{5,4},{6,5},{7,6},{8,15},{9,8},{10,9... | collective-permute-start | bytes 589832 | tf_op jit(solution)/shard_map/while/body/eval_jaxpr/ppermute | solution.py:194
  15.1 9.0 %collective-permute-start.6 = (bf16[256,384]{1,0:T(8,128)(2,1)S(1)}, bf16[256,384]{1,0:T(8,128)(2,1)S(1)}, u32[]{:S(2)}, u32[]{:S(2)}) collective-permute-start(bf16[256,384]{1,0:T(8,128)(2,1)S(1)} %collective-permute-done.2.refs_1_), channel_id=1, source_target_pairs={{0,1},{1,2},{2,3},{3,4},{4,5},{5,6},{6,7},{7,0},{8,9},{9,10},{10,1... | collective-permute-start | bytes 589832 | tf_op jit(solution)/shard_map/while/body/eval_jaxpr/ppermute | solution.py:194
  15.4 10.0 %collective-permute-start.12 = (bf16[256,384]{1,0:T(8,128)(2,1)S(1)}, bf16[256,384]{1,0:T(8,128)(2,1)S(1)}, u32[]{:S(2)}, u32[]{:S(2)}) collective-permute-start(bf16[256,384]{1,0:T(8,128)(2,1)S(1)} %collective-permute-done.1.refs_3_), channel_id=1, source_target_pairs={{0,7},{1,0},{2,1},{3,2},{4,3},{5,4},{6,5},{7,6},{8,15},{9,8},{10,9... | collective-permute-start | bytes 589832 | tf_op jit(solution)/shard_map/while/body/eval_jaxpr/ppermute | solution.py:194
  18.3 10.0 %collective-permute-start.3 = (bf16[256,384]{1,0:T(8,128)(2,1)S(1)}, bf16[256,384]{1,0:T(8,128)(2,1)S(1)}, u32[]{:S(2)}, u32[]{:S(2)}) collective-permute-start(bf16[256,384]{1,0:T(8,128)(2,1)S(1)} %collective-permute-done.refs_2_), channel_id=1, source_target_pairs={{0,1},{1,2},{2,3},{3,4},{4,5},{5,6},{6,7},{7,0},{8,9},{9,10},{10,1... | collective-permute-start | bytes 589832 | tf_op jit(solution)/shard_map/while/body/eval_jaxpr/ppermute | solution.py:194
  21.2 8.4 %collective-permute-start.10 = (bf16[256,384]{1,0:T(8,128)(2,1)S(1)}, bf16[256,384]{1,0:T(8,128)(2,1)S(1)}, u32[]{:S(2)}, u32[]{:S(2)}) collective-permute-start(bf16[256,384]{1,0:T(8,128)(2,1)S(1)} %collective-permute-done.9.refs_7_), channel_id=1, source_target_pairs={{0,7},{1,0},{2,1},{3,2},{4,3},{5,4},{6,5},{7,6},{8,15},{9,8},{10,9... | collective-permute-start | bytes 589832 | tf_op jit(solution)/shard_map/while/body/eval_jaxpr/ppermute | solution.py:194
  24.0 8.8 %collective-permute-start.7 = (bf16[256,384]{1,0:T(8,128)(2,1)S(1)}, bf16[256,384]{1,0:T(8,128)(2,1)S(1)}, u32[]{:S(2)}, u32[]{:S(2)}) collective-permute-start(bf16[256,384]{1,0:T(8,128)(2,1)S(1)} %collective-permute-done.6.refs_6_), channel_id=1, source_target_pairs={{0,1},{1,2},{2,3},{3,4},{4,5},{5,6},{6,7},{7,0},{8,9},{9,10},{10,1... | collective-permute-start | bytes 589832 | tf_op jit(solution)/shard_map/while/body/eval_jaxpr/ppermute | solution.py:194
  25.4 8.4 %collective-permute-start.13 = (bf16[256,384]{1,0:T(8,128)(2,1)S(1)}, bf16[256,384]{1,0:T(8,128)(2,1)S(1)}, u32[]{:S(2)}, u32[]{:S(2)}) collective-permute-start(bf16[256,384]{1,0:T(8,128)(2,1)S(1)} %collective-permute-done.12.refs_5_), channel_id=1, source_target_pairs={{0,7},{1,0},{2,1},{3,2},{4,3},{5,4},{6,5},{7,6},{8,15},{9,8},{10,9... | collective-permute-start | bytes 589832 | tf_op jit(solution)/shard_map/while/body/eval_jaxpr/ppermute | solution.py:194
  28.3 9.0 %collective-permute-start.4 = (bf16[256,384]{1,0:T(8,128)(2,1)S(1)}, bf16[256,384]{1,0:T(8,128)(2,1)S(1)}, u32[]{:S(2)}, u32[]{:S(2)}) collective-permute-start(bf16[256,384]{1,0:T(8,128)(2,1)S(1)} %collective-permute-done.3.refs_4_), channel_id=1, source_target_pairs={{0,1},{1,2},{2,3},{3,4},{4,5},{5,6},{6,7},{7,0},{8,9},{9,10},{10,1... | collective-permute-start | bytes 589832 | tf_op jit(solution)/shard_map/while/body/eval_jaxpr/ppermute | solution.py:194
  29.7 14.3 %collective-permute-start.11 = (bf16[256,384]{1,0:T(8,128)(2,1)S(1)}, bf16[256,384]{1,0:T(8,128)(2,1)S(1)}, u32[]{:S(2)}, u32[]{:S(2)}) collective-permute-start(bf16[256,384]{1,0:T(8,128)(2,1)S(1)} %collective-permute-done.10.refs_11_), channel_id=1, source_target_pairs={{0,7},{1,0},{2,1},{3,2},{4,3},{5,4},{6,5},{7,6},{8,15},{9,8},{10,9... | collective-permute-start | bytes 589832 | tf_op jit(solution)/shard_map/while/body/eval_jaxpr/ppermute | solution.py:194
  32.9 11.1 %collective-permute-start.8 = (bf16[256,384]{1,0:T(8,128)(2,1)S(1)}, bf16[256,384]{1,0:T(8,128)(2,1)S(1)}, u32[]{:S(2)}, u32[]{:S(2)}) collective-permute-start(bf16[256,384]{1,0:T(8,128)(2,1)S(1)} %collective-permute-done.7.refs_10_), channel_id=1, source_target_pairs={{0,1},{1,2},{2,3},{3,4},{4,5},{5,6},{6,7},{7,0},{8,9},{9,10},{10,1... | collective-permute-start | bytes 589832 | tf_op jit(solution)/shard_map/while/body/eval_jaxpr/ppermute | solution.py:194
  33.9 10.1 %collective-permute-start.14 = (bf16[256,384]{1,0:T(8,128)(2,1)S(1)}, bf16[256,384]{1,0:T(8,128)(2,1)S(1)}, u32[]{:S(2)}, u32[]{:S(2)}) collective-permute-start(bf16[256,384]{1,0:T(8,128)(2,1)S(1)} %collective-permute-done.13.refs_9_), channel_id=1, source_target_pairs={{0,15},{1,8},{2,9},{3,10},{4,11},{5,12},{6,13},{7,14},{8,7},{9,0},... | collective-permute-start | bytes 589832 | tf_op jit(solution)/shard_map/while/body/eval_jaxpr/ppermute | solution.py:200
  37.2 6.9 %collective-permute-start.5 = (bf16[256,384]{1,0:T(8,128)(2,1)S(1)}, bf16[256,384]{1,0:T(8,128)(2,1)S(1)}, u32[]{:S(2)}, u32[]{:S(2)}) collective-permute-start(bf16[256,384]{1,0:T(8,128)(2,1)S(1)} %collective-permute-done.4.refs_8_), channel_id=1, source_target_pairs={{0,1},{1,2},{2,3},{3,4},{4,5},{5,6},{6,7},{7,0},{8,9},{9,10},{10,1... | collective-permute-start | bytes 589832 | tf_op jit(solution)/shard_map/while/body/eval_jaxpr/ppermute | solution.py:194
  37.2 6.9 %copy-start.3 = (f32[1,2,128]{2,1,0:T(2,128)S(1)}, f32[1,2,128]{2,1,0:T(2,128)}, u32[]{:S(2)}) copy-start(f32[1,2,128]{2,1,0:T(2,128)} %get-tuple-element.301) | copy-start | bytes 3076 | tf_op jit(solution)/shard_map/while
  43.9 9.9 %copy-start = (bf16[256,6144]{1,0:T(8,128)(2,1)S(1)}, bf16[256,6144]{1,0:T(8,128)(2,1)}, u32[]{:S(2)}) copy-start(bf16[256,6144]{1,0:T(8,128)(2,1)} %get-tuple-element.260.w_own_ref) | copy-start | bytes 9437188 | tf_op jit(solution)/shard_map/while
  46.7 7.0 %collective-permute-start.15 = (bf16[256,256]{1,0:T(8,128)(2,1)S(1)}, bf16[256,256]{1,0:T(8,128)(2,1)S(1)}, u32[]{:S(2)}, u32[]{:S(2)}) collective-permute-start(bf16[256,256]{1,0:T(8,128)(2,1)S(1)} %attention_block.1.own_ref), channel_id=1, source_target_pairs={{0,8},{8,0},{1,9},{9,1},{2,10},{10,2},{3,11},{11,3},{4,12},{12,4},... | collective-permute-start | bytes 393224 | tf_op jit(solution)/shard_map/while/body/eval_jaxpr/ppermute | solution.py:194
  54.6 7.0 %collective-permute-start.17 = (bf16[256,384]{1,0:T(8,128)(2,1)S(1)}, bf16[256,384]{1,0:T(8,128)(2,1)S(1)}, u32[]{:S(2)}, u32[]{:S(2)}) collective-permute-start(bf16[256,384]{1,0:T(8,128)(2,1)S(1)} %projection_block.6), channel_id=1, source_target_pairs={{0,1},{1,2},{2,3},{3,4},{4,5},{5,6},{6,7},{7,0},{8,9},{9,10},{10,1... | collective-permute-start | bytes 589832 | tf_op jit(solution)/shard_map/while/body/eval_jaxpr/ppermute | solution.py:194
  56.4 6.5 %collective-permute-start.21 = (bf16[256,384]{1,0:T(8,128)(2,1)S(1)}, bf16[256,384]{1,0:T(8,128)(2,1)S(1)}, u32[]{:S(2)}, u32[]{:S(2)}) collective-permute-start(bf16[256,384]{1,0:T(8,128)(2,1)S(1)} %get-tuple-element.268), channel_id=1, source_target_pairs={{0,7},{1,0},{2,1},{3,2},{4,3},{5,4},{6,5},{7,6},{8,15},{9,8},{10,9... | collective-permute-start | bytes 589832 | tf_op jit(solution)/shard_map/while/body/eval_jaxpr/ppermute | solution.py:194
  59.8 17.1 %collective-permute-start.24 = (bf16[256,384]{1,0:T(8,128)(2,1)S(1)}, bf16[256,384]{1,0:T(8,128)(2,1)S(1)}, u32[]{:S(2)}, u32[]{:S(2)}) collective-permute-start(bf16[256,384]{1,0:T(8,128)(2,1)S(1)} %add_convert_fusion.19), channel_id=1, source_target_pairs={{0,16},{1,17},{2,18},{3,19},{4,20},{5,21},{6,22},{7,23},{8,24},{9,... | collective-permute-start | bytes 589832 | tf_op jit(solution)/shard_map/while/body/eval_jaxpr/ppermute | solution.py:219
  61.7 8.0 %collective-permute-start.18 = (bf16[256,384]{1,0:T(8,128)(2,1)S(1)}, bf16[256,384]{1,0:T(8,128)(2,1)S(1)}, u32[]{:S(2)}, u32[]{:S(2)}) collective-permute-start(bf16[256,384]{1,0:T(8,128)(2,1)S(1)} %add_convert_fusion.14), channel_id=1, source_target_pairs={{0,1},{1,2},{2,3},{3,4},{4,5},{5,6},{6,7},{7,0},{8,9},{9,10},{10,1... | collective-permute-start | bytes 589832 | tf_op jit(solution)/shard_map/while/body/eval_jaxpr/ppermute | solution.py:194
  62.9 7.0 %collective-permute-start.22 = (bf16[256,384]{1,0:T(8,128)(2,1)S(1)}, bf16[256,384]{1,0:T(8,128)(2,1)S(1)}, u32[]{:S(2)}, u32[]{:S(2)}) collective-permute-start(bf16[256,384]{1,0:T(8,128)(2,1)S(1)} %add_convert_fusion.17), channel_id=1, source_target_pairs={{0,7},{1,0},{2,1},{3,2},{4,3},{5,4},{6,5},{7,6},{8,15},{9,8},{10,9... | collective-permute-start | bytes 589832 | tf_op jit(solution)/shard_map/while/body/eval_jaxpr/ppermute | solution.py:194
  69.7 7.1 %collective-permute-start.19 = (bf16[256,384]{1,0:T(8,128)(2,1)S(1)}, bf16[256,384]{1,0:T(8,128)(2,1)S(1)}, u32[]{:S(2)}, u32[]{:S(2)}) collective-permute-start(bf16[256,384]{1,0:T(8,128)(2,1)S(1)} %add_convert_fusion.15), channel_id=1, source_target_pairs={{0,1},{1,2},{2,3},{3,4},{4,5},{5,6},{6,7},{7,0},{8,9},{9,10},{10,1... | collective-permute-start | bytes 589832 | tf_op jit(solution)/shard_map/while/body/eval_jaxpr/ppermute | solution.py:194
  70.0 10.9 %collective-permute-start.23 = (bf16[256,384]{1,0:T(8,128)(2,1)S(1)}, bf16[256,384]{1,0:T(8,128)(2,1)S(1)}, u32[]{:S(2)}, u32[]{:S(2)}) collective-permute-start(bf16[256,384]{1,0:T(8,128)(2,1)S(1)} %add_convert_fusion.18), channel_id=1, source_target_pairs={{0,23},{1,16},{2,17},{3,18},{4,19},{5,20},{6,21},{7,22},{8,31},{9,... | collective-permute-start | bytes 589832 | tf_op jit(solution)/shard_map/while/body/eval_jaxpr/ppermute | solution.py:219
  76.8 10.6 %collective-permute-start.20 = (bf16[256,384]{1,0:T(8,128)(2,1)S(1)}, bf16[256,384]{1,0:T(8,128)(2,1)S(1)}, u32[]{:S(2)}, u32[]{:S(2)}) collective-permute-start(bf16[256,384]{1,0:T(8,128)(2,1)S(1)} %add_convert_fusion.16), channel_id=1, source_target_pairs={{0,17},{1,18},{2,19},{3,20},{4,21},{5,22},{6,23},{7,16},{8,25},{9,... | collective-permute-start | bytes 589832 | tf_op jit(solution)/shard_map/while/body/eval_jaxpr/ppermute | solution.py:219
  87.5 34.9 %copy-start.2 = (f32[16,1,384]{2,1,0:T(1,128)S(1)}, f32[16,1,384]{2,1,0:T(1,128)}, u32[]{:S(2)}) copy-start(f32[16,1,384]{2,1,0:T(1,128)} %get-tuple-element.299.gain_ref) | copy-start | bytes 73732 | tf_op jit(solution)/shard_map/while
  87.5 7.0 %collective-permute-start = (bf16[256,384]{1,0:T(8,128)(2,1)S(1)}, bf16[256,384]{1,0:T(8,128)(2,1)S(1)}, u32[]{:S(2)}, u32[]{:S(2)}) collective-permute-start(bf16[256,384]{1,0:T(8,128)(2,1)S(1)} %get-tuple-element.283.refs_0_), channel_id=1, source_target_pairs={{0,1},{1,2},{2,3},{3,4},{4,5},{5,6},{6,7},{7,0},{8,9},{9,10},{10,1... | collective-permute-start | bytes 589832 | tf_op jit(solution)/shard_map/while/body/eval_jaxpr/ppermute | solution.py:194
  87.6 8.5 %collective-permute-start.1 = (bf16[256,384]{1,0:T(8,128)(2,1)S(1)}, bf16[256,384]{1,0:T(8,128)(2,1)S(1)}, u32[]{:S(2)}, u32[]{:S(2)}) collective-permute-start(bf16[256,384]{1,0:T(8,128)(2,1)S(1)} %get-tuple-element.283.refs_0_), channel_id=1, source_target_pairs={{0,7},{1,0},{2,1},{3,2},{4,3},{5,4},{6,5},{7,6},{8,15},{9,8},{10,9... | collective-permute-start | bytes 589832 | tf_op jit(solution)/shard_map/while/body/eval_jaxpr/ppermute | solution.py:194
  90.8 7.8 %collective-permute-start.2 = (bf16[256,384]{1,0:T(8,128)(2,1)S(1)}, bf16[256,384]{1,0:T(8,128)(2,1)S(1)}, u32[]{:S(2)}, u32[]{:S(2)}) collective-permute-start(bf16[256,384]{1,0:T(8,128)(2,1)S(1)} %get-tuple-element.283.refs_0_), channel_id=1, source_target_pairs={{0,8},{8,0},{1,9},{9,1},{2,10},{10,2},{3,11},{11,3},{4,12},{12,4},... | collective-permute-start | bytes 589832 | tf_op jit(solution)/shard_map/while/body/eval_jaxpr/ppermute | solution.py:194
  98.7 38.3 %collective-permute-start.16 = (bf16[256,3072]{1,0:T(8,128)(2,1)S(1)}, bf16[256,3072]{1,0:T(8,128)(2,1)S(1)}, u32[]{:S(2)}, u32[]{:S(2)}) collective-permute-start(bf16[256,3072]{1,0:T(8,128)(2,1)S(1)} %constant_dynamic-slice_fusion.2), channel_id=1, source_target_pairs={{0,8},{8,0},{1,9},{9,1},{2,10},{10,2},{3,11},{11,3},{4,12},{12,4},... | collective-permute-start | bytes 4718600 | tf_op jit(solution)/shard_map/while/body/eval_jaxpr/ppermute | solution.py:194
  99.0 7.7 %collective-permute-start.9 = (bf16[256,384]{1,0:T(8,128)(2,1)S(1)}, bf16[256,384]{1,0:T(8,128)(2,1)S(1)}, u32[]{:S(2)}, u32[]{:S(2)}) collective-permute-start(bf16[256,384]{1,0:T(8,128)(2,1)S(1)} %collective-permute-done.2.refs_1_), channel_id=1, source_target_pairs={{0,7},{1,0},{2,1},{3,2},{4,3},{5,4},{6,5},{7,6},{8,15},{9,8},{10,9... | collective-permute-start | bytes 589832 | tf_op jit(solution)/shard_map/while/body/eval_jaxpr/ppermute | solution.py:194
  100.2 8.8 %collective-permute-start.6 = (bf16[256,384]{1,0:T(8,128)(2,1)S(1)}, bf16[256,384]{1,0:T(8,128)(2,1)S(1)}, u32[]{:S(2)}, u32[]{:S(2)}) collective-permute-start(bf16[256,384]{1,0:T(8,128)(2,1)S(1)} %collective-permute-done.2.refs_1_), channel_id=1, source_target_pairs={{0,1},{1,2},{2,3},{3,4},{4,5},{5,6},{6,7},{7,0},{8,9},{9,10},{10,1... | collective-permute-start | bytes 589832 | tf_op jit(solution)/shard_map/while/body/eval_jaxpr/ppermute | solution.py:194
  101.1 9.9 %collective-permute-start.12 = (bf16[256,384]{1,0:T(8,128)(2,1)S(1)}, bf16[256,384]{1,0:T(8,128)(2,1)S(1)}, u32[]{:S(2)}, u32[]{:S(2)}) collective-permute-start(bf16[256,384]{1,0:T(8,128)(2,1)S(1)} %collective-permute-done.1.refs_3_), channel_id=1, source_target_pairs={{0,7},{1,0},{2,1},{3,2},{4,3},{5,4},{6,5},{7,6},{8,15},{9,8},{10,9... | collective-permute-start | bytes 589832 | tf_op jit(solution)/shard_map/while/body/eval_jaxpr/ppermute | solution.py:194
  103.4 9.8 %collective-permute-start.3 = (bf16[256,384]{1,0:T(8,128)(2,1)S(1)}, bf16[256,384]{1,0:T(8,128)(2,1)S(1)}, u32[]{:S(2)}, u32[]{:S(2)}) collective-permute-start(bf16[256,384]{1,0:T(8,128)(2,1)S(1)} %collective-permute-done.refs_2_), channel_id=1, source_target_pairs={{0,1},{1,2},{2,3},{3,4},{4,5},{5,6},{6,7},{7,0},{8,9},{9,10},{10,1... | collective-permute-start | bytes 589832 | tf_op jit(solution)/shard_map/while/body/eval_jaxpr/ppermute | solution.py:194
  106.8 7.7 %collective-permute-start.10 = (bf16[256,384]{1,0:T(8,128)(2,1)S(1)}, bf16[256,384]{1,0:T(8,128)(2,1)S(1)}, u32[]{:S(2)}, u32[]{:S(2)}) collective-permute-start(bf16[256,384]{1,0:T(8,128)(2,1)S(1)} %collective-permute-done.9.refs_7_), channel_id=1, source_target_pairs={{0,7},{1,0},{2,1},{3,2},{4,3},{5,4},{6,5},{7,6},{8,15},{9,8},{10,9... | collective-permute-start | bytes 589832 | tf_op jit(solution)/shard_map/while/body/eval_jaxpr/ppermute | solution.py:194
  109.0 9.0 %collective-permute-start.7 = (bf16[256,384]{1,0:T(8,128)(2,1)S(1)}, bf16[256,384]{1,0:T(8,128)(2,1)S(1)}, u32[]{:S(2)}, u32[]{:S(2)}) collective-permute-start(bf16[256,384]{1,0:T(8,128)(2,1)S(1)} %collective-permute-done.6.refs_6_), channel_id=1, source_target_pairs={{0,1},{1,2},{2,3},{3,4},{4,5},{5,6},{6,7},{7,0},{8,9},{9,10},{10,1... | collective-permute-start | bytes 589832 | tf_op jit(solution)/shard_map/while/body/eval_jaxpr/ppermute | solution.py:194
  111.0 6.9 %collective-permute-start.13 = (bf16[256,384]{1,0:T(8,128)(2,1)S(1)}, bf16[256,384]{1,0:T(8,128)(2,1)S(1)}, u32[]{:S(2)}, u32[]{:S(2)}) collective-permute-start(bf16[256,384]{1,0:T(8,128)(2,1)S(1)} %collective-permute-done.12.refs_5_), channel_id=1, source_target_pairs={{0,7},{1,0},{2,1},{3,2},{4,3},{5,4},{6,5},{7,6},{8,15},{9,8},{10,9... | collective-permute-start | bytes 589832 | tf_op jit(solution)/shard_map/while/body/eval_jaxpr/ppermute | solution.py:194
  113.2 9.2 %collective-permute-start.4 = (bf16[256,384]{1,0:T(8,128)(2,1)S(1)}, bf16[256,384]{1,0:T(8,128)(2,1)S(1)}, u32[]{:S(2)}, u32[]{:S(2)}) collective-permute-start(bf16[256,384]{1,0:T(8,128)(2,1)S(1)} %collective-permute-done.3.refs_4_), channel_id=1, source_target_pairs={{0,1},{1,2},{2,3},{3,4},{4,5},{5,6},{6,7},{7,0},{8,9},{9,10},{10,1... | collective-permute-start | bytes 589832 | tf_op jit(solution)/shard_map/while/body/eval_jaxpr/ppermute | solution.py:194
  114.5 14.6 %collective-permute-start.11 = (bf16[256,384]{1,0:T(8,128)(2,1)S(1)}, bf16[256,384]{1,0:T(8,128)(2,1)S(1)}, u32[]{:S(2)}, u32[]{:S(2)}) collective-permute-start(bf16[256,384]{1,0:T(8,128)(2,1)S(1)} %collective-permute-done.10.refs_11_), channel_id=1, source_target_pairs={{0,7},{1,0},{2,1},{3,2},{4,3},{5,4},{6,5},{7,6},{8,15},{9,8},{10,9... | collective-permute-start | bytes 589832 | tf_op jit(solution)/shard_map/while/body/eval_jaxpr/ppermute | solution.py:194
  117.9 11.2 %collective-permute-start.8 = (bf16[256,384]{1,0:T(8,128)(2,1)S(1)}, bf16[256,384]{1,0:T(8,128)(2,1)S(1)}, u32[]{:S(2)}, u32[]{:S(2)}) collective-permute-start(bf16[256,384]{1,0:T(8,128)(2,1)S(1)} %collective-permute-done.7.refs_10_), channel_id=1, source_target_pairs={{0,1},{1,2},{2,3},{3,4},{4,5},{5,6},{6,7},{7,0},{8,9},{9,10},{10,1... | collective-permute-start | bytes 589832 | tf_op jit(solution)/shard_map/while/body/eval_jaxpr/ppermute | solution.py:194
  117.9 11.2 %collective-permute-start.14 = (bf16[256,384]{1,0:T(8,128)(2,1)S(1)}, bf16[256,384]{1,0:T(8,128)(2,1)S(1)}, u32[]{:S(2)}, u32[]{:S(2)}) collective-permute-start(bf16[256,384]{1,0:T(8,128)(2,1)S(1)} %collective-permute-done.13.refs_9_), channel_id=1, source_target_pairs={{0,15},{1,8},{2,9},{3,10},{4,11},{5,12},{6,13},{7,14},{8,7},{9,0},... | collective-permute-start | bytes 589832 | tf_op jit(solution)/shard_map/while/body/eval_jaxpr/ppermute | solution.py:200
  122.4 6.9 %collective-permute-start.5 = (bf16[256,384]{1,0:T(8,128)(2,1)S(1)}, bf16[256,384]{1,0:T(8,128)(2,1)S(1)}, u32[]{:S(2)}, u32[]{:S(2)}) collective-permute-start(bf16[256,384]{1,0:T(8,128)(2,1)S(1)} %collective-permute-done.4.refs_8_), channel_id=1, source_target_pairs={{0,1},{1,2},{2,3},{3,4},{4,5},{5,6},{6,7},{7,0},{8,9},{9,10},{10,1... | collective-permute-start | bytes 589832 | tf_op jit(solution)/shard_map/while/body/eval_jaxpr/ppermute | solution.py:194
  122.4 6.9 %copy-start.3 = (f32[1,2,128]{2,1,0:T(2,128)S(1)}, f32[1,2,128]{2,1,0:T(2,128)}, u32[]{:S(2)}) copy-start(f32[1,2,128]{2,1,0:T(2,128)} %get-tuple-element.301) | copy-start | bytes 3076 | tf_op jit(solution)/shard_map/while
  129.1 7.9 %copy-start = (bf16[256,6144]{1,0:T(8,128)(2,1)S(1)}, bf16[256,6144]{1,0:T(8,128)(2,1)}, u32[]{:S(2)}) copy-start(bf16[256,6144]{1,0:T(8,128)(2,1)} %get-tuple-element.260.w_own_ref) | copy-start | bytes 9437188 | tf_op jit(solution)/shard_map/while
  131.9 5.1 %collective-permute-start.15 = (bf16[256,256]{1,0:T(8,128)(2,1)S(1)}, bf16[256,256]{1,0:T(8,128)(2,1)S(1)}, u32[]{:S(2)}, u32[]{:S(2)}) collective-permute-start(bf16[256,256]{1,0:T(8,128)(2,1)S(1)} %attention_block.1.own_ref), channel_id=1, source_target_pairs={{0,8},{8,0},{1,9},{9,1},{2,10},{10,2},{3,11},{11,3},{4,12},{12,4},... | collective-permute-start | bytes 393224 | tf_op jit(solution)/shard_map/while/body/eval_jaxpr/ppermute | solution.py:194
  137.8 7.0 %collective-permute-start.17 = (bf16[256,384]{1,0:T(8,128)(2,1)S(1)}, bf16[256,384]{1,0:T(8,128)(2,1)S(1)}, u32[]{:S(2)}, u32[]{:S(2)}) collective-permute-start(bf16[256,384]{1,0:T(8,128)(2,1)S(1)} %projection_block.6), channel_id=1, source_target_pairs={{0,1},{1,2},{2,3},{3,4},{4,5},{5,6},{6,7},{7,0},{8,9},{9,10},{10,1... | collective-permute-start | bytes 589832 | tf_op jit(solution)/shard_map/while/body/eval_jaxpr/ppermute | solution.py:194
  139.6 7.6 %collective-permute-start.21 = (bf16[256,384]{1,0:T(8,128)(2,1)S(1)}, bf16[256,384]{1,0:T(8,128)(2,1)S(1)}, u32[]{:S(2)}, u32[]{:S(2)}) collective-permute-start(bf16[256,384]{1,0:T(8,128)(2,1)S(1)} %get-tuple-element.268), channel_id=1, source_target_pairs={{0,7},{1,0},{2,1},{3,2},{4,3},{5,4},{6,5},{7,6},{8,15},{9,8},{10,9... | collective-permute-start | bytes 589832 | tf_op jit(solution)/shard_map/while/body/eval_jaxpr/ppermute | solution.py:194
  142.9 17.0 %collective-permute-start.24 = (bf16[256,384]{1,0:T(8,128)(2,1)S(1)}, bf16[256,384]{1,0:T(8,128)(2,1)S(1)}, u32[]{:S(2)}, u32[]{:S(2)}) collective-permute-start(bf16[256,384]{1,0:T(8,128)(2,1)S(1)} %add_convert_fusion.19), channel_id=1, source_target_pairs={{0,16},{1,17},{2,18},{3,19},{4,20},{5,21},{6,22},{7,23},{8,24},{9,... | collective-permute-start | bytes 589832 | tf_op jit(solution)/shard_map/while/body/eval_jaxpr/ppermute | solution.py:219
  144.8 8.0 %collective-permute-start.18 = (bf16[256,384]{1,0:T(8,128)(2,1)S(1)}, bf16[256,384]{1,0:T(8,128)(2,1)S(1)}, u32[]{:S(2)}, u32[]{:S(2)}) collective-permute-start(bf16[256,384]{1,0:T(8,128)(2,1)S(1)} %add_convert_fusion.14), channel_id=1, source_target_pairs={{0,1},{1,2},{2,3},{3,4},{4,5},{5,6},{6,7},{7,0},{8,9},{9,10},{10,1... | collective-permute-start | bytes 589832 | tf_op jit(solution)/shard_map/while/body/eval_jaxpr/ppermute | solution.py:194
  147.2 7.0 %collective-permute-start.22 = (bf16[256,384]{1,0:T(8,128)(2,1)S(1)}, bf16[256,384]{1,0:T(8,128)(2,1)S(1)}, u32[]{:S(2)}, u32[]{:S(2)}) collective-permute-start(bf16[256,384]{1,0:T(8,128)(2,1)S(1)} %add_convert_fusion.17), channel_id=1, source_target_pairs={{0,7},{1,0},{2,1},{3,2},{4,3},{5,4},{6,5},{7,6},{8,15},{9,8},{10,9... | collective-permute-start | bytes 589832 | tf_op jit(solution)/shard_map/while/body/eval_jaxpr/ppermute | solution.py:194
  152.9 7.0 %collective-permute-start.19 = (bf16[256,384]{1,0:T(8,128)(2,1)S(1)}, bf16[256,384]{1,0:T(8,128)(2,1)S(1)}, u32[]{:S(2)}, u32[]{:S(2)}) collective-permute-start(bf16[256,384]{1,0:T(8,128)(2,1)S(1)} %add_convert_fusion.15), channel_id=1, source_target_pairs={{0,1},{1,2},{2,3},{3,4},{4,5},{5,6},{6,7},{7,0},{8,9},{9,10},{10,1... | collective-permute-start | bytes 589832 | tf_op jit(solution)/shard_map/while/body/eval_jaxpr/ppermute | solution.py:194
  154.2 9.4 %collective-permute-start.23 = (bf16[256,384]{1,0:T(8,128)(2,1)S(1)}, bf16[256,384]{1,0:T(8,128)(2,1)S(1)}, u32[]{:S(2)}, u32[]{:S(2)}) collective-permute-start(bf16[256,384]{1,0:T(8,128)(2,1)S(1)} %add_convert_fusion.18), channel_id=1, source_target_pairs={{0,23},{1,16},{2,17},{3,18},{4,19},{5,20},{6,21},{7,22},{8,31},{9,... | collective-permute-start | bytes 589832 | tf_op jit(solution)/shard_map/while/body/eval_jaxpr/ppermute | solution.py:219
  159.9 11.2 %collective-permute-start.20 = (bf16[256,384]{1,0:T(8,128)(2,1)S(1)}, bf16[256,384]{1,0:T(8,128)(2,1)S(1)}, u32[]{:S(2)}, u32[]{:S(2)}) collective-permute-start(bf16[256,384]{1,0:T(8,128)(2,1)S(1)} %add_convert_fusion.16), channel_id=1, source_target_pairs={{0,17},{1,18},{2,19},{3,20},{4,21},{5,22},{6,23},{7,16},{8,25},{9,... | collective-permute-start | bytes 589832 | tf_op jit(solution)/shard_map/while/body/eval_jaxpr/ppermute | solution.py:219
  171.2 0.7 copy-start.1

commit v2 on v1

--- a/solution.py
+++ b/solution.py
@@ -249,15 +249,16 @@
     def step(_, own):
         a_up, a_down = shifted(own, RING, 1), shifted(own, RING, -1)
         other = shifted(own, PAIR, 1)
-        a_up, a_down, other = lax.optimization_barrier((a_up, a_down, other))
+        a_up, a_down = lax.optimization_barrier((a_up, a_down))
         w_give = lax.dynamic_slice_in_dim(lax.optimization_barrier((w_own, own))[0], (1 - kept_side) * half, half, 1)
-        w_other = shifted(lax.optimization_barrier((w_give, other))[0], PAIR, 1)
         blocks = [own, other, a_up, a_down]
         b_up = b_down = other
         for _ in range(2):
             a_up, a_down = shifted(a_up, RING, 1), shifted(a_down, RING, -1)
             b_up, b_down = shifted(b_up, RING, 1), shifted(b_down, RING, -1)
             blocks += [a_up, a_down, b_up, b_down]
+            if len(blocks) == 8:
+                w_other = shifted(lax.optimization_barrier((w_give, a_up, a_down, b_up, b_down))[0], PAIR, 1)
         late = [shifted(a_up, RING, 1), shifted(b_up, RING, 1), shifted(b_down, RING, -1), across(a_down, -1)]
 
         sums = partial(early_rows, late_rows, gain, w_planes, blocks)

time: 172 us -> 196 us (1.14)
  the two profiles are of different devices: /device:TPU:0 before, /device:TPU:6 now
where the time goes in v2:
time: 196 us
  waiting for transfers between devices  103 us (53%)
  starting transfers between devices  63.4 us (32%)
  Pallas kernels  23.6 us (12%)
  local copies, waits for them, and re-layouts  4.74 us (2%)
    ppermute x42, waiting for transfers between devices, shifted(): lax.ppermute(block, axis, [(i, (i + by) % peers) for i in range(peers)])  88.4 us
    ppermute x42, starting transfers between devices, shifted(): lax.ppermute(block, axis, [(i, (i + by) % peers) for i in range(peers)])  55.9 us
    ppermute x6, waiting for transfers between devices, to_next_section(): return lax.ppermute(block, SECTION + (PAIR, RING), pairs)  14.4 us
    pallas_call x2, Pallas kernels, partial(): pl.pallas_call(functools.partial(partial_block, count), out_shape=[jax.Sh...  13.3 us
    pallas_call x2, Pallas kernels, attention(): pl.pallas_call(functools.partial(final_block, count, pieces), out_shape=j...  5.23 us
    pallas_call x4, Pallas kernels, projection(): pl.pallas_call(functools.partial(projection_block, places), out_shape=[ja...  5 us
    ppermute x2, starting transfers between devices, across(): return lax.ppermute(block, (PAIR, RING), pairs)  4.25 us
  transfers between devices with their start and end apart: 50, of which 27 were waited for; matrix products, arithmetic and copies ran while one was open for 2% of the time, Pallas kernels for 11%

profile of v2, /device:TPU:6, one launch (start us, length us, event | category | flops | bytes accessed | tf_op | source)
XLA Modules:
  0.0 195.8 jit_solution(2128026380280073556)
XLA Ops:
  0.0 0.9 copy.14
  1.2 193.9 %while.12 = (s32[]{:T(128)}, bf16[256,384]{1,0:T(8,128)(2,1)S(1)}, pred[]{:T(512)}, s32[12]{0:T(128)S(1)}, s32[4]{0:T(128)S(1)}, /*index=5*/f32[16,1,384]{2,1,0:...) while((s32[]{:T(128)}, bf16[256,384]{1,0:T(8,128)(2,1)S(1)}, ...), condition=%wide.region_1.2_spmd, body=%wide.region_0.1_spmd.sunk | while | flops 3047426 | bytes 45257908 | solution.py:280
  1.2 2.0 collective-permute-start
  3.2 4.0 %collective-permute-start.1 = (bf16[256,384]{1,0:T(8,128)(2,1)S(1)}, bf16[256,384]{1,0:T(8,128)(2,1)S(1)}, u32[]{:S(2)}, u32[]{:S(2)}) collective-permute-start(bf16[256,384]{1,0:T(8,128)(2,1)S(1)} %get-tuple-element.280.refs_0_), channel_id=1, source_target_pairs={{0,7},{1,0},{2,1},{3,2},{4,3},{5,4},{6,5},{7,6},{8,15},{9,8},{10,9... | collective-permute-start | bytes 589832 | tf_op jit(solution)/shard_map/while/body/eval_jaxpr/ppermute | solution.py:194
  7.2 1.6 collective-permute-start.5
  8.8 3.2 %collective-permute-done.refs_2_ = bf16[256,384]{1,0:T(8,128)(2,1)S(1)} collective-permute-done((bf16[256,384]{1,0:T(8,128)(2,1)S(1)}, bf16[256,384]{1,0:T(8,128)(2,1)S(1)}, u32[]{:S(2)}, u32[]{:S(2)}) %collective-permute-start) | collective-permute-done | bytes 196640 | tf_op jit(solution)/shard_map/while/body/eval_jaxpr/ppermute | solution.py:194
  12.0 3.0 %collective-permute-start.12 = (bf16[256,384]{1,0:T(8,128)(2,1)S(1)}, bf16[256,384]{1,0:T(8,128)(2,1)S(1)}, u32[]{:S(2)}, u32[]{:S(2)}) collective-permute-start(bf16[256,384]{1,0:T(8,128)(2,1)S(1)} %collective-permute-done.1.refs_3_), channel_id=1, source_target_pairs={{0,7},{1,0},{2,1},{3,2},{4,3},{5,4},{6,5},{7,6},{8,15},{9,8},{10,9... | collective-permute-start | bytes 589832 | tf_op jit(solution)/shard_map/while/body/eval_jaxpr/ppermute | solution.py:194
  15.1 3.2 %collective-permute-start.9 = (bf16[256,384]{1,0:T(8,128)(2,1)S(1)}, bf16[256,384]{1,0:T(8,128)(2,1)S(1)}, u32[]{:S(2)}, u32[]{:S(2)}) collective-permute-start(bf16[256,384]{1,0:T(8,128)(2,1)S(1)} %collective-permute-done.5.refs_1_), channel_id=1, source_target_pairs={{0,7},{1,0},{2,1},{3,2},{4,3},{5,4},{6,5},{7,6},{8,15},{9,8},{10,9... | collective-permute-start | bytes 589832 | tf_op jit(solution)/shard_map/while/body/eval_jaxpr/ppermute | solution.py:194
  18.3 1.5 constant_dynamic-slice_fusion.2
  19.9 3.8 %collective-permute-done.2.refs_4_ = bf16[256,384]{1,0:T(8,128)(2,1)S(1)} collective-permute-done((bf16[256,384]{1,0:T(8,128)(2,1)S(1)}, bf16[256,384]{1,0:T(8,128)(2,1)S(1)}, u32[]{:S(2)}, u32[]{:S(2)}) %collective-permute-start.2) | collective-permute-done | bytes 196640 | tf_op jit(solution)/shard_map/while/body/eval_jaxpr/ppermute | solution.py:194
  23.7 2.4 %collective-permute-done.6.refs_6_ = bf16[256,384]{1,0:T(8,128)(2,1)S(1)} collective-permute-done((bf16[256,384]{1,0:T(8,128)(2,1)S(1)}, bf16[256,384]{1,0:T(8,128)(2,1)S(1)}, u32[]{:S(2)}, u32[]{:S(2)}) %collective-permute-start.6) | collective-permute-done | bytes 196640 | tf_op jit(solution)/shard_map/while/body/eval_jaxpr/ppermute | solution.py:194
  26.1 1.6 collective-permute-start.16
  27.8 1.9 collective-permute-start.3
  29.7 1.3 collective-permute-start.10
  31.1 0.7 collective-permute-start.7
  31.8 3.8 %collective-permute-done.13.refs_9_ = bf16[256,384]{1,0:T(8,128)(2,1)S(1)} collective-permute-done((bf16[256,384]{1,0:T(8,128)(2,1)S(1)}, bf16[256,384]{1,0:T(8,128)(2,1)S(1)}, u32[]{:S(2)}, u32[]{:S(2)}) %collective-permute-start.13) | collective-permute-done | bytes 196640 | tf_op jit(solution)/shard_map/while/body/eval_jaxpr/ppermute | solution.py:194
  35.6 1.1 collective-permute-start.14
  36.8 0.8 collective-permute-start.4
  37.6 2.2 %collective-permute-done.10.refs_11_ = bf16[256,384]{1,0:T(8,128)(2,1)S(1)} collective-permute-done((bf16[256,384]{1,0:T(8,128)(2,1)S(1)}, bf16[256,384]{1,0:T(8,128)(2,1)S(1)}, u32[]{:S(2)}, u32[]{:S(2)}) %collective-permute-start.10) | collective-permute-done | bytes 196640 | tf_op jit(solution)/shard_map/while/body/eval_jaxpr/ppermute | solution.py:194
  39.8 1.2 collective-permute-start.11
  41.0 0.8 collective-permute-start.8
  41.8 6.7 %qkv_partial.3 = (f32[3,272,256]{2,1,0:T(8,128)S(1)}, f32[2,256,128]{2,1,0:T(8,128)S(1)}, f32[256,128]{1,0:T(8,128)S(1)}, bf16[3,1536,256]{2,1,0:T(8,128)(2,1)S(1)}) custom-call(s32[12]{0:T(128)S(1)} %get-tuple-element.294.rows_ref, s32[4]{0:T(128)S(1)} %get-tuple-element.295.late_rows_ref.rows_ref, f32[16,1,384]{2,1,0:T(1,128)S(1)} %copy-done.2, ...), custom_call_target="tpu_custom_call" | custom-call | tf_op jit(solution)/shard_map/while/body/eval_jaxpr/qkv_partial/pallas_call | solution.py:130
  48.5 2.6 %attention_block.1.own_ref = bf16[256,256]{1,0:T(8,128)(2,1)S(1)} custom-call(s32[4]{0:T(128)S(1)} %get-tuple-element.295.late_rows_ref.rows_ref, f32[16,1,384]{2,1,0:T(1,128)S(1)} %copy-done.2, bf16[256,384]{1,0:T(8,128)(2,1)S(1)} %collective-permute-done.4.refs_0_, bf16[256,384]{1,0:T(8,128)(2,1)S(1)} %collective-permute-done.8.refs_1_, ...), custom_call_target="tpu_custom_call" | custom-call | tf_op jit(solution)/shard_map/while/body/eval_jaxpr/attention_block/pallas_call | solution.py:155
  51.3 16.5 %collective-permute-done.15.other_ref = bf16[256,256]{1,0:T(8,128)(2,1)S(1)} collective-permute-done((bf16[256,256]{1,0:T(8,128)(2,1)S(1)}, bf16[256,256]{1,0:T(8,128)(2,1)S(1)}, u32[]{:S(2)}, u32[]{:S(2)}) %collective-permute-start.15) | collective-permute-done | bytes 131104 | tf_op jit(solution)/shard_map/while/body/eval_jaxpr/ppermute | solution.py:194
  67.8 0.8 projection_block.6
  68.7 1.7 projection_block.7
  70.4 3.3 %collective-permute-start.21 = (bf16[256,384]{1,0:T(8,128)(2,1)S(1)}, bf16[256,384]{1,0:T(8,128)(2,1)S(1)}, u32[]{:S(2)}, u32[]{:S(2)}) collective-permute-start(bf16[256,384]{1,0:T(8,128)(2,1)S(1)} %get-tuple-element.265), channel_id=1, source_target_pairs={{0,7},{1,0},{2,1},{3,2},{4,3},{5,4},{6,5},{7,6},{8,15},{9,8},{10,9... | collective-permute-start | bytes 589832 | tf_op jit(solution)/shard_map/while/body/eval_jaxpr/ppermute | solution.py:194
  73.9 1.7 collective-permute-done.17
  75.7 1.1 collective-permute-done.21
  76.9 3.8 %collective-permute-start.22 = (bf16[256,384]{1,0:T(8,128)(2,1)S(1)}, bf16[256,384]{1,0:T(8,128)(2,1)S(1)}, u32[]{:S(2)}, u32[]{:S(2)}) collective-permute-start(bf16[256,384]{1,0:T(8,128)(2,1)S(1)} %add_convert_fusion.17), channel_id=1, source_target_pairs={{0,7},{1,0},{2,1},{3,2},{4,3},{5,4},{6,5},{7,6},{8,15},{9,8},{10,9... | collective-permute-start | bytes 589832 | tf_op jit(solution)/shard_map/while/body/eval_jaxpr/ppermute | solution.py:194
  80.7 3.7 %collective-permute-done.18 = bf16[256,384]{1,0:T(8,128)(2,1)S(1)} collective-permute-done((bf16[256,384]{1,0:T(8,128)(2,1)S(1)}, bf16[256,384]{1,0:T(8,128)(2,1)S(1)}, u32[]{:S(2)}, u32[]{:S(2)}) %collective-permute-start.18) | collective-permute-done | bytes 196640 | tf_op jit(solution)/shard_map/while/body/eval_jaxpr/ppermute | solution.py:194
  84.6 2.8 %collective-permute-start.23 = (bf16[256,384]{1,0:T(8,128)(2,1)S(1)}, bf16[256,384]{1,0:T(8,128)(2,1)S(1)}, u32[]{:S(2)}, u32[]{:S(2)}) collective-permute-start(bf16[256,384]{1,0:T(8,128)(2,1)S(1)} %add_convert_fusion.18), channel_id=1, source_target_pairs={{0,23},{1,16},{2,17},{3,18},{4,19},{5,20},{6,21},{7,22},{8,31},{9,... | collective-permute-start | bytes 589832 | tf_op jit(solution)/shard_map/while/body/eval_jaxpr/ppermute | solution.py:219
  87.4 5.3 %collective-permute-done.19 = bf16[256,384]{1,0:T(8,128)(2,1)S(1)} collective-permute-done((bf16[256,384]{1,0:T(8,128)(2,1)S(1)}, bf16[256,384]{1,0:T(8,128)(2,1)S(1)}, u32[]{:S(2)}, u32[]{:S(2)}) %collective-permute-start.19) | collective-permute-done | bytes 196640 | tf_op jit(solution)/shard_map/while/body/eval_jaxpr/ppermute | solution.py:194
  92.8 7.2 %collective-permute-done.20 = bf16[256,384]{1,0:T(8,128)(2,1)S(1)} collective-permute-done((bf16[256,384]{1,0:T(8,128)(2,1)S(1)}, bf16[256,384]{1,0:T(8,128)(2,1)S(1)}, u32[]{:S(2)}, u32[]{:S(2)}) %collective-permute-start.20) | collective-permute-done | bytes 196640 | tf_op jit(solution)/shard_map/while/body/eval_jaxpr/ppermute | solution.py:219
  100.2 3.2 %collective-permute-start.1 = (bf16[256,384]{1,0:T(8,128)(2,1)S(1)}, bf16[256,384]{1,0:T(8,128)(2,1)S(1)}, u32[]{:S(2)}, u32[]{:S(2)}) collective-permute-start(bf16[256,384]{1,0:T(8,128)(2,1)S(1)} %get-tuple-element.280.refs_0_), channel_id=1, source_target_pairs={{0,7},{1,0},{2,1},{3,2},{4,3},{5,4},{6,5},{7,6},{8,15},{9,8},{10,9... | collective-permute-start | bytes 589832 | tf_op jit(solution)/shard_map/while/body/eval_jaxpr/ppermute | solution.py:194
  103.4 4.7 %collective-permute-done.refs_2_ = bf16[256,384]{1,0:T(8,128)(2,1)S(1)} collective-permute-done((bf16[256,384]{1,0:T(8,128)(2,1)S(1)}, bf16[256,384]{1,0:T(8,128)(2,1)S(1)}, u32[]{:S(2)}, u32[]{:S(2)}) %collective-permute-start) | collective-permute-done | bytes 196640 | tf_op jit(solution)/shard_map/while/body/eval_jaxpr/ppermute | solution.py:194
  108.1 3.0 %collective-permute-start.12 = (bf16[256,384]{1,0:T(8,128)(2,1)S(1)}, bf16[256,384]{1,0:T(8,128)(2,1)S(1)}, u32[]{:S(2)}, u32[]{:S(2)}) collective-permute-start(bf16[256,384]{1,0:T(8,128)(2,1)S(1)} %collective-permute-done.1.refs_3_), channel_id=1, source_target_pairs={{0,7},{1,0},{2,1},{3,2},{4,3},{5,4},{6,5},{7,6},{8,15},{9,8},{10,9... | collective-permute-start | bytes 589832 | tf_op jit(solution)/shard_map/while/body/eval_jaxpr/ppermute | solution.py:194
  111.1 3.2 %collective-permute-start.9 = (bf16[256,384]{1,0:T(8,128)(2,1)S(1)}, bf16[256,384]{1,0:T(8,128)(2,1)S(1)}, u32[]{:S(2)}, u32[]{:S(2)}) collective-permute-start(bf16[256,384]{1,0:T(8,128)(2,1)S(1)} %collective-permute-done.5.refs_1_), channel_id=1, source_target_pairs={{0,7},{1,0},{2,1},{3,2},{4,3},{5,4},{6,5},{7,6},{8,15},{9,8},{10,9... | collective-permute-start | bytes 589832 | tf_op jit(solution)/shard_map/while/body/eval_jaxpr/ppermute | solution.py:194
  114.3 1.5 constant_dynamic-slice_fusion.2
  116.0 3.9 %collective-permute-done.2.refs_4_ = bf16[256,384]{1,0:T(8,128)(2,1)S(1)} collective-permute-done((bf16[256,384]{1,0:T(8,128)(2,1)S(1)}, bf16[256,384]{1,0:T(8,128)(2,1)S(1)}, u32[]{:S(2)}, u32[]{:S(2)}) %collective-permute-start.2) | collective-permute-done | bytes 196640 | tf_op jit(solution)/shard_map/while/body/eval_jaxpr/ppermute | solution.py:194
  119.9 2.3 %collective-permute-done.6.refs_6_ = bf16[256,384]{1,0:T(8,128)(2,1)S(1)} collective-permute-done((bf16[256,384]{1,0:T(8,128)(2,1)S(1)}, bf16[256,384]{1,0:T(8,128)(2,1)S(1)}, u32[]{:S(2)}, u32[]{:S(2)}) %collective-permute-start.6) | collective-permute-done | bytes 196640 | tf_op jit(solution)/shard_map/while/body/eval_jaxpr/ppermute | solution.py:194
  122.2 2.0 %collective-permute-start.3 = (bf16[256,384]{1,0:T(8,128)(2,1)S(1)}, bf16[256,384]{1,0:T(8,128)(2,1)S(1)}, u32[]{:S(2)}, u32[]{:S(2)}) collective-permute-start(bf16[256,384]{1,0:T(8,128)(2,1)S(1)} %collective-permute-done.2.refs_4_), channel_id=1, source_target_pairs={{0,1},{1,2},{2,3},{3,4},{4,5},{5,6},{6,7},{7,0},{8,9},{9,10},{10,1... | collective-permute-start | bytes 589832 | tf_op jit(solution)/shard_map/while/body/eval_jaxpr/ppermute | solution.py:194
  124.2 1.2 collective-permute-start.10
  125.4 0.8 collective-permute-start.7
  126.2 3.3 %collective-permute-done.13.refs_9_ = bf16[256,384]{1,0:T(8,128)(2,1)S(1)} collective-permute-done((bf16[256,384]{1,0:T(8,128)(2,1)S(1)}, bf16[256,384]{1,0:T(8,128)(2,1)S(1)}, u32[]{:S(2)}, u32[]{:S(2)}) %collective-permute-start.13) | collective-permute-done | bytes 196640 | tf_op jit(solution)/shard_map/while/body/eval_jaxpr/ppermute | solution.py:194
  129.5 3.1 %collective-permute-start.14 = (bf16[256,384]{1,0:T(8,128)(2,1)S(1)}, bf16[256,384]{1,0:T(8,128)(2,1)S(1)}, u32[]{:S(2)}, u32[]{:S(2)}) collective-permute-start(bf16[256,384]{1,0:T(8,128)(2,1)S(1)} %collective-permute-done.13.refs_9_), channel_id=1, source_target_pairs={{0,15},{1,8},{2,9},{3,10},{4,11},{5,12},{6,13},{7,14},{8,7},{9,0},... | collective-permute-start | bytes 589832 | tf_op jit(solution)/shard_map/while/body/eval_jaxpr/ppermute | solution.py:200
  132.6 0.9 collective-permute-start.4
  133.5 0.2 collective-permute-done.10.refs_11_
  133.7 2.1 %collective-permute-start.11 = (bf16[256,384]{1,0:T(8,128)(2,1)S(1)}, bf16[256,384]{1,0:T(8,128)(2,1)S(1)}, u32[]{:S(2)}, u32[]{:S(2)}) collective-permute-start(bf16[256,384]{1,0:T(8,128)(2,1)S(1)} %collective-permute-done.10.refs_11_), channel_id=1, source_target_pairs={{0,7},{1,0},{2,1},{3,2},{4,3},{5,4},{6,5},{7,6},{8,15},{9,8},{10,9... | collective-permute-start | bytes 589832 | tf_op jit(solution)/shard_map/while/body/eval_jaxpr/ppermute | solution.py:194
  135.9 6.7 %qkv_partial.3 = (f32[3,272,256]{2,1,0:T(8,128)S(1)}, f32[2,256,128]{2,1,0:T(8,128)S(1)}, f32[256,128]{1,0:T(8,128)S(1)}, bf16[3,1536,256]{2,1,0:T(8,128)(2,1)S(1)}) custom-call(s32[12]{0:T(128)S(1)} %get-tuple-element.294.rows_ref, s32[4]{0:T(128)S(1)} %get-tuple-element.295.late_rows_ref.rows_ref, f32[16,1,384]{2,1,0:T(1,128)S(1)} %copy-done.2, ...), custom_call_target="tpu_custom_call" | custom-call | tf_op jit(solution)/shard_map/while/body/eval_jaxpr/qkv_partial/pallas_call | solution.py:130
  142.8 2.6 %attention_block.1.own_ref = bf16[256,256]{1,0:T(8,128)(2,1)S(1)} custom-call(s32[4]{0:T(128)S(1)} %get-tuple-element.295.late_rows_ref.rows_ref, f32[16,1,384]{2,1,0:T(1,128)S(1)} %copy-done.2, bf16[256,384]{1,0:T(8,128)(2,1)S(1)} %collective-permute-done.4.refs_0_, bf16[256,384]{1,0:T(8,128)(2,1)S(1)} %collective-permute-done.8.refs_1_, ...), custom_call_target="tpu_custom_call" | custom-call | tf_op jit(solution)/shard_map/while/body/eval_jaxpr/attention_block/pallas_call | solution.py:155
  145.4 2.3 %collective-permute-start.15 = (bf16[256,256]{1,0:T(8,128)(2,1)S(1)}, bf16[256,256]{1,0:T(8,128)(2,1)S(1)}, u32[]{:S(2)}, u32[]{:S(2)}) collective-permute-start(bf16[256,256]{1,0:T(8,128)(2,1)S(1)} %attention_block.1.own_ref), channel_id=1, source_target_pairs={{0,8},{8,0},{1,9},{9,1},{2,10},{10,2},{3,11},{11,3},{4,12},{12,4},... | collective-permute-start | bytes 393224 | tf_op jit(solution)/shard_map/while/body/eval_jaxpr/ppermute | solution.py:194
  147.7 15.9 %collective-permute-done.15.other_ref = bf16[256,256]{1,0:T(8,128)(2,1)S(1)} collective-permute-done((bf16[256,256]{1,0:T(8,128)(2,1)S(1)}, bf16[256,256]{1,0:T(8,128)(2,1)S(1)}, u32[]{:S(2)}, u32[]{:S(2)}) %collective-permute-start.15) | collective-permute-done | bytes 131104 | tf_op jit(solution)/shard_map/while/body/eval_jaxpr/ppermute | solution.py:194
  163.7 0.8 projection_block.6
  164.6 1.7 projection_block.7
  166.3 3.3 %collective-permute-start.21 = (bf16[256,384]{1,0:T(8,128)(2,1)S(1)}, bf16[256,384]{1,0:T(8,128)(2,1)S(1)}, u32[]{:S(2)}, u32[]{:S(2)}) collective-permute-start(bf16[256,384]{1,0:T(8,128)(2,1)S(1)} %get-tuple-element.265), channel_id=1, source_target_pairs={{0,7},{1,0},{2,1},{3,2},{4,3},{5,4},{6,5},{7,6},{8,15},{9,8},{10,9... | collective-permute-start | bytes 589832 | tf_op jit(solution)/shard_map/while/body/eval_jaxpr/ppermute | solution.py:194
  169.7 1.7 collective-permute-done.17
  171.6 1.3 collective-permute-done.21
  173.0 3.8 %collective-permute-start.22 = (bf16[256,384]{1,0:T(8,128)(2,1)S(1)}, bf16[256,384]{1,0:T(8,128)(2,1)S(1)}, u32[]{:S(2)}, u32[]{:S(2)}) collective-permute-start(bf16[256,384]{1,0:T(8,128)(2,1)S(1)} %add_convert_fusion.17), channel_id=1, source_target_pairs={{0,7},{1,0},{2,1},{3,2},{4,3},{5,4},{6,5},{7,6},{8,15},{9,8},{10,9... | collective-permute-start | bytes 589832 | tf_op jit(solution)/shard_map/while/body/eval_jaxpr/ppermute | solution.py:194
  176.8 2.8 %collective-permute-done.18 = bf16[256,384]{1,0:T(8,128)(2,1)S(1)} collective-permute-done((bf16[256,384]{1,0:T(8,128)(2,1)S(1)}, bf16[256,384]{1,0:T(8,128)(2,1)S(1)}, u32[]{:S(2)}, u32[]{:S(2)}) %collective-permute-start.18) | collective-permute-done | bytes 196640 | tf_op jit(solution)/shard_map/while/body/eval_jaxpr/ppermute | solution.py:194
  179.8 0.3 collective-permute-done.22
  180.2 7.5 %collective-permute-done.19 = bf16[256,384]{1,0:T(8,128)(2,1)S(1)} collective-permute-done((bf16[256,384]{1,0:T(8,128)(2,1)S(1)}, bf16[256,384]{1,0:T(8,128)(2,1)S(1)}, u32[]{:S(2)}, u32[]{:S(2)}) %collective-permute-start.19) | collective-permute-done | bytes 196640 | tf_op jit(solution)/shard_map/while/body/eval_jaxpr/ppermute | solution.py:194
  187.9 7.2 %collective-permute-done.20 = bf16[256,384]{1,0:T(8,128)(2,1)S(1)} collective-permute-done((bf16[256,384]{1,0:T(8,128)(2,1)S(1)}, bf16[256,384]{1,0:T(8,128)(2,1)S(1)}, u32[]{:S(2)}, u32[]{:S(2)}) %collective-permute-start.20) | collective-permute-done | bytes 196640 | tf_op jit(solution)/shard_map/while/body/eval_jaxpr/ppermute | solution.py:219
  195.1 0.7 copy-done.1
  (80 shorter events, 2.9 us)
Async XLA Ops:
  1.2 40.6 %copy-start.2 = (f32[16,1,384]{2,1,0:T(1,128)S(1)}, f32[16,1,384]{2,1,0:T(1,128)}, u32[]{:S(2)}) copy-start(f32[16,1,384]{2,1,0:T(1,128)} %get-tuple-element.296.gain_ref) | copy-start | bytes 73732 | tf_op jit(solution)/shard_map/while
  1.2 10.8 %collective-permute-start = (bf16[256,384]{1,0:T(8,128)(2,1)S(1)}, bf16[256,384]{1,0:T(8,128)(2,1)S(1)}, u32[]{:S(2)}, u32[]{:S(2)}) collective-permute-start(bf16[256,384]{1,0:T(8,128)(2,1)S(1)} %get-tuple-element.280.refs_0_), channel_id=1, source_target_pairs={{0,1},{1,2},{2,3},{3,4},{4,5},{5,6},{6,7},{7,0},{8,9},{9,10},{10,1... | collective-permute-start | bytes 589832 | tf_op jit(solution)/shard_map/while/body/eval_jaxpr/ppermute | solution.py:194
  3.2 8.8 %collective-permute-start.1 = (bf16[256,384]{1,0:T(8,128)(2,1)S(1)}, bf16[256,384]{1,0:T(8,128)(2,1)S(1)}, u32[]{:S(2)}, u32[]{:S(2)}) collective-permute-start(bf16[256,384]{1,0:T(8,128)(2,1)S(1)} %get-tuple-element.280.refs_0_), channel_id=1, source_target_pairs={{0,7},{1,0},{2,1},{3,2},{4,3},{5,4},{6,5},{7,6},{8,15},{9,8},{10,9... | collective-permute-start | bytes 589832 | tf_op jit(solution)/shard_map/while/body/eval_jaxpr/ppermute | solution.py:194
  7.2 7.9 %collective-permute-start.5 = (bf16[256,384]{1,0:T(8,128)(2,1)S(1)}, bf16[256,384]{1,0:T(8,128)(2,1)S(1)}, u32[]{:S(2)}, u32[]{:S(2)}) collective-permute-start(bf16[256,384]{1,0:T(8,128)(2,1)S(1)} %get-tuple-element.280.refs_0_), channel_id=1, source_target_pairs={{0,8},{8,0},{1,9},{9,1},{2,10},{10,2},{3,11},{11,3},{4,12},{12,4},... | collective-permute-start | bytes 589832 | tf_op jit(solution)/shard_map/while/body/eval_jaxpr/ppermute | solution.py:194
  12.0 7.9 %collective-permute-start.12 = (bf16[256,384]{1,0:T(8,128)(2,1)S(1)}, bf16[256,384]{1,0:T(8,128)(2,1)S(1)}, u32[]{:S(2)}, u32[]{:S(2)}) collective-permute-start(bf16[256,384]{1,0:T(8,128)(2,1)S(1)} %collective-permute-done.1.refs_3_), channel_id=1, source_target_pairs={{0,7},{1,0},{2,1},{3,2},{4,3},{5,4},{6,5},{7,6},{8,15},{9,8},{10,9... | collective-permute-start | bytes 589832 | tf_op jit(solution)/shard_map/while/body/eval_jaxpr/ppermute | solution.py:194
  15.0 8.7 %collective-permute-start.2 = (bf16[256,384]{1,0:T(8,128)(2,1)S(1)}, bf16[256,384]{1,0:T(8,128)(2,1)S(1)}, u32[]{:S(2)}, u32[]{:S(2)}) collective-permute-start(bf16[256,384]{1,0:T(8,128)(2,1)S(1)} %collective-permute-done.refs_2_), channel_id=1, source_target_pairs={{0,1},{1,2},{2,3},{3,4},{4,5},{5,6},{6,7},{7,0},{8,9},{9,10},{10,1... | collective-permute-start | bytes 589832 | tf_op jit(solution)/shard_map/while/body/eval_jaxpr/ppermute | solution.py:194
  15.1 8.7 %collective-permute-start.9 = (bf16[256,384]{1,0:T(8,128)(2,1)S(1)}, bf16[256,384]{1,0:T(8,128)(2,1)S(1)}, u32[]{:S(2)}, u32[]{:S(2)}) collective-permute-start(bf16[256,384]{1,0:T(8,128)(2,1)S(1)} %collective-permute-done.5.refs_1_), channel_id=1, source_target_pairs={{0,7},{1,0},{2,1},{3,2},{4,3},{5,4},{6,5},{7,6},{8,15},{9,8},{10,9... | collective-permute-start | bytes 589832 | tf_op jit(solution)/shard_map/while/body/eval_jaxpr/ppermute | solution.py:194
  18.3 7.9 %collective-permute-start.6 = (bf16[256,384]{1,0:T(8,128)(2,1)S(1)}, bf16[256,384]{1,0:T(8,128)(2,1)S(1)}, u32[]{:S(2)}, u32[]{:S(2)}) collective-permute-start(bf16[256,384]{1,0:T(8,128)(2,1)S(1)} %collective-permute-done.5.refs_1_), channel_id=1, source_target_pairs={{0,1},{1,2},{2,3},{3,4},{4,5},{5,6},{6,7},{7,0},{8,9},{9,10},{10,1... | collective-permute-start | bytes 589832 | tf_op jit(solution)/shard_map/while/body/eval_jaxpr/ppermute | solution.py:194
  26.1 41.6 %collective-permute-start.16 = (bf16[256,3072]{1,0:T(8,128)(2,1)S(1)}, bf16[256,3072]{1,0:T(8,128)(2,1)S(1)}, u32[]{:S(2)}, u32[]{:S(2)}) collective-permute-start(bf16[256,3072]{1,0:T(8,128)(2,1)S(1)} %constant_dynamic-slice_fusion.2), channel_id=1, source_target_pairs={{0,8},{8,0},{1,9},{9,1},{2,10},{10,2},{3,11},{11,3},{4,12},{12,4},... | collective-permute-start | bytes 4718600 | tf_op jit(solution)/shard_map/while/body/eval_jaxpr/ppermute | solution.py:194
  27.7 7.8 %collective-permute-start.13 = (bf16[256,384]{1,0:T(8,128)(2,1)S(1)}, bf16[256,384]{1,0:T(8,128)(2,1)S(1)}, u32[]{:S(2)}, u32[]{:S(2)}) collective-permute-start(bf16[256,384]{1,0:T(8,128)(2,1)S(1)} %collective-permute-done.12.refs_5_), channel_id=1, source_target_pairs={{0,7},{1,0},{2,1},{3,2},{4,3},{5,4},{6,5},{7,6},{8,15},{9,8},{10,9... | collective-permute-start | bytes 589832 | tf_op jit(solution)/shard_map/while/body/eval_jaxpr/ppermute | solution.py:194
  27.8 9.0 %collective-permute-start.3 = (bf16[256,384]{1,0:T(8,128)(2,1)S(1)}, bf16[256,384]{1,0:T(8,128)(2,1)S(1)}, u32[]{:S(2)}, u32[]{:S(2)}) collective-permute-start(bf16[256,384]{1,0:T(8,128)(2,1)S(1)} %collective-permute-done.2.refs_4_), channel_id=1, source_target_pairs={{0,1},{1,2},{2,3},{3,4},{4,5},{5,6},{6,7},{7,0},{8,9},{9,10},{10,1... | collective-permute-start | bytes 589832 | tf_op jit(solution)/shard_map/while/body/eval_jaxpr/ppermute | solution.py:194
  29.7 10.0 %collective-permute-start.10 = (bf16[256,384]{1,0:T(8,128)(2,1)S(1)}, bf16[256,384]{1,0:T(8,128)(2,1)S(1)}, u32[]{:S(2)}, u32[]{:S(2)}) collective-permute-start(bf16[256,384]{1,0:T(8,128)(2,1)S(1)} %collective-permute-done.9.refs_7_), channel_id=1, source_target_pairs={{0,7},{1,0},{2,1},{3,2},{4,3},{5,4},{6,5},{7,6},{8,15},{9,8},{10,9... | collective-permute-start | bytes 589832 | tf_op jit(solution)/shard_map/while/body/eval_jaxpr/ppermute | solution.py:194
  31.1 10.0 %collective-permute-start.7 = (bf16[256,384]{1,0:T(8,128)(2,1)S(1)}, bf16[256,384]{1,0:T(8,128)(2,1)S(1)}, u32[]{:S(2)}, u32[]{:S(2)}) collective-permute-start(bf16[256,384]{1,0:T(8,128)(2,1)S(1)} %collective-permute-done.6.refs_6_), channel_id=1, source_target_pairs={{0,1},{1,2},{2,3},{3,4},{4,5},{5,6},{6,7},{7,0},{8,9},{9,10},{10,1... | collective-permute-start | bytes 589832 | tf_op jit(solution)/shard_map/while/body/eval_jaxpr/ppermute | solution.py:194
  35.6 12.9 %collective-permute-start.14 = (bf16[256,384]{1,0:T(8,128)(2,1)S(1)}, bf16[256,384]{1,0:T(8,128)(2,1)S(1)}, u32[]{:S(2)}, u32[]{:S(2)}) collective-permute-start(bf16[256,384]{1,0:T(8,128)(2,1)S(1)} %collective-permute-done.13.refs_9_), channel_id=1, source_target_pairs={{0,15},{1,8},{2,9},{3,10},{4,11},{5,12},{6,13},{7,14},{8,7},{9,0},... | collective-permute-start | bytes 589832 | tf_op jit(solution)/shard_map/while/body/eval_jaxpr/ppermute | solution.py:200
  36.8 11.7 %collective-permute-start.4 = (bf16[256,384]{1,0:T(8,128)(2,1)S(1)}, bf16[256,384]{1,0:T(8,128)(2,1)S(1)}, u32[]{:S(2)}, u32[]{:S(2)}) collective-permute-start(bf16[256,384]{1,0:T(8,128)(2,1)S(1)} %collective-permute-done.3.refs_8_), channel_id=1, source_target_pairs={{0,1},{1,2},{2,3},{3,4},{4,5},{5,6},{6,7},{7,0},{8,9},{9,10},{10,1... | collective-permute-start | bytes 589832 | tf_op jit(solution)/shard_map/while/body/eval_jaxpr/ppermute | solution.py:194
  39.8 8.7 %collective-permute-start.11 = (bf16[256,384]{1,0:T(8,128)(2,1)S(1)}, bf16[256,384]{1,0:T(8,128)(2,1)S(1)}, u32[]{:S(2)}, u32[]{:S(2)}) collective-permute-start(bf16[256,384]{1,0:T(8,128)(2,1)S(1)} %collective-permute-done.10.refs_11_), channel_id=1, source_target_pairs={{0,7},{1,0},{2,1},{3,2},{4,3},{5,4},{6,5},{7,6},{8,15},{9,8},{10,9... | collective-permute-start | bytes 589832 | tf_op jit(solution)/shard_map/while/body/eval_jaxpr/ppermute | solution.py:194
  41.0 7.5 %collective-permute-start.8 = (bf16[256,384]{1,0:T(8,128)(2,1)S(1)}, bf16[256,384]{1,0:T(8,128)(2,1)S(1)}, u32[]{:S(2)}, u32[]{:S(2)}) collective-permute-start(bf16[256,384]{1,0:T(8,128)(2,1)S(1)} %collective-permute-done.7.refs_10_), channel_id=1, source_target_pairs={{0,1},{1,2},{2,3},{3,4},{4,5},{5,6},{6,7},{7,0},{8,9},{9,10},{10,1... | collective-permute-start | bytes 589832 | tf_op jit(solution)/shard_map/while/body/eval_jaxpr/ppermute | solution.py:194
  41.8 6.7 %copy-start.3 = (f32[1,2,128]{2,1,0:T(2,128)S(1)}, f32[1,2,128]{2,1,0:T(2,128)}, u32[]{:S(2)}) copy-start(f32[1,2,128]{2,1,0:T(2,128)} %get-tuple-element.298) | copy-start | bytes 3076 | tf_op jit(solution)/shard_map/while
  48.5 19.3 %copy-start = (bf16[256,6144]{1,0:T(8,128)(2,1)S(1)}, bf16[256,6144]{1,0:T(8,128)(2,1)}, u32[]{:S(2)}) copy-start(bf16[256,6144]{1,0:T(8,128)(2,1)} %get-tuple-element.257.w_own_ref) | copy-start | bytes 9437188 | tf_op jit(solution)/shard_map/while
  51.2 16.6 %collective-permute-start.15 = (bf16[256,256]{1,0:T(8,128)(2,1)S(1)}, bf16[256,256]{1,0:T(8,128)(2,1)S(1)}, u32[]{:S(2)}, u32[]{:S(2)}) collective-permute-start(bf16[256,256]{1,0:T(8,128)(2,1)S(1)} %attention_block.1.own_ref), channel_id=1, source_target_pairs={{0,8},{8,0},{1,9},{9,1},{2,10},{10,2},{3,11},{11,3},{4,12},{12,4},... | collective-permute-start | bytes 393224 | tf_op jit(solution)/shard_map/while/body/eval_jaxpr/ppermute | solution.py:194
  68.6 7.0 %collective-permute-start.17 = (bf16[256,384]{1,0:T(8,128)(2,1)S(1)}, bf16[256,384]{1,0:T(8,128)(2,1)S(1)}, u32[]{:S(2)}, u32[]{:S(2)}) collective-permute-start(bf16[256,384]{1,0:T(8,128)(2,1)S(1)} %projection_block.6), channel_id=1, source_target_pairs={{0,1},{1,2},{2,3},{3,4},{4,5},{5,6},{6,7},{7,0},{8,9},{9,10},{10,1... | collective-permute-start | bytes 589832 | tf_op jit(solution)/shard_map/while/body/eval_jaxpr/ppermute | solution.py:194
  70.4 6.5 %collective-permute-start.21 = (bf16[256,384]{1,0:T(8,128)(2,1)S(1)}, bf16[256,384]{1,0:T(8,128)(2,1)S(1)}, u32[]{:S(2)}, u32[]{:S(2)}) collective-permute-start(bf16[256,384]{1,0:T(8,128)(2,1)S(1)} %get-tuple-element.265), channel_id=1, source_target_pairs={{0,7},{1,0},{2,1},{3,2},{4,3},{5,4},{6,5},{7,6},{8,15},{9,8},{10,9... | collective-permute-start | bytes 589832 | tf_op jit(solution)/shard_map/while/body/eval_jaxpr/ppermute | solution.py:194
  73.8 19.1 %collective-permute-start.24 = (bf16[256,384]{1,0:T(8,128)(2,1)S(1)}, bf16[256,384]{1,0:T(8,128)(2,1)S(1)}, u32[]{:S(2)}, u32[]{:S(2)}) collective-permute-start(bf16[256,384]{1,0:T(8,128)(2,1)S(1)} %add_convert_fusion.19), channel_id=1, source_target_pairs={{0,16},{1,17},{2,18},{3,19},{4,20},{5,21},{6,22},{7,23},{8,24},{9,... | collective-permute-start | bytes 589832 | tf_op jit(solution)/shard_map/while/body/eval_jaxpr/ppermute | solution.py:219
  75.6 8.7 %collective-permute-start.18 = (bf16[256,384]{1,0:T(8,128)(2,1)S(1)}, bf16[256,384]{1,0:T(8,128)(2,1)S(1)}, u32[]{:S(2)}, u32[]{:S(2)}) collective-permute-start(bf16[256,384]{1,0:T(8,128)(2,1)S(1)} %add_convert_fusion.14), channel_id=1, source_target_pairs={{0,1},{1,2},{2,3},{3,4},{4,5},{5,6},{6,7},{7,0},{8,9},{9,10},{10,1... | collective-permute-start | bytes 589832 | tf_op jit(solution)/shard_map/while/body/eval_jaxpr/ppermute | solution.py:194
  76.9 7.6 %collective-permute-start.22 = (bf16[256,384]{1,0:T(8,128)(2,1)S(1)}, bf16[256,384]{1,0:T(8,128)(2,1)S(1)}, u32[]{:S(2)}, u32[]{:S(2)}) collective-permute-start(bf16[256,384]{1,0:T(8,128)(2,1)S(1)} %add_convert_fusion.17), channel_id=1, source_target_pairs={{0,7},{1,0},{2,1},{3,2},{4,3},{5,4},{6,5},{7,6},{8,15},{9,8},{10,9... | collective-permute-start | bytes 589832 | tf_op jit(solution)/shard_map/while/body/eval_jaxpr/ppermute | solution.py:194
  84.4 8.3 %collective-permute-start.19 = (bf16[256,384]{1,0:T(8,128)(2,1)S(1)}, bf16[256,384]{1,0:T(8,128)(2,1)S(1)}, u32[]{:S(2)}, u32[]{:S(2)}) collective-permute-start(bf16[256,384]{1,0:T(8,128)(2,1)S(1)} %add_convert_fusion.15), channel_id=1, source_target_pairs={{0,1},{1,2},{2,3},{3,4},{4,5},{5,6},{6,7},{7,0},{8,9},{9,10},{10,1... | collective-permute-start | bytes 589832 | tf_op jit(solution)/shard_map/while/body/eval_jaxpr/ppermute | solution.py:194
  84.6 8.3 %collective-permute-start.23 = (bf16[256,384]{1,0:T(8,128)(2,1)S(1)}, bf16[256,384]{1,0:T(8,128)(2,1)S(1)}, u32[]{:S(2)}, u32[]{:S(2)}) collective-permute-start(bf16[256,384]{1,0:T(8,128)(2,1)S(1)} %add_convert_fusion.18), channel_id=1, source_target_pairs={{0,23},{1,16},{2,17},{3,18},{4,19},{5,20},{6,21},{7,22},{8,31},{9,... | collective-permute-start | bytes 589832 | tf_op jit(solution)/shard_map/while/body/eval_jaxpr/ppermute | solution.py:219
  92.7 7.3 %collective-permute-start.20 = (bf16[256,384]{1,0:T(8,128)(2,1)S(1)}, bf16[256,384]{1,0:T(8,128)(2,1)S(1)}, u32[]{:S(2)}, u32[]{:S(2)}) collective-permute-start(bf16[256,384]{1,0:T(8,128)(2,1)S(1)} %add_convert_fusion.16), channel_id=1, source_target_pairs={{0,17},{1,18},{2,19},{3,20},{4,21},{5,22},{6,23},{7,16},{8,25},{9,... | collective-permute-start | bytes 589832 | tf_op jit(solution)/shard_map/while/body/eval_jaxpr/ppermute | solution.py:219
  100.1 35.8 %copy-start.2 = (f32[16,1,384]{2,1,0:T(1,128)S(1)}, f32[16,1,384]{2,1,0:T(1,128)}, u32[]{:S(2)}) copy-start(f32[16,1,384]{2,1,0:T(1,128)} %get-tuple-element.296.gain_ref) | copy-start | bytes 73732 | tf_op jit(solution)/shard_map/while
  100.1 8.0 %collective-permute-start = (bf16[256,384]{1,0:T(8,128)(2,1)S(1)}, bf16[256,384]{1,0:T(8,128)(2,1)S(1)}, u32[]{:S(2)}, u32[]{:S(2)}) collective-permute-start(bf16[256,384]{1,0:T(8,128)(2,1)S(1)} %get-tuple-element.280.refs_0_), channel_id=1, source_target_pairs={{0,1},{1,2},{2,3},{3,4},{4,5},{5,6},{6,7},{7,0},{8,9},{9,10},{10,1... | collective-permute-start | bytes 589832 | tf_op jit(solution)/shard_map/while/body/eval_jaxpr/ppermute | solution.py:194
  100.2 7.9 %collective-permute-start.1 = (bf16[256,384]{1,0:T(8,128)(2,1)S(1)}, bf16[256,384]{1,0:T(8,128)(2,1)S(1)}, u32[]{:S(2)}, u32[]{:S(2)}) collective-permute-start(bf16[256,384]{1,0:T(8,128)(2,1)S(1)} %get-tuple-element.280.refs_0_), channel_id=1, source_target_pairs={{0,7},{1,0},{2,1},{3,2},{4,3},{5,4},{6,5},{7,6},{8,15},{9,8},{10,9... | collective-permute-start | bytes 589832 | tf_op jit(solution)/shard_map/while/body/eval_jaxpr/ppermute | solution.py:194
  103.4 7.7 %collective-permute-start.5 = (bf16[256,384]{1,0:T(8,128)(2,1)S(1)}, bf16[256,384]{1,0:T(8,128)(2,1)S(1)}, u32[]{:S(2)}, u32[]{:S(2)}) collective-permute-start(bf16[256,384]{1,0:T(8,128)(2,1)S(1)} %get-tuple-element.280.refs_0_), channel_id=1, source_target_pairs={{0,8},{8,0},{1,9},{9,1},{2,10},{10,2},{3,11},{11,3},{4,12},{12,4},... | collective-permute-start | bytes 589832 | tf_op jit(solution)/shard_map/while/body/eval_jaxpr/ppermute | solution.py:194
  108.1 7.9 %collective-permute-start.12 = (bf16[256,384]{1,0:T(8,128)(2,1)S(1)}, bf16[256,384]{1,0:T(8,128)(2,1)S(1)}, u32[]{:S(2)}, u32[]{:S(2)}) collective-permute-start(bf16[256,384]{1,0:T(8,128)(2,1)S(1)} %collective-permute-done.1.refs_3_), channel_id=1, source_target_pairs={{0,7},{1,0},{2,1},{3,2},{4,3},{5,4},{6,5},{7,6},{8,15},{9,8},{10,9... | collective-permute-start | bytes 589832 | tf_op jit(solution)/shard_map/while/body/eval_jaxpr/ppermute | solution.py:194
  111.1 8.8 %collective-permute-start.2 = (bf16[256,384]{1,0:T(8,128)(2,1)S(1)}, bf16[256,384]{1,0:T(8,128)(2,1)S(1)}, u32[]{:S(2)}, u32[]{:S(2)}) collective-permute-start(bf16[256,384]{1,0:T(8,128)(2,1)S(1)} %collective-permute-done.refs_2_), channel_id=1, source_target_pairs={{0,1},{1,2},{2,3},{3,4},{4,5},{5,6},{6,7},{7,0},{8,9},{9,10},{10,1... | collective-permute-start | bytes 589832 | tf_op jit(solution)/shard_map/while/body/eval_jaxpr/ppermute | solution.py:194
  111.1 8.8 %collective-permute-start.9 = (bf16[256,384]{1,0:T(8,128)(2,1)S(1)}, bf16[256,384]{1,0:T(8,128)(2,1)S(1)}, u32[]{:S(2)}, u32[]{:S(2)}) collective-permute-start(bf16[256,384]{1,0:T(8,128)(2,1)S(1)} %collective-permute-done.5.refs_1_), channel_id=1, source_target_pairs={{0,7},{1,0},{2,1},{3,2},{4,3},{5,4},{6,5},{7,6},{8,15},{9,8},{10,9... | collective-permute-start | bytes 589832 | tf_op jit(solution)/shard_map/while/body/eval_jaxpr/ppermute | solution.py:194
  114.3 7.9 %collective-permute-start.6 = (bf16[256,384]{1,0:T(8,128)(2,1)S(1)}, bf16[256,384]{1,0:T(8,128)(2,1)S(1)}, u32[]{:S(2)}, u32[]{:S(2)}) collective-permute-start(bf16[256,384]{1,0:T(8,128)(2,1)S(1)} %collective-permute-done.5.refs_1_), channel_id=1, source_target_pairs={{0,1},{1,2},{2,3},{3,4},{4,5},{5,6},{6,7},{7,0},{8,9},{9,10},{10,1... | collective-permute-start | bytes 589832 | tf_op jit(solution)/shard_map/while/body/eval_jaxpr/ppermute | solution.py:194
  122.2 41.5 %collective-permute-start.16 = (bf16[256,3072]{1,0:T(8,128)(2,1)S(1)}, bf16[256,3072]{1,0:T(8,128)(2,1)S(1)}, u32[]{:S(2)}, u32[]{:S(2)}) collective-permute-start(bf16[256,3072]{1,0:T(8,128)(2,1)S(1)} %constant_dynamic-slice_fusion.2), channel_id=1, source_target_pairs={{0,8},{8,0},{1,9},{9,1},{2,10},{10,2},{3,11},{11,3},{4,12},{12,4},... | collective-permute-start | bytes 4718600 | tf_op jit(solution)/shard_map/while/body/eval_jaxpr/ppermute | solution.py:194
  122.2 7.3 %collective-permute-start.13 = (bf16[256,384]{1,0:T(8,128)(2,1)S(1)}, bf16[256,384]{1,0:T(8,128)(2,1)S(1)}, u32[]{:S(2)}, u32[]{:S(2)}) collective-permute-start(bf16[256,384]{1,0:T(8,128)(2,1)S(1)} %collective-permute-done.12.refs_5_), channel_id=1, source_target_pairs={{0,7},{1,0},{2,1},{3,2},{4,3},{5,4},{6,5},{7,6},{8,15},{9,8},{10,9... | collective-permute-start | bytes 589832 | tf_op jit(solution)/shard_map/while/body/eval_jaxpr/ppermute | solution.py:194
  122.2 10.4 %collective-permute-start.3 = (bf16[256,384]{1,0:T(8,128)(2,1)S(1)}, bf16[256,384]{1,0:T(8,128)(2,1)S(1)}, u32[]{:S(2)}, u32[]{:S(2)}) collective-permute-start(bf16[256,384]{1,0:T(8,128)(2,1)S(1)} %collective-permute-done.2.refs_4_), channel_id=1, source_target_pairs={{0,1},{1,2},{2,3},{3,4},{4,5},{5,6},{6,7},{7,0},{8,9},{9,10},{10,1... | collective-permute-start | bytes 589832 | tf_op jit(solution)/shard_map/while/body/eval_jaxpr/ppermute | solution.py:194
  124.2 9.5 %collective-permute-start.10 = (bf16[256,384]{1,0:T(8,128)(2,1)S(1)}, bf16[256,384]{1,0:T(8,128)(2,1)S(1)}, u32[]{:S(2)}, u32[]{:S(2)}) collective-permute-start(bf16[256,384]{1,0:T(8,128)(2,1)S(1)} %collective-permute-done.9.refs_7_), channel_id=1, source_target_pairs={{0,7},{1,0},{2,1},{3,2},{4,3},{5,4},{6,5},{7,6},{8,15},{9,8},{10,9... | collective-permute-start | bytes 589832 | tf_op jit(solution)/shard_map/while/body/eval_jaxpr/ppermute | solution.py:194
  125.4 10.5 %collective-permute-start.7 = (bf16[256,384]{1,0:T(8,128)(2,1)S(1)}, bf16[256,384]{1,0:T(8,128)(2,1)S(1)}, u32[]{:S(2)}, u32[]{:S(2)}) collective-permute-start(bf16[256,384]{1,0:T(8,128)(2,1)S(1)} %collective-permute-done.6.refs_6_), channel_id=1, source_target_pairs={{0,1},{1,2},{2,3},{3,4},{4,5},{5,6},{6,7},{7,0},{8,9},{9,10},{10,1... | collective-permute-start | bytes 589832 | tf_op jit(solution)/shard_map/while/body/eval_jaxpr/ppermute | solution.py:194
  129.5 13.1 %collective-permute-start.14 = (bf16[256,384]{1,0:T(8,128)(2,1)S(1)}, bf16[256,384]{1,0:T(8,128)(2,1)S(1)}, u32[]{:S(2)}, u32[]{:S(2)}) collective-permute-start(bf16[256,384]{1,0:T(8,128)(2,1)S(1)} %collective-permute-done.13.refs_9_), channel_id=1, source_target_pairs={{0,15},{1,8},{2,9},{3,10},{4,11},{5,12},{6,13},{7,14},{8,7},{9,0},... | collective-permute-start | bytes 589832 | tf_op jit(solution)/shard_map/while/body/eval_jaxpr/ppermute | solution.py:200
  132.6 10.0 %collective-permute-start.4 = (bf16[256,384]{1,0:T(8,128)(2,1)S(1)}, bf16[256,384]{1,0:T(8,128)(2,1)S(1)}, u32[]{:S(2)}, u32[]{:S(2)}) collective-permute-start(bf16[256,384]{1,0:T(8,128)(2,1)S(1)} %collective-permute-done.3.refs_8_), channel_id=1, source_target_pairs={{0,1},{1,2},{2,3},{3,4},{4,5},{5,6},{6,7},{7,0},{8,9},{9,10},{10,1... | collective-permute-start | bytes 589832 | tf_op jit(solution)/shard_map/while/body/eval_jaxpr/ppermute | solution.py:194
  133.7 8.9 %collective-permute-start.11 = (bf16[256,384]{1,0:T(8,128)(2,1)S(1)}, bf16[256,384]{1,0:T(8,128)(2,1)S(1)}, u32[]{:S(2)}, u32[]{:S(2)}) collective-permute-start(bf16[256,384]{1,0:T(8,128)(2,1)S(1)} %collective-permute-done.10.refs_11_), channel_id=1, source_target_pairs={{0,7},{1,0},{2,1},{3,2},{4,3},{5,4},{6,5},{7,6},{8,15},{9,8},{10,9... | collective-permute-start | bytes 589832 | tf_op jit(solution)/shard_map/while/body/eval_jaxpr/ppermute | solution.py:194
  135.9 6.9 %collective-permute-start.8 = (bf16[256,384]{1,0:T(8,128)(2,1)S(1)}, bf16[256,384]{1,0:T(8,128)(2,1)S(1)}, u32[]{:S(2)}, u32[]{:S(2)}) collective-permute-start(bf16[256,384]{1,0:T(8,128)(2,1)S(1)} %collective-permute-done.7.refs_10_), channel_id=1, source_target_pairs={{0,1},{1,2},{2,3},{3,4},{4,5},{5,6},{6,7},{7,0},{8,9},{9,10},{10,1... | collective-permute-start | bytes 589832 | tf_op jit(solution)/shard_map/while/body/eval_jaxpr/ppermute | solution.py:194
  135.9 6.9 %copy-start.3 = (f32[1,2,128]{2,1,0:T(2,128)S(1)}, f32[1,2,128]{2,1,0:T(2,128)}, u32[]{:S(2)}) copy-start(f32[1,2,128]{2,1,0:T(2,128)} %get-tuple-element.298) | copy-start | bytes 3076 | tf_op jit(solution)/shard_map/while
  142.6 21.1 %copy-start = (bf16[256,6144]{1,0:T(8,128)(2,1)S(1)}, bf16[256,6144]{1,0:T(8,128)(2,1)}, u32[]{:S(2)}) copy-start(bf16[256,6144]{1,0:T(8,128)(2,1)} %get-tuple-element.257.w_own_ref) | copy-start | bytes 9437188 | tf_op jit(solution)/shard_map/while
  145.4 18.3 %collective-permute-start.15 = (bf16[256,256]{1,0:T(8,128)(2,1)S(1)}, bf16[256,256]{1,0:T(8,128)(2,1)S(1)}, u32[]{:S(2)}, u32[]{:S(2)}) collective-permute-start(bf16[256,256]{1,0:T(8,128)(2,1)S(1)} %attention_block.1.own_ref), channel_id=1, source_target_pairs={{0,8},{8,0},{1,9},{9,1},{2,10},{10,2},{3,11},{11,3},{4,12},{12,4},... | collective-permute-start | bytes 393224 | tf_op jit(solution)/shard_map/while/body/eval_jaxpr/ppermute | solution.py:194
  164.5 7.0 %collective-permute-start.17 = (bf16[256,384]{1,0:T(8,128)(2,1)S(1)}, bf16[256,384]{1,0:T(8,128)(2,1)S(1)}, u32[]{:S(2)}, u32[]{:S(2)}) collective-permute-start(bf16[256,384]{1,0:T(8,128)(2,1)S(1)} %projection_block.6), channel_id=1, source_target_pairs={{0,1},{1,2},{2,3},{3,4},{4,5},{5,6},{6,7},{7,0},{8,9},{9,10},{10,1... | collective-permute-start | bytes 589832 | tf_op jit(solution)/shard_map/while/body/eval_jaxpr/ppermute | solution.py:194
  166.3 6.7 %collective-permute-start.21 = (bf16[256,384]{1,0:T(8,128)(2,1)S(1)}, bf16[256,384]{1,0:T(8,128)(2,1)S(1)}, u32[]{:S(2)}, u32[]{:S(2)}) collective-permute-start(bf16[256,384]{1,0:T(8,128)(2,1)S(1)} %get-tuple-element.265), channel_id=1, source_target_pairs={{0,7},{1,0},{2,1},{3,2},{4,3},{5,4},{6,5},{7,6},{8,15},{9,8},{10,9... | collective-permute-start | bytes 589832 | tf_op jit(solution)/shard_map/while/body/eval_jaxpr/ppermute | solution.py:194
  169.6 18.2 %collective-permute-start.24 = (bf16[256,384]{1,0:T(8,128)(2,1)S(1)}, bf16[256,384]{1,0:T(8,128)(2,1)S(1)}, u32[]{:S(2)}, u32[]{:S(2)}) collective-permute-start(bf16[256,384]{1,0:T(8,128)(2,1)S(1)} %add_convert_fusion.19), channel_id=1, source_target_pairs={{0,16},{1,17},{2,18},{3,19},{4,20},{5,21},{6,22},{7,23},{8,24},{9,... | collective-permute-start | bytes 589832 | tf_op jit(solution)/shard_map/while/body/eval_jaxpr/ppermute | solution.py:219
  171.5 8.1 %collective-permute-start.18 = (bf16[256,384]{1,0:T(8,128)(2,1)S(1)}, bf16[256,384]{1,0:T(8,128)(2,1)S(1)}, u32[]{:S(2)}, u32[]{:S(2)}) collective-permute-start(bf16[256,384]{1,0:T(8,128)(2,1)S(1)} %add_convert_fusion.14), channel_id=1, source_target_pairs={{0,1},{1,2},{2,3},{3,4},{4,5},{5,6},{6,7},{7,0},{8,9},{9,10},{10,1... | collective-permute-start | bytes 589832 | tf_op jit(solution)/shard_map/while/body/eval_jaxpr/ppermute | solution.py:194
  173.0 7.0 %collective-permute-start.22 = (bf16[256,384]{1,0:T(8,128)(2,1)S(1)}, bf16[256,384]{1,0:T(8,128)(2,1)S(1)}, u32[]{:S(2)}, u32[]{:S(2)}) collective-permute-start(bf16[256,384]{1,0:T(8,128)(2,1)S(1)} %add_convert_fusion.17), channel_id=1, source_target_pairs={{0,7},{1,0},{2,1},{3,2},{4,3},{5,4},{6,5},{7,6},{8,15},{9,8},{10,9... | collective-permute-start | bytes 589832 | tf_op jit(solution)/shard_map/while/body/eval_jaxpr/ppermute | solution.py:194
  179.7 8.0 %collective-permute-start.19 = (bf16[256,384]{1,0:T(8,128)(2,1)S(1)}, bf16[256,384]{1,0:T(8,128)(2,1)S(1)}, u32[]{:S(2)}, u32[]{:S(2)}) collective-permute-start(bf16[256,384]{1,0:T(8,128)(2,1)S(1)} %add_convert_fusion.15), channel_id=1, source_target_pairs={{0,1},{1,2},{2,3},{3,4},{4,5},{5,6},{6,7},{7,0},{8,9},{9,10},{10,1... | collective-permute-start | bytes 589832 | tf_op jit(solution)/shard_map/while/body/eval_jaxpr/ppermute | solution.py:194
  180.1 7.8 %collective-permute-start.23 = (bf16[256,384]{1,0:T(8,128)(2,1)S(1)}, bf16[256,384]{1,0:T(8,128)(2,1)S(1)}, u32[]{:S(2)}, u32[]{:S(2)}) collective-permute-start(bf16[256,384]{1,0:T(8,128)(2,1)S(1)} %add_convert_fusion.18), channel_id=1, source_target_pairs={{0,23},{1,16},{2,17},{3,18},{4,19},{5,20},{6,21},{7,22},{8,31},{9,... | collective-permute-start | bytes 589832 | tf_op jit(solution)/shard_map/while/body/eval_jaxpr/ppermute | solution.py:219
  187.8 7.3 %collective-permute-start.20 = (bf16[256,384]{1,0:T(8,128)(2,1)S(1)}, bf16[256,384]{1,0:T(8,128)(2,1)S(1)}, u32[]{:S(2)}, u32[]{:S(2)}) collective-permute-start(bf16[256,384]{1,0:T(8,128)(2,1)S(1)} %add_convert_fusion.16), channel_id=1, source_target_pairs={{0,17},{1,18},{2,19},{3,20},{4,21},{5,22},{6,23},{7,16},{8,25},{9,... | collective-permute-start | bytes 589832 | tf_op jit(solution)/shard_map/while/body/eval_jaxpr/ppermute | solution.py:219
  195.1 0.7 copy-start.1

commit v3 on v1

--- a/solution.py
+++ b/solution.py
@@ -62,9 +62,14 @@
         sums_ref[1, part, :] = squares
 
 
-def partial_block(blocks, rows_ref, late_rows_ref, gain_ref, w_hbm, *refs):
-    x_refs, (acc_ref, sums_ref, shift_ref, w_late_ref, scaled_ref, w_ref, w_sem, late_sem) = refs[:blocks], refs[blocks:]
-    width = x_refs[0].shape[1]
+def single(refs):
+    return [view for ref in refs for view in ([ref] if len(ref.shape) == 2 else [ref.at[i] for i in range(ref.shape[0])])]
+
+
+def partial_block(arrays, rows_ref, late_rows_ref, gain_ref, w_hbm, *refs):
+    acc_ref, sums_ref, shift_ref, w_late_ref, scaled_ref, w_ref, w_sem, late_sem = refs[arrays:]
+    x_refs = single(refs[:arrays])
+    blocks, width = len(x_refs), x_refs[0].shape[1]
     now = fetches(rows_ref, w_hbm, w_ref, w_sem, blocks, width)
     late = fetches(late_rows_ref, w_hbm, w_late_ref, late_sem, LATE, width)
     for copy in now + late:
@@ -88,11 +93,9 @@
         copy.wait()
 
 
-def final_block(blocks, pieces, rows_ref, gain_ref, *refs):
-    x_refs, (acc_ref, before_ref, shift_ref, w_ref, qk_gain_ref, out_ref, sums_ref, scaled_ref) = (
-        refs[:blocks],
-        refs[blocks:],
-    )
+def final_block(arrays, pieces, rows_ref, gain_ref, *refs):
+    acc_ref, before_ref, shift_ref, w_ref, qk_gain_ref, out_ref, sums_ref, scaled_ref = refs[arrays:]
+    x_refs = single(refs[:arrays])
     patches, width = x_refs[0].shape
     full_width = pieces * width
     scale_blocks(False, rows_ref, gain_ref, x_refs, before_ref, sums_ref, shift_ref, scaled_ref)
@@ -126,16 +129,16 @@
 def partial(rows, late_rows, gain, w_planes, blocks):
     patches, width = blocks[0].shape
     planes, _, cols = w_planes.shape
-    count = len(blocks)
+    count = rows.shape[0]
     return pl.pallas_call(
-        functools.partial(partial_block, count),
+        functools.partial(partial_block, len(blocks)),
         out_shape=[
             jax.ShapeDtypeStruct((planes, patches + EXTRA, cols), jnp.float32),
             jax.ShapeDtypeStruct((2, patches, 128), jnp.float32),
             jax.ShapeDtypeStruct((patches, 128), jnp.float32),
             jax.ShapeDtypeStruct((planes, LATE * width, cols), jnp.bfloat16),
         ],
-        in_specs=[SMEM, SMEM, VMEM, pl.BlockSpec(memory_space=pltpu.HBM)] + [VMEM] * count,
+        in_specs=[SMEM, SMEM, VMEM, pl.BlockSpec(memory_space=pltpu.HBM)] + [VMEM] * len(blocks),
         out_specs=[VMEM] * 4,
         scratch_shapes=[
             pltpu.VMEM((patches + EXTRA, count * width), jnp.bfloat16),
@@ -149,13 +152,13 @@
 
 
 def attention(rows, gain, blocks, carried, qk_gain, pieces):
-    patches, width = blocks[0].shape
+    patches, width = blocks[-1].shape
     cols = carried[0].shape[2]
-    count = len(blocks)
+    count = rows.shape[0]
     return pl.pallas_call(
-        functools.partial(final_block, count, pieces),
+        functools.partial(final_block, len(blocks), pieces),
         out_shape=jax.ShapeDtypeStruct((patches, cols), jnp.bfloat16),
-        in_specs=[SMEM] + [VMEM] * (count + 6),
+        in_specs=[SMEM] + [VMEM] * (len(blocks) + 6),
         out_specs=VMEM,
         scratch_shapes=[
             pltpu.VMEM((2, patches, 128), jnp.float32),
@@ -239,7 +242,7 @@
         return jnp.stack([(side ^ y) * ring + (here + o) % ring for y, o in places]).astype(jnp.int32)
 
     early_rows = rows(
-        (0, 0), (1, 0), (0, -1), (0, 1), (0, -2), (0, 2), (1, -1), (1, 1), (0, -3), (0, 3), (1, -2), (1, 2)
+        (0, 0), (1, 0), (0, -1), (0, 1), (0, -2), (1, -1), (0, 2), (1, 1), (0, -3), (1, -2), (0, 3), (1, 2)
     )
     late_rows = rows((0, -4), (1, -3), (1, 3), (1, 4))
     order = jnp.concatenate([kept_side[None] * ring, (here + jnp.arange(ring)) % ring]).astype(jnp.int32)
@@ -253,12 +256,11 @@
         w_give = lax.dynamic_slice_in_dim(lax.optimization_barrier((w_own, own))[0], (1 - kept_side) * half, half, 1)
         w_other = shifted(lax.optimization_barrier((w_give, other))[0], PAIR, 1)
         blocks = [own, other, a_up, a_down]
-        b_up = b_down = other
+        up, down = jnp.stack([a_up, other]), jnp.stack([a_down, other])
         for _ in range(2):
-            a_up, a_down = shifted(a_up, RING, 1), shifted(a_down, RING, -1)
-            b_up, b_down = shifted(b_up, RING, 1), shifted(b_down, RING, -1)
-            blocks += [a_up, a_down, b_up, b_down]
-        late = [shifted(a_up, RING, 1), shifted(b_up, RING, 1), shifted(b_down, RING, -1), across(a_down, -1)]
+            up, down = shifted(up, RING, 1), shifted(down, RING, -1)
+            blocks += [up, down]
+        late = [shifted(up, RING, 1), shifted(down[1], RING, -1), across(down[0], -1)]
 
         sums = partial(early_rows, late_rows, gain, w_planes, blocks)
         mixed = attention(late_rows, gain, late, sums, qk_gain[0], 2 * ring)

time: 172 us -> 176 us (1.023)
  waiting for transfers between devices: 79.5 us -> 92.1 us
  starting transfers between devices: 62.7 us -> 52.8 us
    ppermute x42 -> x32, waiting for transfers between devices: 57.8 us -> 71.1 us  [shifted(): lax.ppermute(block, axis, [(i, (i + by) % peers) for i in range(peers)])]
    ppermute x2, starting transfers between devices: 7.14 us -> 0.01 us  [across(): return lax.ppermute(block, (PAIR, RING), pairs)]
    ppermute x42 -> x32, starting transfers between devices: 53.6 us -> 48.7 us  [shifted(): lax.ppermute(block, axis, [(i, (i + by) % peers) for i in range(peers)])]
    ppermute x6, starting transfers between devices: 1.9 us -> 4.08 us  [to_next_section(): return lax.ppermute(block, SECTION + (PAIR, RING), pairs)]
  transfers between devices with their start and end apart: 50 -> 40, of which waited for: 33 -> 23; matrix products, arithmetic and copies ran while one was open for 2% -> 2% of each run, Pallas kernels for 13% -> 13%
where the time goes in v3:
time: 176 us; the launch traced here: 175 us
  waiting for transfers between devices  92.1 us (52%)
  starting transfers between devices  52.8 us (30%)
  Pallas kernels  23.6 us (13%)
  local copies, waits for them, and re-layouts  4.83 us (3%)
    ppermute x32, waiting for transfers between devices, shifted(): lax.ppermute(block, axis, [(i, (i + by) % peers) for i in range(peers)])  71.1 us
    ppermute x32, starting transfers between devices, shifted(): lax.ppermute(block, axis, [(i, (i + by) % peers) for i in range(peers)])  48.7 us
    ppermute x6, waiting for transfers between devices, to_next_section(): return lax.ppermute(block, SECTION + (PAIR, RING), pairs)  21 us
    pallas_call x2, Pallas kernels, partial(): pl.pallas_call(functools.partial(partial_block, len(blocks)), out_shape=[...  13.3 us
    pallas_call x2, Pallas kernels, attention(): pl.pallas_call(functools.partial(final_block, len(blocks), pieces), out_s...  5.25 us
    pallas_call x4, Pallas kernels, projection(): pl.pallas_call(functools.partial(projection_block, places), out_shape=[ja...  5 us
    ppermute x6, starting transfers between devices, to_next_section(): return lax.ppermute(block, SECTION + (PAIR, RING), pairs)  4.08 us
  transfers between devices with their start and end apart: 40, of which 23 were waited for; matrix products, arithmetic and copies ran while one was open for 2% of the time, Pallas kernels for 13%

profile of v3, /device:TPU:0, one launch (start us, length us, event | category | flops | bytes accessed | tf_op | source)
XLA Modules:
  0.0 174.9 jit_solution(2461562674290287806)
XLA Ops:
  0.0 0.9 copy.14
  1.0 0.1 stack.92
  1.2 173.0 %while.12 = (s32[]{:T(128)}, bf16[256,384]{1,0:T(8,128)(2,1)S(1)}, pred[]{:T(512)}, s32[12]{0:T(128)S(1)}, s32[4]{0:T(128)S(1)}, /*index=5*/f32[16,1,384]{2,1,0:...) while((s32[]{:T(128)}, bf16[256,384]{1,0:T(8,128)(2,1)S(1)}, ...), condition=%wide.region_1.2_spmd, body=%wide.region_0.1_spmd.sunk | while | flops 3440642 | bytes 47420396 | solution.py:281
  1.2 0.2 collective-permute-start
  1.4 4.0 %collective-permute-start.1 = (bf16[256,384]{1,0:T(8,128)(2,1)S(1)}, bf16[256,384]{1,0:T(8,128)(2,1)S(1)}, u32[]{:S(2)}, u32[]{:S(2)}) collective-permute-start(bf16[256,384]{1,0:T(8,128)(2,1)S(1)} %get-tuple-element.295.refs_0_), channel_id=1, source_target_pairs={{0,7},{1,0},{2,1},{3,2},{4,3},{5,4},{6,5},{7,6},{8,15},{9,8},{10,9... | collective-permute-start | bytes 589832 | tf_op jit(solution)/shard_map/while/body/eval_jaxpr/ppermute | solution.py:197
  5.5 1.6 collective-permute-start.2
  7.0 1.5 constant_dynamic-slice_fusion.2
  8.5 1.7 collective-permute-done.refs_2_
  10.3 1.5 collective-permute-done.2.refs_1_
  11.8 1.6 collective-permute-start.11
  13.5 0.1 collective-permute-start.3
  13.6 3.2 %collective-permute-start.6 = (bf16[2,256,384]{2,1,0:T(8,128)(2,1)S(1)}, bf16[2,256,384]{2,1,0:T(8,128)(2,1)S(1)}, u32[]{:S(2)}, u32[]{:S(2)}) collective-permute-start(bf16[2,256,384]{2,1,0:T(8,128)(2,1)S(1)} %get-tuple-element.265), channel_id=1, source_target_pairs={{0,7},{1,0},{2,1},{3,2},{4,3},{5,4},{6,5},{7,6},{8,15},{9,8},{10,9... | collective-permute-start | bytes 1179656 | tf_op jit(solution)/shard_map/while/body/eval_jaxpr/ppermute | solution.py:197
  16.8 7.4 %collective-permute-done.3.refs_4_ = bf16[2,256,384]{2,1,0:T(8,128)(2,1)S(1)} collective-permute-done((bf16[2,256,384]{2,1,0:T(8,128)(2,1)S(1)}, bf16[2,256,384]{2,1,0:T(8,128)(2,1)S(1)}, u32[]{:S(2)}, u32[]{:S(2)}) %collective-permute-start.3) | collective-permute-done | bytes 393248 | tf_op jit(solution)/shard_map/while/body/eval_jaxpr/ppermute | solution.py:197
  24.2 3.2 %collective-permute-start.7 = (bf16[2,256,384]{2,1,0:T(8,128)(2,1)S(1)}, bf16[2,256,384]{2,1,0:T(8,128)(2,1)S(1)}, u32[]{:S(2)}, u32[]{:S(2)}) collective-permute-start(bf16[2,256,384]{2,1,0:T(8,128)(2,1)S(1)} %collective-permute-done.6.refs_5_), channel_id=1, source_target_pairs={{0,7},{1,0},{2,1},{3,2},{4,3},{5,4},{6,5},{7,6},{8,15},{9,8},{10,9... | collective-permute-start | bytes 1179656 | tf_op jit(solution)/shard_map/while/body/eval_jaxpr/ppermute | solution.py:197
  27.4 6.4 %collective-permute-done.4.refs_6_ = bf16[2,256,384]{2,1,0:T(8,128)(2,1)S(1)} collective-permute-done((bf16[2,256,384]{2,1,0:T(8,128)(2,1)S(1)}, bf16[2,256,384]{2,1,0:T(8,128)(2,1)S(1)}, u32[]{:S(2)}, u32[]{:S(2)}) %collective-permute-start.4) | collective-permute-done | bytes 393248 | tf_op jit(solution)/shard_map/while/body/eval_jaxpr/ppermute | solution.py:197
  33.9 3.3 %collective-permute-start.8 = (bf16[256,384]{1,0:T(8,128)(2,1)S(1)}, bf16[256,384]{1,0:T(8,128)(2,1)S(1)}, u32[]{:S(2)}, u32[]{:S(2)}) collective-permute-start(bf16[256,384]{1,0:T(8,128)(2,1)S(1)} %get-tuple-element.266), channel_id=1, source_target_pairs={{0,7},{1,0},{2,1},{3,2},{4,3},{5,4},{6,5},{7,6},{8,15},{9,8},{10,9... | collective-permute-start | bytes 589832 | tf_op jit(solution)/shard_map/while/body/eval_jaxpr/ppermute | solution.py:197
  37.2 6.7 %qkv_partial.3 = (f32[3,272,256]{2,1,0:T(8,128)S(1)}, f32[2,256,128]{2,1,0:T(8,128)S(1)}, f32[256,128]{1,0:T(8,128)S(1)}, bf16[3,1536,256]{2,1,0:T(8,128)(2,1)S(1)}) custom-call(s32[12]{0:T(128)S(1)} %get-tuple-element.309.rows_ref, s32[4]{0:T(128)S(1)} %get-tuple-element.310.late_rows_ref.rows_ref, f32[16,1,384]{2,1,0:T(1,128)S(1)} %copy-done.2, ...), custom_call_target="tpu_custom_call" | custom-call | tf_op jit(solution)/shard_map/while/body/eval_jaxpr/qkv_partial/pallas_call | solution.py:133
  43.9 2.6 %attention_block.1.own_ref = bf16[256,256]{1,0:T(8,128)(2,1)S(1)} custom-call(s32[4]{0:T(128)S(1)} %get-tuple-element.310.late_rows_ref.rows_ref, f32[16,1,384]{2,1,0:T(1,128)S(1)} %copy-done.2, bf16[2,256,384]{2,1,0:T(8,128)(2,1)S(1)} %collective-permute-done.5.refs_0_, bf16[256,384]{1,0:T(8,128)(2,1)S(1)} %collective-permute-done.8.refs_1_, ...), custom_call_target="tpu_custom_call" | custom-call | tf_op jit(solution)/shard_map/while/body/eval_jaxpr/attention_block/pallas_call | solution.py:158
  46.5 1.6 collective-permute-start.10
  48.2 5.6 %collective-permute-done.10.other_ref = bf16[256,256]{1,0:T(8,128)(2,1)S(1)} collective-permute-done((bf16[256,256]{1,0:T(8,128)(2,1)S(1)}, bf16[256,256]{1,0:T(8,128)(2,1)S(1)}, u32[]{:S(2)}, u32[]{:S(2)}) %collective-permute-start.10) | collective-permute-done | bytes 131104 | tf_op jit(solution)/shard_map/while/body/eval_jaxpr/ppermute | solution.py:197
  53.8 0.8 projection_block.6
  54.6 0.1 collective-permute-start.12
  54.7 1.7 projection_block.7
  56.4 3.3 %collective-permute-start.16 = (bf16[256,384]{1,0:T(8,128)(2,1)S(1)}, bf16[256,384]{1,0:T(8,128)(2,1)S(1)}, u32[]{:S(2)}, u32[]{:S(2)}) collective-permute-start(bf16[256,384]{1,0:T(8,128)(2,1)S(1)} %get-tuple-element.280), channel_id=1, source_target_pairs={{0,7},{1,0},{2,1},{3,2},{4,3},{5,4},{6,5},{7,6},{8,15},{9,8},{10,9... | collective-permute-start | bytes 589832 | tf_op jit(solution)/shard_map/while/body/eval_jaxpr/ppermute | solution.py:197
  59.9 1.7 collective-permute-done.12
  61.6 0.1 collective-permute-start.13
  61.7 1.1 collective-permute-done.16
  62.9 3.8 %collective-permute-start.17 = (bf16[256,384]{1,0:T(8,128)(2,1)S(1)}, bf16[256,384]{1,0:T(8,128)(2,1)S(1)}, u32[]{:S(2)}, u32[]{:S(2)}) collective-permute-start(bf16[256,384]{1,0:T(8,128)(2,1)S(1)} %add_convert_fusion.17), channel_id=1, source_target_pairs={{0,7},{1,0},{2,1},{3,2},{4,3},{5,4},{6,5},{7,6},{8,15},{9,8},{10,9... | collective-permute-start | bytes 589832 | tf_op jit(solution)/shard_map/while/body/eval_jaxpr/ppermute | solution.py:197
  66.7 2.9 %collective-permute-done.13 = bf16[256,384]{1,0:T(8,128)(2,1)S(1)} collective-permute-done((bf16[256,384]{1,0:T(8,128)(2,1)S(1)}, bf16[256,384]{1,0:T(8,128)(2,1)S(1)}, u32[]{:S(2)}, u32[]{:S(2)}) %collective-permute-start.13) | collective-permute-done | bytes 196640 | tf_op jit(solution)/shard_map/while/body/eval_jaxpr/ppermute | solution.py:197
  69.7 0.1 collective-permute-start.14
  69.7 0.1 collective-permute-done.17
  69.9 1.5 collective-permute-start.18
  71.4 5.3 %collective-permute-done.14 = bf16[256,384]{1,0:T(8,128)(2,1)S(1)} collective-permute-done((bf16[256,384]{1,0:T(8,128)(2,1)S(1)}, bf16[256,384]{1,0:T(8,128)(2,1)S(1)}, u32[]{:S(2)}, u32[]{:S(2)}) %collective-permute-start.14) | collective-permute-done | bytes 196640 | tf_op jit(solution)/shard_map/while/body/eval_jaxpr/ppermute | solution.py:197
  76.9 4.0 %collective-permute-done.18 = bf16[256,384]{1,0:T(8,128)(2,1)S(1)} collective-permute-done((bf16[256,384]{1,0:T(8,128)(2,1)S(1)}, bf16[256,384]{1,0:T(8,128)(2,1)S(1)}, u32[]{:S(2)}, u32[]{:S(2)}) %collective-permute-start.18) | collective-permute-done | bytes 196640 | tf_op jit(solution)/shard_map/while/body/eval_jaxpr/ppermute | solution.py:222
  80.9 6.5 %collective-permute-done.15 = bf16[256,384]{1,0:T(8,128)(2,1)S(1)} collective-permute-done((bf16[256,384]{1,0:T(8,128)(2,1)S(1)}, bf16[256,384]{1,0:T(8,128)(2,1)S(1)}, u32[]{:S(2)}, u32[]{:S(2)}) %collective-permute-start.15) | collective-permute-done | bytes 196640 | tf_op jit(solution)/shard_map/while/body/eval_jaxpr/ppermute | solution.py:222
  87.6 3.2 %collective-permute-start.1 = (bf16[256,384]{1,0:T(8,128)(2,1)S(1)}, bf16[256,384]{1,0:T(8,128)(2,1)S(1)}, u32[]{:S(2)}, u32[]{:S(2)}) collective-permute-start(bf16[256,384]{1,0:T(8,128)(2,1)S(1)} %get-tuple-element.295.refs_0_), channel_id=1, source_target_pairs={{0,7},{1,0},{2,1},{3,2},{4,3},{5,4},{6,5},{7,6},{8,15},{9,8},{10,9... | collective-permute-start | bytes 589832 | tf_op jit(solution)/shard_map/while/body/eval_jaxpr/ppermute | solution.py:197
  90.8 0.4 collective-permute-start.2
  91.2 1.5 constant_dynamic-slice_fusion.2
  92.7 2.2 %collective-permute-done.refs_2_ = bf16[256,384]{1,0:T(8,128)(2,1)S(1)} collective-permute-done((bf16[256,384]{1,0:T(8,128)(2,1)S(1)}, bf16[256,384]{1,0:T(8,128)(2,1)S(1)}, u32[]{:S(2)}, u32[]{:S(2)}) %collective-permute-start) | collective-permute-done | bytes 196640 | tf_op jit(solution)/shard_map/while/body/eval_jaxpr/ppermute | solution.py:197
  95.0 3.7 %collective-permute-done.2.refs_1_ = bf16[256,384]{1,0:T(8,128)(2,1)S(1)} collective-permute-done((bf16[256,384]{1,0:T(8,128)(2,1)S(1)}, bf16[256,384]{1,0:T(8,128)(2,1)S(1)}, u32[]{:S(2)}, u32[]{:S(2)}) %collective-permute-start.2) | collective-permute-done | bytes 196640 | tf_op jit(solution)/shard_map/while/body/eval_jaxpr/ppermute | solution.py:197
  98.7 0.4 collective-permute-start.11
  99.2 3.2 %collective-permute-start.6 = (bf16[2,256,384]{2,1,0:T(8,128)(2,1)S(1)}, bf16[2,256,384]{2,1,0:T(8,128)(2,1)S(1)}, u32[]{:S(2)}, u32[]{:S(2)}) collective-permute-start(bf16[2,256,384]{2,1,0:T(8,128)(2,1)S(1)} %get-tuple-element.265), channel_id=1, source_target_pairs={{0,7},{1,0},{2,1},{3,2},{4,3},{5,4},{6,5},{7,6},{8,15},{9,8},{10,9... | collective-permute-start | bytes 1179656 | tf_op jit(solution)/shard_map/while/body/eval_jaxpr/ppermute | solution.py:197
  102.4 8.3 %collective-permute-done.3.refs_4_ = bf16[2,256,384]{2,1,0:T(8,128)(2,1)S(1)} collective-permute-done((bf16[2,256,384]{2,1,0:T(8,128)(2,1)S(1)}, bf16[2,256,384]{2,1,0:T(8,128)(2,1)S(1)}, u32[]{:S(2)}, u32[]{:S(2)}) %collective-permute-start.3) | collective-permute-done | bytes 393248 | tf_op jit(solution)/shard_map/while/body/eval_jaxpr/ppermute | solution.py:197
  110.7 3.2 %collective-permute-start.7 = (bf16[2,256,384]{2,1,0:T(8,128)(2,1)S(1)}, bf16[2,256,384]{2,1,0:T(8,128)(2,1)S(1)}, u32[]{:S(2)}, u32[]{:S(2)}) collective-permute-start(bf16[2,256,384]{2,1,0:T(8,128)(2,1)S(1)} %collective-permute-done.6.refs_5_), channel_id=1, source_target_pairs={{0,7},{1,0},{2,1},{3,2},{4,3},{5,4},{6,5},{7,6},{8,15},{9,8},{10,9... | collective-permute-start | bytes 1179656 | tf_op jit(solution)/shard_map/while/body/eval_jaxpr/ppermute | solution.py:197
  114.0 7.4 %collective-permute-done.4.refs_6_ = bf16[2,256,384]{2,1,0:T(8,128)(2,1)S(1)} collective-permute-done((bf16[2,256,384]{2,1,0:T(8,128)(2,1)S(1)}, bf16[2,256,384]{2,1,0:T(8,128)(2,1)S(1)}, u32[]{:S(2)}, u32[]{:S(2)}) %collective-permute-start.4) | collective-permute-done | bytes 393248 | tf_op jit(solution)/shard_map/while/body/eval_jaxpr/ppermute | solution.py:197
  121.4 3.4 %collective-permute-start.8 = (bf16[256,384]{1,0:T(8,128)(2,1)S(1)}, bf16[256,384]{1,0:T(8,128)(2,1)S(1)}, u32[]{:S(2)}, u32[]{:S(2)}) collective-permute-start(bf16[256,384]{1,0:T(8,128)(2,1)S(1)} %get-tuple-element.266), channel_id=1, source_target_pairs={{0,7},{1,0},{2,1},{3,2},{4,3},{5,4},{6,5},{7,6},{8,15},{9,8},{10,9... | collective-permute-start | bytes 589832 | tf_op jit(solution)/shard_map/while/body/eval_jaxpr/ppermute | solution.py:197
  124.8 6.7 %qkv_partial.3 = (f32[3,272,256]{2,1,0:T(8,128)S(1)}, f32[2,256,128]{2,1,0:T(8,128)S(1)}, f32[256,128]{1,0:T(8,128)S(1)}, bf16[3,1536,256]{2,1,0:T(8,128)(2,1)S(1)}) custom-call(s32[12]{0:T(128)S(1)} %get-tuple-element.309.rows_ref, s32[4]{0:T(128)S(1)} %get-tuple-element.310.late_rows_ref.rows_ref, f32[16,1,384]{2,1,0:T(1,128)S(1)} %copy-done.2, ...), custom_call_target="tpu_custom_call" | custom-call | tf_op jit(solution)/shard_map/while/body/eval_jaxpr/qkv_partial/pallas_call | solution.py:133
  131.5 2.6 %attention_block.1.own_ref = bf16[256,256]{1,0:T(8,128)(2,1)S(1)} custom-call(s32[4]{0:T(128)S(1)} %get-tuple-element.310.late_rows_ref.rows_ref, f32[16,1,384]{2,1,0:T(1,128)S(1)} %copy-done.2, bf16[2,256,384]{2,1,0:T(8,128)(2,1)S(1)} %collective-permute-done.5.refs_0_, bf16[256,384]{1,0:T(8,128)(2,1)S(1)} %collective-permute-done.8.refs_1_, ...), custom_call_target="tpu_custom_call" | custom-call | tf_op jit(solution)/shard_map/while/body/eval_jaxpr/attention_block/pallas_call | solution.py:158
  134.2 1.6 collective-permute-start.10
  135.8 3.4 %collective-permute-done.10.other_ref = bf16[256,256]{1,0:T(8,128)(2,1)S(1)} collective-permute-done((bf16[256,256]{1,0:T(8,128)(2,1)S(1)}, bf16[256,256]{1,0:T(8,128)(2,1)S(1)}, u32[]{:S(2)}, u32[]{:S(2)}) %collective-permute-start.10) | collective-permute-done | bytes 131104 | tf_op jit(solution)/shard_map/while/body/eval_jaxpr/ppermute | solution.py:197
  139.2 0.8 projection_block.6
  140.1 1.5 collective-permute-start.12
  141.6 1.7 projection_block.7
  143.3 1.9 %collective-permute-start.16 = (bf16[256,384]{1,0:T(8,128)(2,1)S(1)}, bf16[256,384]{1,0:T(8,128)(2,1)S(1)}, u32[]{:S(2)}, u32[]{:S(2)}) collective-permute-start(bf16[256,384]{1,0:T(8,128)(2,1)S(1)} %get-tuple-element.280), channel_id=1, source_target_pairs={{0,7},{1,0},{2,1},{3,2},{4,3},{5,4},{6,5},{7,6},{8,15},{9,8},{10,9... | collective-permute-start | bytes 589832 | tf_op jit(solution)/shard_map/while/body/eval_jaxpr/ppermute | solution.py:197
  145.3 1.7 collective-permute-done.12
  147.1 0.3 collective-permute-start.13
  147.4 1.6 collective-permute-done.16
  149.1 3.1 %collective-permute-start.17 = (bf16[256,384]{1,0:T(8,128)(2,1)S(1)}, bf16[256,384]{1,0:T(8,128)(2,1)S(1)}, u32[]{:S(2)}, u32[]{:S(2)}) collective-permute-start(bf16[256,384]{1,0:T(8,128)(2,1)S(1)} %add_convert_fusion.17), channel_id=1, source_target_pairs={{0,7},{1,0},{2,1},{3,2},{4,3},{5,4},{6,5},{7,6},{8,15},{9,8},{10,9... | collective-permute-start | bytes 589832 | tf_op jit(solution)/shard_map/while/body/eval_jaxpr/ppermute | solution.py:197
  152.2 3.5 %collective-permute-done.13 = bf16[256,384]{1,0:T(8,128)(2,1)S(1)} collective-permute-done((bf16[256,384]{1,0:T(8,128)(2,1)S(1)}, bf16[256,384]{1,0:T(8,128)(2,1)S(1)}, u32[]{:S(2)}, u32[]{:S(2)}) %collective-permute-start.13) | collective-permute-done | bytes 196640 | tf_op jit(solution)/shard_map/while/body/eval_jaxpr/ppermute | solution.py:197
  155.9 2.3 %collective-permute-start.18 = (bf16[256,384]{1,0:T(8,128)(2,1)S(1)}, bf16[256,384]{1,0:T(8,128)(2,1)S(1)}, u32[]{:S(2)}, u32[]{:S(2)}) collective-permute-start(bf16[256,384]{1,0:T(8,128)(2,1)S(1)} %add_convert_fusion.18), channel_id=1, source_target_pairs={{0,23},{1,16},{2,17},{3,18},{4,19},{5,20},{6,21},{7,22},{8,31},{9,... | collective-permute-start | bytes 589832 | tf_op jit(solution)/shard_map/while/body/eval_jaxpr/ppermute | solution.py:222
  158.1 5.3 %collective-permute-done.14 = bf16[256,384]{1,0:T(8,128)(2,1)S(1)} collective-permute-done((bf16[256,384]{1,0:T(8,128)(2,1)S(1)}, bf16[256,384]{1,0:T(8,128)(2,1)S(1)}, u32[]{:S(2)}, u32[]{:S(2)}) %collective-permute-start.14) | collective-permute-done | bytes 196640 | tf_op jit(solution)/shard_map/while/body/eval_jaxpr/ppermute | solution.py:197
  163.6 3.2 %collective-permute-done.18 = bf16[256,384]{1,0:T(8,128)(2,1)S(1)} collective-permute-done((bf16[256,384]{1,0:T(8,128)(2,1)S(1)}, bf16[256,384]{1,0:T(8,128)(2,1)S(1)}, u32[]{:S(2)}, u32[]{:S(2)}) %collective-permute-start.18) | collective-permute-done | bytes 196640 | tf_op jit(solution)/shard_map/while/body/eval_jaxpr/ppermute | solution.py:222
  166.8 7.3 %collective-permute-done.15 = bf16[256,384]{1,0:T(8,128)(2,1)S(1)} collective-permute-done((bf16[256,384]{1,0:T(8,128)(2,1)S(1)}, bf16[256,384]{1,0:T(8,128)(2,1)S(1)}, u32[]{:S(2)}, u32[]{:S(2)}) %collective-permute-start.15) | collective-permute-done | bytes 196640 | tf_op jit(solution)/shard_map/while/body/eval_jaxpr/ppermute | solution.py:222
  174.2 0.7 copy-done.1
  (64 shorter events, 1.9 us)
Async XLA Ops:
  1.2 9.1 %collective-permute-start = (bf16[256,384]{1,0:T(8,128)(2,1)S(1)}, bf16[256,384]{1,0:T(8,128)(2,1)S(1)}, u32[]{:S(2)}, u32[]{:S(2)}) collective-permute-start(bf16[256,384]{1,0:T(8,128)(2,1)S(1)} %get-tuple-element.295.refs_0_), channel_id=1, source_target_pairs={{0,1},{1,2},{2,3},{3,4},{4,5},{5,6},{6,7},{7,0},{8,9},{9,10},{10,1... | collective-permute-start | bytes 589832 | tf_op jit(solution)/shard_map/while/body/eval_jaxpr/ppermute | solution.py:197
  1.4 8.8 %collective-permute-start.1 = (bf16[256,384]{1,0:T(8,128)(2,1)S(1)}, bf16[256,384]{1,0:T(8,128)(2,1)S(1)}, u32[]{:S(2)}, u32[]{:S(2)}) collective-permute-start(bf16[256,384]{1,0:T(8,128)(2,1)S(1)} %get-tuple-element.295.refs_0_), channel_id=1, source_target_pairs={{0,7},{1,0},{2,1},{3,2},{4,3},{5,4},{6,5},{7,6},{8,15},{9,8},{10,9... | collective-permute-start | bytes 589832 | tf_op jit(solution)/shard_map/while/body/eval_jaxpr/ppermute | solution.py:197
  5.5 6.4 %collective-permute-start.2 = (bf16[256,384]{1,0:T(8,128)(2,1)S(1)}, bf16[256,384]{1,0:T(8,128)(2,1)S(1)}, u32[]{:S(2)}, u32[]{:S(2)}) collective-permute-start(bf16[256,384]{1,0:T(8,128)(2,1)S(1)} %get-tuple-element.295.refs_0_), channel_id=1, source_target_pairs={{0,8},{8,0},{1,9},{9,1},{2,10},{10,2},{3,11},{11,3},{4,12},{12,4},... | collective-permute-start | bytes 589832 | tf_op jit(solution)/shard_map/while/body/eval_jaxpr/ppermute | solution.py:197
  7.0 30.2 %copy-start.2 = (f32[16,1,384]{2,1,0:T(1,128)S(1)}, f32[16,1,384]{2,1,0:T(1,128)}, u32[]{:S(2)}) copy-start(f32[16,1,384]{2,1,0:T(1,128)} %get-tuple-element.311.gain_ref) | copy-start | bytes 73732 | tf_op jit(solution)/shard_map/while
  11.8 42.0 %collective-permute-start.11 = (bf16[256,3072]{1,0:T(8,128)(2,1)S(1)}, bf16[256,3072]{1,0:T(8,128)(2,1)S(1)}, u32[]{:S(2)}, u32[]{:S(2)}) collective-permute-start(bf16[256,3072]{1,0:T(8,128)(2,1)S(1)} %constant_dynamic-slice_fusion.2), channel_id=1, source_target_pairs={{0,8},{8,0},{1,9},{9,1},{2,10},{10,2},{3,11},{11,3},{4,12},{12,4},... | collective-permute-start | bytes 4718600 | tf_op jit(solution)/shard_map/while/body/eval_jaxpr/ppermute | solution.py:197
  13.5 10.7 %collective-permute-start.3 = (bf16[2,256,384]{2,1,0:T(8,128)(2,1)S(1)}, bf16[2,256,384]{2,1,0:T(8,128)(2,1)S(1)}, u32[]{:S(2)}, u32[]{:S(2)}) collective-permute-start(bf16[2,256,384]{2,1,0:T(8,128)(2,1)S(1)} %get-tuple-element.264), channel_id=1, source_target_pairs={{0,1},{1,2},{2,3},{3,4},{4,5},{5,6},{6,7},{7,0},{8,9},{9,10},{10,1... | collective-permute-start | bytes 1179656 | tf_op jit(solution)/shard_map/while/body/eval_jaxpr/ppermute | solution.py:197
  13.6 10.6 %collective-permute-start.6 = (bf16[2,256,384]{2,1,0:T(8,128)(2,1)S(1)}, bf16[2,256,384]{2,1,0:T(8,128)(2,1)S(1)}, u32[]{:S(2)}, u32[]{:S(2)}) collective-permute-start(bf16[2,256,384]{2,1,0:T(8,128)(2,1)S(1)} %get-tuple-element.265), channel_id=1, source_target_pairs={{0,7},{1,0},{2,1},{3,2},{4,3},{5,4},{6,5},{7,6},{8,15},{9,8},{10,9... | collective-permute-start | bytes 1179656 | tf_op jit(solution)/shard_map/while/body/eval_jaxpr/ppermute | solution.py:197
  24.1 9.7 %collective-permute-start.4 = (bf16[2,256,384]{2,1,0:T(8,128)(2,1)S(1)}, bf16[2,256,384]{2,1,0:T(8,128)(2,1)S(1)}, u32[]{:S(2)}, u32[]{:S(2)}) collective-permute-start(bf16[2,256,384]{2,1,0:T(8,128)(2,1)S(1)} %collective-permute-done.3.refs_4_), channel_id=1, source_target_pairs={{0,1},{1,2},{2,3},{3,4},{4,5},{5,6},{6,7},{7,0},{8,9},{9,10},{10,1... | collective-permute-start | bytes 1179656 | tf_op jit(solution)/shard_map/while/body/eval_jaxpr/ppermute | solution.py:197
  24.2 9.7 %collective-permute-start.7 = (bf16[2,256,384]{2,1,0:T(8,128)(2,1)S(1)}, bf16[2,256,384]{2,1,0:T(8,128)(2,1)S(1)}, u32[]{:S(2)}, u32[]{:S(2)}) collective-permute-start(bf16[2,256,384]{2,1,0:T(8,128)(2,1)S(1)} %collective-permute-done.6.refs_5_), channel_id=1, source_target_pairs={{0,7},{1,0},{2,1},{3,2},{4,3},{5,4},{6,5},{7,6},{8,15},{9,8},{10,9... | collective-permute-start | bytes 1179656 | tf_op jit(solution)/shard_map/while/body/eval_jaxpr/ppermute | solution.py:197
  33.8 10.1 %collective-permute-start.5 = (bf16[2,256,384]{2,1,0:T(8,128)(2,1)S(1)}, bf16[2,256,384]{2,1,0:T(8,128)(2,1)S(1)}, u32[]{:S(2)}, u32[]{:S(2)}) collective-permute-start(bf16[2,256,384]{2,1,0:T(8,128)(2,1)S(1)} %collective-permute-done.4.refs_6_), channel_id=1, source_target_pairs={{0,1},{1,2},{2,3},{3,4},{4,5},{5,6},{6,7},{7,0},{8,9},{9,10},{10,1... | collective-permute-start | bytes 1179656 | tf_op jit(solution)/shard_map/while/body/eval_jaxpr/ppermute | solution.py:197
  33.9 10.0 %collective-permute-start.8 = (bf16[256,384]{1,0:T(8,128)(2,1)S(1)}, bf16[256,384]{1,0:T(8,128)(2,1)S(1)}, u32[]{:S(2)}, u32[]{:S(2)}) collective-permute-start(bf16[256,384]{1,0:T(8,128)(2,1)S(1)} %get-tuple-element.266), channel_id=1, source_target_pairs={{0,7},{1,0},{2,1},{3,2},{4,3},{5,4},{6,5},{7,6},{8,15},{9,8},{10,9... | collective-permute-start | bytes 589832 | tf_op jit(solution)/shard_map/while/body/eval_jaxpr/ppermute | solution.py:197
  37.2 6.7 %collective-permute-start.9 = (bf16[256,384]{1,0:T(8,128)(2,1)S(1)}, bf16[256,384]{1,0:T(8,128)(2,1)S(1)}, u32[]{:S(2)}, u32[]{:S(2)}) collective-permute-start(bf16[256,384]{1,0:T(8,128)(2,1)S(1)} %get-tuple-element.267), channel_id=1, source_target_pairs={{0,15},{1,8},{2,9},{3,10},{4,11},{5,12},{6,13},{7,14},{8,7},{9,0},... | collective-permute-start | bytes 589832 | tf_op jit(solution)/shard_map/while/body/eval_jaxpr/ppermute | solution.py:203
  37.2 6.7 %copy-start.3 = (f32[1,2,128]{2,1,0:T(2,128)S(1)}, f32[1,2,128]{2,1,0:T(2,128)}, u32[]{:S(2)}) copy-start(f32[1,2,128]{2,1,0:T(2,128)} %get-tuple-element.313) | copy-start | bytes 3076 | tf_op jit(solution)/shard_map/while
  43.9 9.9 %copy-start = (bf16[256,6144]{1,0:T(8,128)(2,1)S(1)}, bf16[256,6144]{1,0:T(8,128)(2,1)}, u32[]{:S(2)}) copy-start(bf16[256,6144]{1,0:T(8,128)(2,1)} %get-tuple-element.272.w_own_ref) | copy-start | bytes 9437188 | tf_op jit(solution)/shard_map/while
  46.5 7.2 %collective-permute-start.10 = (bf16[256,256]{1,0:T(8,128)(2,1)S(1)}, bf16[256,256]{1,0:T(8,128)(2,1)S(1)}, u32[]{:S(2)}, u32[]{:S(2)}) collective-permute-start(bf16[256,256]{1,0:T(8,128)(2,1)S(1)} %attention_block.1.own_ref), channel_id=1, source_target_pairs={{0,8},{8,0},{1,9},{9,1},{2,10},{10,2},{3,11},{11,3},{4,12},{12,4},... | collective-permute-start | bytes 393224 | tf_op jit(solution)/shard_map/while/body/eval_jaxpr/ppermute | solution.py:197
  54.6 7.0 %collective-permute-start.12 = (bf16[256,384]{1,0:T(8,128)(2,1)S(1)}, bf16[256,384]{1,0:T(8,128)(2,1)S(1)}, u32[]{:S(2)}, u32[]{:S(2)}) collective-permute-start(bf16[256,384]{1,0:T(8,128)(2,1)S(1)} %projection_block.6), channel_id=1, source_target_pairs={{0,1},{1,2},{2,3},{3,4},{4,5},{5,6},{6,7},{7,0},{8,9},{9,10},{10,1... | collective-permute-start | bytes 589832 | tf_op jit(solution)/shard_map/while/body/eval_jaxpr/ppermute | solution.py:197
  56.4 6.5 %collective-permute-start.16 = (bf16[256,384]{1,0:T(8,128)(2,1)S(1)}, bf16[256,384]{1,0:T(8,128)(2,1)S(1)}, u32[]{:S(2)}, u32[]{:S(2)}) collective-permute-start(bf16[256,384]{1,0:T(8,128)(2,1)S(1)} %get-tuple-element.280), channel_id=1, source_target_pairs={{0,7},{1,0},{2,1},{3,2},{4,3},{5,4},{6,5},{7,6},{8,15},{9,8},{10,9... | collective-permute-start | bytes 589832 | tf_op jit(solution)/shard_map/while/body/eval_jaxpr/ppermute | solution.py:197
  59.8 17.1 %collective-permute-start.19 = (bf16[256,384]{1,0:T(8,128)(2,1)S(1)}, bf16[256,384]{1,0:T(8,128)(2,1)S(1)}, u32[]{:S(2)}, u32[]{:S(2)}) collective-permute-start(bf16[256,384]{1,0:T(8,128)(2,1)S(1)} %add_convert_fusion.19), channel_id=1, source_target_pairs={{0,16},{1,17},{2,18},{3,19},{4,20},{5,21},{6,22},{7,23},{8,24},{9,... | collective-permute-start | bytes 589832 | tf_op jit(solution)/shard_map/while/body/eval_jaxpr/ppermute | solution.py:222
  61.6 8.0 %collective-permute-start.13 = (bf16[256,384]{1,0:T(8,128)(2,1)S(1)}, bf16[256,384]{1,0:T(8,128)(2,1)S(1)}, u32[]{:S(2)}, u32[]{:S(2)}) collective-permute-start(bf16[256,384]{1,0:T(8,128)(2,1)S(1)} %add_convert_fusion.14), channel_id=1, source_target_pairs={{0,1},{1,2},{2,3},{3,4},{4,5},{5,6},{6,7},{7,0},{8,9},{9,10},{10,1... | collective-permute-start | bytes 589832 | tf_op jit(solution)/shard_map/while/body/eval_jaxpr/ppermute | solution.py:197
  62.9 7.0 %collective-permute-start.17 = (bf16[256,384]{1,0:T(8,128)(2,1)S(1)}, bf16[256,384]{1,0:T(8,128)(2,1)S(1)}, u32[]{:S(2)}, u32[]{:S(2)}) collective-permute-start(bf16[256,384]{1,0:T(8,128)(2,1)S(1)} %add_convert_fusion.17), channel_id=1, source_target_pairs={{0,7},{1,0},{2,1},{3,2},{4,3},{5,4},{6,5},{7,6},{8,15},{9,8},{10,9... | collective-permute-start | bytes 589832 | tf_op jit(solution)/shard_map/while/body/eval_jaxpr/ppermute | solution.py:197
  69.7 7.1 %collective-permute-start.14 = (bf16[256,384]{1,0:T(8,128)(2,1)S(1)}, bf16[256,384]{1,0:T(8,128)(2,1)S(1)}, u32[]{:S(2)}, u32[]{:S(2)}) collective-permute-start(bf16[256,384]{1,0:T(8,128)(2,1)S(1)} %add_convert_fusion.15), channel_id=1, source_target_pairs={{0,1},{1,2},{2,3},{3,4},{4,5},{5,6},{6,7},{7,0},{8,9},{9,10},{10,1... | collective-permute-start | bytes 589832 | tf_op jit(solution)/shard_map/while/body/eval_jaxpr/ppermute | solution.py:197
  69.9 10.9 %collective-permute-start.18 = (bf16[256,384]{1,0:T(8,128)(2,1)S(1)}, bf16[256,384]{1,0:T(8,128)(2,1)S(1)}, u32[]{:S(2)}, u32[]{:S(2)}) collective-permute-start(bf16[256,384]{1,0:T(8,128)(2,1)S(1)} %add_convert_fusion.18), channel_id=1, source_target_pairs={{0,23},{1,16},{2,17},{3,18},{4,19},{5,20},{6,21},{7,22},{8,31},{9,... | collective-permute-start | bytes 589832 | tf_op jit(solution)/shard_map/while/body/eval_jaxpr/ppermute | solution.py:222
  76.8 10.6 %collective-permute-start.15 = (bf16[256,384]{1,0:T(8,128)(2,1)S(1)}, bf16[256,384]{1,0:T(8,128)(2,1)S(1)}, u32[]{:S(2)}, u32[]{:S(2)}) collective-permute-start(bf16[256,384]{1,0:T(8,128)(2,1)S(1)} %add_convert_fusion.16), channel_id=1, source_target_pairs={{0,17},{1,18},{2,19},{3,20},{4,21},{5,22},{6,23},{7,16},{8,25},{9,... | collective-permute-start | bytes 589832 | tf_op jit(solution)/shard_map/while/body/eval_jaxpr/ppermute | solution.py:222
  87.5 7.5 %collective-permute-start = (bf16[256,384]{1,0:T(8,128)(2,1)S(1)}, bf16[256,384]{1,0:T(8,128)(2,1)S(1)}, u32[]{:S(2)}, u32[]{:S(2)}) collective-permute-start(bf16[256,384]{1,0:T(8,128)(2,1)S(1)} %get-tuple-element.295.refs_0_), channel_id=1, source_target_pairs={{0,1},{1,2},{2,3},{3,4},{4,5},{5,6},{6,7},{7,0},{8,9},{9,10},{10,1... | collective-permute-start | bytes 589832 | tf_op jit(solution)/shard_map/while/body/eval_jaxpr/ppermute | solution.py:197
  87.6 7.4 %collective-permute-start.1 = (bf16[256,384]{1,0:T(8,128)(2,1)S(1)}, bf16[256,384]{1,0:T(8,128)(2,1)S(1)}, u32[]{:S(2)}, u32[]{:S(2)}) collective-permute-start(bf16[256,384]{1,0:T(8,128)(2,1)S(1)} %get-tuple-element.295.refs_0_), channel_id=1, source_target_pairs={{0,7},{1,0},{2,1},{3,2},{4,3},{5,4},{6,5},{7,6},{8,15},{9,8},{10,9... | collective-permute-start | bytes 589832 | tf_op jit(solution)/shard_map/while/body/eval_jaxpr/ppermute | solution.py:197
  90.8 7.8 %collective-permute-start.2 = (bf16[256,384]{1,0:T(8,128)(2,1)S(1)}, bf16[256,384]{1,0:T(8,128)(2,1)S(1)}, u32[]{:S(2)}, u32[]{:S(2)}) collective-permute-start(bf16[256,384]{1,0:T(8,128)(2,1)S(1)} %get-tuple-element.295.refs_0_), channel_id=1, source_target_pairs={{0,8},{8,0},{1,9},{9,1},{2,10},{10,2},{3,11},{11,3},{4,12},{12,4},... | collective-permute-start | bytes 589832 | tf_op jit(solution)/shard_map/while/body/eval_jaxpr/ppermute | solution.py:197
  91.2 33.6 %copy-start.2 = (f32[16,1,384]{2,1,0:T(1,128)S(1)}, f32[16,1,384]{2,1,0:T(1,128)}, u32[]{:S(2)}) copy-start(f32[16,1,384]{2,1,0:T(1,128)} %get-tuple-element.311.gain_ref) | copy-start | bytes 73732 | tf_op jit(solution)/shard_map/while
  98.7 40.6 %collective-permute-start.11 = (bf16[256,3072]{1,0:T(8,128)(2,1)S(1)}, bf16[256,3072]{1,0:T(8,128)(2,1)S(1)}, u32[]{:S(2)}, u32[]{:S(2)}) collective-permute-start(bf16[256,3072]{1,0:T(8,128)(2,1)S(1)} %constant_dynamic-slice_fusion.2), channel_id=1, source_target_pairs={{0,8},{8,0},{1,9},{9,1},{2,10},{10,2},{3,11},{11,3},{4,12},{12,4},... | collective-permute-start | bytes 4718600 | tf_op jit(solution)/shard_map/while/body/eval_jaxpr/ppermute | solution.py:197
  99.1 11.6 %collective-permute-start.3 = (bf16[2,256,384]{2,1,0:T(8,128)(2,1)S(1)}, bf16[2,256,384]{2,1,0:T(8,128)(2,1)S(1)}, u32[]{:S(2)}, u32[]{:S(2)}) collective-permute-start(bf16[2,256,384]{2,1,0:T(8,128)(2,1)S(1)} %get-tuple-element.264), channel_id=1, source_target_pairs={{0,1},{1,2},{2,3},{3,4},{4,5},{5,6},{6,7},{7,0},{8,9},{9,10},{10,1... | collective-permute-start | bytes 1179656 | tf_op jit(solution)/shard_map/while/body/eval_jaxpr/ppermute | solution.py:197
  99.2 11.5 %collective-permute-start.6 = (bf16[2,256,384]{2,1,0:T(8,128)(2,1)S(1)}, bf16[2,256,384]{2,1,0:T(8,128)(2,1)S(1)}, u32[]{:S(2)}, u32[]{:S(2)}) collective-permute-start(bf16[2,256,384]{2,1,0:T(8,128)(2,1)S(1)} %get-tuple-element.265), channel_id=1, source_target_pairs={{0,7},{1,0},{2,1},{3,2},{4,3},{5,4},{6,5},{7,6},{8,15},{9,8},{10,9... | collective-permute-start | bytes 1179656 | tf_op jit(solution)/shard_map/while/body/eval_jaxpr/ppermute | solution.py:197
  110.7 10.6 %collective-permute-start.4 = (bf16[2,256,384]{2,1,0:T(8,128)(2,1)S(1)}, bf16[2,256,384]{2,1,0:T(8,128)(2,1)S(1)}, u32[]{:S(2)}, u32[]{:S(2)}) collective-permute-start(bf16[2,256,384]{2,1,0:T(8,128)(2,1)S(1)} %collective-permute-done.3.refs_4_), channel_id=1, source_target_pairs={{0,1},{1,2},{2,3},{3,4},{4,5},{5,6},{6,7},{7,0},{8,9},{9,10},{10,1... | collective-permute-start | bytes 1179656 | tf_op jit(solution)/shard_map/while/body/eval_jaxpr/ppermute | solution.py:197
  110.7 10.6 %collective-permute-start.7 = (bf16[2,256,384]{2,1,0:T(8,128)(2,1)S(1)}, bf16[2,256,384]{2,1,0:T(8,128)(2,1)S(1)}, u32[]{:S(2)}, u32[]{:S(2)}) collective-permute-start(bf16[2,256,384]{2,1,0:T(8,128)(2,1)S(1)} %collective-permute-done.6.refs_5_), channel_id=1, source_target_pairs={{0,7},{1,0},{2,1},{3,2},{4,3},{5,4},{6,5},{7,6},{8,15},{9,8},{10,9... | collective-permute-start | bytes 1179656 | tf_op jit(solution)/shard_map/while/body/eval_jaxpr/ppermute | solution.py:197
  121.3 10.2 %collective-permute-start.5 = (bf16[2,256,384]{2,1,0:T(8,128)(2,1)S(1)}, bf16[2,256,384]{2,1,0:T(8,128)(2,1)S(1)}, u32[]{:S(2)}, u32[]{:S(2)}) collective-permute-start(bf16[2,256,384]{2,1,0:T(8,128)(2,1)S(1)} %collective-permute-done.4.refs_6_), channel_id=1, source_target_pairs={{0,1},{1,2},{2,3},{3,4},{4,5},{5,6},{6,7},{7,0},{8,9},{9,10},{10,1... | collective-permute-start | bytes 1179656 | tf_op jit(solution)/shard_map/while/body/eval_jaxpr/ppermute | solution.py:197
  121.4 10.1 %collective-permute-start.8 = (bf16[256,384]{1,0:T(8,128)(2,1)S(1)}, bf16[256,384]{1,0:T(8,128)(2,1)S(1)}, u32[]{:S(2)}, u32[]{:S(2)}) collective-permute-start(bf16[256,384]{1,0:T(8,128)(2,1)S(1)} %get-tuple-element.266), channel_id=1, source_target_pairs={{0,7},{1,0},{2,1},{3,2},{4,3},{5,4},{6,5},{7,6},{8,15},{9,8},{10,9... | collective-permute-start | bytes 589832 | tf_op jit(solution)/shard_map/while/body/eval_jaxpr/ppermute | solution.py:197
  124.8 6.7 %collective-permute-start.9 = (bf16[256,384]{1,0:T(8,128)(2,1)S(1)}, bf16[256,384]{1,0:T(8,128)(2,1)S(1)}, u32[]{:S(2)}, u32[]{:S(2)}) collective-permute-start(bf16[256,384]{1,0:T(8,128)(2,1)S(1)} %get-tuple-element.267), channel_id=1, source_target_pairs={{0,15},{1,8},{2,9},{3,10},{4,11},{5,12},{6,13},{7,14},{8,7},{9,0},... | collective-permute-start | bytes 589832 | tf_op jit(solution)/shard_map/while/body/eval_jaxpr/ppermute | solution.py:203
  124.8 6.7 %copy-start.3 = (f32[1,2,128]{2,1,0:T(2,128)S(1)}, f32[1,2,128]{2,1,0:T(2,128)}, u32[]{:S(2)}) copy-start(f32[1,2,128]{2,1,0:T(2,128)} %get-tuple-element.313) | copy-start | bytes 3076 | tf_op jit(solution)/shard_map/while
  131.5 7.7 %copy-start = (bf16[256,6144]{1,0:T(8,128)(2,1)S(1)}, bf16[256,6144]{1,0:T(8,128)(2,1)}, u32[]{:S(2)}) copy-start(bf16[256,6144]{1,0:T(8,128)(2,1)} %get-tuple-element.272.w_own_ref) | copy-start | bytes 9437188 | tf_op jit(solution)/shard_map/while
  134.2 5.1 %collective-permute-start.10 = (bf16[256,256]{1,0:T(8,128)(2,1)S(1)}, bf16[256,256]{1,0:T(8,128)(2,1)S(1)}, u32[]{:S(2)}, u32[]{:S(2)}) collective-permute-start(bf16[256,256]{1,0:T(8,128)(2,1)S(1)} %attention_block.1.own_ref), channel_id=1, source_target_pairs={{0,8},{8,0},{1,9},{9,1},{2,10},{10,2},{3,11},{11,3},{4,12},{12,4},... | collective-permute-start | bytes 393224 | tf_op jit(solution)/shard_map/while/body/eval_jaxpr/ppermute | solution.py:197
  140.1 7.0 %collective-permute-start.12 = (bf16[256,384]{1,0:T(8,128)(2,1)S(1)}, bf16[256,384]{1,0:T(8,128)(2,1)S(1)}, u32[]{:S(2)}, u32[]{:S(2)}) collective-permute-start(bf16[256,384]{1,0:T(8,128)(2,1)S(1)} %projection_block.6), channel_id=1, source_target_pairs={{0,1},{1,2},{2,3},{3,4},{4,5},{5,6},{6,7},{7,0},{8,9},{9,10},{10,1... | collective-permute-start | bytes 589832 | tf_op jit(solution)/shard_map/while/body/eval_jaxpr/ppermute | solution.py:197
  143.3 5.7 %collective-permute-start.16 = (bf16[256,384]{1,0:T(8,128)(2,1)S(1)}, bf16[256,384]{1,0:T(8,128)(2,1)S(1)}, u32[]{:S(2)}, u32[]{:S(2)}) collective-permute-start(bf16[256,384]{1,0:T(8,128)(2,1)S(1)} %get-tuple-element.280), channel_id=1, source_target_pairs={{0,7},{1,0},{2,1},{3,2},{4,3},{5,4},{6,5},{7,6},{8,15},{9,8},{10,9... | collective-permute-start | bytes 589832 | tf_op jit(solution)/shard_map/while/body/eval_jaxpr/ppermute | solution.py:197
  145.2 18.4 %collective-permute-start.19 = (bf16[256,384]{1,0:T(8,128)(2,1)S(1)}, bf16[256,384]{1,0:T(8,128)(2,1)S(1)}, u32[]{:S(2)}, u32[]{:S(2)}) collective-permute-start(bf16[256,384]{1,0:T(8,128)(2,1)S(1)} %add_convert_fusion.19), channel_id=1, source_target_pairs={{0,16},{1,17},{2,18},{3,19},{4,20},{5,21},{6,22},{7,23},{8,24},{9,... | collective-permute-start | bytes 589832 | tf_op jit(solution)/shard_map/while/body/eval_jaxpr/ppermute | solution.py:222
  147.1 8.5 %collective-permute-start.13 = (bf16[256,384]{1,0:T(8,128)(2,1)S(1)}, bf16[256,384]{1,0:T(8,128)(2,1)S(1)}, u32[]{:S(2)}, u32[]{:S(2)}) collective-permute-start(bf16[256,384]{1,0:T(8,128)(2,1)S(1)} %add_convert_fusion.14), channel_id=1, source_target_pairs={{0,1},{1,2},{2,3},{3,4},{4,5},{5,6},{6,7},{7,0},{8,9},{9,10},{10,1... | collective-permute-start | bytes 589832 | tf_op jit(solution)/shard_map/while/body/eval_jaxpr/ppermute | solution.py:197
  149.1 6.7 %collective-permute-start.17 = (bf16[256,384]{1,0:T(8,128)(2,1)S(1)}, bf16[256,384]{1,0:T(8,128)(2,1)S(1)}, u32[]{:S(2)}, u32[]{:S(2)}) collective-permute-start(bf16[256,384]{1,0:T(8,128)(2,1)S(1)} %add_convert_fusion.17), channel_id=1, source_target_pairs={{0,7},{1,0},{2,1},{3,2},{4,3},{5,4},{6,5},{7,6},{8,15},{9,8},{10,9... | collective-permute-start | bytes 589832 | tf_op jit(solution)/shard_map/while/body/eval_jaxpr/ppermute | solution.py:197
  155.7 7.7 %collective-permute-start.14 = (bf16[256,384]{1,0:T(8,128)(2,1)S(1)}, bf16[256,384]{1,0:T(8,128)(2,1)S(1)}, u32[]{:S(2)}, u32[]{:S(2)}) collective-permute-start(bf16[256,384]{1,0:T(8,128)(2,1)S(1)} %add_convert_fusion.15), channel_id=1, source_target_pairs={{0,1},{1,2},{2,3},{3,4},{4,5},{5,6},{6,7},{7,0},{8,9},{9,10},{10,1... | collective-permute-start | bytes 589832 | tf_op jit(solution)/shard_map/while/body/eval_jaxpr/ppermute | solution.py:197
  155.9 11.0 %collective-permute-start.18 = (bf16[256,384]{1,0:T(8,128)(2,1)S(1)}, bf16[256,384]{1,0:T(8,128)(2,1)S(1)}, u32[]{:S(2)}, u32[]{:S(2)}) collective-permute-start(bf16[256,384]{1,0:T(8,128)(2,1)S(1)} %add_convert_fusion.18), channel_id=1, source_target_pairs={{0,23},{1,16},{2,17},{3,18},{4,19},{5,20},{6,21},{7,22},{8,31},{9,... | collective-permute-start | bytes 589832 | tf_op jit(solution)/shard_map/while/body/eval_jaxpr/ppermute | solution.py:222
  163.5 10.6 %collective-permute-start.15 = (bf16[256,384]{1,0:T(8,128)(2,1)S(1)}, bf16[256,384]{1,0:T(8,128)(2,1)S(1)}, u32[]{:S(2)}, u32[]{:S(2)}) collective-permute-start(bf16[256,384]{1,0:T(8,128)(2,1)S(1)} %add_convert_fusion.16), channel_id=1, source_target_pairs={{0,17},{1,18},{2,19},{3,20},{4,21},{5,22},{6,23},{7,16},{8,25},{9,... | collective-permute-start | bytes 589832 | tf_op jit(solution)/shard_map/while/body/eval_jaxpr/ppermute | solution.py:222
  174.2 0.7 copy-start.1

commit v4 on v1

--- a/solution.py
+++ b/solution.py
@@ -17,8 +17,8 @@
 VMEM = pl.BlockSpec(memory_space=pltpu.VMEM)
 SMEM = pl.BlockSpec(memory_space=pltpu.SMEM)
 ROWS = 64
-GROUP = 4
-LATE = 4
+GROUP = 2
+LATE = 2
 
 
 def fetches(rows_ref, w_hbm, w_ref, w_sem, count, width):
@@ -194,12 +194,6 @@
     return lax.ppermute(block, axis, [(i, (i + by) % peers) for i in range(peers)])
 
 
-def across(block, by):
-    ring = lax.axis_size(RING)
-    pairs = [(y * ring + z, (1 - y) * ring + (z + by) % ring) for y in range(2) for z in range(ring)]
-    return lax.ppermute(block, (PAIR, RING), pairs)
-
-
 def turns(section):
     return section % 8 == 7
 
@@ -239,26 +233,25 @@
         return jnp.stack([(side ^ y) * ring + (here + o) % ring for y, o in places]).astype(jnp.int32)
 
     early_rows = rows(
-        (0, 0), (1, 0), (0, -1), (0, 1), (0, -2), (0, 2), (1, -1), (1, 1), (0, -3), (0, 3), (1, -2), (1, 2)
+        (0, 0), (1, 0), *((y, o) for k in (1, 2, 3) for y, o in ((0, -k), (0, k), (1, -k), (1, k)))
     )
-    late_rows = rows((0, -4), (1, -3), (1, 3), (1, 4))
+    late_rows = rows((0, -4), (1, 4))
     order = jnp.concatenate([kept_side[None] * ring, (here + jnp.arange(ring)) % ring]).astype(jnp.int32)
 
     half = w_own.shape[1] // 2
 
     def step(_, own):
-        a_up, a_down = shifted(own, RING, 1), shifted(own, RING, -1)
         other = shifted(own, PAIR, 1)
-        a_up, a_down, other = lax.optimization_barrier((a_up, a_down, other))
         w_give = lax.dynamic_slice_in_dim(lax.optimization_barrier((w_own, own))[0], (1 - kept_side) * half, half, 1)
         w_other = shifted(lax.optimization_barrier((w_give, other))[0], PAIR, 1)
-        blocks = [own, other, a_up, a_down]
+        blocks = [own, other]
+        a_up = a_down = own
         b_up = b_down = other
-        for _ in range(2):
+        for _ in range(3):
             a_up, a_down = shifted(a_up, RING, 1), shifted(a_down, RING, -1)
             b_up, b_down = shifted(b_up, RING, 1), shifted(b_down, RING, -1)
             blocks += [a_up, a_down, b_up, b_down]
-        late = [shifted(a_up, RING, 1), shifted(b_up, RING, 1), shifted(b_down, RING, -1), across(a_down, -1)]
+        late = [shifted(a_up, RING, 1), shifted(b_down, RING, -1)]
 
         sums = partial(early_rows, late_rows, gain, w_planes, blocks)
         mixed = attention(late_rows, gain, late, sums, qk_gain[0], 2 * ring)

time: 172 us -> 181 us (1.052)
  starting transfers between devices: 62.7 us -> 67.3 us
  waiting for transfers between devices: 79.5 us -> 82.4 us
    ppermute x42 -> x44, starting transfers between devices: 53.6 us -> 65.4 us  [shifted(): lax.ppermute(block, axis, [(i, (i + by) % peers) for i in range(peers)])]
    ppermute x2 -> x0, starting transfers between devices: 7.14 us -> none  [across(): return lax.ppermute(block, (PAIR, RING), pairs)]
    ppermute x42 -> x44, waiting for transfers between devices: 57.8 us -> 59.5 us  [shifted(): lax.ppermute(block, axis, [(i, (i + by) % peers) for i in range(peers)])]
  transfers between devices with their start and end apart: 50 -> 50, of which waited for: 33 -> 30; matrix products, arithmetic and copies ran while one was open for 2% -> 2% of each run, Pallas kernels for 13% -> 12%
where the time goes in v4:
time: 181 us; the launch traced here: 180 us
  waiting for transfers between devices  82.4 us (46%)
  starting transfers between devices  67.3 us (37%)
  Pallas kernels  24 us (13%)
  local copies, waits for them, and re-layouts  4.75 us (3%)
    ppermute x44, starting transfers between devices, shifted(): lax.ppermute(block, axis, [(i, (i + by) % peers) for i in range(peers)])  65.4 us
    ppermute x44, waiting for transfers between devices, shifted(): lax.ppermute(block, axis, [(i, (i + by) % peers) for i in range(peers)])  59.5 us
    ppermute x6, waiting for transfers between devices, to_next_section(): return lax.ppermute(block, SECTION + (PAIR, RING), pairs)  22.9 us
    pallas_call x2, Pallas kernels, partial(): pl.pallas_call(functools.partial(partial_block, count), out_shape=[jax.Sh...  14.5 us
    pallas_call x4, Pallas kernels, projection(): pl.pallas_call(functools.partial(projection_block, places), out_shape=[ja...  5 us
    pallas_call x2, Pallas kernels, attention(): pl.pallas_call(functools.partial(final_block, count, pieces), out_shape=j...  4.49 us
  transfers between devices with their start and end apart: 50, of which 30 were waited for; matrix products, arithmetic and copies ran while one was open for 2% of the time, Pallas kernels for 12%

profile of v4, /device:TPU:0, one launch (start us, length us, event | category | flops | bytes accessed | tf_op | source)
XLA Modules:
  0.0 179.9 jit_solution(5419168017930299740)
XLA Ops:
  0.0 0.9 copy.14
  1.2 178.0 %while.12 = (s32[]{:T(128)}, bf16[256,384]{1,0:T(8,128)(2,1)S(1)}, pred[]{:T(512)}, s32[14]{0:T(128)S(1)}, s32[2]{0:T(128)S(1)}, /*index=5*/f32[16,1,384]{2,1,0:...) while((s32[]{:T(128)}, bf16[256,384]{1,0:T(8,128)(2,1)S(1)}, ...), condition=%wide.region_1.2_spmd, body=%wide.region_0.1_spmd.sunk | while | flops 3047426 | bytes 45257908 | solution.py:272
  1.2 1.5 constant_dynamic-slice_fusion.2
  2.8 4.1 %collective-permute-done.4.refs_1_ = bf16[256,384]{1,0:T(8,128)(2,1)S(1)} collective-permute-done((bf16[256,384]{1,0:T(8,128)(2,1)S(1)}, bf16[256,384]{1,0:T(8,128)(2,1)S(1)}, u32[]{:S(2)}, u32[]{:S(2)}) %collective-permute-start.4) | collective-permute-done | bytes 196640 | tf_op jit(solution)/shard_map/while/body/eval_jaxpr/ppermute | solution.py:194
  6.9 0.8 collective-permute-start.16
  7.7 1.9 %collective-permute-start = (bf16[256,384]{1,0:T(8,128)(2,1)S(1)}, bf16[256,384]{1,0:T(8,128)(2,1)S(1)}, u32[]{:S(2)}, u32[]{:S(2)}) collective-permute-start(bf16[256,384]{1,0:T(8,128)(2,1)S(1)} %get-tuple-element.274.refs_0_), channel_id=1, source_target_pairs={{0,1},{1,2},{2,3},{3,4},{4,5},{5,6},{6,7},{7,0},{8,9},{9,10},{10,1... | collective-permute-start | bytes 589832 | tf_op jit(solution)/shard_map/while/body/eval_jaxpr/ppermute | solution.py:194
  9.6 3.9 %collective-permute-start.5 = (bf16[256,384]{1,0:T(8,128)(2,1)S(1)}, bf16[256,384]{1,0:T(8,128)(2,1)S(1)}, u32[]{:S(2)}, u32[]{:S(2)}) collective-permute-start(bf16[256,384]{1,0:T(8,128)(2,1)S(1)} %collective-permute-done.4.refs_1_), channel_id=1, source_target_pairs={{0,7},{1,0},{2,1},{3,2},{4,3},{5,4},{6,5},{7,6},{8,15},{9,8},{10,9... | collective-permute-start | bytes 589832 | tf_op jit(solution)/shard_map/while/body/eval_jaxpr/ppermute | solution.py:194
  13.6 2.0 %collective-permute-start.9 = (bf16[256,384]{1,0:T(8,128)(2,1)S(1)}, bf16[256,384]{1,0:T(8,128)(2,1)S(1)}, u32[]{:S(2)}, u32[]{:S(2)}) collective-permute-start(bf16[256,384]{1,0:T(8,128)(2,1)S(1)} %get-tuple-element.274.refs_0_), channel_id=1, source_target_pairs={{0,7},{1,0},{2,1},{3,2},{4,3},{5,4},{6,5},{7,6},{8,15},{9,8},{10,9... | collective-permute-start | bytes 589832 | tf_op jit(solution)/shard_map/while/body/eval_jaxpr/ppermute | solution.py:194
  15.6 1.7 collective-permute-done.refs_2_
  17.3 1.6 collective-permute-done.5.refs_5_
  18.9 3.7 %collective-permute-start.6 = (bf16[256,384]{1,0:T(8,128)(2,1)S(1)}, bf16[256,384]{1,0:T(8,128)(2,1)S(1)}, u32[]{:S(2)}, u32[]{:S(2)}) collective-permute-start(bf16[256,384]{1,0:T(8,128)(2,1)S(1)} %collective-permute-done.5.refs_5_), channel_id=1, source_target_pairs={{0,7},{1,0},{2,1},{3,2},{4,3},{5,4},{6,5},{7,6},{8,15},{9,8},{10,9... | collective-permute-start | bytes 589832 | tf_op jit(solution)/shard_map/while/body/eval_jaxpr/ppermute | solution.py:194
  22.6 0.5 collective-permute-done.9.refs_3_
  23.1 3.7 %collective-permute-start.11 = (bf16[256,384]{1,0:T(8,128)(2,1)S(1)}, bf16[256,384]{1,0:T(8,128)(2,1)S(1)}, u32[]{:S(2)}, u32[]{:S(2)}) collective-permute-start(bf16[256,384]{1,0:T(8,128)(2,1)S(1)} %collective-permute-done.9.refs_3_), channel_id=1, source_target_pairs={{0,7},{1,0},{2,1},{3,2},{4,3},{5,4},{6,5},{7,6},{8,15},{9,8},{10,9... | collective-permute-start | bytes 589832 | tf_op jit(solution)/shard_map/while/body/eval_jaxpr/ppermute | solution.py:194
  26.9 0.6 collective-permute-done.6.refs_9_
  27.6 3.7 %collective-permute-start.7 = (bf16[256,384]{1,0:T(8,128)(2,1)S(1)}, bf16[256,384]{1,0:T(8,128)(2,1)S(1)}, u32[]{:S(2)}, u32[]{:S(2)}) collective-permute-start(bf16[256,384]{1,0:T(8,128)(2,1)S(1)} %collective-permute-done.6.refs_9_), channel_id=1, source_target_pairs={{0,7},{1,0},{2,1},{3,2},{4,3},{5,4},{6,5},{7,6},{8,15},{9,8},{10,9... | collective-permute-start | bytes 589832 | tf_op jit(solution)/shard_map/while/body/eval_jaxpr/ppermute | solution.py:194
  31.3 0.9 collective-permute-done.11.refs_7_
  32.2 3.7 %collective-permute-start.13 = (bf16[256,384]{1,0:T(8,128)(2,1)S(1)}, bf16[256,384]{1,0:T(8,128)(2,1)S(1)}, u32[]{:S(2)}, u32[]{:S(2)}) collective-permute-start(bf16[256,384]{1,0:T(8,128)(2,1)S(1)} %collective-permute-done.11.refs_7_), channel_id=1, source_target_pairs={{0,7},{1,0},{2,1},{3,2},{4,3},{5,4},{6,5},{7,6},{8,15},{9,8},{10,9... | collective-permute-start | bytes 589832 | tf_op jit(solution)/shard_map/while/body/eval_jaxpr/ppermute | solution.py:194
  35.9 2.1 %collective-permute-done.2.refs_10_ = bf16[256,384]{1,0:T(8,128)(2,1)S(1)} collective-permute-done((bf16[256,384]{1,0:T(8,128)(2,1)S(1)}, bf16[256,384]{1,0:T(8,128)(2,1)S(1)}, u32[]{:S(2)}, u32[]{:S(2)}) %collective-permute-start.2) | collective-permute-done | bytes 196640 | tf_op jit(solution)/shard_map/while/body/eval_jaxpr/ppermute | solution.py:194
  38.0 3.2 %collective-permute-start.8 = (bf16[256,384]{1,0:T(8,128)(2,1)S(1)}, bf16[256,384]{1,0:T(8,128)(2,1)S(1)}, u32[]{:S(2)}, u32[]{:S(2)}) collective-permute-start(bf16[256,384]{1,0:T(8,128)(2,1)S(1)} %collective-permute-done.7.refs_13_), channel_id=1, source_target_pairs={{0,7},{1,0},{2,1},{3,2},{4,3},{5,4},{6,5},{7,6},{8,15},{9,8},{10,9... | collective-permute-start | bytes 589832 | tf_op jit(solution)/shard_map/while/body/eval_jaxpr/ppermute | solution.py:194
  41.2 1.5 collective-permute-done.14.refs_12_
  42.7 7.3 %qkv_partial.3 = (f32[3,272,256]{2,1,0:T(8,128)S(1)}, f32[2,256,128]{2,1,0:T(8,128)S(1)}, f32[256,128]{1,0:T(8,128)S(1)}, bf16[3,768,256]{2,1,0:T(8,128)(2,1)S(1)}) custom-call(s32[14]{0:T(128)S(1)} %get-tuple-element.288.rows_ref, s32[2]{0:T(128)S(1)} %get-tuple-element.289.late_rows_ref.rows_ref, f32[16,1,384]{2,1,0:T(1,128)S(1)} %copy-done.2, ...), custom_call_target="tpu_custom_call" | custom-call | tf_op jit(solution)/shard_map/while/body/eval_jaxpr/qkv_partial/pallas_call | solution.py:130
  50.0 2.2 %attention_block.1.own_ref = bf16[256,256]{1,0:T(8,128)(2,1)S(1)} custom-call(s32[2]{0:T(128)S(1)} %get-tuple-element.289.late_rows_ref.rows_ref, f32[16,1,384]{2,1,0:T(1,128)S(1)} %copy-done.2, bf16[256,384]{1,0:T(8,128)(2,1)S(1)} %collective-permute-done.3.refs_0_, bf16[256,384]{1,0:T(8,128)(2,1)S(1)} %collective-permute-done.8.refs_1_, ...), custom_call_target="tpu_custom_call" | custom-call | tf_op jit(solution)/shard_map/while/body/eval_jaxpr/attention_block/pallas_call | solution.py:155
  52.3 0.5 collective-permute-start.15
  52.8 4.5 %collective-permute-done.15.other_ref = bf16[256,256]{1,0:T(8,128)(2,1)S(1)} collective-permute-done((bf16[256,256]{1,0:T(8,128)(2,1)S(1)}, bf16[256,256]{1,0:T(8,128)(2,1)S(1)}, u32[]{:S(2)}, u32[]{:S(2)}) %collective-permute-start.15) | collective-permute-done | bytes 131104 | tf_op jit(solution)/shard_map/while/body/eval_jaxpr/ppermute | solution.py:194
  57.4 0.8 projection_block.6
  58.3 1.7 projection_block.7
  60.0 3.3 %collective-permute-start.21 = (bf16[256,384]{1,0:T(8,128)(2,1)S(1)}, bf16[256,384]{1,0:T(8,128)(2,1)S(1)}, u32[]{:S(2)}, u32[]{:S(2)}) collective-permute-start(bf16[256,384]{1,0:T(8,128)(2,1)S(1)} %get-tuple-element.259), channel_id=1, source_target_pairs={{0,7},{1,0},{2,1},{3,2},{4,3},{5,4},{6,5},{7,6},{8,15},{9,8},{10,9... | collective-permute-start | bytes 589832 | tf_op jit(solution)/shard_map/while/body/eval_jaxpr/ppermute | solution.py:194
  63.4 1.7 collective-permute-done.17
  65.3 1.1 collective-permute-done.21
  66.5 3.8 %collective-permute-start.22 = (bf16[256,384]{1,0:T(8,128)(2,1)S(1)}, bf16[256,384]{1,0:T(8,128)(2,1)S(1)}, u32[]{:S(2)}, u32[]{:S(2)}) collective-permute-start(bf16[256,384]{1,0:T(8,128)(2,1)S(1)} %add_convert_fusion.17), channel_id=1, source_target_pairs={{0,7},{1,0},{2,1},{3,2},{4,3},{5,4},{6,5},{7,6},{8,15},{9,8},{10,9... | collective-permute-start | bytes 589832 | tf_op jit(solution)/shard_map/while/body/eval_jaxpr/ppermute | solution.py:194
  70.3 2.9 %collective-permute-done.18 = bf16[256,384]{1,0:T(8,128)(2,1)S(1)} collective-permute-done((bf16[256,384]{1,0:T(8,128)(2,1)S(1)}, bf16[256,384]{1,0:T(8,128)(2,1)S(1)}, u32[]{:S(2)}, u32[]{:S(2)}) %collective-permute-start.18) | collective-permute-done | bytes 196640 | tf_op jit(solution)/shard_map/while/body/eval_jaxpr/ppermute | solution.py:194
  73.5 1.5 collective-permute-start.23
  75.0 5.3 %collective-permute-done.19 = bf16[256,384]{1,0:T(8,128)(2,1)S(1)} collective-permute-done((bf16[256,384]{1,0:T(8,128)(2,1)S(1)}, bf16[256,384]{1,0:T(8,128)(2,1)S(1)}, u32[]{:S(2)}, u32[]{:S(2)}) %collective-permute-start.19) | collective-permute-done | bytes 196640 | tf_op jit(solution)/shard_map/while/body/eval_jaxpr/ppermute | solution.py:194
  80.5 2.9 %collective-permute-done.23 = bf16[256,384]{1,0:T(8,128)(2,1)S(1)} collective-permute-done((bf16[256,384]{1,0:T(8,128)(2,1)S(1)}, bf16[256,384]{1,0:T(8,128)(2,1)S(1)}, u32[]{:S(2)}, u32[]{:S(2)}) %collective-permute-start.23) | collective-permute-done | bytes 196640 | tf_op jit(solution)/shard_map/while/body/eval_jaxpr/ppermute | solution.py:213
  83.4 7.6 %collective-permute-done.20 = bf16[256,384]{1,0:T(8,128)(2,1)S(1)} collective-permute-done((bf16[256,384]{1,0:T(8,128)(2,1)S(1)}, bf16[256,384]{1,0:T(8,128)(2,1)S(1)}, u32[]{:S(2)}, u32[]{:S(2)}) %collective-permute-start.20) | collective-permute-done | bytes 196640 | tf_op jit(solution)/shard_map/while/body/eval_jaxpr/ppermute | solution.py:213
  91.2 1.5 constant_dynamic-slice_fusion.2
  92.7 6.3 %collective-permute-done.4.refs_1_ = bf16[256,384]{1,0:T(8,128)(2,1)S(1)} collective-permute-done((bf16[256,384]{1,0:T(8,128)(2,1)S(1)}, bf16[256,384]{1,0:T(8,128)(2,1)S(1)}, u32[]{:S(2)}, u32[]{:S(2)}) %collective-permute-start.4) | collective-permute-done | bytes 196640 | tf_op jit(solution)/shard_map/while/body/eval_jaxpr/ppermute | solution.py:194
  99.0 3.2 %collective-permute-start.5 = (bf16[256,384]{1,0:T(8,128)(2,1)S(1)}, bf16[256,384]{1,0:T(8,128)(2,1)S(1)}, u32[]{:S(2)}, u32[]{:S(2)}) collective-permute-start(bf16[256,384]{1,0:T(8,128)(2,1)S(1)} %collective-permute-done.4.refs_1_), channel_id=1, source_target_pairs={{0,7},{1,0},{2,1},{3,2},{4,3},{5,4},{6,5},{7,6},{8,15},{9,8},{10,9... | collective-permute-start | bytes 589832 | tf_op jit(solution)/shard_map/while/body/eval_jaxpr/ppermute | solution.py:194
  102.3 2.0 %collective-permute-start.10 = (bf16[256,384]{1,0:T(8,128)(2,1)S(1)}, bf16[256,384]{1,0:T(8,128)(2,1)S(1)}, u32[]{:S(2)}, u32[]{:S(2)}) collective-permute-start(bf16[256,384]{1,0:T(8,128)(2,1)S(1)} %collective-permute-done.4.refs_1_), channel_id=1, source_target_pairs={{0,1},{1,2},{2,3},{3,4},{4,5},{5,6},{6,7},{7,0},{8,9},{9,10},{10,1... | collective-permute-start | bytes 589832 | tf_op jit(solution)/shard_map/while/body/eval_jaxpr/ppermute | solution.py:194
  104.3 3.2 %collective-permute-done.refs_2_ = bf16[256,384]{1,0:T(8,128)(2,1)S(1)} collective-permute-done((bf16[256,384]{1,0:T(8,128)(2,1)S(1)}, bf16[256,384]{1,0:T(8,128)(2,1)S(1)}, u32[]{:S(2)}, u32[]{:S(2)}) %collective-permute-start) | collective-permute-done | bytes 196640 | tf_op jit(solution)/shard_map/while/body/eval_jaxpr/ppermute | solution.py:194
  107.5 3.2 %collective-permute-start.6 = (bf16[256,384]{1,0:T(8,128)(2,1)S(1)}, bf16[256,384]{1,0:T(8,128)(2,1)S(1)}, u32[]{:S(2)}, u32[]{:S(2)}) collective-permute-start(bf16[256,384]{1,0:T(8,128)(2,1)S(1)} %collective-permute-done.5.refs_5_), channel_id=1, source_target_pairs={{0,7},{1,0},{2,1},{3,2},{4,3},{5,4},{6,5},{7,6},{8,15},{9,8},{10,9... | collective-permute-start | bytes 589832 | tf_op jit(solution)/shard_map/while/body/eval_jaxpr/ppermute | solution.py:194
  111.1 2.7 %collective-permute-start.11 = (bf16[256,384]{1,0:T(8,128)(2,1)S(1)}, bf16[256,384]{1,0:T(8,128)(2,1)S(1)}, u32[]{:S(2)}, u32[]{:S(2)}) collective-permute-start(bf16[256,384]{1,0:T(8,128)(2,1)S(1)} %collective-permute-done.9.refs_3_), channel_id=1, source_target_pairs={{0,7},{1,0},{2,1},{3,2},{4,3},{5,4},{6,5},{7,6},{8,15},{9,8},{10,9... | collective-permute-start | bytes 589832 | tf_op jit(solution)/shard_map/while/body/eval_jaxpr/ppermute | solution.py:194
  113.7 2.7 %collective-permute-done.1.refs_6_ = bf16[256,384]{1,0:T(8,128)(2,1)S(1)} collective-permute-done((bf16[256,384]{1,0:T(8,128)(2,1)S(1)}, bf16[256,384]{1,0:T(8,128)(2,1)S(1)}, u32[]{:S(2)}, u32[]{:S(2)}) %collective-permute-start.1) | collective-permute-done | bytes 196640 | tf_op jit(solution)/shard_map/while/body/eval_jaxpr/ppermute | solution.py:194
  116.4 3.2 %collective-permute-start.7 = (bf16[256,384]{1,0:T(8,128)(2,1)S(1)}, bf16[256,384]{1,0:T(8,128)(2,1)S(1)}, u32[]{:S(2)}, u32[]{:S(2)}) collective-permute-start(bf16[256,384]{1,0:T(8,128)(2,1)S(1)} %collective-permute-done.6.refs_9_), channel_id=1, source_target_pairs={{0,7},{1,0},{2,1},{3,2},{4,3},{5,4},{6,5},{7,6},{8,15},{9,8},{10,9... | collective-permute-start | bytes 589832 | tf_op jit(solution)/shard_map/while/body/eval_jaxpr/ppermute | solution.py:194
  119.7 2.8 %collective-permute-start.13 = (bf16[256,384]{1,0:T(8,128)(2,1)S(1)}, bf16[256,384]{1,0:T(8,128)(2,1)S(1)}, u32[]{:S(2)}, u32[]{:S(2)}) collective-permute-start(bf16[256,384]{1,0:T(8,128)(2,1)S(1)} %collective-permute-done.11.refs_7_), channel_id=1, source_target_pairs={{0,7},{1,0},{2,1},{3,2},{4,3},{5,4},{6,5},{7,6},{8,15},{9,8},{10,9... | collective-permute-start | bytes 589832 | tf_op jit(solution)/shard_map/while/body/eval_jaxpr/ppermute | solution.py:194
  122.4 0.9 collective-permute-done.2.refs_10_
  123.3 3.2 %collective-permute-start.8 = (bf16[256,384]{1,0:T(8,128)(2,1)S(1)}, bf16[256,384]{1,0:T(8,128)(2,1)S(1)}, u32[]{:S(2)}, u32[]{:S(2)}) collective-permute-start(bf16[256,384]{1,0:T(8,128)(2,1)S(1)} %collective-permute-done.7.refs_13_), channel_id=1, source_target_pairs={{0,7},{1,0},{2,1},{3,2},{4,3},{5,4},{6,5},{7,6},{8,15},{9,8},{10,9... | collective-permute-start | bytes 589832 | tf_op jit(solution)/shard_map/while/body/eval_jaxpr/ppermute | solution.py:194
  126.5 2.8 %collective-permute-done.14.refs_12_ = bf16[256,384]{1,0:T(8,128)(2,1)S(1)} collective-permute-done((bf16[256,384]{1,0:T(8,128)(2,1)S(1)}, bf16[256,384]{1,0:T(8,128)(2,1)S(1)}, u32[]{:S(2)}, u32[]{:S(2)}) %collective-permute-start.14) | collective-permute-done | bytes 196640 | tf_op jit(solution)/shard_map/while/body/eval_jaxpr/ppermute | solution.py:194
  129.3 7.3 %qkv_partial.3 = (f32[3,272,256]{2,1,0:T(8,128)S(1)}, f32[2,256,128]{2,1,0:T(8,128)S(1)}, f32[256,128]{1,0:T(8,128)S(1)}, bf16[3,768,256]{2,1,0:T(8,128)(2,1)S(1)}) custom-call(s32[14]{0:T(128)S(1)} %get-tuple-element.288.rows_ref, s32[2]{0:T(128)S(1)} %get-tuple-element.289.late_rows_ref.rows_ref, f32[16,1,384]{2,1,0:T(1,128)S(1)} %copy-done.2, ...), custom_call_target="tpu_custom_call" | custom-call | tf_op jit(solution)/shard_map/while/body/eval_jaxpr/qkv_partial/pallas_call | solution.py:130
  136.6 2.2 %attention_block.1.own_ref = bf16[256,256]{1,0:T(8,128)(2,1)S(1)} custom-call(s32[2]{0:T(128)S(1)} %get-tuple-element.289.late_rows_ref.rows_ref, f32[16,1,384]{2,1,0:T(1,128)S(1)} %copy-done.2, bf16[256,384]{1,0:T(8,128)(2,1)S(1)} %collective-permute-done.3.refs_0_, bf16[256,384]{1,0:T(8,128)(2,1)S(1)} %collective-permute-done.8.refs_1_, ...), custom_call_target="tpu_custom_call" | custom-call | tf_op jit(solution)/shard_map/while/body/eval_jaxpr/attention_block/pallas_call | solution.py:155
  138.9 2.9 %collective-permute-start.15 = (bf16[256,256]{1,0:T(8,128)(2,1)S(1)}, bf16[256,256]{1,0:T(8,128)(2,1)S(1)}, u32[]{:S(2)}, u32[]{:S(2)}) collective-permute-start(bf16[256,256]{1,0:T(8,128)(2,1)S(1)} %attention_block.1.own_ref), channel_id=1, source_target_pairs={{0,8},{8,0},{1,9},{9,1},{2,10},{10,2},{3,11},{11,3},{4,12},{12,4},... | collective-permute-start | bytes 393224 | tf_op jit(solution)/shard_map/while/body/eval_jaxpr/ppermute | solution.py:194
  141.8 2.9 %collective-permute-done.15.other_ref = bf16[256,256]{1,0:T(8,128)(2,1)S(1)} collective-permute-done((bf16[256,256]{1,0:T(8,128)(2,1)S(1)}, bf16[256,256]{1,0:T(8,128)(2,1)S(1)}, u32[]{:S(2)}, u32[]{:S(2)}) %collective-permute-start.15) | collective-permute-done | bytes 131104 | tf_op jit(solution)/shard_map/while/body/eval_jaxpr/ppermute | solution.py:194
  144.7 0.8 projection_block.6
  145.7 1.7 projection_block.7
  147.3 3.3 %collective-permute-start.21 = (bf16[256,384]{1,0:T(8,128)(2,1)S(1)}, bf16[256,384]{1,0:T(8,128)(2,1)S(1)}, u32[]{:S(2)}, u32[]{:S(2)}) collective-permute-start(bf16[256,384]{1,0:T(8,128)(2,1)S(1)} %get-tuple-element.259), channel_id=1, source_target_pairs={{0,7},{1,0},{2,1},{3,2},{4,3},{5,4},{6,5},{7,6},{8,15},{9,8},{10,9... | collective-permute-start | bytes 589832 | tf_op jit(solution)/shard_map/while/body/eval_jaxpr/ppermute | solution.py:194
  150.8 1.7 collective-permute-done.17
  152.7 1.7 collective-permute-done.21
  154.4 3.8 %collective-permute-start.22 = (bf16[256,384]{1,0:T(8,128)(2,1)S(1)}, bf16[256,384]{1,0:T(8,128)(2,1)S(1)}, u32[]{:S(2)}, u32[]{:S(2)}) collective-permute-start(bf16[256,384]{1,0:T(8,128)(2,1)S(1)} %add_convert_fusion.17), channel_id=1, source_target_pairs={{0,7},{1,0},{2,1},{3,2},{4,3},{5,4},{6,5},{7,6},{8,15},{9,8},{10,9... | collective-permute-start | bytes 589832 | tf_op jit(solution)/shard_map/while/body/eval_jaxpr/ppermute | solution.py:194
  158.2 1.3 collective-permute-done.18
  159.7 1.7 collective-permute-done.22
  161.5 5.0 %collective-permute-done.19 = bf16[256,384]{1,0:T(8,128)(2,1)S(1)} collective-permute-done((bf16[256,384]{1,0:T(8,128)(2,1)S(1)}, bf16[256,384]{1,0:T(8,128)(2,1)S(1)}, u32[]{:S(2)}, u32[]{:S(2)}) %collective-permute-start.19) | collective-permute-done | bytes 196640 | tf_op jit(solution)/shard_map/while/body/eval_jaxpr/ppermute | solution.py:194
  166.7 4.1 %collective-permute-done.23 = bf16[256,384]{1,0:T(8,128)(2,1)S(1)} collective-permute-done((bf16[256,384]{1,0:T(8,128)(2,1)S(1)}, bf16[256,384]{1,0:T(8,128)(2,1)S(1)}, u32[]{:S(2)}, u32[]{:S(2)}) %collective-permute-start.23) | collective-permute-done | bytes 196640 | tf_op jit(solution)/shard_map/while/body/eval_jaxpr/ppermute | solution.py:213
  170.8 8.3 %collective-permute-done.20 = bf16[256,384]{1,0:T(8,128)(2,1)S(1)} collective-permute-done((bf16[256,384]{1,0:T(8,128)(2,1)S(1)}, bf16[256,384]{1,0:T(8,128)(2,1)S(1)}, u32[]{:S(2)}, u32[]{:S(2)}) %collective-permute-start.20) | collective-permute-done | bytes 196640 | tf_op jit(solution)/shard_map/while/body/eval_jaxpr/ppermute | solution.py:213
  179.2 0.7 copy-done.1
  (80 shorter events, 2.8 us)
Async XLA Ops:
  1.2 5.7 %collective-permute-start.4 = (bf16[256,384]{1,0:T(8,128)(2,1)S(1)}, bf16[256,384]{1,0:T(8,128)(2,1)S(1)}, u32[]{:S(2)}, u32[]{:S(2)}) collective-permute-start(bf16[256,384]{1,0:T(8,128)(2,1)S(1)} %get-tuple-element.274.refs_0_), channel_id=1, source_target_pairs={{0,8},{8,0},{1,9},{9,1},{2,10},{10,2},{3,11},{11,3},{4,12},{12,4},... | collective-permute-start | bytes 589832 | tf_op jit(solution)/shard_map/while/body/eval_jaxpr/ppermute | solution.py:194
  1.2 41.5 %copy-start.2 = (f32[16,1,384]{2,1,0:T(1,128)S(1)}, f32[16,1,384]{2,1,0:T(1,128)}, u32[]{:S(2)}) copy-start(f32[16,1,384]{2,1,0:T(1,128)} %get-tuple-element.290.gain_ref) | copy-start | bytes 73732 | tf_op jit(solution)/shard_map/while
  6.9 50.5 %collective-permute-start.16 = (bf16[256,3072]{1,0:T(8,128)(2,1)S(1)}, bf16[256,3072]{1,0:T(8,128)(2,1)S(1)}, u32[]{:S(2)}, u32[]{:S(2)}) collective-permute-start(bf16[256,3072]{1,0:T(8,128)(2,1)S(1)} %constant_dynamic-slice_fusion.2), channel_id=1, source_target_pairs={{0,8},{8,0},{1,9},{9,1},{2,10},{10,2},{3,11},{11,3},{4,12},{12,4},... | collective-permute-start | bytes 4718600 | tf_op jit(solution)/shard_map/while/body/eval_jaxpr/ppermute | solution.py:194
  7.7 9.6 %collective-permute-start = (bf16[256,384]{1,0:T(8,128)(2,1)S(1)}, bf16[256,384]{1,0:T(8,128)(2,1)S(1)}, u32[]{:S(2)}, u32[]{:S(2)}) collective-permute-start(bf16[256,384]{1,0:T(8,128)(2,1)S(1)} %get-tuple-element.274.refs_0_), channel_id=1, source_target_pairs={{0,1},{1,2},{2,3},{3,4},{4,5},{5,6},{6,7},{7,0},{8,9},{9,10},{10,1... | collective-permute-start | bytes 589832 | tf_op jit(solution)/shard_map/while/body/eval_jaxpr/ppermute | solution.py:194
  9.6 9.3 %collective-permute-start.5 = (bf16[256,384]{1,0:T(8,128)(2,1)S(1)}, bf16[256,384]{1,0:T(8,128)(2,1)S(1)}, u32[]{:S(2)}, u32[]{:S(2)}) collective-permute-start(bf16[256,384]{1,0:T(8,128)(2,1)S(1)} %collective-permute-done.4.refs_1_), channel_id=1, source_target_pairs={{0,7},{1,0},{2,1},{3,2},{4,3},{5,4},{6,5},{7,6},{8,15},{9,8},{10,9... | collective-permute-start | bytes 589832 | tf_op jit(solution)/shard_map/while/body/eval_jaxpr/ppermute | solution.py:194
  13.6 9.6 %collective-permute-start.9 = (bf16[256,384]{1,0:T(8,128)(2,1)S(1)}, bf16[256,384]{1,0:T(8,128)(2,1)S(1)}, u32[]{:S(2)}, u32[]{:S(2)}) collective-permute-start(bf16[256,384]{1,0:T(8,128)(2,1)S(1)} %get-tuple-element.274.refs_0_), channel_id=1, source_target_pairs={{0,7},{1,0},{2,1},{3,2},{4,3},{5,4},{6,5},{7,6},{8,15},{9,8},{10,9... | collective-permute-start | bytes 589832 | tf_op jit(solution)/shard_map/while/body/eval_jaxpr/ppermute | solution.py:194
  15.6 11.2 %collective-permute-start.10 = (bf16[256,384]{1,0:T(8,128)(2,1)S(1)}, bf16[256,384]{1,0:T(8,128)(2,1)S(1)}, u32[]{:S(2)}, u32[]{:S(2)}) collective-permute-start(bf16[256,384]{1,0:T(8,128)(2,1)S(1)} %collective-permute-done.4.refs_1_), channel_id=1, source_target_pairs={{0,1},{1,2},{2,3},{3,4},{4,5},{5,6},{6,7},{7,0},{8,9},{9,10},{10,1... | collective-permute-start | bytes 589832 | tf_op jit(solution)/shard_map/while/body/eval_jaxpr/ppermute | solution.py:194
  17.3 9.5 %collective-permute-start.1 = (bf16[256,384]{1,0:T(8,128)(2,1)S(1)}, bf16[256,384]{1,0:T(8,128)(2,1)S(1)}, u32[]{:S(2)}, u32[]{:S(2)}) collective-permute-start(bf16[256,384]{1,0:T(8,128)(2,1)S(1)} %collective-permute-done.refs_2_), channel_id=1, source_target_pairs={{0,1},{1,2},{2,3},{3,4},{4,5},{5,6},{6,7},{7,0},{8,9},{9,10},{10,1... | collective-permute-start | bytes 589832 | tf_op jit(solution)/shard_map/while/body/eval_jaxpr/ppermute | solution.py:194
  18.9 8.7 %collective-permute-start.6 = (bf16[256,384]{1,0:T(8,128)(2,1)S(1)}, bf16[256,384]{1,0:T(8,128)(2,1)S(1)}, u32[]{:S(2)}, u32[]{:S(2)}) collective-permute-start(bf16[256,384]{1,0:T(8,128)(2,1)S(1)} %collective-permute-done.5.refs_5_), channel_id=1, source_target_pairs={{0,7},{1,0},{2,1},{3,2},{4,3},{5,4},{6,5},{7,6},{8,15},{9,8},{10,9... | collective-permute-start | bytes 589832 | tf_op jit(solution)/shard_map/while/body/eval_jaxpr/ppermute | solution.py:194
  23.1 9.0 %collective-permute-start.11 = (bf16[256,384]{1,0:T(8,128)(2,1)S(1)}, bf16[256,384]{1,0:T(8,128)(2,1)S(1)}, u32[]{:S(2)}, u32[]{:S(2)}) collective-permute-start(bf16[256,384]{1,0:T(8,128)(2,1)S(1)} %collective-permute-done.9.refs_3_), channel_id=1, source_target_pairs={{0,7},{1,0},{2,1},{3,2},{4,3},{5,4},{6,5},{7,6},{8,15},{9,8},{10,9... | collective-permute-start | bytes 589832 | tf_op jit(solution)/shard_map/while/body/eval_jaxpr/ppermute | solution.py:194
  26.8 9.0 %collective-permute-start.12 = (bf16[256,384]{1,0:T(8,128)(2,1)S(1)}, bf16[256,384]{1,0:T(8,128)(2,1)S(1)}, u32[]{:S(2)}, u32[]{:S(2)}) collective-permute-start(bf16[256,384]{1,0:T(8,128)(2,1)S(1)} %collective-permute-done.10.refs_4_), channel_id=1, source_target_pairs={{0,1},{1,2},{2,3},{3,4},{4,5},{5,6},{6,7},{7,0},{8,9},{9,10},{10,1... | collective-permute-start | bytes 589832 | tf_op jit(solution)/shard_map/while/body/eval_jaxpr/ppermute | solution.py:194
  26.8 11.2 %collective-permute-start.2 = (bf16[256,384]{1,0:T(8,128)(2,1)S(1)}, bf16[256,384]{1,0:T(8,128)(2,1)S(1)}, u32[]{:S(2)}, u32[]{:S(2)}) collective-permute-start(bf16[256,384]{1,0:T(8,128)(2,1)S(1)} %collective-permute-done.1.refs_6_), channel_id=1, source_target_pairs={{0,1},{1,2},{2,3},{3,4},{4,5},{5,6},{6,7},{7,0},{8,9},{9,10},{10,1... | collective-permute-start | bytes 589832 | tf_op jit(solution)/shard_map/while/body/eval_jaxpr/ppermute | solution.py:194
  27.6 10.4 %collective-permute-start.7 = (bf16[256,384]{1,0:T(8,128)(2,1)S(1)}, bf16[256,384]{1,0:T(8,128)(2,1)S(1)}, u32[]{:S(2)}, u32[]{:S(2)}) collective-permute-start(bf16[256,384]{1,0:T(8,128)(2,1)S(1)} %collective-permute-done.6.refs_9_), channel_id=1, source_target_pairs={{0,7},{1,0},{2,1},{3,2},{4,3},{5,4},{6,5},{7,6},{8,15},{9,8},{10,9... | collective-permute-start | bytes 589832 | tf_op jit(solution)/shard_map/while/body/eval_jaxpr/ppermute | solution.py:194
  32.2 9.1 %collective-permute-start.13 = (bf16[256,384]{1,0:T(8,128)(2,1)S(1)}, bf16[256,384]{1,0:T(8,128)(2,1)S(1)}, u32[]{:S(2)}, u32[]{:S(2)}) collective-permute-start(bf16[256,384]{1,0:T(8,128)(2,1)S(1)} %collective-permute-done.11.refs_7_), channel_id=1, source_target_pairs={{0,7},{1,0},{2,1},{3,2},{4,3},{5,4},{6,5},{7,6},{8,15},{9,8},{10,9... | collective-permute-start | bytes 589832 | tf_op jit(solution)/shard_map/while/body/eval_jaxpr/ppermute | solution.py:194
  35.9 6.9 %collective-permute-start.14 = (bf16[256,384]{1,0:T(8,128)(2,1)S(1)}, bf16[256,384]{1,0:T(8,128)(2,1)S(1)}, u32[]{:S(2)}, u32[]{:S(2)}) collective-permute-start(bf16[256,384]{1,0:T(8,128)(2,1)S(1)} %collective-permute-done.12.refs_8_), channel_id=1, source_target_pairs={{0,1},{1,2},{2,3},{3,4},{4,5},{5,6},{6,7},{7,0},{8,9},{9,10},{10,1... | collective-permute-start | bytes 589832 | tf_op jit(solution)/shard_map/while/body/eval_jaxpr/ppermute | solution.py:194
  38.0 12.0 %collective-permute-start.3 = (bf16[256,384]{1,0:T(8,128)(2,1)S(1)}, bf16[256,384]{1,0:T(8,128)(2,1)S(1)}, u32[]{:S(2)}, u32[]{:S(2)}) collective-permute-start(bf16[256,384]{1,0:T(8,128)(2,1)S(1)} %collective-permute-done.2.refs_10_), channel_id=1, source_target_pairs={{0,1},{1,2},{2,3},{3,4},{4,5},{5,6},{6,7},{7,0},{8,9},{9,10},{10,1... | collective-permute-start | bytes 589832 | tf_op jit(solution)/shard_map/while/body/eval_jaxpr/ppermute | solution.py:194
  38.0 12.0 %collective-permute-start.8 = (bf16[256,384]{1,0:T(8,128)(2,1)S(1)}, bf16[256,384]{1,0:T(8,128)(2,1)S(1)}, u32[]{:S(2)}, u32[]{:S(2)}) collective-permute-start(bf16[256,384]{1,0:T(8,128)(2,1)S(1)} %collective-permute-done.7.refs_13_), channel_id=1, source_target_pairs={{0,7},{1,0},{2,1},{3,2},{4,3},{5,4},{6,5},{7,6},{8,15},{9,8},{10,9... | collective-permute-start | bytes 589832 | tf_op jit(solution)/shard_map/while/body/eval_jaxpr/ppermute | solution.py:194
  42.7 7.3 %copy-start.3 = (f32[1,2,128]{2,1,0:T(2,128)S(1)}, f32[1,2,128]{2,1,0:T(2,128)}, u32[]{:S(2)}) copy-start(f32[1,2,128]{2,1,0:T(2,128)} %get-tuple-element.292) | copy-start | bytes 3076 | tf_op jit(solution)/shard_map/while
  42.7 14.6 %copy-start = (bf16[256,6144]{1,0:T(8,128)(2,1)S(1)}, bf16[256,6144]{1,0:T(8,128)(2,1)}, u32[]{:S(2)}) copy-start(bf16[256,6144]{1,0:T(8,128)(2,1)} %get-tuple-element.251.w_own_ref) | copy-start | bytes 9437188 | tf_op jit(solution)/shard_map/while
  52.3 5.1 %collective-permute-start.15 = (bf16[256,256]{1,0:T(8,128)(2,1)S(1)}, bf16[256,256]{1,0:T(8,128)(2,1)S(1)}, u32[]{:S(2)}, u32[]{:S(2)}) collective-permute-start(bf16[256,256]{1,0:T(8,128)(2,1)S(1)} %attention_block.1.own_ref), channel_id=1, source_target_pairs={{0,8},{8,0},{1,9},{9,1},{2,10},{10,2},{3,11},{11,3},{4,12},{12,4},... | collective-permute-start | bytes 393224 | tf_op jit(solution)/shard_map/while/body/eval_jaxpr/ppermute | solution.py:194
  58.2 7.0 %collective-permute-start.17 = (bf16[256,384]{1,0:T(8,128)(2,1)S(1)}, bf16[256,384]{1,0:T(8,128)(2,1)S(1)}, u32[]{:S(2)}, u32[]{:S(2)}) collective-permute-start(bf16[256,384]{1,0:T(8,128)(2,1)S(1)} %projection_block.6), channel_id=1, source_target_pairs={{0,1},{1,2},{2,3},{3,4},{4,5},{5,6},{6,7},{7,0},{8,9},{9,10},{10,1... | collective-permute-start | bytes 589832 | tf_op jit(solution)/shard_map/while/body/eval_jaxpr/ppermute | solution.py:194
  60.0 6.5 %collective-permute-start.21 = (bf16[256,384]{1,0:T(8,128)(2,1)S(1)}, bf16[256,384]{1,0:T(8,128)(2,1)S(1)}, u32[]{:S(2)}, u32[]{:S(2)}) collective-permute-start(bf16[256,384]{1,0:T(8,128)(2,1)S(1)} %get-tuple-element.259), channel_id=1, source_target_pairs={{0,7},{1,0},{2,1},{3,2},{4,3},{5,4},{6,5},{7,6},{8,15},{9,8},{10,9... | collective-permute-start | bytes 589832 | tf_op jit(solution)/shard_map/while/body/eval_jaxpr/ppermute | solution.py:194
  63.3 17.1 %collective-permute-start.24 = (bf16[256,384]{1,0:T(8,128)(2,1)S(1)}, bf16[256,384]{1,0:T(8,128)(2,1)S(1)}, u32[]{:S(2)}, u32[]{:S(2)}) collective-permute-start(bf16[256,384]{1,0:T(8,128)(2,1)S(1)} %add_convert_fusion.19), channel_id=1, source_target_pairs={{0,16},{1,17},{2,18},{3,19},{4,20},{5,21},{6,22},{7,23},{8,24},{9,... | collective-permute-start | bytes 589832 | tf_op jit(solution)/shard_map/while/body/eval_jaxpr/ppermute | solution.py:213
  65.2 8.0 %collective-permute-start.18 = (bf16[256,384]{1,0:T(8,128)(2,1)S(1)}, bf16[256,384]{1,0:T(8,128)(2,1)S(1)}, u32[]{:S(2)}, u32[]{:S(2)}) collective-permute-start(bf16[256,384]{1,0:T(8,128)(2,1)S(1)} %add_convert_fusion.14), channel_id=1, source_target_pairs={{0,1},{1,2},{2,3},{3,4},{4,5},{5,6},{6,7},{7,0},{8,9},{9,10},{10,1... | collective-permute-start | bytes 589832 | tf_op jit(solution)/shard_map/while/body/eval_jaxpr/ppermute | solution.py:194
  66.5 7.0 %collective-permute-start.22 = (bf16[256,384]{1,0:T(8,128)(2,1)S(1)}, bf16[256,384]{1,0:T(8,128)(2,1)S(1)}, u32[]{:S(2)}, u32[]{:S(2)}) collective-permute-start(bf16[256,384]{1,0:T(8,128)(2,1)S(1)} %add_convert_fusion.17), channel_id=1, source_target_pairs={{0,7},{1,0},{2,1},{3,2},{4,3},{5,4},{6,5},{7,6},{8,15},{9,8},{10,9... | collective-permute-start | bytes 589832 | tf_op jit(solution)/shard_map/while/body/eval_jaxpr/ppermute | solution.py:194
  73.2 7.1 %collective-permute-start.19 = (bf16[256,384]{1,0:T(8,128)(2,1)S(1)}, bf16[256,384]{1,0:T(8,128)(2,1)S(1)}, u32[]{:S(2)}, u32[]{:S(2)}) collective-permute-start(bf16[256,384]{1,0:T(8,128)(2,1)S(1)} %add_convert_fusion.15), channel_id=1, source_target_pairs={{0,1},{1,2},{2,3},{3,4},{4,5},{5,6},{6,7},{7,0},{8,9},{9,10},{10,1... | collective-permute-start | bytes 589832 | tf_op jit(solution)/shard_map/while/body/eval_jaxpr/ppermute | solution.py:194
  73.5 9.9 %collective-permute-start.23 = (bf16[256,384]{1,0:T(8,128)(2,1)S(1)}, bf16[256,384]{1,0:T(8,128)(2,1)S(1)}, u32[]{:S(2)}, u32[]{:S(2)}) collective-permute-start(bf16[256,384]{1,0:T(8,128)(2,1)S(1)} %add_convert_fusion.18), channel_id=1, source_target_pairs={{0,23},{1,16},{2,17},{3,18},{4,19},{5,20},{6,21},{7,22},{8,31},{9,... | collective-permute-start | bytes 589832 | tf_op jit(solution)/shard_map/while/body/eval_jaxpr/ppermute | solution.py:213
  80.4 10.6 %collective-permute-start.20 = (bf16[256,384]{1,0:T(8,128)(2,1)S(1)}, bf16[256,384]{1,0:T(8,128)(2,1)S(1)}, u32[]{:S(2)}, u32[]{:S(2)}) collective-permute-start(bf16[256,384]{1,0:T(8,128)(2,1)S(1)} %add_convert_fusion.16), channel_id=1, source_target_pairs={{0,17},{1,18},{2,19},{3,20},{4,21},{5,22},{6,23},{7,16},{8,25},{9,... | collective-permute-start | bytes 589832 | tf_op jit(solution)/shard_map/while/body/eval_jaxpr/ppermute | solution.py:213
  91.1 7.9 %collective-permute-start.4 = (bf16[256,384]{1,0:T(8,128)(2,1)S(1)}, bf16[256,384]{1,0:T(8,128)(2,1)S(1)}, u32[]{:S(2)}, u32[]{:S(2)}) collective-permute-start(bf16[256,384]{1,0:T(8,128)(2,1)S(1)} %get-tuple-element.274.refs_0_), channel_id=1, source_target_pairs={{0,8},{8,0},{1,9},{9,1},{2,10},{10,2},{3,11},{11,3},{4,12},{12,4},... | collective-permute-start | bytes 589832 | tf_op jit(solution)/shard_map/while/body/eval_jaxpr/ppermute | solution.py:194
  91.2 38.1 %copy-start.2 = (f32[16,1,384]{2,1,0:T(1,128)S(1)}, f32[16,1,384]{2,1,0:T(1,128)}, u32[]{:S(2)}) copy-start(f32[16,1,384]{2,1,0:T(1,128)} %get-tuple-element.290.gain_ref) | copy-start | bytes 73732 | tf_op jit(solution)/shard_map/while
  99.0 45.7 %collective-permute-start.16 = (bf16[256,3072]{1,0:T(8,128)(2,1)S(1)}, bf16[256,3072]{1,0:T(8,128)(2,1)S(1)}, u32[]{:S(2)}, u32[]{:S(2)}) collective-permute-start(bf16[256,3072]{1,0:T(8,128)(2,1)S(1)} %constant_dynamic-slice_fusion.2), channel_id=1, source_target_pairs={{0,8},{8,0},{1,9},{9,1},{2,10},{10,2},{3,11},{11,3},{4,12},{12,4},... | collective-permute-start | bytes 4718600 | tf_op jit(solution)/shard_map/while/body/eval_jaxpr/ppermute | solution.py:194
  99.0 8.5 %collective-permute-start = (bf16[256,384]{1,0:T(8,128)(2,1)S(1)}, bf16[256,384]{1,0:T(8,128)(2,1)S(1)}, u32[]{:S(2)}, u32[]{:S(2)}) collective-permute-start(bf16[256,384]{1,0:T(8,128)(2,1)S(1)} %get-tuple-element.274.refs_0_), channel_id=1, source_target_pairs={{0,1},{1,2},{2,3},{3,4},{4,5},{5,6},{6,7},{7,0},{8,9},{9,10},{10,1... | collective-permute-start | bytes 589832 | tf_op jit(solution)/shard_map/while/body/eval_jaxpr/ppermute | solution.py:194
  99.0 8.5 %collective-permute-start.5 = (bf16[256,384]{1,0:T(8,128)(2,1)S(1)}, bf16[256,384]{1,0:T(8,128)(2,1)S(1)}, u32[]{:S(2)}, u32[]{:S(2)}) collective-permute-start(bf16[256,384]{1,0:T(8,128)(2,1)S(1)} %collective-permute-done.4.refs_1_), channel_id=1, source_target_pairs={{0,7},{1,0},{2,1},{3,2},{4,3},{5,4},{6,5},{7,6},{8,15},{9,8},{10,9... | collective-permute-start | bytes 589832 | tf_op jit(solution)/shard_map/while/body/eval_jaxpr/ppermute | solution.py:194
  102.3 8.8 %collective-permute-start.9 = (bf16[256,384]{1,0:T(8,128)(2,1)S(1)}, bf16[256,384]{1,0:T(8,128)(2,1)S(1)}, u32[]{:S(2)}, u32[]{:S(2)}) collective-permute-start(bf16[256,384]{1,0:T(8,128)(2,1)S(1)} %get-tuple-element.274.refs_0_), channel_id=1, source_target_pairs={{0,7},{1,0},{2,1},{3,2},{4,3},{5,4},{6,5},{7,6},{8,15},{9,8},{10,9... | collective-permute-start | bytes 589832 | tf_op jit(solution)/shard_map/while/body/eval_jaxpr/ppermute | solution.py:194
  102.3 11.4 %collective-permute-start.10 = (bf16[256,384]{1,0:T(8,128)(2,1)S(1)}, bf16[256,384]{1,0:T(8,128)(2,1)S(1)}, u32[]{:S(2)}, u32[]{:S(2)}) collective-permute-start(bf16[256,384]{1,0:T(8,128)(2,1)S(1)} %collective-permute-done.4.refs_1_), channel_id=1, source_target_pairs={{0,1},{1,2},{2,3},{3,4},{4,5},{5,6},{6,7},{7,0},{8,9},{9,10},{10,1... | collective-permute-start | bytes 589832 | tf_op jit(solution)/shard_map/while/body/eval_jaxpr/ppermute | solution.py:194
  107.5 8.9 %collective-permute-start.1 = (bf16[256,384]{1,0:T(8,128)(2,1)S(1)}, bf16[256,384]{1,0:T(8,128)(2,1)S(1)}, u32[]{:S(2)}, u32[]{:S(2)}) collective-permute-start(bf16[256,384]{1,0:T(8,128)(2,1)S(1)} %collective-permute-done.refs_2_), channel_id=1, source_target_pairs={{0,1},{1,2},{2,3},{3,4},{4,5},{5,6},{6,7},{7,0},{8,9},{9,10},{10,1... | collective-permute-start | bytes 589832 | tf_op jit(solution)/shard_map/while/body/eval_jaxpr/ppermute | solution.py:194
  107.5 8.9 %collective-permute-start.6 = (bf16[256,384]{1,0:T(8,128)(2,1)S(1)}, bf16[256,384]{1,0:T(8,128)(2,1)S(1)}, u32[]{:S(2)}, u32[]{:S(2)}) collective-permute-start(bf16[256,384]{1,0:T(8,128)(2,1)S(1)} %collective-permute-done.5.refs_5_), channel_id=1, source_target_pairs={{0,7},{1,0},{2,1},{3,2},{4,3},{5,4},{6,5},{7,6},{8,15},{9,8},{10,9... | collective-permute-start | bytes 589832 | tf_op jit(solution)/shard_map/while/body/eval_jaxpr/ppermute | solution.py:194
  111.1 8.6 %collective-permute-start.11 = (bf16[256,384]{1,0:T(8,128)(2,1)S(1)}, bf16[256,384]{1,0:T(8,128)(2,1)S(1)}, u32[]{:S(2)}, u32[]{:S(2)}) collective-permute-start(bf16[256,384]{1,0:T(8,128)(2,1)S(1)} %collective-permute-done.9.refs_3_), channel_id=1, source_target_pairs={{0,7},{1,0},{2,1},{3,2},{4,3},{5,4},{6,5},{7,6},{8,15},{9,8},{10,9... | collective-permute-start | bytes 589832 | tf_op jit(solution)/shard_map/while/body/eval_jaxpr/ppermute | solution.py:194
  113.7 8.7 %collective-permute-start.12 = (bf16[256,384]{1,0:T(8,128)(2,1)S(1)}, bf16[256,384]{1,0:T(8,128)(2,1)S(1)}, u32[]{:S(2)}, u32[]{:S(2)}) collective-permute-start(bf16[256,384]{1,0:T(8,128)(2,1)S(1)} %collective-permute-done.10.refs_4_), channel_id=1, source_target_pairs={{0,1},{1,2},{2,3},{3,4},{4,5},{5,6},{6,7},{7,0},{8,9},{9,10},{10,1... | collective-permute-start | bytes 589832 | tf_op jit(solution)/shard_map/while/body/eval_jaxpr/ppermute | solution.py:194
  116.4 6.9 %collective-permute-start.2 = (bf16[256,384]{1,0:T(8,128)(2,1)S(1)}, bf16[256,384]{1,0:T(8,128)(2,1)S(1)}, u32[]{:S(2)}, u32[]{:S(2)}) collective-permute-start(bf16[256,384]{1,0:T(8,128)(2,1)S(1)} %collective-permute-done.1.refs_6_), channel_id=1, source_target_pairs={{0,1},{1,2},{2,3},{3,4},{4,5},{5,6},{6,7},{7,0},{8,9},{9,10},{10,1... | collective-permute-start | bytes 589832 | tf_op jit(solution)/shard_map/while/body/eval_jaxpr/ppermute | solution.py:194
  116.4 6.9 %collective-permute-start.7 = (bf16[256,384]{1,0:T(8,128)(2,1)S(1)}, bf16[256,384]{1,0:T(8,128)(2,1)S(1)}, u32[]{:S(2)}, u32[]{:S(2)}) collective-permute-start(bf16[256,384]{1,0:T(8,128)(2,1)S(1)} %collective-permute-done.6.refs_9_), channel_id=1, source_target_pairs={{0,7},{1,0},{2,1},{3,2},{4,3},{5,4},{6,5},{7,6},{8,15},{9,8},{10,9... | collective-permute-start | bytes 589832 | tf_op jit(solution)/shard_map/while/body/eval_jaxpr/ppermute | solution.py:194
  119.7 6.9 %collective-permute-start.13 = (bf16[256,384]{1,0:T(8,128)(2,1)S(1)}, bf16[256,384]{1,0:T(8,128)(2,1)S(1)}, u32[]{:S(2)}, u32[]{:S(2)}) collective-permute-start(bf16[256,384]{1,0:T(8,128)(2,1)S(1)} %collective-permute-done.11.refs_7_), channel_id=1, source_target_pairs={{0,7},{1,0},{2,1},{3,2},{4,3},{5,4},{6,5},{7,6},{8,15},{9,8},{10,9... | collective-permute-start | bytes 589832 | tf_op jit(solution)/shard_map/while/body/eval_jaxpr/ppermute | solution.py:194
  122.4 6.9 %collective-permute-start.14 = (bf16[256,384]{1,0:T(8,128)(2,1)S(1)}, bf16[256,384]{1,0:T(8,128)(2,1)S(1)}, u32[]{:S(2)}, u32[]{:S(2)}) collective-permute-start(bf16[256,384]{1,0:T(8,128)(2,1)S(1)} %collective-permute-done.12.refs_8_), channel_id=1, source_target_pairs={{0,1},{1,2},{2,3},{3,4},{4,5},{5,6},{6,7},{7,0},{8,9},{9,10},{10,1... | collective-permute-start | bytes 589832 | tf_op jit(solution)/shard_map/while/body/eval_jaxpr/ppermute | solution.py:194
  123.3 13.3 %collective-permute-start.3 = (bf16[256,384]{1,0:T(8,128)(2,1)S(1)}, bf16[256,384]{1,0:T(8,128)(2,1)S(1)}, u32[]{:S(2)}, u32[]{:S(2)}) collective-permute-start(bf16[256,384]{1,0:T(8,128)(2,1)S(1)} %collective-permute-done.2.refs_10_), channel_id=1, source_target_pairs={{0,1},{1,2},{2,3},{3,4},{4,5},{5,6},{6,7},{7,0},{8,9},{9,10},{10,1... | collective-permute-start | bytes 589832 | tf_op jit(solution)/shard_map/while/body/eval_jaxpr/ppermute | solution.py:194
  123.3 13.3 %collective-permute-start.8 = (bf16[256,384]{1,0:T(8,128)(2,1)S(1)}, bf16[256,384]{1,0:T(8,128)(2,1)S(1)}, u32[]{:S(2)}, u32[]{:S(2)}) collective-permute-start(bf16[256,384]{1,0:T(8,128)(2,1)S(1)} %collective-permute-done.7.refs_13_), channel_id=1, source_target_pairs={{0,7},{1,0},{2,1},{3,2},{4,3},{5,4},{6,5},{7,6},{8,15},{9,8},{10,9... | collective-permute-start | bytes 589832 | tf_op jit(solution)/shard_map/while/body/eval_jaxpr/ppermute | solution.py:194
  129.3 7.3 %copy-start.3 = (f32[1,2,128]{2,1,0:T(2,128)S(1)}, f32[1,2,128]{2,1,0:T(2,128)}, u32[]{:S(2)}) copy-start(f32[1,2,128]{2,1,0:T(2,128)} %get-tuple-element.292) | copy-start | bytes 3076 | tf_op jit(solution)/shard_map/while
  129.3 15.4 %copy-start = (bf16[256,6144]{1,0:T(8,128)(2,1)S(1)}, bf16[256,6144]{1,0:T(8,128)(2,1)}, u32[]{:S(2)}) copy-start(bf16[256,6144]{1,0:T(8,128)(2,1)} %get-tuple-element.251.w_own_ref) | copy-start | bytes 9437188 | tf_op jit(solution)/shard_map/while
  138.9 5.8 %collective-permute-start.15 = (bf16[256,256]{1,0:T(8,128)(2,1)S(1)}, bf16[256,256]{1,0:T(8,128)(2,1)S(1)}, u32[]{:S(2)}, u32[]{:S(2)}) collective-permute-start(bf16[256,256]{1,0:T(8,128)(2,1)S(1)} %attention_block.1.own_ref), channel_id=1, source_target_pairs={{0,8},{8,0},{1,9},{9,1},{2,10},{10,2},{3,11},{11,3},{4,12},{12,4},... | collective-permute-start | bytes 393224 | tf_op jit(solution)/shard_map/while/body/eval_jaxpr/ppermute | solution.py:194
  145.6 7.0 %collective-permute-start.17 = (bf16[256,384]{1,0:T(8,128)(2,1)S(1)}, bf16[256,384]{1,0:T(8,128)(2,1)S(1)}, u32[]{:S(2)}, u32[]{:S(2)}) collective-permute-start(bf16[256,384]{1,0:T(8,128)(2,1)S(1)} %projection_block.6), channel_id=1, source_target_pairs={{0,1},{1,2},{2,3},{3,4},{4,5},{5,6},{6,7},{7,0},{8,9},{9,10},{10,1... | collective-permute-start | bytes 589832 | tf_op jit(solution)/shard_map/while/body/eval_jaxpr/ppermute | solution.py:194
  147.3 7.1 %collective-permute-start.21 = (bf16[256,384]{1,0:T(8,128)(2,1)S(1)}, bf16[256,384]{1,0:T(8,128)(2,1)S(1)}, u32[]{:S(2)}, u32[]{:S(2)}) collective-permute-start(bf16[256,384]{1,0:T(8,128)(2,1)S(1)} %get-tuple-element.259), channel_id=1, source_target_pairs={{0,7},{1,0},{2,1},{3,2},{4,3},{5,4},{6,5},{7,6},{8,15},{9,8},{10,9... | collective-permute-start | bytes 589832 | tf_op jit(solution)/shard_map/while/body/eval_jaxpr/ppermute | solution.py:194
  150.7 16.0 %collective-permute-start.24 = (bf16[256,384]{1,0:T(8,128)(2,1)S(1)}, bf16[256,384]{1,0:T(8,128)(2,1)S(1)}, u32[]{:S(2)}, u32[]{:S(2)}) collective-permute-start(bf16[256,384]{1,0:T(8,128)(2,1)S(1)} %add_convert_fusion.19), channel_id=1, source_target_pairs={{0,16},{1,17},{2,18},{3,19},{4,20},{5,21},{6,22},{7,23},{8,24},{9,... | collective-permute-start | bytes 589832 | tf_op jit(solution)/shard_map/while/body/eval_jaxpr/ppermute | solution.py:213
  152.6 7.0 %collective-permute-start.18 = (bf16[256,384]{1,0:T(8,128)(2,1)S(1)}, bf16[256,384]{1,0:T(8,128)(2,1)S(1)}, u32[]{:S(2)}, u32[]{:S(2)}) collective-permute-start(bf16[256,384]{1,0:T(8,128)(2,1)S(1)} %add_convert_fusion.14), channel_id=1, source_target_pairs={{0,1},{1,2},{2,3},{3,4},{4,5},{5,6},{6,7},{7,0},{8,9},{9,10},{10,1... | collective-permute-start | bytes 589832 | tf_op jit(solution)/shard_map/while/body/eval_jaxpr/ppermute | solution.py:194
  154.4 7.0 %collective-permute-start.22 = (bf16[256,384]{1,0:T(8,128)(2,1)S(1)}, bf16[256,384]{1,0:T(8,128)(2,1)S(1)}, u32[]{:S(2)}, u32[]{:S(2)}) collective-permute-start(bf16[256,384]{1,0:T(8,128)(2,1)S(1)} %add_convert_fusion.17), channel_id=1, source_target_pairs={{0,7},{1,0},{2,1},{3,2},{4,3},{5,4},{6,5},{7,6},{8,15},{9,8},{10,9... | collective-permute-start | bytes 589832 | tf_op jit(solution)/shard_map/while/body/eval_jaxpr/ppermute | solution.py:194
  159.6 7.0 %collective-permute-start.19 = (bf16[256,384]{1,0:T(8,128)(2,1)S(1)}, bf16[256,384]{1,0:T(8,128)(2,1)S(1)}, u32[]{:S(2)}, u32[]{:S(2)}) collective-permute-start(bf16[256,384]{1,0:T(8,128)(2,1)S(1)} %add_convert_fusion.15), channel_id=1, source_target_pairs={{0,1},{1,2},{2,3},{3,4},{4,5},{5,6},{6,7},{7,0},{8,9},{9,10},{10,1... | collective-permute-start | bytes 589832 | tf_op jit(solution)/shard_map/while/body/eval_jaxpr/ppermute | solution.py:194
  161.4 9.4 %collective-permute-start.23 = (bf16[256,384]{1,0:T(8,128)(2,1)S(1)}, bf16[256,384]{1,0:T(8,128)(2,1)S(1)}, u32[]{:S(2)}, u32[]{:S(2)}) collective-permute-start(bf16[256,384]{1,0:T(8,128)(2,1)S(1)} %add_convert_fusion.18), channel_id=1, source_target_pairs={{0,23},{1,16},{2,17},{3,18},{4,19},{5,20},{6,21},{7,22},{8,31},{9,... | collective-permute-start | bytes 589832 | tf_op jit(solution)/shard_map/while/body/eval_jaxpr/ppermute | solution.py:213
  166.6 12.5 %collective-permute-start.20 = (bf16[256,384]{1,0:T(8,128)(2,1)S(1)}, bf16[256,384]{1,0:T(8,128)(2,1)S(1)}, u32[]{:S(2)}, u32[]{:S(2)}) collective-permute-start(bf16[256,384]{1,0:T(8,128)(2,1)S(1)} %add_convert_fusion.16), channel_id=1, source_target_pairs={{0,17},{1,18},{2,19},{3,20},{4,21},{5,22},{6,23},{7,16},{8,25},{9,... | collective-permute-start | bytes 589832 | tf_op jit(solution)/shard_map/while/body/eval_jaxpr/ppermute | solution.py:213
  179.2 0.7 copy-start.1

commit v5 on v1

--- a/solution.py
+++ b/solution.py
@@ -70,14 +70,14 @@
     for copy in now + late:
         copy.start()
     scale_blocks(True, rows_ref, gain_ref, x_refs, None, sums_ref, shift_ref, scaled_ref)
-    for copy in now:
-        copy.wait()
     depth = GROUP * width
-
-    @pl.loop(0, 3)
-    def _(plane):
-        for group in range(blocks // GROUP):
-            span = slice(group * depth, (group + 1) * depth)
+    for group in range(blocks // GROUP):
+        span = slice(group * depth, (group + 1) * depth)
+        for copy in now[group * GROUP : (group + 1) * GROUP]:
+            copy.wait()
+
+        @pl.loop(0, 3)
+        def _(plane):
             out = jnp.dot(scaled_ref[:, span], w_ref[plane, span, :], preferred_element_type=jnp.float32)
             if group == 0:
                 acc_ref[plane] = out

time: 172 us -> 172 us (level)
  Pallas kernels: 23.6 us -> 21.8 us
  waiting for transfers between devices: 79.5 us -> 81.3 us
    pallas_call x2, Pallas kernels: 13.3 us -> 11.6 us  [partial(): pl.pallas_call(functools.partial(partial_block, count), out_shape=[jax.Sh...]
  transfers between devices with their start and end apart: 50 -> 50, of which waited for: 33 -> 33; matrix products, arithmetic and copies ran while one was open for 2% -> 2% of each run, Pallas kernels for 13% -> 12%
where the time goes in v5:
time: 172 us
  waiting for transfers between devices  81.3 us (47%)
  starting transfers between devices  62.5 us (36%)
  Pallas kernels  21.8 us (13%)
  local copies, waits for them, and re-layouts  4.74 us (3%)
    ppermute x42, waiting for transfers between devices, shifted(): lax.ppermute(block, axis, [(i, (i + by) % peers) for i in range(peers)])  59 us
    ppermute x42, starting transfers between devices, shifted(): lax.ppermute(block, axis, [(i, (i + by) % peers) for i in range(peers)])  53.5 us
    ppermute x6, waiting for transfers between devices, to_next_section(): return lax.ppermute(block, SECTION + (PAIR, RING), pairs)  22.3 us
    pallas_call x2, Pallas kernels, partial(): pl.pallas_call(functools.partial(partial_block, count), out_shape=[jax.Sh...  11.6 us
    ppermute x2, starting transfers between devices, across(): return lax.ppermute(block, (PAIR, RING), pairs)  7.14 us
    pallas_call x2, Pallas kernels, attention(): pl.pallas_call(functools.partial(final_block, count, pieces), out_shape=j...  5.24 us
    pallas_call x4, Pallas kernels, projection(): pl.pallas_call(functools.partial(projection_block, places), out_shape=[ja...  5 us
  transfers between devices with their start and end apart: 50, of which 33 were waited for; matrix products, arithmetic and copies ran while one was open for 2% of the time, Pallas kernels for 12%

profile of v5, /device:TPU:0, one launch (start us, length us, event | category | flops | bytes accessed | tf_op | source)
XLA Modules:
  0.0 171.8 jit_solution(61916042639190945)
XLA Ops:
  0.0 0.9 copy.14
  1.2 170.0 %while.12 = (s32[]{:T(128)}, bf16[256,384]{1,0:T(8,128)(2,1)S(1)}, pred[]{:T(512)}, s32[12]{0:T(128)S(1)}, s32[4]{0:T(128)S(1)}, /*index=5*/f32[16,1,384]{2,1,0:...) while((s32[]{:T(128)}, bf16[256,384]{1,0:T(8,128)(2,1)S(1)}, ...), condition=%wide.region_1.2_spmd, body=%wide.region_0.1_spmd.sunk | while | flops 3047426 | bytes 45257908 | solution.py:279
  1.4 4.0 %collective-permute-start.1 = (bf16[256,384]{1,0:T(8,128)(2,1)S(1)}, bf16[256,384]{1,0:T(8,128)(2,1)S(1)}, u32[]{:S(2)}, u32[]{:S(2)}) collective-permute-start(bf16[256,384]{1,0:T(8,128)(2,1)S(1)} %get-tuple-element.283.refs_0_), channel_id=1, source_target_pairs={{0,7},{1,0},{2,1},{3,2},{4,3},{5,4},{6,5},{7,6},{8,15},{9,8},{10,9... | collective-permute-start | bytes 589832 | tf_op jit(solution)/shard_map/while/body/eval_jaxpr/ppermute | solution.py:194
  5.5 1.6 collective-permute-start.2
  7.0 1.5 constant_dynamic-slice_fusion.2
  8.6 1.7 %collective-permute-done.refs_2_ = bf16[256,384]{1,0:T(8,128)(2,1)S(1)} collective-permute-done((bf16[256,384]{1,0:T(8,128)(2,1)S(1)}, bf16[256,384]{1,0:T(8,128)(2,1)S(1)}, u32[]{:S(2)}, u32[]{:S(2)}) %collective-permute-start) | collective-permute-done | bytes 196640 | tf_op jit(solution)/shard_map/while/body/eval_jaxpr/ppermute | solution.py:194
  10.3 1.5 collective-permute-done.2.refs_1_
  11.8 1.6 collective-permute-start.16
  13.4 1.7 collective-permute-start.9
  15.4 2.9 %collective-permute-start.12 = (bf16[256,384]{1,0:T(8,128)(2,1)S(1)}, bf16[256,384]{1,0:T(8,128)(2,1)S(1)}, u32[]{:S(2)}, u32[]{:S(2)}) collective-permute-start(bf16[256,384]{1,0:T(8,128)(2,1)S(1)} %collective-permute-done.1.refs_3_), channel_id=1, source_target_pairs={{0,7},{1,0},{2,1},{3,2},{4,3},{5,4},{6,5},{7,6},{8,15},{9,8},{10,9... | collective-permute-start | bytes 589832 | tf_op jit(solution)/shard_map/while/body/eval_jaxpr/ppermute | solution.py:194
  18.3 2.9 %collective-permute-done.9.refs_7_ = bf16[256,384]{1,0:T(8,128)(2,1)S(1)} collective-permute-done((bf16[256,384]{1,0:T(8,128)(2,1)S(1)}, bf16[256,384]{1,0:T(8,128)(2,1)S(1)}, u32[]{:S(2)}, u32[]{:S(2)}) %collective-permute-start.9) | collective-permute-done | bytes 196640 | tf_op jit(solution)/shard_map/while/body/eval_jaxpr/ppermute | solution.py:194
  21.2 2.6 %collective-permute-start.10 = (bf16[256,384]{1,0:T(8,128)(2,1)S(1)}, bf16[256,384]{1,0:T(8,128)(2,1)S(1)}, u32[]{:S(2)}, u32[]{:S(2)}) collective-permute-start(bf16[256,384]{1,0:T(8,128)(2,1)S(1)} %collective-permute-done.9.refs_7_), channel_id=1, source_target_pairs={{0,7},{1,0},{2,1},{3,2},{4,3},{5,4},{6,5},{7,6},{8,15},{9,8},{10,9... | collective-permute-start | bytes 589832 | tf_op jit(solution)/shard_map/while/body/eval_jaxpr/ppermute | solution.py:194
  24.0 1.4 collective-permute-done.12.refs_5_
  25.4 2.6 %collective-permute-start.13 = (bf16[256,384]{1,0:T(8,128)(2,1)S(1)}, bf16[256,384]{1,0:T(8,128)(2,1)S(1)}, u32[]{:S(2)}, u32[]{:S(2)}) collective-permute-start(bf16[256,384]{1,0:T(8,128)(2,1)S(1)} %collective-permute-done.12.refs_5_), channel_id=1, source_target_pairs={{0,7},{1,0},{2,1},{3,2},{4,3},{5,4},{6,5},{7,6},{8,15},{9,8},{10,9... | collective-permute-start | bytes 589832 | tf_op jit(solution)/shard_map/while/body/eval_jaxpr/ppermute | solution.py:194
  28.3 1.4 collective-permute-done.10.refs_11_
  29.7 3.2 %collective-permute-start.11 = (bf16[256,384]{1,0:T(8,128)(2,1)S(1)}, bf16[256,384]{1,0:T(8,128)(2,1)S(1)}, u32[]{:S(2)}, u32[]{:S(2)}) collective-permute-start(bf16[256,384]{1,0:T(8,128)(2,1)S(1)} %collective-permute-done.10.refs_11_), channel_id=1, source_target_pairs={{0,7},{1,0},{2,1},{3,2},{4,3},{5,4},{6,5},{7,6},{8,15},{9,8},{10,9... | collective-permute-start | bytes 589832 | tf_op jit(solution)/shard_map/while/body/eval_jaxpr/ppermute | solution.py:194
  32.9 1.0 collective-permute-done.13.refs_9_
  33.9 2.7 %collective-permute-start.14 = (bf16[256,384]{1,0:T(8,128)(2,1)S(1)}, bf16[256,384]{1,0:T(8,128)(2,1)S(1)}, u32[]{:S(2)}, u32[]{:S(2)}) collective-permute-start(bf16[256,384]{1,0:T(8,128)(2,1)S(1)} %collective-permute-done.13.refs_9_), channel_id=1, source_target_pairs={{0,15},{1,8},{2,9},{3,10},{4,11},{5,12},{6,13},{7,14},{8,7},{9,0},... | collective-permute-start | bytes 589832 | tf_op jit(solution)/shard_map/while/body/eval_jaxpr/ppermute | solution.py:200
  37.2 5.8 %qkv_partial.3 = (f32[3,272,256]{2,1,0:T(8,128)S(1)}, f32[2,256,128]{2,1,0:T(8,128)S(1)}, f32[256,128]{1,0:T(8,128)S(1)}, bf16[3,1536,256]{2,1,0:T(8,128)(2,1)S(1)}) custom-call(s32[12]{0:T(128)S(1)} %get-tuple-element.297.rows_ref, s32[4]{0:T(128)S(1)} %get-tuple-element.298.late_rows_ref.rows_ref, f32[16,1,384]{2,1,0:T(1,128)S(1)} %copy-done.2, ...), custom_call_target="tpu_custom_call" | custom-call | tf_op jit(solution)/shard_map/while/body/eval_jaxpr/qkv_partial/pallas_call | solution.py:130
  43.1 1.0 collective-permute-done.5.refs_0_
  44.1 2.6 %attention_block.1.own_ref = bf16[256,256]{1,0:T(8,128)(2,1)S(1)} custom-call(s32[4]{0:T(128)S(1)} %get-tuple-element.298.late_rows_ref.rows_ref, f32[16,1,384]{2,1,0:T(1,128)S(1)} %copy-done.2, bf16[256,384]{1,0:T(8,128)(2,1)S(1)} %collective-permute-done.5.refs_0_, bf16[256,384]{1,0:T(8,128)(2,1)S(1)} %collective-permute-done.8.refs_1_, ...), custom_call_target="tpu_custom_call" | custom-call | tf_op jit(solution)/shard_map/while/body/eval_jaxpr/attention_block/pallas_call | solution.py:155
  46.7 1.4 collective-permute-start.15
  48.1 5.6 %collective-permute-done.15.other_ref = bf16[256,256]{1,0:T(8,128)(2,1)S(1)} collective-permute-done((bf16[256,256]{1,0:T(8,128)(2,1)S(1)}, bf16[256,256]{1,0:T(8,128)(2,1)S(1)}, u32[]{:S(2)}, u32[]{:S(2)}) %collective-permute-start.15) | collective-permute-done | bytes 131104 | tf_op jit(solution)/shard_map/while/body/eval_jaxpr/ppermute | solution.py:194
  53.8 0.8 projection_block.6
  54.7 1.7 projection_block.7
  56.4 3.3 %collective-permute-start.21 = (bf16[256,384]{1,0:T(8,128)(2,1)S(1)}, bf16[256,384]{1,0:T(8,128)(2,1)S(1)}, u32[]{:S(2)}, u32[]{:S(2)}) collective-permute-start(bf16[256,384]{1,0:T(8,128)(2,1)S(1)} %get-tuple-element.268), channel_id=1, source_target_pairs={{0,7},{1,0},{2,1},{3,2},{4,3},{5,4},{6,5},{7,6},{8,15},{9,8},{10,9... | collective-permute-start | bytes 589832 | tf_op jit(solution)/shard_map/while/body/eval_jaxpr/ppermute | solution.py:194
  59.9 1.7 %collective-permute-done.17 = bf16[256,384]{1,0:T(8,128)(2,1)S(1)} collective-permute-done((bf16[256,384]{1,0:T(8,128)(2,1)S(1)}, bf16[256,384]{1,0:T(8,128)(2,1)S(1)}, u32[]{:S(2)}, u32[]{:S(2)}) %collective-permute-start.17) | collective-permute-done | bytes 196640 | tf_op jit(solution)/shard_map/while/body/eval_jaxpr/ppermute | solution.py:194
  61.7 1.1 collective-permute-done.21
  62.9 3.8 %collective-permute-start.22 = (bf16[256,384]{1,0:T(8,128)(2,1)S(1)}, bf16[256,384]{1,0:T(8,128)(2,1)S(1)}, u32[]{:S(2)}, u32[]{:S(2)}) collective-permute-start(bf16[256,384]{1,0:T(8,128)(2,1)S(1)} %add_convert_fusion.17), channel_id=1, source_target_pairs={{0,7},{1,0},{2,1},{3,2},{4,3},{5,4},{6,5},{7,6},{8,15},{9,8},{10,9... | collective-permute-start | bytes 589832 | tf_op jit(solution)/shard_map/while/body/eval_jaxpr/ppermute | solution.py:194
  66.7 2.9 %collective-permute-done.18 = bf16[256,384]{1,0:T(8,128)(2,1)S(1)} collective-permute-done((bf16[256,384]{1,0:T(8,128)(2,1)S(1)}, bf16[256,384]{1,0:T(8,128)(2,1)S(1)}, u32[]{:S(2)}, u32[]{:S(2)}) %collective-permute-start.18) | collective-permute-done | bytes 196640 | tf_op jit(solution)/shard_map/while/body/eval_jaxpr/ppermute | solution.py:194
  70.0 1.5 collective-permute-start.23
  71.4 5.3 %collective-permute-done.19 = bf16[256,384]{1,0:T(8,128)(2,1)S(1)} collective-permute-done((bf16[256,384]{1,0:T(8,128)(2,1)S(1)}, bf16[256,384]{1,0:T(8,128)(2,1)S(1)}, u32[]{:S(2)}, u32[]{:S(2)}) %collective-permute-start.19) | collective-permute-done | bytes 196640 | tf_op jit(solution)/shard_map/while/body/eval_jaxpr/ppermute | solution.py:194
  76.9 4.0 %collective-permute-done.23 = bf16[256,384]{1,0:T(8,128)(2,1)S(1)} collective-permute-done((bf16[256,384]{1,0:T(8,128)(2,1)S(1)}, bf16[256,384]{1,0:T(8,128)(2,1)S(1)}, u32[]{:S(2)}, u32[]{:S(2)}) %collective-permute-start.23) | collective-permute-done | bytes 196640 | tf_op jit(solution)/shard_map/while/body/eval_jaxpr/ppermute | solution.py:219
  80.9 6.5 %collective-permute-done.20 = bf16[256,384]{1,0:T(8,128)(2,1)S(1)} collective-permute-done((bf16[256,384]{1,0:T(8,128)(2,1)S(1)}, bf16[256,384]{1,0:T(8,128)(2,1)S(1)}, u32[]{:S(2)}, u32[]{:S(2)}) %collective-permute-start.20) | collective-permute-done | bytes 196640 | tf_op jit(solution)/shard_map/while/body/eval_jaxpr/ppermute | solution.py:219
  87.6 3.2 %collective-permute-start.1 = (bf16[256,384]{1,0:T(8,128)(2,1)S(1)}, bf16[256,384]{1,0:T(8,128)(2,1)S(1)}, u32[]{:S(2)}, u32[]{:S(2)}) collective-permute-start(bf16[256,384]{1,0:T(8,128)(2,1)S(1)} %get-tuple-element.283.refs_0_), channel_id=1, source_target_pairs={{0,7},{1,0},{2,1},{3,2},{4,3},{5,4},{6,5},{7,6},{8,15},{9,8},{10,9... | collective-permute-start | bytes 589832 | tf_op jit(solution)/shard_map/while/body/eval_jaxpr/ppermute | solution.py:194
  91.2 1.5 constant_dynamic-slice_fusion.2
  92.7 1.8 %collective-permute-done.refs_2_ = bf16[256,384]{1,0:T(8,128)(2,1)S(1)} collective-permute-done((bf16[256,384]{1,0:T(8,128)(2,1)S(1)}, bf16[256,384]{1,0:T(8,128)(2,1)S(1)}, u32[]{:S(2)}, u32[]{:S(2)}) %collective-permute-start) | collective-permute-done | bytes 196640 | tf_op jit(solution)/shard_map/while/body/eval_jaxpr/ppermute | solution.py:194
  94.5 1.6 collective-permute-done.1.refs_3_
  96.1 2.5 %collective-permute-done.2.refs_1_ = bf16[256,384]{1,0:T(8,128)(2,1)S(1)} collective-permute-done((bf16[256,384]{1,0:T(8,128)(2,1)S(1)}, bf16[256,384]{1,0:T(8,128)(2,1)S(1)}, u32[]{:S(2)}, u32[]{:S(2)}) %collective-permute-start.2) | collective-permute-done | bytes 196640 | tf_op jit(solution)/shard_map/while/body/eval_jaxpr/ppermute | solution.py:194
  99.0 1.1 collective-permute-start.9
  100.2 0.9 collective-permute-start.6
  101.1 2.4 %collective-permute-start.12 = (bf16[256,384]{1,0:T(8,128)(2,1)S(1)}, bf16[256,384]{1,0:T(8,128)(2,1)S(1)}, u32[]{:S(2)}, u32[]{:S(2)}) collective-permute-start(bf16[256,384]{1,0:T(8,128)(2,1)S(1)} %collective-permute-done.1.refs_3_), channel_id=1, source_target_pairs={{0,7},{1,0},{2,1},{3,2},{4,3},{5,4},{6,5},{7,6},{8,15},{9,8},{10,9... | collective-permute-start | bytes 589832 | tf_op jit(solution)/shard_map/while/body/eval_jaxpr/ppermute | solution.py:194
  103.4 3.4 %collective-permute-done.9.refs_7_ = bf16[256,384]{1,0:T(8,128)(2,1)S(1)} collective-permute-done((bf16[256,384]{1,0:T(8,128)(2,1)S(1)}, bf16[256,384]{1,0:T(8,128)(2,1)S(1)}, u32[]{:S(2)}, u32[]{:S(2)}) %collective-permute-start.9) | collective-permute-done | bytes 196640 | tf_op jit(solution)/shard_map/while/body/eval_jaxpr/ppermute | solution.py:194
  106.8 2.2 %collective-permute-start.10 = (bf16[256,384]{1,0:T(8,128)(2,1)S(1)}, bf16[256,384]{1,0:T(8,128)(2,1)S(1)}, u32[]{:S(2)}, u32[]{:S(2)}) collective-permute-start(bf16[256,384]{1,0:T(8,128)(2,1)S(1)} %collective-permute-done.9.refs_7_), channel_id=1, source_target_pairs={{0,7},{1,0},{2,1},{3,2},{4,3},{5,4},{6,5},{7,6},{8,15},{9,8},{10,9... | collective-permute-start | bytes 589832 | tf_op jit(solution)/shard_map/while/body/eval_jaxpr/ppermute | solution.py:194
  109.0 2.0 %collective-permute-done.12.refs_5_ = bf16[256,384]{1,0:T(8,128)(2,1)S(1)} collective-permute-done((bf16[256,384]{1,0:T(8,128)(2,1)S(1)}, bf16[256,384]{1,0:T(8,128)(2,1)S(1)}, u32[]{:S(2)}, u32[]{:S(2)}) %collective-permute-start.12) | collective-permute-done | bytes 196640 | tf_op jit(solution)/shard_map/while/body/eval_jaxpr/ppermute | solution.py:194
  111.0 2.2 %collective-permute-start.13 = (bf16[256,384]{1,0:T(8,128)(2,1)S(1)}, bf16[256,384]{1,0:T(8,128)(2,1)S(1)}, u32[]{:S(2)}, u32[]{:S(2)}) collective-permute-start(bf16[256,384]{1,0:T(8,128)(2,1)S(1)} %collective-permute-done.12.refs_5_), channel_id=1, source_target_pairs={{0,7},{1,0},{2,1},{3,2},{4,3},{5,4},{6,5},{7,6},{8,15},{9,8},{10,9... | collective-permute-start | bytes 589832 | tf_op jit(solution)/shard_map/while/body/eval_jaxpr/ppermute | solution.py:194
  113.2 1.3 collective-permute-done.10.refs_11_
  114.5 3.4 %collective-permute-start.11 = (bf16[256,384]{1,0:T(8,128)(2,1)S(1)}, bf16[256,384]{1,0:T(8,128)(2,1)S(1)}, u32[]{:S(2)}, u32[]{:S(2)}) collective-permute-start(bf16[256,384]{1,0:T(8,128)(2,1)S(1)} %collective-permute-done.10.refs_11_), channel_id=1, source_target_pairs={{0,7},{1,0},{2,1},{3,2},{4,3},{5,4},{6,5},{7,6},{8,15},{9,8},{10,9... | collective-permute-start | bytes 589832 | tf_op jit(solution)/shard_map/while/body/eval_jaxpr/ppermute | solution.py:194
  117.9 4.5 %collective-permute-start.14 = (bf16[256,384]{1,0:T(8,128)(2,1)S(1)}, bf16[256,384]{1,0:T(8,128)(2,1)S(1)}, u32[]{:S(2)}, u32[]{:S(2)}) collective-permute-start(bf16[256,384]{1,0:T(8,128)(2,1)S(1)} %collective-permute-done.13.refs_9_), channel_id=1, source_target_pairs={{0,15},{1,8},{2,9},{3,10},{4,11},{5,12},{6,13},{7,14},{8,7},{9,0},... | collective-permute-start | bytes 589832 | tf_op jit(solution)/shard_map/while/body/eval_jaxpr/ppermute | solution.py:200
  122.4 5.8 %qkv_partial.3 = (f32[3,272,256]{2,1,0:T(8,128)S(1)}, f32[2,256,128]{2,1,0:T(8,128)S(1)}, f32[256,128]{1,0:T(8,128)S(1)}, bf16[3,1536,256]{2,1,0:T(8,128)(2,1)S(1)}) custom-call(s32[12]{0:T(128)S(1)} %get-tuple-element.297.rows_ref, s32[4]{0:T(128)S(1)} %get-tuple-element.298.late_rows_ref.rows_ref, f32[16,1,384]{2,1,0:T(1,128)S(1)} %copy-done.2, ...), custom_call_target="tpu_custom_call" | custom-call | tf_op jit(solution)/shard_map/while/body/eval_jaxpr/qkv_partial/pallas_call | solution.py:130
  128.3 1.0 collective-permute-done.5.refs_0_
  129.3 2.6 %attention_block.1.own_ref = bf16[256,256]{1,0:T(8,128)(2,1)S(1)} custom-call(s32[4]{0:T(128)S(1)} %get-tuple-element.298.late_rows_ref.rows_ref, f32[16,1,384]{2,1,0:T(1,128)S(1)} %copy-done.2, bf16[256,384]{1,0:T(8,128)(2,1)S(1)} %collective-permute-done.5.refs_0_, bf16[256,384]{1,0:T(8,128)(2,1)S(1)} %collective-permute-done.8.refs_1_, ...), custom_call_target="tpu_custom_call" | custom-call | tf_op jit(solution)/shard_map/while/body/eval_jaxpr/attention_block/pallas_call | solution.py:155
  132.2 4.7 %collective-permute-done.15.other_ref = bf16[256,256]{1,0:T(8,128)(2,1)S(1)} collective-permute-done((bf16[256,256]{1,0:T(8,128)(2,1)S(1)}, bf16[256,256]{1,0:T(8,128)(2,1)S(1)}, u32[]{:S(2)}, u32[]{:S(2)}) %collective-permute-start.15) | collective-permute-done | bytes 131104 | tf_op jit(solution)/shard_map/while/body/eval_jaxpr/ppermute | solution.py:194
  137.0 0.8 projection_block.6
  137.9 1.7 projection_block.7
  139.6 3.3 %collective-permute-start.21 = (bf16[256,384]{1,0:T(8,128)(2,1)S(1)}, bf16[256,384]{1,0:T(8,128)(2,1)S(1)}, u32[]{:S(2)}, u32[]{:S(2)}) collective-permute-start(bf16[256,384]{1,0:T(8,128)(2,1)S(1)} %get-tuple-element.268), channel_id=1, source_target_pairs={{0,7},{1,0},{2,1},{3,2},{4,3},{5,4},{6,5},{7,6},{8,15},{9,8},{10,9... | collective-permute-start | bytes 589832 | tf_op jit(solution)/shard_map/while/body/eval_jaxpr/ppermute | solution.py:194
  143.0 1.7 %collective-permute-done.17 = bf16[256,384]{1,0:T(8,128)(2,1)S(1)} collective-permute-done((bf16[256,384]{1,0:T(8,128)(2,1)S(1)}, bf16[256,384]{1,0:T(8,128)(2,1)S(1)}, u32[]{:S(2)}, u32[]{:S(2)}) %collective-permute-start.17) | collective-permute-done | bytes 196640 | tf_op jit(solution)/shard_map/while/body/eval_jaxpr/ppermute | solution.py:194
  144.9 2.3 %collective-permute-done.21 = bf16[256,384]{1,0:T(8,128)(2,1)S(1)} collective-permute-done((bf16[256,384]{1,0:T(8,128)(2,1)S(1)}, bf16[256,384]{1,0:T(8,128)(2,1)S(1)}, u32[]{:S(2)}, u32[]{:S(2)}) %collective-permute-start.21) | collective-permute-done | bytes 196640 | tf_op jit(solution)/shard_map/while/body/eval_jaxpr/ppermute | solution.py:194
  147.2 3.8 %collective-permute-start.22 = (bf16[256,384]{1,0:T(8,128)(2,1)S(1)}, bf16[256,384]{1,0:T(8,128)(2,1)S(1)}, u32[]{:S(2)}, u32[]{:S(2)}) collective-permute-start(bf16[256,384]{1,0:T(8,128)(2,1)S(1)} %add_convert_fusion.17), channel_id=1, source_target_pairs={{0,7},{1,0},{2,1},{3,2},{4,3},{5,4},{6,5},{7,6},{8,15},{9,8},{10,9... | collective-permute-start | bytes 589832 | tf_op jit(solution)/shard_map/while/body/eval_jaxpr/ppermute | solution.py:194
  151.0 1.1 collective-permute-done.18
  152.5 1.7 %collective-permute-done.22 = bf16[256,384]{1,0:T(8,128)(2,1)S(1)} collective-permute-done((bf16[256,384]{1,0:T(8,128)(2,1)S(1)}, bf16[256,384]{1,0:T(8,128)(2,1)S(1)}, u32[]{:S(2)}, u32[]{:S(2)}) %collective-permute-start.22) | collective-permute-done | bytes 196640 | tf_op jit(solution)/shard_map/while/body/eval_jaxpr/ppermute | solution.py:194
  154.3 4.8 %collective-permute-done.19 = bf16[256,384]{1,0:T(8,128)(2,1)S(1)} collective-permute-done((bf16[256,384]{1,0:T(8,128)(2,1)S(1)}, bf16[256,384]{1,0:T(8,128)(2,1)S(1)}, u32[]{:S(2)}, u32[]{:S(2)}) %collective-permute-start.19) | collective-permute-done | bytes 196640 | tf_op jit(solution)/shard_map/while/body/eval_jaxpr/ppermute | solution.py:194
  159.3 4.4 %collective-permute-done.23 = bf16[256,384]{1,0:T(8,128)(2,1)S(1)} collective-permute-done((bf16[256,384]{1,0:T(8,128)(2,1)S(1)}, bf16[256,384]{1,0:T(8,128)(2,1)S(1)}, u32[]{:S(2)}, u32[]{:S(2)}) %collective-permute-start.23) | collective-permute-done | bytes 196640 | tf_op jit(solution)/shard_map/while/body/eval_jaxpr/ppermute | solution.py:219
  163.6 7.4 %collective-permute-done.20 = bf16[256,384]{1,0:T(8,128)(2,1)S(1)} collective-permute-done((bf16[256,384]{1,0:T(8,128)(2,1)S(1)}, bf16[256,384]{1,0:T(8,128)(2,1)S(1)}, u32[]{:S(2)}, u32[]{:S(2)}) %collective-permute-start.20) | collective-permute-done | bytes 196640 | tf_op jit(solution)/shard_map/while/body/eval_jaxpr/ppermute | solution.py:219
  (80 shorter events, 6.0 us)
Async XLA Ops:
  1.2 36.0 %copy-start.2 = (f32[16,1,384]{2,1,0:T(1,128)S(1)}, f32[16,1,384]{2,1,0:T(1,128)}, u32[]{:S(2)}) copy-start(f32[16,1,384]{2,1,0:T(1,128)} %get-tuple-element.299.gain_ref) | copy-start | bytes 73732 | tf_op jit(solution)/shard_map/while
  1.2 9.1 %collective-permute-start = (bf16[256,384]{1,0:T(8,128)(2,1)S(1)}, bf16[256,384]{1,0:T(8,128)(2,1)S(1)}, u32[]{:S(2)}, u32[]{:S(2)}) collective-permute-start(bf16[256,384]{1,0:T(8,128)(2,1)S(1)} %get-tuple-element.283.refs_0_), channel_id=1, source_target_pairs={{0,1},{1,2},{2,3},{3,4},{4,5},{5,6},{6,7},{7,0},{8,9},{9,10},{10,1... | collective-permute-start | bytes 589832 | tf_op jit(solution)/shard_map/while/body/eval_jaxpr/ppermute | solution.py:194
  1.4 8.8 %collective-permute-start.1 = (bf16[256,384]{1,0:T(8,128)(2,1)S(1)}, bf16[256,384]{1,0:T(8,128)(2,1)S(1)}, u32[]{:S(2)}, u32[]{:S(2)}) collective-permute-start(bf16[256,384]{1,0:T(8,128)(2,1)S(1)} %get-tuple-element.283.refs_0_), channel_id=1, source_target_pairs={{0,7},{1,0},{2,1},{3,2},{4,3},{5,4},{6,5},{7,6},{8,15},{9,8},{10,9... | collective-permute-start | bytes 589832 | tf_op jit(solution)/shard_map/while/body/eval_jaxpr/ppermute | solution.py:194
  5.5 6.4 %collective-permute-start.2 = (bf16[256,384]{1,0:T(8,128)(2,1)S(1)}, bf16[256,384]{1,0:T(8,128)(2,1)S(1)}, u32[]{:S(2)}, u32[]{:S(2)}) collective-permute-start(bf16[256,384]{1,0:T(8,128)(2,1)S(1)} %get-tuple-element.283.refs_0_), channel_id=1, source_target_pairs={{0,8},{8,0},{1,9},{9,1},{2,10},{10,2},{3,11},{11,3},{4,12},{12,4},... | collective-permute-start | bytes 589832 | tf_op jit(solution)/shard_map/while/body/eval_jaxpr/ppermute | solution.py:194
  11.8 42.0 %collective-permute-start.16 = (bf16[256,3072]{1,0:T(8,128)(2,1)S(1)}, bf16[256,3072]{1,0:T(8,128)(2,1)S(1)}, u32[]{:S(2)}, u32[]{:S(2)}) collective-permute-start(bf16[256,3072]{1,0:T(8,128)(2,1)S(1)} %constant_dynamic-slice_fusion.2), channel_id=1, source_target_pairs={{0,8},{8,0},{1,9},{9,1},{2,10},{10,2},{3,11},{11,3},{4,12},{12,4},... | collective-permute-start | bytes 4718600 | tf_op jit(solution)/shard_map/while/body/eval_jaxpr/ppermute | solution.py:194
  13.4 7.8 %collective-permute-start.9 = (bf16[256,384]{1,0:T(8,128)(2,1)S(1)}, bf16[256,384]{1,0:T(8,128)(2,1)S(1)}, u32[]{:S(2)}, u32[]{:S(2)}) collective-permute-start(bf16[256,384]{1,0:T(8,128)(2,1)S(1)} %collective-permute-done.2.refs_1_), channel_id=1, source_target_pairs={{0,7},{1,0},{2,1},{3,2},{4,3},{5,4},{6,5},{7,6},{8,15},{9,8},{10,9... | collective-permute-start | bytes 589832 | tf_op jit(solution)/shard_map/while/body/eval_jaxpr/ppermute | solution.py:194
  15.1 9.0 %collective-permute-start.6 = (bf16[256,384]{1,0:T(8,128)(2,1)S(1)}, bf16[256,384]{1,0:T(8,128)(2,1)S(1)}, u32[]{:S(2)}, u32[]{:S(2)}) collective-permute-start(bf16[256,384]{1,0:T(8,128)(2,1)S(1)} %collective-permute-done.2.refs_1_), channel_id=1, source_target_pairs={{0,1},{1,2},{2,3},{3,4},{4,5},{5,6},{6,7},{7,0},{8,9},{9,10},{10,1... | collective-permute-start | bytes 589832 | tf_op jit(solution)/shard_map/while/body/eval_jaxpr/ppermute | solution.py:194
  15.4 10.0 %collective-permute-start.12 = (bf16[256,384]{1,0:T(8,128)(2,1)S(1)}, bf16[256,384]{1,0:T(8,128)(2,1)S(1)}, u32[]{:S(2)}, u32[]{:S(2)}) collective-permute-start(bf16[256,384]{1,0:T(8,128)(2,1)S(1)} %collective-permute-done.1.refs_3_), channel_id=1, source_target_pairs={{0,7},{1,0},{2,1},{3,2},{4,3},{5,4},{6,5},{7,6},{8,15},{9,8},{10,9... | collective-permute-start | bytes 589832 | tf_op jit(solution)/shard_map/while/body/eval_jaxpr/ppermute | solution.py:194
  18.3 10.0 %collective-permute-start.3 = (bf16[256,384]{1,0:T(8,128)(2,1)S(1)}, bf16[256,384]{1,0:T(8,128)(2,1)S(1)}, u32[]{:S(2)}, u32[]{:S(2)}) collective-permute-start(bf16[256,384]{1,0:T(8,128)(2,1)S(1)} %collective-permute-done.refs_2_), channel_id=1, source_target_pairs={{0,1},{1,2},{2,3},{3,4},{4,5},{5,6},{6,7},{7,0},{8,9},{9,10},{10,1... | collective-permute-start | bytes 589832 | tf_op jit(solution)/shard_map/while/body/eval_jaxpr/ppermute | solution.py:194
  21.2 8.4 %collective-permute-start.10 = (bf16[256,384]{1,0:T(8,128)(2,1)S(1)}, bf16[256,384]{1,0:T(8,128)(2,1)S(1)}, u32[]{:S(2)}, u32[]{:S(2)}) collective-permute-start(bf16[256,384]{1,0:T(8,128)(2,1)S(1)} %collective-permute-done.9.refs_7_), channel_id=1, source_target_pairs={{0,7},{1,0},{2,1},{3,2},{4,3},{5,4},{6,5},{7,6},{8,15},{9,8},{10,9... | collective-permute-start | bytes 589832 | tf_op jit(solution)/shard_map/while/body/eval_jaxpr/ppermute | solution.py:194
  24.0 8.8 %collective-permute-start.7 = (bf16[256,384]{1,0:T(8,128)(2,1)S(1)}, bf16[256,384]{1,0:T(8,128)(2,1)S(1)}, u32[]{:S(2)}, u32[]{:S(2)}) collective-permute-start(bf16[256,384]{1,0:T(8,128)(2,1)S(1)} %collective-permute-done.6.refs_6_), channel_id=1, source_target_pairs={{0,1},{1,2},{2,3},{3,4},{4,5},{5,6},{6,7},{7,0},{8,9},{9,10},{10,1... | collective-permute-start | bytes 589832 | tf_op jit(solution)/shard_map/while/body/eval_jaxpr/ppermute | solution.py:194
  25.4 8.4 %collective-permute-start.13 = (bf16[256,384]{1,0:T(8,128)(2,1)S(1)}, bf16[256,384]{1,0:T(8,128)(2,1)S(1)}, u32[]{:S(2)}, u32[]{:S(2)}) collective-permute-start(bf16[256,384]{1,0:T(8,128)(2,1)S(1)} %collective-permute-done.12.refs_5_), channel_id=1, source_target_pairs={{0,7},{1,0},{2,1},{3,2},{4,3},{5,4},{6,5},{7,6},{8,15},{9,8},{10,9... | collective-permute-start | bytes 589832 | tf_op jit(solution)/shard_map/while/body/eval_jaxpr/ppermute | solution.py:194
  28.3 9.0 %collective-permute-start.4 = (bf16[256,384]{1,0:T(8,128)(2,1)S(1)}, bf16[256,384]{1,0:T(8,128)(2,1)S(1)}, u32[]{:S(2)}, u32[]{:S(2)}) collective-permute-start(bf16[256,384]{1,0:T(8,128)(2,1)S(1)} %collective-permute-done.3.refs_4_), channel_id=1, source_target_pairs={{0,1},{1,2},{2,3},{3,4},{4,5},{5,6},{6,7},{7,0},{8,9},{9,10},{10,1... | collective-permute-start | bytes 589832 | tf_op jit(solution)/shard_map/while/body/eval_jaxpr/ppermute | solution.py:194
  29.7 13.4 %collective-permute-start.11 = (bf16[256,384]{1,0:T(8,128)(2,1)S(1)}, bf16[256,384]{1,0:T(8,128)(2,1)S(1)}, u32[]{:S(2)}, u32[]{:S(2)}) collective-permute-start(bf16[256,384]{1,0:T(8,128)(2,1)S(1)} %collective-permute-done.10.refs_11_), channel_id=1, source_target_pairs={{0,7},{1,0},{2,1},{3,2},{4,3},{5,4},{6,5},{7,6},{8,15},{9,8},{10,9... | collective-permute-start | bytes 589832 | tf_op jit(solution)/shard_map/while/body/eval_jaxpr/ppermute | solution.py:194
  32.9 10.2 %collective-permute-start.8 = (bf16[256,384]{1,0:T(8,128)(2,1)S(1)}, bf16[256,384]{1,0:T(8,128)(2,1)S(1)}, u32[]{:S(2)}, u32[]{:S(2)}) collective-permute-start(bf16[256,384]{1,0:T(8,128)(2,1)S(1)} %collective-permute-done.7.refs_10_), channel_id=1, source_target_pairs={{0,1},{1,2},{2,3},{3,4},{4,5},{5,6},{6,7},{7,0},{8,9},{9,10},{10,1... | collective-permute-start | bytes 589832 | tf_op jit(solution)/shard_map/while/body/eval_jaxpr/ppermute | solution.py:194
  33.9 9.2 %collective-permute-start.14 = (bf16[256,384]{1,0:T(8,128)(2,1)S(1)}, bf16[256,384]{1,0:T(8,128)(2,1)S(1)}, u32[]{:S(2)}, u32[]{:S(2)}) collective-permute-start(bf16[256,384]{1,0:T(8,128)(2,1)S(1)} %collective-permute-done.13.refs_9_), channel_id=1, source_target_pairs={{0,15},{1,8},{2,9},{3,10},{4,11},{5,12},{6,13},{7,14},{8,7},{9,0},... | collective-permute-start | bytes 589832 | tf_op jit(solution)/shard_map/while/body/eval_jaxpr/ppermute | solution.py:200
  37.2 6.9 %collective-permute-start.5 = (bf16[256,384]{1,0:T(8,128)(2,1)S(1)}, bf16[256,384]{1,0:T(8,128)(2,1)S(1)}, u32[]{:S(2)}, u32[]{:S(2)}) collective-permute-start(bf16[256,384]{1,0:T(8,128)(2,1)S(1)} %collective-permute-done.4.refs_8_), channel_id=1, source_target_pairs={{0,1},{1,2},{2,3},{3,4},{4,5},{5,6},{6,7},{7,0},{8,9},{9,10},{10,1... | collective-permute-start | bytes 589832 | tf_op jit(solution)/shard_map/while/body/eval_jaxpr/ppermute | solution.py:194
  37.2 6.9 %copy-start.3 = (f32[1,2,128]{2,1,0:T(2,128)S(1)}, f32[1,2,128]{2,1,0:T(2,128)}, u32[]{:S(2)}) copy-start(f32[1,2,128]{2,1,0:T(2,128)} %get-tuple-element.301) | copy-start | bytes 3076 | tf_op jit(solution)/shard_map/while
  43.1 10.7 %copy-start = (bf16[256,6144]{1,0:T(8,128)(2,1)S(1)}, bf16[256,6144]{1,0:T(8,128)(2,1)}, u32[]{:S(2)}) copy-start(bf16[256,6144]{1,0:T(8,128)(2,1)} %get-tuple-element.260.w_own_ref) | copy-start | bytes 9437188 | tf_op jit(solution)/shard_map/while
  46.7 7.0 %collective-permute-start.15 = (bf16[256,256]{1,0:T(8,128)(2,1)S(1)}, bf16[256,256]{1,0:T(8,128)(2,1)S(1)}, u32[]{:S(2)}, u32[]{:S(2)}) collective-permute-start(bf16[256,256]{1,0:T(8,128)(2,1)S(1)} %attention_block.1.own_ref), channel_id=1, source_target_pairs={{0,8},{8,0},{1,9},{9,1},{2,10},{10,2},{3,11},{11,3},{4,12},{12,4},... | collective-permute-start | bytes 393224 | tf_op jit(solution)/shard_map/while/body/eval_jaxpr/ppermute | solution.py:194
  54.6 7.0 %collective-permute-start.17 = (bf16[256,384]{1,0:T(8,128)(2,1)S(1)}, bf16[256,384]{1,0:T(8,128)(2,1)S(1)}, u32[]{:S(2)}, u32[]{:S(2)}) collective-permute-start(bf16[256,384]{1,0:T(8,128)(2,1)S(1)} %projection_block.6), channel_id=1, source_target_pairs={{0,1},{1,2},{2,3},{3,4},{4,5},{5,6},{6,7},{7,0},{8,9},{9,10},{10,1... | collective-permute-start | bytes 589832 | tf_op jit(solution)/shard_map/while/body/eval_jaxpr/ppermute | solution.py:194
  56.4 6.5 %collective-permute-start.21 = (bf16[256,384]{1,0:T(8,128)(2,1)S(1)}, bf16[256,384]{1,0:T(8,128)(2,1)S(1)}, u32[]{:S(2)}, u32[]{:S(2)}) collective-permute-start(bf16[256,384]{1,0:T(8,128)(2,1)S(1)} %get-tuple-element.268), channel_id=1, source_target_pairs={{0,7},{1,0},{2,1},{3,2},{4,3},{5,4},{6,5},{7,6},{8,15},{9,8},{10,9... | collective-permute-start | bytes 589832 | tf_op jit(solution)/shard_map/while/body/eval_jaxpr/ppermute | solution.py:194
  59.8 17.1 %collective-permute-start.24 = (bf16[256,384]{1,0:T(8,128)(2,1)S(1)}, bf16[256,384]{1,0:T(8,128)(2,1)S(1)}, u32[]{:S(2)}, u32[]{:S(2)}) collective-permute-start(bf16[256,384]{1,0:T(8,128)(2,1)S(1)} %add_convert_fusion.19), channel_id=1, source_target_pairs={{0,16},{1,17},{2,18},{3,19},{4,20},{5,21},{6,22},{7,23},{8,24},{9,... | collective-permute-start | bytes 589832 | tf_op jit(solution)/shard_map/while/body/eval_jaxpr/ppermute | solution.py:219
  61.7 8.0 %collective-permute-start.18 = (bf16[256,384]{1,0:T(8,128)(2,1)S(1)}, bf16[256,384]{1,0:T(8,128)(2,1)S(1)}, u32[]{:S(2)}, u32[]{:S(2)}) collective-permute-start(bf16[256,384]{1,0:T(8,128)(2,1)S(1)} %add_convert_fusion.14), channel_id=1, source_target_pairs={{0,1},{1,2},{2,3},{3,4},{4,5},{5,6},{6,7},{7,0},{8,9},{9,10},{10,1... | collective-permute-start | bytes 589832 | tf_op jit(solution)/shard_map/while/body/eval_jaxpr/ppermute | solution.py:194
  62.9 7.0 %collective-permute-start.22 = (bf16[256,384]{1,0:T(8,128)(2,1)S(1)}, bf16[256,384]{1,0:T(8,128)(2,1)S(1)}, u32[]{:S(2)}, u32[]{:S(2)}) collective-permute-start(bf16[256,384]{1,0:T(8,128)(2,1)S(1)} %add_convert_fusion.17), channel_id=1, source_target_pairs={{0,7},{1,0},{2,1},{3,2},{4,3},{5,4},{6,5},{7,6},{8,15},{9,8},{10,9... | collective-permute-start | bytes 589832 | tf_op jit(solution)/shard_map/while/body/eval_jaxpr/ppermute | solution.py:194
  69.7 7.1 %collective-permute-start.19 = (bf16[256,384]{1,0:T(8,128)(2,1)S(1)}, bf16[256,384]{1,0:T(8,128)(2,1)S(1)}, u32[]{:S(2)}, u32[]{:S(2)}) collective-permute-start(bf16[256,384]{1,0:T(8,128)(2,1)S(1)} %add_convert_fusion.15), channel_id=1, source_target_pairs={{0,1},{1,2},{2,3},{3,4},{4,5},{5,6},{6,7},{7,0},{8,9},{9,10},{10,1... | collective-permute-start | bytes 589832 | tf_op jit(solution)/shard_map/while/body/eval_jaxpr/ppermute | solution.py:194
  70.0 10.9 %collective-permute-start.23 = (bf16[256,384]{1,0:T(8,128)(2,1)S(1)}, bf16[256,384]{1,0:T(8,128)(2,1)S(1)}, u32[]{:S(2)}, u32[]{:S(2)}) collective-permute-start(bf16[256,384]{1,0:T(8,128)(2,1)S(1)} %add_convert_fusion.18), channel_id=1, source_target_pairs={{0,23},{1,16},{2,17},{3,18},{4,19},{5,20},{6,21},{7,22},{8,31},{9,... | collective-permute-start | bytes 589832 | tf_op jit(solution)/shard_map/while/body/eval_jaxpr/ppermute | solution.py:219
  76.8 10.6 %collective-permute-start.20 = (bf16[256,384]{1,0:T(8,128)(2,1)S(1)}, bf16[256,384]{1,0:T(8,128)(2,1)S(1)}, u32[]{:S(2)}, u32[]{:S(2)}) collective-permute-start(bf16[256,384]{1,0:T(8,128)(2,1)S(1)} %add_convert_fusion.16), channel_id=1, source_target_pairs={{0,17},{1,18},{2,19},{3,20},{4,21},{5,22},{6,23},{7,16},{8,25},{9,... | collective-permute-start | bytes 589832 | tf_op jit(solution)/shard_map/while/body/eval_jaxpr/ppermute | solution.py:219
  87.5 34.9 %copy-start.2 = (f32[16,1,384]{2,1,0:T(1,128)S(1)}, f32[16,1,384]{2,1,0:T(1,128)}, u32[]{:S(2)}) copy-start(f32[16,1,384]{2,1,0:T(1,128)} %get-tuple-element.299.gain_ref) | copy-start | bytes 73732 | tf_op jit(solution)/shard_map/while
  87.5 7.0 %collective-permute-start = (bf16[256,384]{1,0:T(8,128)(2,1)S(1)}, bf16[256,384]{1,0:T(8,128)(2,1)S(1)}, u32[]{:S(2)}, u32[]{:S(2)}) collective-permute-start(bf16[256,384]{1,0:T(8,128)(2,1)S(1)} %get-tuple-element.283.refs_0_), channel_id=1, source_target_pairs={{0,1},{1,2},{2,3},{3,4},{4,5},{5,6},{6,7},{7,0},{8,9},{9,10},{10,1... | collective-permute-start | bytes 589832 | tf_op jit(solution)/shard_map/while/body/eval_jaxpr/ppermute | solution.py:194
  87.6 8.5 %collective-permute-start.1 = (bf16[256,384]{1,0:T(8,128)(2,1)S(1)}, bf16[256,384]{1,0:T(8,128)(2,1)S(1)}, u32[]{:S(2)}, u32[]{:S(2)}) collective-permute-start(bf16[256,384]{1,0:T(8,128)(2,1)S(1)} %get-tuple-element.283.refs_0_), channel_id=1, source_target_pairs={{0,7},{1,0},{2,1},{3,2},{4,3},{5,4},{6,5},{7,6},{8,15},{9,8},{10,9... | collective-permute-start | bytes 589832 | tf_op jit(solution)/shard_map/while/body/eval_jaxpr/ppermute | solution.py:194
  90.8 7.8 %collective-permute-start.2 = (bf16[256,384]{1,0:T(8,128)(2,1)S(1)}, bf16[256,384]{1,0:T(8,128)(2,1)S(1)}, u32[]{:S(2)}, u32[]{:S(2)}) collective-permute-start(bf16[256,384]{1,0:T(8,128)(2,1)S(1)} %get-tuple-element.283.refs_0_), channel_id=1, source_target_pairs={{0,8},{8,0},{1,9},{9,1},{2,10},{10,2},{3,11},{11,3},{4,12},{12,4},... | collective-permute-start | bytes 589832 | tf_op jit(solution)/shard_map/while/body/eval_jaxpr/ppermute | solution.py:194
  98.7 38.3 %collective-permute-start.16 = (bf16[256,3072]{1,0:T(8,128)(2,1)S(1)}, bf16[256,3072]{1,0:T(8,128)(2,1)S(1)}, u32[]{:S(2)}, u32[]{:S(2)}) collective-permute-start(bf16[256,3072]{1,0:T(8,128)(2,1)S(1)} %constant_dynamic-slice_fusion.2), channel_id=1, source_target_pairs={{0,8},{8,0},{1,9},{9,1},{2,10},{10,2},{3,11},{11,3},{4,12},{12,4},... | collective-permute-start | bytes 4718600 | tf_op jit(solution)/shard_map/while/body/eval_jaxpr/ppermute | solution.py:194
  99.0 7.7 %collective-permute-start.9 = (bf16[256,384]{1,0:T(8,128)(2,1)S(1)}, bf16[256,384]{1,0:T(8,128)(2,1)S(1)}, u32[]{:S(2)}, u32[]{:S(2)}) collective-permute-start(bf16[256,384]{1,0:T(8,128)(2,1)S(1)} %collective-permute-done.2.refs_1_), channel_id=1, source_target_pairs={{0,7},{1,0},{2,1},{3,2},{4,3},{5,4},{6,5},{7,6},{8,15},{9,8},{10,9... | collective-permute-start | bytes 589832 | tf_op jit(solution)/shard_map/while/body/eval_jaxpr/ppermute | solution.py:194
  100.2 8.8 %collective-permute-start.6 = (bf16[256,384]{1,0:T(8,128)(2,1)S(1)}, bf16[256,384]{1,0:T(8,128)(2,1)S(1)}, u32[]{:S(2)}, u32[]{:S(2)}) collective-permute-start(bf16[256,384]{1,0:T(8,128)(2,1)S(1)} %collective-permute-done.2.refs_1_), channel_id=1, source_target_pairs={{0,1},{1,2},{2,3},{3,4},{4,5},{5,6},{6,7},{7,0},{8,9},{9,10},{10,1... | collective-permute-start | bytes 589832 | tf_op jit(solution)/shard_map/while/body/eval_jaxpr/ppermute | solution.py:194
  101.1 9.9 %collective-permute-start.12 = (bf16[256,384]{1,0:T(8,128)(2,1)S(1)}, bf16[256,384]{1,0:T(8,128)(2,1)S(1)}, u32[]{:S(2)}, u32[]{:S(2)}) collective-permute-start(bf16[256,384]{1,0:T(8,128)(2,1)S(1)} %collective-permute-done.1.refs_3_), channel_id=1, source_target_pairs={{0,7},{1,0},{2,1},{3,2},{4,3},{5,4},{6,5},{7,6},{8,15},{9,8},{10,9... | collective-permute-start | bytes 589832 | tf_op jit(solution)/shard_map/while/body/eval_jaxpr/ppermute | solution.py:194
  103.4 9.8 %collective-permute-start.3 = (bf16[256,384]{1,0:T(8,128)(2,1)S(1)}, bf16[256,384]{1,0:T(8,128)(2,1)S(1)}, u32[]{:S(2)}, u32[]{:S(2)}) collective-permute-start(bf16[256,384]{1,0:T(8,128)(2,1)S(1)} %collective-permute-done.refs_2_), channel_id=1, source_target_pairs={{0,1},{1,2},{2,3},{3,4},{4,5},{5,6},{6,7},{7,0},{8,9},{9,10},{10,1... | collective-permute-start | bytes 589832 | tf_op jit(solution)/shard_map/while/body/eval_jaxpr/ppermute | solution.py:194
  106.8 7.7 %collective-permute-start.10 = (bf16[256,384]{1,0:T(8,128)(2,1)S(1)}, bf16[256,384]{1,0:T(8,128)(2,1)S(1)}, u32[]{:S(2)}, u32[]{:S(2)}) collective-permute-start(bf16[256,384]{1,0:T(8,128)(2,1)S(1)} %collective-permute-done.9.refs_7_), channel_id=1, source_target_pairs={{0,7},{1,0},{2,1},{3,2},{4,3},{5,4},{6,5},{7,6},{8,15},{9,8},{10,9... | collective-permute-start | bytes 589832 | tf_op jit(solution)/shard_map/while/body/eval_jaxpr/ppermute | solution.py:194
  109.0 9.0 %collective-permute-start.7 = (bf16[256,384]{1,0:T(8,128)(2,1)S(1)}, bf16[256,384]{1,0:T(8,128)(2,1)S(1)}, u32[]{:S(2)}, u32[]{:S(2)}) collective-permute-start(bf16[256,384]{1,0:T(8,128)(2,1)S(1)} %collective-permute-done.6.refs_6_), channel_id=1, source_target_pairs={{0,1},{1,2},{2,3},{3,4},{4,5},{5,6},{6,7},{7,0},{8,9},{9,10},{10,1... | collective-permute-start | bytes 589832 | tf_op jit(solution)/shard_map/while/body/eval_jaxpr/ppermute | solution.py:194
  111.0 6.9 %collective-permute-start.13 = (bf16[256,384]{1,0:T(8,128)(2,1)S(1)}, bf16[256,384]{1,0:T(8,128)(2,1)S(1)}, u32[]{:S(2)}, u32[]{:S(2)}) collective-permute-start(bf16[256,384]{1,0:T(8,128)(2,1)S(1)} %collective-permute-done.12.refs_5_), channel_id=1, source_target_pairs={{0,7},{1,0},{2,1},{3,2},{4,3},{5,4},{6,5},{7,6},{8,15},{9,8},{10,9... | collective-permute-start | bytes 589832 | tf_op jit(solution)/shard_map/while/body/eval_jaxpr/ppermute | solution.py:194
  113.2 9.2 %collective-permute-start.4 = (bf16[256,384]{1,0:T(8,128)(2,1)S(1)}, bf16[256,384]{1,0:T(8,128)(2,1)S(1)}, u32[]{:S(2)}, u32[]{:S(2)}) collective-permute-start(bf16[256,384]{1,0:T(8,128)(2,1)S(1)} %collective-permute-done.3.refs_4_), channel_id=1, source_target_pairs={{0,1},{1,2},{2,3},{3,4},{4,5},{5,6},{6,7},{7,0},{8,9},{9,10},{10,1... | collective-permute-start | bytes 589832 | tf_op jit(solution)/shard_map/while/body/eval_jaxpr/ppermute | solution.py:194
  114.5 13.8 %collective-permute-start.11 = (bf16[256,384]{1,0:T(8,128)(2,1)S(1)}, bf16[256,384]{1,0:T(8,128)(2,1)S(1)}, u32[]{:S(2)}, u32[]{:S(2)}) collective-permute-start(bf16[256,384]{1,0:T(8,128)(2,1)S(1)} %collective-permute-done.10.refs_11_), channel_id=1, source_target_pairs={{0,7},{1,0},{2,1},{3,2},{4,3},{5,4},{6,5},{7,6},{8,15},{9,8},{10,9... | collective-permute-start | bytes 589832 | tf_op jit(solution)/shard_map/while/body/eval_jaxpr/ppermute | solution.py:194
  117.9 10.3 %collective-permute-start.8 = (bf16[256,384]{1,0:T(8,128)(2,1)S(1)}, bf16[256,384]{1,0:T(8,128)(2,1)S(1)}, u32[]{:S(2)}, u32[]{:S(2)}) collective-permute-start(bf16[256,384]{1,0:T(8,128)(2,1)S(1)} %collective-permute-done.7.refs_10_), channel_id=1, source_target_pairs={{0,1},{1,2},{2,3},{3,4},{4,5},{5,6},{6,7},{7,0},{8,9},{9,10},{10,1... | collective-permute-start | bytes 589832 | tf_op jit(solution)/shard_map/while/body/eval_jaxpr/ppermute | solution.py:194
  117.9 10.3 %collective-permute-start.14 = (bf16[256,384]{1,0:T(8,128)(2,1)S(1)}, bf16[256,384]{1,0:T(8,128)(2,1)S(1)}, u32[]{:S(2)}, u32[]{:S(2)}) collective-permute-start(bf16[256,384]{1,0:T(8,128)(2,1)S(1)} %collective-permute-done.13.refs_9_), channel_id=1, source_target_pairs={{0,15},{1,8},{2,9},{3,10},{4,11},{5,12},{6,13},{7,14},{8,7},{9,0},... | collective-permute-start | bytes 589832 | tf_op jit(solution)/shard_map/while/body/eval_jaxpr/ppermute | solution.py:200
  122.4 6.9 %collective-permute-start.5 = (bf16[256,384]{1,0:T(8,128)(2,1)S(1)}, bf16[256,384]{1,0:T(8,128)(2,1)S(1)}, u32[]{:S(2)}, u32[]{:S(2)}) collective-permute-start(bf16[256,384]{1,0:T(8,128)(2,1)S(1)} %collective-permute-done.4.refs_8_), channel_id=1, source_target_pairs={{0,1},{1,2},{2,3},{3,4},{4,5},{5,6},{6,7},{7,0},{8,9},{9,10},{10,1... | collective-permute-start | bytes 589832 | tf_op jit(solution)/shard_map/while/body/eval_jaxpr/ppermute | solution.py:194
  122.4 6.9 %copy-start.3 = (f32[1,2,128]{2,1,0:T(2,128)S(1)}, f32[1,2,128]{2,1,0:T(2,128)}, u32[]{:S(2)}) copy-start(f32[1,2,128]{2,1,0:T(2,128)} %get-tuple-element.301) | copy-start | bytes 3076 | tf_op jit(solution)/shard_map/while
  128.2 8.7 %copy-start = (bf16[256,6144]{1,0:T(8,128)(2,1)S(1)}, bf16[256,6144]{1,0:T(8,128)(2,1)}, u32[]{:S(2)}) copy-start(bf16[256,6144]{1,0:T(8,128)(2,1)} %get-tuple-element.260.w_own_ref) | copy-start | bytes 9437188 | tf_op jit(solution)/shard_map/while
  131.9 5.1 %collective-permute-start.15 = (bf16[256,256]{1,0:T(8,128)(2,1)S(1)}, bf16[256,256]{1,0:T(8,128)(2,1)S(1)}, u32[]{:S(2)}, u32[]{:S(2)}) collective-permute-start(bf16[256,256]{1,0:T(8,128)(2,1)S(1)} %attention_block.1.own_ref), channel_id=1, source_target_pairs={{0,8},{8,0},{1,9},{9,1},{2,10},{10,2},{3,11},{11,3},{4,12},{12,4},... | collective-permute-start | bytes 393224 | tf_op jit(solution)/shard_map/while/body/eval_jaxpr/ppermute | solution.py:194
  137.8 7.0 %collective-permute-start.17 = (bf16[256,384]{1,0:T(8,128)(2,1)S(1)}, bf16[256,384]{1,0:T(8,128)(2,1)S(1)}, u32[]{:S(2)}, u32[]{:S(2)}) collective-permute-start(bf16[256,384]{1,0:T(8,128)(2,1)S(1)} %projection_block.6), channel_id=1, source_target_pairs={{0,1},{1,2},{2,3},{3,4},{4,5},{5,6},{6,7},{7,0},{8,9},{9,10},{10,1... | collective-permute-start | bytes 589832 | tf_op jit(solution)/shard_map/while/body/eval_jaxpr/ppermute | solution.py:194
  139.6 7.6 %collective-permute-start.21 = (bf16[256,384]{1,0:T(8,128)(2,1)S(1)}, bf16[256,384]{1,0:T(8,128)(2,1)S(1)}, u32[]{:S(2)}, u32[]{:S(2)}) collective-permute-start(bf16[256,384]{1,0:T(8,128)(2,1)S(1)} %get-tuple-element.268), channel_id=1, source_target_pairs={{0,7},{1,0},{2,1},{3,2},{4,3},{5,4},{6,5},{7,6},{8,15},{9,8},{10,9... | collective-permute-start | bytes 589832 | tf_op jit(solution)/shard_map/while/body/eval_jaxpr/ppermute | solution.py:194
  142.9 16.3 %collective-permute-start.24 = (bf16[256,384]{1,0:T(8,128)(2,1)S(1)}, bf16[256,384]{1,0:T(8,128)(2,1)S(1)}, u32[]{:S(2)}, u32[]{:S(2)}) collective-permute-start(bf16[256,384]{1,0:T(8,128)(2,1)S(1)} %add_convert_fusion.19), channel_id=1, source_target_pairs={{0,16},{1,17},{2,18},{3,19},{4,20},{5,21},{6,22},{7,23},{8,24},{9,... | collective-permute-start | bytes 589832 | tf_op jit(solution)/shard_map/while/body/eval_jaxpr/ppermute | solution.py:219
  144.8 7.3 %collective-permute-start.18 = (bf16[256,384]{1,0:T(8,128)(2,1)S(1)}, bf16[256,384]{1,0:T(8,128)(2,1)S(1)}, u32[]{:S(2)}, u32[]{:S(2)}) collective-permute-start(bf16[256,384]{1,0:T(8,128)(2,1)S(1)} %add_convert_fusion.14), channel_id=1, source_target_pairs={{0,1},{1,2},{2,3},{3,4},{4,5},{5,6},{6,7},{7,0},{8,9},{9,10},{10,1... | collective-permute-start | bytes 589832 | tf_op jit(solution)/shard_map/while/body/eval_jaxpr/ppermute | solution.py:194
  147.2 7.0 %collective-permute-start.22 = (bf16[256,384]{1,0:T(8,128)(2,1)S(1)}, bf16[256,384]{1,0:T(8,128)(2,1)S(1)}, u32[]{:S(2)}, u32[]{:S(2)}) collective-permute-start(bf16[256,384]{1,0:T(8,128)(2,1)S(1)} %add_convert_fusion.17), channel_id=1, source_target_pairs={{0,7},{1,0},{2,1},{3,2},{4,3},{5,4},{6,5},{7,6},{8,15},{9,8},{10,9... | collective-permute-start | bytes 589832 | tf_op jit(solution)/shard_map/while/body/eval_jaxpr/ppermute | solution.py:194
  152.2 7.0 %collective-permute-start.19 = (bf16[256,384]{1,0:T(8,128)(2,1)S(1)}, bf16[256,384]{1,0:T(8,128)(2,1)S(1)}, u32[]{:S(2)}, u32[]{:S(2)}) collective-permute-start(bf16[256,384]{1,0:T(8,128)(2,1)S(1)} %add_convert_fusion.15), channel_id=1, source_target_pairs={{0,1},{1,2},{2,3},{3,4},{4,5},{5,6},{6,7},{7,0},{8,9},{9,10},{10,1... | collective-permute-start | bytes 589832 | tf_op jit(solution)/shard_map/while/body/eval_jaxpr/ppermute | solution.py:194
  154.2 9.4 %collective-permute-start.23 = (bf16[256,384]{1,0:T(8,128)(2,1)S(1)}, bf16[256,384]{1,0:T(8,128)(2,1)S(1)}, u32[]{:S(2)}, u32[]{:S(2)}) collective-permute-start(bf16[256,384]{1,0:T(8,128)(2,1)S(1)} %add_convert_fusion.18), channel_id=1, source_target_pairs={{0,23},{1,16},{2,17},{3,18},{4,19},{5,20},{6,21},{7,22},{8,31},{9,... | collective-permute-start | bytes 589832 | tf_op jit(solution)/shard_map/while/body/eval_jaxpr/ppermute | solution.py:219
  159.2 11.9 %collective-permute-start.20 = (bf16[256,384]{1,0:T(8,128)(2,1)S(1)}, bf16[256,384]{1,0:T(8,128)(2,1)S(1)}, u32[]{:S(2)}, u32[]{:S(2)}) collective-permute-start(bf16[256,384]{1,0:T(8,128)(2,1)S(1)} %add_convert_fusion.16), channel_id=1, source_target_pairs={{0,17},{1,18},{2,19},{3,20},{4,21},{5,22},{6,23},{7,16},{8,25},{9,... | collective-permute-start | bytes 589832 | tf_op jit(solution)/shard_map/while/body/eval_jaxpr/ppermute | solution.py:219
  171.2 0.7 copy-start.1

commit v6 on v5

--- a/solution.py
+++ b/solution.py
@@ -263,18 +263,16 @@
         sums = partial(early_rows, late_rows, gain, w_planes, blocks)
         mixed = attention(late_rows, gain, late, sums, qk_gain[0], 2 * ring)
         mixed_other = shifted(mixed, PAIR, 1)
-        parts = projection(order, mixed, mixed_other, w_own, w_other, ring, (4,))
-        up = shifted(parts[4], RING, 1)
-        mixed_other = lax.optimization_barrier((mixed_other, parts[4]))[0]
-        parts |= projection(order, mixed, mixed_other, w_own, w_other, ring, (5, 3, 6, 0, 7, 2, 1))
-        down = shifted(parts[5], RING, -1)
-
-        kept = to_next_section(added(jnp.where(flip, other, own), parts[0]), 0)
-        down = to_next_section(added(shifted(added(down, parts[6]), RING, -1), parts[7]), -1)
+        parts = projection(order, mixed, mixed_other, w_own, w_other, ring, (4, 5))
+        up, down = shifted(parts[4], RING, 1), shifted(parts[5], RING, -1)
+        parts |= projection(order, mixed, mixed_other, w_own, w_other, ring, (3, 6, 2, 7, 1, 0))
+
         for k in (3, 2):
             up = shifted(added(up, parts[k]), RING, 1)
+            down = shifted(added(down, parts[9 - k]), RING, -1)
         up = to_next_section(added(up, parts[1]), 1)
-        return added(kept, down, up)
+        own = to_next_section(added(jnp.where(flip, other, own), down, parts[0]), 0)
+        return added(own, up)
 
     return lax.fori_loop(0, STEPS, step, own)[None]
 

time: 172 us -> 175 us (1.017); the launches traced: 172 us -> 172 us
    ppermute x42 -> x44, waiting for transfers between devices: 59 us -> 61.7 us  [shifted(): lax.ppermute(block, axis, [(i, (i + by) % peers) for i in range(peers)])]
    ppermute x42 -> x44, starting transfers between devices: 53.5 us -> 55.7 us  [shifted(): lax.ppermute(block, axis, [(i, (i + by) % peers) for i in range(peers)])]
    ppermute x6 -> x4, waiting for transfers between devices: 22.3 us -> 21 us  [to_next_section(): return lax.ppermute(block, SECTION + (PAIR, RING), pairs)]
  transfers between devices with their start and end apart: 50 -> 50, of which waited for: 33 -> 32; matrix products, arithmetic and copies ran while one was open for 2% -> 2% of each run, Pallas kernels for 12% -> 12%
where the time goes in v6:
time: 175 us; the launch traced here: 172 us
  waiting for transfers between devices  82.8 us (47%)
  starting transfers between devices  61.8 us (35%)
  Pallas kernels  21.8 us (12%)
  local copies, waits for them, and re-layouts  4.74 us (3%)
    ppermute x44, waiting for transfers between devices, shifted(): lax.ppermute(block, axis, [(i, (i + by) % peers) for i in range(peers)])  61.7 us
    ppermute x44, starting transfers between devices, shifted(): lax.ppermute(block, axis, [(i, (i + by) % peers) for i in range(peers)])  55.7 us
    ppermute x4, waiting for transfers between devices, to_next_section(): return lax.ppermute(block, SECTION + (PAIR, RING), pairs)  21 us
    pallas_call x2, Pallas kernels, partial(): pl.pallas_call(functools.partial(partial_block, count), out_shape=[jax.Sh...  11.6 us
    ppermute x2, starting transfers between devices, across(): return lax.ppermute(block, (PAIR, RING), pairs)  5.77 us
    pallas_call x2, Pallas kernels, attention(): pl.pallas_call(functools.partial(final_block, count, pieces), out_shape=j...  5.23 us
    pallas_call x4, Pallas kernels, projection(): pl.pallas_call(functools.partial(projection_block, places), out_shape=[ja...  4.98 us
  transfers between devices with their start and end apart: 50, of which 32 were waited for; matrix products, arithmetic and copies ran while one was open for 2% of the time, Pallas kernels for 12%

profile of v6, /device:TPU:0, one launch (start us, length us, event | category | flops | bytes accessed | tf_op | source)
XLA Modules:
  0.0 172.5 jit_solution(262788839024658967)
XLA Ops:
  0.0 0.9 copy.14
  1.2 170.6 %while.12 = (s32[]{:T(128)}, bf16[256,384]{1,0:T(8,128)(2,1)S(1)}, pred[]{:T(512)}, s32[12]{0:T(128)S(1)}, s32[4]{0:T(128)S(1)}, /*index=5*/f32[16,1,384]{2,1,0:...) while((s32[]{:T(128)}, bf16[256,384]{1,0:T(8,128)(2,1)S(1)}, ...), condition=%wide.region_1.2_spmd, body=%wide.region_0.1_spmd.sunk | while | flops 3047426 | bytes 45257908 | solution.py:277
  1.4 4.0 %collective-permute-start.1 = (bf16[256,384]{1,0:T(8,128)(2,1)S(1)}, bf16[256,384]{1,0:T(8,128)(2,1)S(1)}, u32[]{:S(2)}, u32[]{:S(2)}) collective-permute-start(bf16[256,384]{1,0:T(8,128)(2,1)S(1)} %get-tuple-element.283.refs_0_), channel_id=1, source_target_pairs={{0,7},{1,0},{2,1},{3,2},{4,3},{5,4},{6,5},{7,6},{8,15},{9,8},{10,9... | collective-permute-start | bytes 589832 | tf_op jit(solution)/shard_map/while/body/eval_jaxpr/ppermute | solution.py:194
  5.5 1.6 collective-permute-start.2
  7.0 1.5 constant_dynamic-slice_fusion.2
  8.6 1.7 collective-permute-done.refs_2_
  10.3 1.5 collective-permute-done.2.refs_1_
  11.8 1.6 collective-permute-start.16
  13.4 1.7 collective-permute-start.9
  15.4 2.9 %collective-permute-start.12 = (bf16[256,384]{1,0:T(8,128)(2,1)S(1)}, bf16[256,384]{1,0:T(8,128)(2,1)S(1)}, u32[]{:S(2)}, u32[]{:S(2)}) collective-permute-start(bf16[256,384]{1,0:T(8,128)(2,1)S(1)} %collective-permute-done.1.refs_3_), channel_id=1, source_target_pairs={{0,7},{1,0},{2,1},{3,2},{4,3},{5,4},{6,5},{7,6},{8,15},{9,8},{10,9... | collective-permute-start | bytes 589832 | tf_op jit(solution)/shard_map/while/body/eval_jaxpr/ppermute | solution.py:194
  18.3 2.9 %collective-permute-done.9.refs_7_ = bf16[256,384]{1,0:T(8,128)(2,1)S(1)} collective-permute-done((bf16[256,384]{1,0:T(8,128)(2,1)S(1)}, bf16[256,384]{1,0:T(8,128)(2,1)S(1)}, u32[]{:S(2)}, u32[]{:S(2)}) %collective-permute-start.9) | collective-permute-done | bytes 196640 | tf_op jit(solution)/shard_map/while/body/eval_jaxpr/ppermute | solution.py:194
  21.2 2.6 %collective-permute-start.10 = (bf16[256,384]{1,0:T(8,128)(2,1)S(1)}, bf16[256,384]{1,0:T(8,128)(2,1)S(1)}, u32[]{:S(2)}, u32[]{:S(2)}) collective-permute-start(bf16[256,384]{1,0:T(8,128)(2,1)S(1)} %collective-permute-done.9.refs_7_), channel_id=1, source_target_pairs={{0,7},{1,0},{2,1},{3,2},{4,3},{5,4},{6,5},{7,6},{8,15},{9,8},{10,9... | collective-permute-start | bytes 589832 | tf_op jit(solution)/shard_map/while/body/eval_jaxpr/ppermute | solution.py:194
  24.0 1.4 collective-permute-done.12.refs_5_
  25.4 2.6 %collective-permute-start.13 = (bf16[256,384]{1,0:T(8,128)(2,1)S(1)}, bf16[256,384]{1,0:T(8,128)(2,1)S(1)}, u32[]{:S(2)}, u32[]{:S(2)}) collective-permute-start(bf16[256,384]{1,0:T(8,128)(2,1)S(1)} %collective-permute-done.12.refs_5_), channel_id=1, source_target_pairs={{0,7},{1,0},{2,1},{3,2},{4,3},{5,4},{6,5},{7,6},{8,15},{9,8},{10,9... | collective-permute-start | bytes 589832 | tf_op jit(solution)/shard_map/while/body/eval_jaxpr/ppermute | solution.py:194
  28.3 1.4 collective-permute-done.10.refs_11_
  29.7 3.2 %collective-permute-start.11 = (bf16[256,384]{1,0:T(8,128)(2,1)S(1)}, bf16[256,384]{1,0:T(8,128)(2,1)S(1)}, u32[]{:S(2)}, u32[]{:S(2)}) collective-permute-start(bf16[256,384]{1,0:T(8,128)(2,1)S(1)} %collective-permute-done.10.refs_11_), channel_id=1, source_target_pairs={{0,7},{1,0},{2,1},{3,2},{4,3},{5,4},{6,5},{7,6},{8,15},{9,8},{10,9... | collective-permute-start | bytes 589832 | tf_op jit(solution)/shard_map/while/body/eval_jaxpr/ppermute | solution.py:194
  32.9 1.0 collective-permute-done.13.refs_9_
  33.9 2.7 %collective-permute-start.14 = (bf16[256,384]{1,0:T(8,128)(2,1)S(1)}, bf16[256,384]{1,0:T(8,128)(2,1)S(1)}, u32[]{:S(2)}, u32[]{:S(2)}) collective-permute-start(bf16[256,384]{1,0:T(8,128)(2,1)S(1)} %collective-permute-done.13.refs_9_), channel_id=1, source_target_pairs={{0,15},{1,8},{2,9},{3,10},{4,11},{5,12},{6,13},{7,14},{8,7},{9,0},... | collective-permute-start | bytes 589832 | tf_op jit(solution)/shard_map/while/body/eval_jaxpr/ppermute | solution.py:200
  37.2 5.8 %qkv_partial.3 = (f32[3,272,256]{2,1,0:T(8,128)S(1)}, f32[2,256,128]{2,1,0:T(8,128)S(1)}, f32[256,128]{1,0:T(8,128)S(1)}, bf16[3,1536,256]{2,1,0:T(8,128)(2,1)S(1)}) custom-call(s32[12]{0:T(128)S(1)} %get-tuple-element.297.rows_ref, s32[4]{0:T(128)S(1)} %get-tuple-element.298.late_rows_ref.rows_ref, f32[16,1,384]{2,1,0:T(1,128)S(1)} %copy-done.2, ...), custom_call_target="tpu_custom_call" | custom-call | tf_op jit(solution)/shard_map/while/body/eval_jaxpr/qkv_partial/pallas_call | solution.py:130
  43.1 1.0 collective-permute-done.5.refs_0_
  44.1 2.6 %attention_block.1.own_ref = bf16[256,256]{1,0:T(8,128)(2,1)S(1)} custom-call(s32[4]{0:T(128)S(1)} %get-tuple-element.298.late_rows_ref.rows_ref, f32[16,1,384]{2,1,0:T(1,128)S(1)} %copy-done.2, bf16[256,384]{1,0:T(8,128)(2,1)S(1)} %collective-permute-done.5.refs_0_, bf16[256,384]{1,0:T(8,128)(2,1)S(1)} %collective-permute-done.8.refs_1_, ...), custom_call_target="tpu_custom_call" | custom-call | tf_op jit(solution)/shard_map/while/body/eval_jaxpr/attention_block/pallas_call | solution.py:155
  46.7 1.4 collective-permute-start.15
  48.1 5.6 %collective-permute-done.15.other_ref = bf16[256,256]{1,0:T(8,128)(2,1)S(1)} collective-permute-done((bf16[256,256]{1,0:T(8,128)(2,1)S(1)}, bf16[256,256]{1,0:T(8,128)(2,1)S(1)}, u32[]{:S(2)}, u32[]{:S(2)}) %collective-permute-start.15) | collective-permute-done | bytes 131104 | tf_op jit(solution)/shard_map/while/body/eval_jaxpr/ppermute | solution.py:194
  53.8 1.0 projection_block.7
  54.8 1.9 %collective-permute-start.21 = (bf16[256,384]{1,0:T(8,128)(2,1)S(1)}, bf16[256,384]{1,0:T(8,128)(2,1)S(1)}, u32[]{:S(2)}, u32[]{:S(2)}) collective-permute-start(bf16[256,384]{1,0:T(8,128)(2,1)S(1)} %get-tuple-element.269), channel_id=1, source_target_pairs={{0,7},{1,0},{2,1},{3,2},{4,3},{5,4},{6,5},{7,6},{8,15},{9,8},{10,9... | collective-permute-start | bytes 589832 | tf_op jit(solution)/shard_map/while/body/eval_jaxpr/ppermute | solution.py:194
  56.9 1.5 projection_block.6
  58.4 2.8 %collective-permute-done.21 = bf16[256,384]{1,0:T(8,128)(2,1)S(1)} collective-permute-done((bf16[256,384]{1,0:T(8,128)(2,1)S(1)}, bf16[256,384]{1,0:T(8,128)(2,1)S(1)}, u32[]{:S(2)}, u32[]{:S(2)}) %collective-permute-start.21) | collective-permute-done | bytes 196640 | tf_op jit(solution)/shard_map/while/body/eval_jaxpr/ppermute | solution.py:194
  61.2 2.5 %collective-permute-start.22 = (bf16[256,384]{1,0:T(8,128)(2,1)S(1)}, bf16[256,384]{1,0:T(8,128)(2,1)S(1)}, u32[]{:S(2)}, u32[]{:S(2)}) collective-permute-start(bf16[256,384]{1,0:T(8,128)(2,1)S(1)} %add_convert_fusion.17), channel_id=1, source_target_pairs={{0,7},{1,0},{2,1},{3,2},{4,3},{5,4},{6,5},{7,6},{8,15},{9,8},{10,9... | collective-permute-start | bytes 589832 | tf_op jit(solution)/shard_map/while/body/eval_jaxpr/ppermute | solution.py:194
  63.8 4.7 %collective-permute-done.22 = bf16[256,384]{1,0:T(8,128)(2,1)S(1)} collective-permute-done((bf16[256,384]{1,0:T(8,128)(2,1)S(1)}, bf16[256,384]{1,0:T(8,128)(2,1)S(1)}, u32[]{:S(2)}, u32[]{:S(2)}) %collective-permute-start.22) | collective-permute-done | bytes 196640 | tf_op jit(solution)/shard_map/while/body/eval_jaxpr/ppermute | solution.py:194
  68.6 2.5 %collective-permute-start.23 = (bf16[256,384]{1,0:T(8,128)(2,1)S(1)}, bf16[256,384]{1,0:T(8,128)(2,1)S(1)}, u32[]{:S(2)}, u32[]{:S(2)}) collective-permute-start(bf16[256,384]{1,0:T(8,128)(2,1)S(1)} %add_convert_fusion.18), channel_id=1, source_target_pairs={{0,7},{1,0},{2,1},{3,2},{4,3},{5,4},{6,5},{7,6},{8,15},{9,8},{10,9... | collective-permute-start | bytes 589832 | tf_op jit(solution)/shard_map/while/body/eval_jaxpr/ppermute | solution.py:194
  71.6 2.8 %collective-permute-done.23 = bf16[256,384]{1,0:T(8,128)(2,1)S(1)} collective-permute-done((bf16[256,384]{1,0:T(8,128)(2,1)S(1)}, bf16[256,384]{1,0:T(8,128)(2,1)S(1)}, u32[]{:S(2)}, u32[]{:S(2)}) %collective-permute-start.23) | collective-permute-done | bytes 196640 | tf_op jit(solution)/shard_map/while/body/eval_jaxpr/ppermute | solution.py:194
  74.5 3.9 %collective-permute-done.19 = bf16[256,384]{1,0:T(8,128)(2,1)S(1)} collective-permute-done((bf16[256,384]{1,0:T(8,128)(2,1)S(1)}, bf16[256,384]{1,0:T(8,128)(2,1)S(1)}, u32[]{:S(2)}, u32[]{:S(2)}) %collective-permute-start.19) | collective-permute-done | bytes 196640 | tf_op jit(solution)/shard_map/while/body/eval_jaxpr/ppermute | solution.py:194
  78.6 4.3 %collective-permute-done.24 = bf16[256,384]{1,0:T(8,128)(2,1)S(1)} collective-permute-done((bf16[256,384]{1,0:T(8,128)(2,1)S(1)}, bf16[256,384]{1,0:T(8,128)(2,1)S(1)}, u32[]{:S(2)}, u32[]{:S(2)}) %collective-permute-start.24) | collective-permute-done | bytes 196640 | tf_op jit(solution)/shard_map/while/body/eval_jaxpr/ppermute | solution.py:219
  82.9 6.2 %collective-permute-done.20 = bf16[256,384]{1,0:T(8,128)(2,1)S(1)} collective-permute-done((bf16[256,384]{1,0:T(8,128)(2,1)S(1)}, bf16[256,384]{1,0:T(8,128)(2,1)S(1)}, u32[]{:S(2)}, u32[]{:S(2)}) %collective-permute-start.20) | collective-permute-done | bytes 196640 | tf_op jit(solution)/shard_map/while/body/eval_jaxpr/ppermute | solution.py:219
  89.3 3.2 %collective-permute-start.1 = (bf16[256,384]{1,0:T(8,128)(2,1)S(1)}, bf16[256,384]{1,0:T(8,128)(2,1)S(1)}, u32[]{:S(2)}, u32[]{:S(2)}) collective-permute-start(bf16[256,384]{1,0:T(8,128)(2,1)S(1)} %get-tuple-element.283.refs_0_), channel_id=1, source_target_pairs={{0,7},{1,0},{2,1},{3,2},{4,3},{5,4},{6,5},{7,6},{8,15},{9,8},{10,9... | collective-permute-start | bytes 589832 | tf_op jit(solution)/shard_map/while/body/eval_jaxpr/ppermute | solution.py:194
  92.9 1.5 constant_dynamic-slice_fusion.2
  94.4 1.8 %collective-permute-done.refs_2_ = bf16[256,384]{1,0:T(8,128)(2,1)S(1)} collective-permute-done((bf16[256,384]{1,0:T(8,128)(2,1)S(1)}, bf16[256,384]{1,0:T(8,128)(2,1)S(1)}, u32[]{:S(2)}, u32[]{:S(2)}) %collective-permute-start) | collective-permute-done | bytes 196640 | tf_op jit(solution)/shard_map/while/body/eval_jaxpr/ppermute | solution.py:194
  96.1 0.8 collective-permute-done.1.refs_3_
  97.0 3.4 %collective-permute-done.2.refs_1_ = bf16[256,384]{1,0:T(8,128)(2,1)S(1)} collective-permute-done((bf16[256,384]{1,0:T(8,128)(2,1)S(1)}, bf16[256,384]{1,0:T(8,128)(2,1)S(1)}, u32[]{:S(2)}, u32[]{:S(2)}) %collective-permute-start.2) | collective-permute-done | bytes 196640 | tf_op jit(solution)/shard_map/while/body/eval_jaxpr/ppermute | solution.py:194
  100.9 1.7 %collective-permute-start.6 = (bf16[256,384]{1,0:T(8,128)(2,1)S(1)}, bf16[256,384]{1,0:T(8,128)(2,1)S(1)}, u32[]{:S(2)}, u32[]{:S(2)}) collective-permute-start(bf16[256,384]{1,0:T(8,128)(2,1)S(1)} %collective-permute-done.2.refs_1_), channel_id=1, source_target_pairs={{0,1},{1,2},{2,3},{3,4},{4,5},{5,6},{6,7},{7,0},{8,9},{9,10},{10,1... | collective-permute-start | bytes 589832 | tf_op jit(solution)/shard_map/while/body/eval_jaxpr/ppermute | solution.py:194
  102.7 1.5 collective-permute-start.12
  104.7 3.3 %collective-permute-done.9.refs_7_ = bf16[256,384]{1,0:T(8,128)(2,1)S(1)} collective-permute-done((bf16[256,384]{1,0:T(8,128)(2,1)S(1)}, bf16[256,384]{1,0:T(8,128)(2,1)S(1)}, u32[]{:S(2)}, u32[]{:S(2)}) %collective-permute-start.9) | collective-permute-done | bytes 196640 | tf_op jit(solution)/shard_map/while/body/eval_jaxpr/ppermute | solution.py:194
  108.0 1.9 %collective-permute-start.10 = (bf16[256,384]{1,0:T(8,128)(2,1)S(1)}, bf16[256,384]{1,0:T(8,128)(2,1)S(1)}, u32[]{:S(2)}, u32[]{:S(2)}) collective-permute-start(bf16[256,384]{1,0:T(8,128)(2,1)S(1)} %collective-permute-done.9.refs_7_), channel_id=1, source_target_pairs={{0,7},{1,0},{2,1},{3,2},{4,3},{5,4},{6,5},{7,6},{8,15},{9,8},{10,9... | collective-permute-start | bytes 589832 | tf_op jit(solution)/shard_map/while/body/eval_jaxpr/ppermute | solution.py:194
  110.1 2.1 %collective-permute-done.12.refs_5_ = bf16[256,384]{1,0:T(8,128)(2,1)S(1)} collective-permute-done((bf16[256,384]{1,0:T(8,128)(2,1)S(1)}, bf16[256,384]{1,0:T(8,128)(2,1)S(1)}, u32[]{:S(2)}, u32[]{:S(2)}) %collective-permute-start.12) | collective-permute-done | bytes 196640 | tf_op jit(solution)/shard_map/while/body/eval_jaxpr/ppermute | solution.py:194
  112.2 1.9 %collective-permute-start.13 = (bf16[256,384]{1,0:T(8,128)(2,1)S(1)}, bf16[256,384]{1,0:T(8,128)(2,1)S(1)}, u32[]{:S(2)}, u32[]{:S(2)}) collective-permute-start(bf16[256,384]{1,0:T(8,128)(2,1)S(1)} %collective-permute-done.12.refs_5_), channel_id=1, source_target_pairs={{0,7},{1,0},{2,1},{3,2},{4,3},{5,4},{6,5},{7,6},{8,15},{9,8},{10,9... | collective-permute-start | bytes 589832 | tf_op jit(solution)/shard_map/while/body/eval_jaxpr/ppermute | solution.py:194
  114.2 2.1 %collective-permute-done.10.refs_11_ = bf16[256,384]{1,0:T(8,128)(2,1)S(1)} collective-permute-done((bf16[256,384]{1,0:T(8,128)(2,1)S(1)}, bf16[256,384]{1,0:T(8,128)(2,1)S(1)}, u32[]{:S(2)}, u32[]{:S(2)}) %collective-permute-start.10) | collective-permute-done | bytes 196640 | tf_op jit(solution)/shard_map/while/body/eval_jaxpr/ppermute | solution.py:194
  116.3 2.6 %collective-permute-start.11 = (bf16[256,384]{1,0:T(8,128)(2,1)S(1)}, bf16[256,384]{1,0:T(8,128)(2,1)S(1)}, u32[]{:S(2)}, u32[]{:S(2)}) collective-permute-start(bf16[256,384]{1,0:T(8,128)(2,1)S(1)} %collective-permute-done.10.refs_11_), channel_id=1, source_target_pairs={{0,7},{1,0},{2,1},{3,2},{4,3},{5,4},{6,5},{7,6},{8,15},{9,8},{10,9... | collective-permute-start | bytes 589832 | tf_op jit(solution)/shard_map/while/body/eval_jaxpr/ppermute | solution.py:194
  118.9 3.1 %collective-permute-start.14 = (bf16[256,384]{1,0:T(8,128)(2,1)S(1)}, bf16[256,384]{1,0:T(8,128)(2,1)S(1)}, u32[]{:S(2)}, u32[]{:S(2)}) collective-permute-start(bf16[256,384]{1,0:T(8,128)(2,1)S(1)} %collective-permute-done.13.refs_9_), channel_id=1, source_target_pairs={{0,15},{1,8},{2,9},{3,10},{4,11},{5,12},{6,13},{7,14},{8,7},{9,0},... | collective-permute-start | bytes 589832 | tf_op jit(solution)/shard_map/while/body/eval_jaxpr/ppermute | solution.py:200
  122.0 5.8 %qkv_partial.3 = (f32[3,272,256]{2,1,0:T(8,128)S(1)}, f32[2,256,128]{2,1,0:T(8,128)S(1)}, f32[256,128]{1,0:T(8,128)S(1)}, bf16[3,1536,256]{2,1,0:T(8,128)(2,1)S(1)}) custom-call(s32[12]{0:T(128)S(1)} %get-tuple-element.297.rows_ref, s32[4]{0:T(128)S(1)} %get-tuple-element.298.late_rows_ref.rows_ref, f32[16,1,384]{2,1,0:T(1,128)S(1)} %copy-done.2, ...), custom_call_target="tpu_custom_call" | custom-call | tf_op jit(solution)/shard_map/while/body/eval_jaxpr/qkv_partial/pallas_call | solution.py:130
  127.9 1.0 collective-permute-done.5.refs_0_
  128.9 2.6 %attention_block.1.own_ref = bf16[256,256]{1,0:T(8,128)(2,1)S(1)} custom-call(s32[4]{0:T(128)S(1)} %get-tuple-element.298.late_rows_ref.rows_ref, f32[16,1,384]{2,1,0:T(1,128)S(1)} %copy-done.2, bf16[256,384]{1,0:T(8,128)(2,1)S(1)} %collective-permute-done.5.refs_0_, bf16[256,384]{1,0:T(8,128)(2,1)S(1)} %collective-permute-done.8.refs_1_, ...), custom_call_target="tpu_custom_call" | custom-call | tf_op jit(solution)/shard_map/while/body/eval_jaxpr/attention_block/pallas_call | solution.py:155
  131.5 1.7 collective-permute-start.15
  133.2 3.3 %collective-permute-done.15.other_ref = bf16[256,256]{1,0:T(8,128)(2,1)S(1)} collective-permute-done((bf16[256,256]{1,0:T(8,128)(2,1)S(1)}, bf16[256,256]{1,0:T(8,128)(2,1)S(1)}, u32[]{:S(2)}, u32[]{:S(2)}) %collective-permute-start.15) | collective-permute-done | bytes 131104 | tf_op jit(solution)/shard_map/while/body/eval_jaxpr/ppermute | solution.py:194
  136.6 1.0 projection_block.7
  137.6 2.3 %collective-permute-start.21 = (bf16[256,384]{1,0:T(8,128)(2,1)S(1)}, bf16[256,384]{1,0:T(8,128)(2,1)S(1)}, u32[]{:S(2)}, u32[]{:S(2)}) collective-permute-start(bf16[256,384]{1,0:T(8,128)(2,1)S(1)} %get-tuple-element.269), channel_id=1, source_target_pairs={{0,7},{1,0},{2,1},{3,2},{4,3},{5,4},{6,5},{7,6},{8,15},{9,8},{10,9... | collective-permute-start | bytes 589832 | tf_op jit(solution)/shard_map/while/body/eval_jaxpr/ppermute | solution.py:194
  139.9 1.5 projection_block.6
  141.4 1.9 %collective-permute-done.21 = bf16[256,384]{1,0:T(8,128)(2,1)S(1)} collective-permute-done((bf16[256,384]{1,0:T(8,128)(2,1)S(1)}, bf16[256,384]{1,0:T(8,128)(2,1)S(1)}, u32[]{:S(2)}, u32[]{:S(2)}) %collective-permute-start.21) | collective-permute-done | bytes 196640 | tf_op jit(solution)/shard_map/while/body/eval_jaxpr/ppermute | solution.py:194
  143.4 3.7 %collective-permute-start.22 = (bf16[256,384]{1,0:T(8,128)(2,1)S(1)}, bf16[256,384]{1,0:T(8,128)(2,1)S(1)}, u32[]{:S(2)}, u32[]{:S(2)}) collective-permute-start(bf16[256,384]{1,0:T(8,128)(2,1)S(1)} %add_convert_fusion.17), channel_id=1, source_target_pairs={{0,7},{1,0},{2,1},{3,2},{4,3},{5,4},{6,5},{7,6},{8,15},{9,8},{10,9... | collective-permute-start | bytes 589832 | tf_op jit(solution)/shard_map/while/body/eval_jaxpr/ppermute | solution.py:194
  147.2 3.0 %collective-permute-done.22 = bf16[256,384]{1,0:T(8,128)(2,1)S(1)} collective-permute-done((bf16[256,384]{1,0:T(8,128)(2,1)S(1)}, bf16[256,384]{1,0:T(8,128)(2,1)S(1)}, u32[]{:S(2)}, u32[]{:S(2)}) %collective-permute-start.22) | collective-permute-done | bytes 196640 | tf_op jit(solution)/shard_map/while/body/eval_jaxpr/ppermute | solution.py:194
  150.3 3.8 %collective-permute-start.23 = (bf16[256,384]{1,0:T(8,128)(2,1)S(1)}, bf16[256,384]{1,0:T(8,128)(2,1)S(1)}, u32[]{:S(2)}, u32[]{:S(2)}) collective-permute-start(bf16[256,384]{1,0:T(8,128)(2,1)S(1)} %add_convert_fusion.18), channel_id=1, source_target_pairs={{0,7},{1,0},{2,1},{3,2},{4,3},{5,4},{6,5},{7,6},{8,15},{9,8},{10,9... | collective-permute-start | bytes 589832 | tf_op jit(solution)/shard_map/while/body/eval_jaxpr/ppermute | solution.py:194
  154.2 3.0 %collective-permute-done.23 = bf16[256,384]{1,0:T(8,128)(2,1)S(1)} collective-permute-done((bf16[256,384]{1,0:T(8,128)(2,1)S(1)}, bf16[256,384]{1,0:T(8,128)(2,1)S(1)}, u32[]{:S(2)}, u32[]{:S(2)}) %collective-permute-start.23) | collective-permute-done | bytes 196640 | tf_op jit(solution)/shard_map/while/body/eval_jaxpr/ppermute | solution.py:194
  157.4 3.6 %collective-permute-done.19 = bf16[256,384]{1,0:T(8,128)(2,1)S(1)} collective-permute-done((bf16[256,384]{1,0:T(8,128)(2,1)S(1)}, bf16[256,384]{1,0:T(8,128)(2,1)S(1)}, u32[]{:S(2)}, u32[]{:S(2)}) %collective-permute-start.19) | collective-permute-done | bytes 196640 | tf_op jit(solution)/shard_map/while/body/eval_jaxpr/ppermute | solution.py:194
  161.2 4.6 %collective-permute-done.24 = bf16[256,384]{1,0:T(8,128)(2,1)S(1)} collective-permute-done((bf16[256,384]{1,0:T(8,128)(2,1)S(1)}, bf16[256,384]{1,0:T(8,128)(2,1)S(1)}, u32[]{:S(2)}, u32[]{:S(2)}) %collective-permute-start.24) | collective-permute-done | bytes 196640 | tf_op jit(solution)/shard_map/while/body/eval_jaxpr/ppermute | solution.py:219
  165.8 5.9 %collective-permute-done.20 = bf16[256,384]{1,0:T(8,128)(2,1)S(1)} collective-permute-done((bf16[256,384]{1,0:T(8,128)(2,1)S(1)}, bf16[256,384]{1,0:T(8,128)(2,1)S(1)}, u32[]{:S(2)}, u32[]{:S(2)}) %collective-permute-start.20) | collective-permute-done | bytes 196640 | tf_op jit(solution)/shard_map/while/body/eval_jaxpr/ppermute | solution.py:219
  (80 shorter events, 6.7 us)
Async XLA Ops:
  1.2 36.0 %copy-start.2 = (f32[16,1,384]{2,1,0:T(1,128)S(1)}, f32[16,1,384]{2,1,0:T(1,128)}, u32[]{:S(2)}) copy-start(f32[16,1,384]{2,1,0:T(1,128)} %get-tuple-element.299.gain_ref) | copy-start | bytes 73732 | tf_op jit(solution)/shard_map/while
  1.2 9.1 %collective-permute-start = (bf16[256,384]{1,0:T(8,128)(2,1)S(1)}, bf16[256,384]{1,0:T(8,128)(2,1)S(1)}, u32[]{:S(2)}, u32[]{:S(2)}) collective-permute-start(bf16[256,384]{1,0:T(8,128)(2,1)S(1)} %get-tuple-element.283.refs_0_), channel_id=1, source_target_pairs={{0,1},{1,2},{2,3},{3,4},{4,5},{5,6},{6,7},{7,0},{8,9},{9,10},{10,1... | collective-permute-start | bytes 589832 | tf_op jit(solution)/shard_map/while/body/eval_jaxpr/ppermute | solution.py:194
  1.4 8.8 %collective-permute-start.1 = (bf16[256,384]{1,0:T(8,128)(2,1)S(1)}, bf16[256,384]{1,0:T(8,128)(2,1)S(1)}, u32[]{:S(2)}, u32[]{:S(2)}) collective-permute-start(bf16[256,384]{1,0:T(8,128)(2,1)S(1)} %get-tuple-element.283.refs_0_), channel_id=1, source_target_pairs={{0,7},{1,0},{2,1},{3,2},{4,3},{5,4},{6,5},{7,6},{8,15},{9,8},{10,9... | collective-permute-start | bytes 589832 | tf_op jit(solution)/shard_map/while/body/eval_jaxpr/ppermute | solution.py:194
  5.5 6.4 %collective-permute-start.2 = (bf16[256,384]{1,0:T(8,128)(2,1)S(1)}, bf16[256,384]{1,0:T(8,128)(2,1)S(1)}, u32[]{:S(2)}, u32[]{:S(2)}) collective-permute-start(bf16[256,384]{1,0:T(8,128)(2,1)S(1)} %get-tuple-element.283.refs_0_), channel_id=1, source_target_pairs={{0,8},{8,0},{1,9},{9,1},{2,10},{10,2},{3,11},{11,3},{4,12},{12,4},... | collective-permute-start | bytes 589832 | tf_op jit(solution)/shard_map/while/body/eval_jaxpr/ppermute | solution.py:194
  11.8 42.0 %collective-permute-start.16 = (bf16[256,3072]{1,0:T(8,128)(2,1)S(1)}, bf16[256,3072]{1,0:T(8,128)(2,1)S(1)}, u32[]{:S(2)}, u32[]{:S(2)}) collective-permute-start(bf16[256,3072]{1,0:T(8,128)(2,1)S(1)} %constant_dynamic-slice_fusion.2), channel_id=1, source_target_pairs={{0,8},{8,0},{1,9},{9,1},{2,10},{10,2},{3,11},{11,3},{4,12},{12,4},... | collective-permute-start | bytes 4718600 | tf_op jit(solution)/shard_map/while/body/eval_jaxpr/ppermute | solution.py:194
  13.4 7.8 %collective-permute-start.9 = (bf16[256,384]{1,0:T(8,128)(2,1)S(1)}, bf16[256,384]{1,0:T(8,128)(2,1)S(1)}, u32[]{:S(2)}, u32[]{:S(2)}) collective-permute-start(bf16[256,384]{1,0:T(8,128)(2,1)S(1)} %collective-permute-done.2.refs_1_), channel_id=1, source_target_pairs={{0,7},{1,0},{2,1},{3,2},{4,3},{5,4},{6,5},{7,6},{8,15},{9,8},{10,9... | collective-permute-start | bytes 589832 | tf_op jit(solution)/shard_map/while/body/eval_jaxpr/ppermute | solution.py:194
  15.1 9.0 %collective-permute-start.6 = (bf16[256,384]{1,0:T(8,128)(2,1)S(1)}, bf16[256,384]{1,0:T(8,128)(2,1)S(1)}, u32[]{:S(2)}, u32[]{:S(2)}) collective-permute-start(bf16[256,384]{1,0:T(8,128)(2,1)S(1)} %collective-permute-done.2.refs_1_), channel_id=1, source_target_pairs={{0,1},{1,2},{2,3},{3,4},{4,5},{5,6},{6,7},{7,0},{8,9},{9,10},{10,1... | collective-permute-start | bytes 589832 | tf_op jit(solution)/shard_map/while/body/eval_jaxpr/ppermute | solution.py:194
  15.4 10.0 %collective-permute-start.12 = (bf16[256,384]{1,0:T(8,128)(2,1)S(1)}, bf16[256,384]{1,0:T(8,128)(2,1)S(1)}, u32[]{:S(2)}, u32[]{:S(2)}) collective-permute-start(bf16[256,384]{1,0:T(8,128)(2,1)S(1)} %collective-permute-done.1.refs_3_), channel_id=1, source_target_pairs={{0,7},{1,0},{2,1},{3,2},{4,3},{5,4},{6,5},{7,6},{8,15},{9,8},{10,9... | collective-permute-start | bytes 589832 | tf_op jit(solution)/shard_map/while/body/eval_jaxpr/ppermute | solution.py:194
  18.3 10.0 %collective-permute-start.3 = (bf16[256,384]{1,0:T(8,128)(2,1)S(1)}, bf16[256,384]{1,0:T(8,128)(2,1)S(1)}, u32[]{:S(2)}, u32[]{:S(2)}) collective-permute-start(bf16[256,384]{1,0:T(8,128)(2,1)S(1)} %collective-permute-done.refs_2_), channel_id=1, source_target_pairs={{0,1},{1,2},{2,3},{3,4},{4,5},{5,6},{6,7},{7,0},{8,9},{9,10},{10,1... | collective-permute-start | bytes 589832 | tf_op jit(solution)/shard_map/while/body/eval_jaxpr/ppermute | solution.py:194
  21.2 8.4 %collective-permute-start.10 = (bf16[256,384]{1,0:T(8,128)(2,1)S(1)}, bf16[256,384]{1,0:T(8,128)(2,1)S(1)}, u32[]{:S(2)}, u32[]{:S(2)}) collective-permute-start(bf16[256,384]{1,0:T(8,128)(2,1)S(1)} %collective-permute-done.9.refs_7_), channel_id=1, source_target_pairs={{0,7},{1,0},{2,1},{3,2},{4,3},{5,4},{6,5},{7,6},{8,15},{9,8},{10,9... | collective-permute-start | bytes 589832 | tf_op jit(solution)/shard_map/while/body/eval_jaxpr/ppermute | solution.py:194
  24.0 8.8 %collective-permute-start.7 = (bf16[256,384]{1,0:T(8,128)(2,1)S(1)}, bf16[256,384]{1,0:T(8,128)(2,1)S(1)}, u32[]{:S(2)}, u32[]{:S(2)}) collective-permute-start(bf16[256,384]{1,0:T(8,128)(2,1)S(1)} %collective-permute-done.6.refs_6_), channel_id=1, source_target_pairs={{0,1},{1,2},{2,3},{3,4},{4,5},{5,6},{6,7},{7,0},{8,9},{9,10},{10,1... | collective-permute-start | bytes 589832 | tf_op jit(solution)/shard_map/while/body/eval_jaxpr/ppermute | solution.py:194
  25.4 8.4 %collective-permute-start.13 = (bf16[256,384]{1,0:T(8,128)(2,1)S(1)}, bf16[256,384]{1,0:T(8,128)(2,1)S(1)}, u32[]{:S(2)}, u32[]{:S(2)}) collective-permute-start(bf16[256,384]{1,0:T(8,128)(2,1)S(1)} %collective-permute-done.12.refs_5_), channel_id=1, source_target_pairs={{0,7},{1,0},{2,1},{3,2},{4,3},{5,4},{6,5},{7,6},{8,15},{9,8},{10,9... | collective-permute-start | bytes 589832 | tf_op jit(solution)/shard_map/while/body/eval_jaxpr/ppermute | solution.py:194
  28.3 9.0 %collective-permute-start.4 = (bf16[256,384]{1,0:T(8,128)(2,1)S(1)}, bf16[256,384]{1,0:T(8,128)(2,1)S(1)}, u32[]{:S(2)}, u32[]{:S(2)}) collective-permute-start(bf16[256,384]{1,0:T(8,128)(2,1)S(1)} %collective-permute-done.3.refs_4_), channel_id=1, source_target_pairs={{0,1},{1,2},{2,3},{3,4},{4,5},{5,6},{6,7},{7,0},{8,9},{9,10},{10,1... | collective-permute-start | bytes 589832 | tf_op jit(solution)/shard_map/while/body/eval_jaxpr/ppermute | solution.py:194
  29.7 13.4 %collective-permute-start.11 = (bf16[256,384]{1,0:T(8,128)(2,1)S(1)}, bf16[256,384]{1,0:T(8,128)(2,1)S(1)}, u32[]{:S(2)}, u32[]{:S(2)}) collective-permute-start(bf16[256,384]{1,0:T(8,128)(2,1)S(1)} %collective-permute-done.10.refs_11_), channel_id=1, source_target_pairs={{0,7},{1,0},{2,1},{3,2},{4,3},{5,4},{6,5},{7,6},{8,15},{9,8},{10,9... | collective-permute-start | bytes 589832 | tf_op jit(solution)/shard_map/while/body/eval_jaxpr/ppermute | solution.py:194
  32.9 10.2 %collective-permute-start.8 = (bf16[256,384]{1,0:T(8,128)(2,1)S(1)}, bf16[256,384]{1,0:T(8,128)(2,1)S(1)}, u32[]{:S(2)}, u32[]{:S(2)}) collective-permute-start(bf16[256,384]{1,0:T(8,128)(2,1)S(1)} %collective-permute-done.7.refs_10_), channel_id=1, source_target_pairs={{0,1},{1,2},{2,3},{3,4},{4,5},{5,6},{6,7},{7,0},{8,9},{9,10},{10,1... | collective-permute-start | bytes 589832 | tf_op jit(solution)/shard_map/while/body/eval_jaxpr/ppermute | solution.py:194
  33.9 9.2 %collective-permute-start.14 = (bf16[256,384]{1,0:T(8,128)(2,1)S(1)}, bf16[256,384]{1,0:T(8,128)(2,1)S(1)}, u32[]{:S(2)}, u32[]{:S(2)}) collective-permute-start(bf16[256,384]{1,0:T(8,128)(2,1)S(1)} %collective-permute-done.13.refs_9_), channel_id=1, source_target_pairs={{0,15},{1,8},{2,9},{3,10},{4,11},{5,12},{6,13},{7,14},{8,7},{9,0},... | collective-permute-start | bytes 589832 | tf_op jit(solution)/shard_map/while/body/eval_jaxpr/ppermute | solution.py:200
  37.2 6.9 %collective-permute-start.5 = (bf16[256,384]{1,0:T(8,128)(2,1)S(1)}, bf16[256,384]{1,0:T(8,128)(2,1)S(1)}, u32[]{:S(2)}, u32[]{:S(2)}) collective-permute-start(bf16[256,384]{1,0:T(8,128)(2,1)S(1)} %collective-permute-done.4.refs_8_), channel_id=1, source_target_pairs={{0,1},{1,2},{2,3},{3,4},{4,5},{5,6},{6,7},{7,0},{8,9},{9,10},{10,1... | collective-permute-start | bytes 589832 | tf_op jit(solution)/shard_map/while/body/eval_jaxpr/ppermute | solution.py:194
  37.2 6.9 %copy-start.3 = (f32[1,2,128]{2,1,0:T(2,128)S(1)}, f32[1,2,128]{2,1,0:T(2,128)}, u32[]{:S(2)}) copy-start(f32[1,2,128]{2,1,0:T(2,128)} %get-tuple-element.301) | copy-start | bytes 3076 | tf_op jit(solution)/shard_map/while
  43.1 10.7 %copy-start = (bf16[256,6144]{1,0:T(8,128)(2,1)S(1)}, bf16[256,6144]{1,0:T(8,128)(2,1)}, u32[]{:S(2)}) copy-start(bf16[256,6144]{1,0:T(8,128)(2,1)} %get-tuple-element.260.w_own_ref) | copy-start | bytes 9437188 | tf_op jit(solution)/shard_map/while
  46.7 7.0 %collective-permute-start.15 = (bf16[256,256]{1,0:T(8,128)(2,1)S(1)}, bf16[256,256]{1,0:T(8,128)(2,1)S(1)}, u32[]{:S(2)}, u32[]{:S(2)}) collective-permute-start(bf16[256,256]{1,0:T(8,128)(2,1)S(1)} %attention_block.1.own_ref), channel_id=1, source_target_pairs={{0,8},{8,0},{1,9},{9,1},{2,10},{10,2},{3,11},{11,3},{4,12},{12,4},... | collective-permute-start | bytes 393224 | tf_op jit(solution)/shard_map/while/body/eval_jaxpr/ppermute | solution.py:194
  54.8 6.4 %collective-permute-start.21 = (bf16[256,384]{1,0:T(8,128)(2,1)S(1)}, bf16[256,384]{1,0:T(8,128)(2,1)S(1)}, u32[]{:S(2)}, u32[]{:S(2)}) collective-permute-start(bf16[256,384]{1,0:T(8,128)(2,1)S(1)} %get-tuple-element.269), channel_id=1, source_target_pairs={{0,7},{1,0},{2,1},{3,2},{4,3},{5,4},{6,5},{7,6},{8,15},{9,8},{10,9... | collective-permute-start | bytes 589832 | tf_op jit(solution)/shard_map/while/body/eval_jaxpr/ppermute | solution.py:194
  56.7 7.0 %collective-permute-start.17 = (bf16[256,384]{1,0:T(8,128)(2,1)S(1)}, bf16[256,384]{1,0:T(8,128)(2,1)S(1)}, u32[]{:S(2)}, u32[]{:S(2)}) collective-permute-start(bf16[256,384]{1,0:T(8,128)(2,1)S(1)} %get-tuple-element.265), channel_id=1, source_target_pairs={{0,1},{1,2},{2,3},{3,4},{4,5},{5,6},{6,7},{7,0},{8,9},{9,10},{10,1... | collective-permute-start | bytes 589832 | tf_op jit(solution)/shard_map/while/body/eval_jaxpr/ppermute | solution.py:194
  61.2 7.3 %collective-permute-start.22 = (bf16[256,384]{1,0:T(8,128)(2,1)S(1)}, bf16[256,384]{1,0:T(8,128)(2,1)S(1)}, u32[]{:S(2)}, u32[]{:S(2)}) collective-permute-start(bf16[256,384]{1,0:T(8,128)(2,1)S(1)} %add_convert_fusion.17), channel_id=1, source_target_pairs={{0,7},{1,0},{2,1},{3,2},{4,3},{5,4},{6,5},{7,6},{8,15},{9,8},{10,9... | collective-permute-start | bytes 589832 | tf_op jit(solution)/shard_map/while/body/eval_jaxpr/ppermute | solution.py:194
  63.7 7.7 %collective-permute-start.18 = (bf16[256,384]{1,0:T(8,128)(2,1)S(1)}, bf16[256,384]{1,0:T(8,128)(2,1)S(1)}, u32[]{:S(2)}, u32[]{:S(2)}) collective-permute-start(bf16[256,384]{1,0:T(8,128)(2,1)S(1)} %add_convert_fusion.14), channel_id=1, source_target_pairs={{0,1},{1,2},{2,3},{3,4},{4,5},{5,6},{6,7},{7,0},{8,9},{9,10},{10,1... | collective-permute-start | bytes 589832 | tf_op jit(solution)/shard_map/while/body/eval_jaxpr/ppermute | solution.py:194
  68.6 5.7 %collective-permute-start.23 = (bf16[256,384]{1,0:T(8,128)(2,1)S(1)}, bf16[256,384]{1,0:T(8,128)(2,1)S(1)}, u32[]{:S(2)}, u32[]{:S(2)}) collective-permute-start(bf16[256,384]{1,0:T(8,128)(2,1)S(1)} %add_convert_fusion.18), channel_id=1, source_target_pairs={{0,7},{1,0},{2,1},{3,2},{4,3},{5,4},{6,5},{7,6},{8,15},{9,8},{10,9... | collective-permute-start | bytes 589832 | tf_op jit(solution)/shard_map/while/body/eval_jaxpr/ppermute | solution.py:194
  71.5 7.0 %collective-permute-start.19 = (bf16[256,384]{1,0:T(8,128)(2,1)S(1)}, bf16[256,384]{1,0:T(8,128)(2,1)S(1)}, u32[]{:S(2)}, u32[]{:S(2)}) collective-permute-start(bf16[256,384]{1,0:T(8,128)(2,1)S(1)} %add_convert_fusion.15), channel_id=1, source_target_pairs={{0,1},{1,2},{2,3},{3,4},{4,5},{5,6},{6,7},{7,0},{8,9},{9,10},{10,1... | collective-permute-start | bytes 589832 | tf_op jit(solution)/shard_map/while/body/eval_jaxpr/ppermute | solution.py:194
  74.4 8.5 %collective-permute-start.24 = (bf16[256,384]{1,0:T(8,128)(2,1)S(1)}, bf16[256,384]{1,0:T(8,128)(2,1)S(1)}, u32[]{:S(2)}, u32[]{:S(2)}) collective-permute-start(bf16[256,384]{1,0:T(8,128)(2,1)S(1)} %add_convert_fusion.19), channel_id=1, source_target_pairs={{0,16},{1,17},{2,18},{3,19},{4,20},{5,21},{6,22},{7,23},{8,24},{9,... | collective-permute-start | bytes 589832 | tf_op jit(solution)/shard_map/while/body/eval_jaxpr/ppermute | solution.py:219
  78.5 10.6 %collective-permute-start.20 = (bf16[256,384]{1,0:T(8,128)(2,1)S(1)}, bf16[256,384]{1,0:T(8,128)(2,1)S(1)}, u32[]{:S(2)}, u32[]{:S(2)}) collective-permute-start(bf16[256,384]{1,0:T(8,128)(2,1)S(1)} %add_convert_fusion.16), channel_id=1, source_target_pairs={{0,17},{1,18},{2,19},{3,20},{4,21},{5,22},{6,23},{7,16},{8,25},{9,... | collective-permute-start | bytes 589832 | tf_op jit(solution)/shard_map/while/body/eval_jaxpr/ppermute | solution.py:219
  89.2 32.9 %copy-start.2 = (f32[16,1,384]{2,1,0:T(1,128)S(1)}, f32[16,1,384]{2,1,0:T(1,128)}, u32[]{:S(2)}) copy-start(f32[16,1,384]{2,1,0:T(1,128)} %get-tuple-element.299.gain_ref) | copy-start | bytes 73732 | tf_op jit(solution)/shard_map/while
  89.2 7.0 %collective-permute-start = (bf16[256,384]{1,0:T(8,128)(2,1)S(1)}, bf16[256,384]{1,0:T(8,128)(2,1)S(1)}, u32[]{:S(2)}, u32[]{:S(2)}) collective-permute-start(bf16[256,384]{1,0:T(8,128)(2,1)S(1)} %get-tuple-element.283.refs_0_), channel_id=1, source_target_pairs={{0,1},{1,2},{2,3},{3,4},{4,5},{5,6},{6,7},{7,0},{8,9},{9,10},{10,1... | collective-permute-start | bytes 589832 | tf_op jit(solution)/shard_map/while/body/eval_jaxpr/ppermute | solution.py:194
  89.3 7.7 %collective-permute-start.1 = (bf16[256,384]{1,0:T(8,128)(2,1)S(1)}, bf16[256,384]{1,0:T(8,128)(2,1)S(1)}, u32[]{:S(2)}, u32[]{:S(2)}) collective-permute-start(bf16[256,384]{1,0:T(8,128)(2,1)S(1)} %get-tuple-element.283.refs_0_), channel_id=1, source_target_pairs={{0,7},{1,0},{2,1},{3,2},{4,3},{5,4},{6,5},{7,6},{8,15},{9,8},{10,9... | collective-permute-start | bytes 589832 | tf_op jit(solution)/shard_map/while/body/eval_jaxpr/ppermute | solution.py:194
  92.5 7.8 %collective-permute-start.2 = (bf16[256,384]{1,0:T(8,128)(2,1)S(1)}, bf16[256,384]{1,0:T(8,128)(2,1)S(1)}, u32[]{:S(2)}, u32[]{:S(2)}) collective-permute-start(bf16[256,384]{1,0:T(8,128)(2,1)S(1)} %get-tuple-element.283.refs_0_), channel_id=1, source_target_pairs={{0,8},{8,0},{1,9},{9,1},{2,10},{10,2},{3,11},{11,3},{4,12},{12,4},... | collective-permute-start | bytes 589832 | tf_op jit(solution)/shard_map/while/body/eval_jaxpr/ppermute | solution.py:194
  100.3 36.2 %collective-permute-start.16 = (bf16[256,3072]{1,0:T(8,128)(2,1)S(1)}, bf16[256,3072]{1,0:T(8,128)(2,1)S(1)}, u32[]{:S(2)}, u32[]{:S(2)}) collective-permute-start(bf16[256,3072]{1,0:T(8,128)(2,1)S(1)} %constant_dynamic-slice_fusion.2), channel_id=1, source_target_pairs={{0,8},{8,0},{1,9},{9,1},{2,10},{10,2},{3,11},{11,3},{4,12},{12,4},... | collective-permute-start | bytes 4718600 | tf_op jit(solution)/shard_map/while/body/eval_jaxpr/ppermute | solution.py:194
  100.6 7.3 %collective-permute-start.9 = (bf16[256,384]{1,0:T(8,128)(2,1)S(1)}, bf16[256,384]{1,0:T(8,128)(2,1)S(1)}, u32[]{:S(2)}, u32[]{:S(2)}) collective-permute-start(bf16[256,384]{1,0:T(8,128)(2,1)S(1)} %collective-permute-done.2.refs_1_), channel_id=1, source_target_pairs={{0,7},{1,0},{2,1},{3,2},{4,3},{5,4},{6,5},{7,6},{8,15},{9,8},{10,9... | collective-permute-start | bytes 589832 | tf_op jit(solution)/shard_map/while/body/eval_jaxpr/ppermute | solution.py:194
  100.9 9.0 %collective-permute-start.6 = (bf16[256,384]{1,0:T(8,128)(2,1)S(1)}, bf16[256,384]{1,0:T(8,128)(2,1)S(1)}, u32[]{:S(2)}, u32[]{:S(2)}) collective-permute-start(bf16[256,384]{1,0:T(8,128)(2,1)S(1)} %collective-permute-done.2.refs_1_), channel_id=1, source_target_pairs={{0,1},{1,2},{2,3},{3,4},{4,5},{5,6},{6,7},{7,0},{8,9},{9,10},{10,1... | collective-permute-start | bytes 589832 | tf_op jit(solution)/shard_map/while/body/eval_jaxpr/ppermute | solution.py:194
  102.7 9.5 %collective-permute-start.12 = (bf16[256,384]{1,0:T(8,128)(2,1)S(1)}, bf16[256,384]{1,0:T(8,128)(2,1)S(1)}, u32[]{:S(2)}, u32[]{:S(2)}) collective-permute-start(bf16[256,384]{1,0:T(8,128)(2,1)S(1)} %collective-permute-done.1.refs_3_), channel_id=1, source_target_pairs={{0,7},{1,0},{2,1},{3,2},{4,3},{5,4},{6,5},{7,6},{8,15},{9,8},{10,9... | collective-permute-start | bytes 589832 | tf_op jit(solution)/shard_map/while/body/eval_jaxpr/ppermute | solution.py:194
  104.2 9.9 %collective-permute-start.3 = (bf16[256,384]{1,0:T(8,128)(2,1)S(1)}, bf16[256,384]{1,0:T(8,128)(2,1)S(1)}, u32[]{:S(2)}, u32[]{:S(2)}) collective-permute-start(bf16[256,384]{1,0:T(8,128)(2,1)S(1)} %collective-permute-done.refs_2_), channel_id=1, source_target_pairs={{0,1},{1,2},{2,3},{3,4},{4,5},{5,6},{6,7},{7,0},{8,9},{9,10},{10,1... | collective-permute-start | bytes 589832 | tf_op jit(solution)/shard_map/while/body/eval_jaxpr/ppermute | solution.py:194
  108.0 8.4 %collective-permute-start.10 = (bf16[256,384]{1,0:T(8,128)(2,1)S(1)}, bf16[256,384]{1,0:T(8,128)(2,1)S(1)}, u32[]{:S(2)}, u32[]{:S(2)}) collective-permute-start(bf16[256,384]{1,0:T(8,128)(2,1)S(1)} %collective-permute-done.9.refs_7_), channel_id=1, source_target_pairs={{0,7},{1,0},{2,1},{3,2},{4,3},{5,4},{6,5},{7,6},{8,15},{9,8},{10,9... | collective-permute-start | bytes 589832 | tf_op jit(solution)/shard_map/while/body/eval_jaxpr/ppermute | solution.py:194
  109.9 9.0 %collective-permute-start.7 = (bf16[256,384]{1,0:T(8,128)(2,1)S(1)}, bf16[256,384]{1,0:T(8,128)(2,1)S(1)}, u32[]{:S(2)}, u32[]{:S(2)}) collective-permute-start(bf16[256,384]{1,0:T(8,128)(2,1)S(1)} %collective-permute-done.6.refs_6_), channel_id=1, source_target_pairs={{0,1},{1,2},{2,3},{3,4},{4,5},{5,6},{6,7},{7,0},{8,9},{9,10},{10,1... | collective-permute-start | bytes 589832 | tf_op jit(solution)/shard_map/while/body/eval_jaxpr/ppermute | solution.py:194
  112.2 6.7 %collective-permute-start.13 = (bf16[256,384]{1,0:T(8,128)(2,1)S(1)}, bf16[256,384]{1,0:T(8,128)(2,1)S(1)}, u32[]{:S(2)}, u32[]{:S(2)}) collective-permute-start(bf16[256,384]{1,0:T(8,128)(2,1)S(1)} %collective-permute-done.12.refs_5_), channel_id=1, source_target_pairs={{0,7},{1,0},{2,1},{3,2},{4,3},{5,4},{6,5},{7,6},{8,15},{9,8},{10,9... | collective-permute-start | bytes 589832 | tf_op jit(solution)/shard_map/while/body/eval_jaxpr/ppermute | solution.py:194
  114.1 7.9 %collective-permute-start.4 = (bf16[256,384]{1,0:T(8,128)(2,1)S(1)}, bf16[256,384]{1,0:T(8,128)(2,1)S(1)}, u32[]{:S(2)}, u32[]{:S(2)}) collective-permute-start(bf16[256,384]{1,0:T(8,128)(2,1)S(1)} %collective-permute-done.3.refs_4_), channel_id=1, source_target_pairs={{0,1},{1,2},{2,3},{3,4},{4,5},{5,6},{6,7},{7,0},{8,9},{9,10},{10,1... | collective-permute-start | bytes 589832 | tf_op jit(solution)/shard_map/while/body/eval_jaxpr/ppermute | solution.py:194
  116.3 11.5 %collective-permute-start.11 = (bf16[256,384]{1,0:T(8,128)(2,1)S(1)}, bf16[256,384]{1,0:T(8,128)(2,1)S(1)}, u32[]{:S(2)}, u32[]{:S(2)}) collective-permute-start(bf16[256,384]{1,0:T(8,128)(2,1)S(1)} %collective-permute-done.10.refs_11_), channel_id=1, source_target_pairs={{0,7},{1,0},{2,1},{3,2},{4,3},{5,4},{6,5},{7,6},{8,15},{9,8},{10,9... | collective-permute-start | bytes 589832 | tf_op jit(solution)/shard_map/while/body/eval_jaxpr/ppermute | solution.py:194
  118.9 8.9 %collective-permute-start.8 = (bf16[256,384]{1,0:T(8,128)(2,1)S(1)}, bf16[256,384]{1,0:T(8,128)(2,1)S(1)}, u32[]{:S(2)}, u32[]{:S(2)}) collective-permute-start(bf16[256,384]{1,0:T(8,128)(2,1)S(1)} %collective-permute-done.7.refs_10_), channel_id=1, source_target_pairs={{0,1},{1,2},{2,3},{3,4},{4,5},{5,6},{6,7},{7,0},{8,9},{9,10},{10,1... | collective-permute-start | bytes 589832 | tf_op jit(solution)/shard_map/while/body/eval_jaxpr/ppermute | solution.py:194
  118.9 8.9 %collective-permute-start.14 = (bf16[256,384]{1,0:T(8,128)(2,1)S(1)}, bf16[256,384]{1,0:T(8,128)(2,1)S(1)}, u32[]{:S(2)}, u32[]{:S(2)}) collective-permute-start(bf16[256,384]{1,0:T(8,128)(2,1)S(1)} %collective-permute-done.13.refs_9_), channel_id=1, source_target_pairs={{0,15},{1,8},{2,9},{3,10},{4,11},{5,12},{6,13},{7,14},{8,7},{9,0},... | collective-permute-start | bytes 589832 | tf_op jit(solution)/shard_map/while/body/eval_jaxpr/ppermute | solution.py:200
  122.0 6.9 %collective-permute-start.5 = (bf16[256,384]{1,0:T(8,128)(2,1)S(1)}, bf16[256,384]{1,0:T(8,128)(2,1)S(1)}, u32[]{:S(2)}, u32[]{:S(2)}) collective-permute-start(bf16[256,384]{1,0:T(8,128)(2,1)S(1)} %collective-permute-done.4.refs_8_), channel_id=1, source_target_pairs={{0,1},{1,2},{2,3},{3,4},{4,5},{5,6},{6,7},{7,0},{8,9},{9,10},{10,1... | collective-permute-start | bytes 589832 | tf_op jit(solution)/shard_map/while/body/eval_jaxpr/ppermute | solution.py:194
  122.0 6.9 %copy-start.3 = (f32[1,2,128]{2,1,0:T(2,128)S(1)}, f32[1,2,128]{2,1,0:T(2,128)}, u32[]{:S(2)}) copy-start(f32[1,2,128]{2,1,0:T(2,128)} %get-tuple-element.301) | copy-start | bytes 3076 | tf_op jit(solution)/shard_map/while
  127.8 8.7 %copy-start = (bf16[256,6144]{1,0:T(8,128)(2,1)S(1)}, bf16[256,6144]{1,0:T(8,128)(2,1)}, u32[]{:S(2)}) copy-start(bf16[256,6144]{1,0:T(8,128)(2,1)} %get-tuple-element.260.w_own_ref) | copy-start | bytes 9437188 | tf_op jit(solution)/shard_map/while
  131.5 5.1 %collective-permute-start.15 = (bf16[256,256]{1,0:T(8,128)(2,1)S(1)}, bf16[256,256]{1,0:T(8,128)(2,1)S(1)}, u32[]{:S(2)}, u32[]{:S(2)}) collective-permute-start(bf16[256,256]{1,0:T(8,128)(2,1)S(1)} %attention_block.1.own_ref), channel_id=1, source_target_pairs={{0,8},{8,0},{1,9},{9,1},{2,10},{10,2},{3,11},{11,3},{4,12},{12,4},... | collective-permute-start | bytes 393224 | tf_op jit(solution)/shard_map/while/body/eval_jaxpr/ppermute | solution.py:194
  137.6 5.7 %collective-permute-start.21 = (bf16[256,384]{1,0:T(8,128)(2,1)S(1)}, bf16[256,384]{1,0:T(8,128)(2,1)S(1)}, u32[]{:S(2)}, u32[]{:S(2)}) collective-permute-start(bf16[256,384]{1,0:T(8,128)(2,1)S(1)} %get-tuple-element.269), channel_id=1, source_target_pairs={{0,7},{1,0},{2,1},{3,2},{4,3},{5,4},{6,5},{7,6},{8,15},{9,8},{10,9... | collective-permute-start | bytes 589832 | tf_op jit(solution)/shard_map/while/body/eval_jaxpr/ppermute | solution.py:194
  139.8 7.2 %collective-permute-start.17 = (bf16[256,384]{1,0:T(8,128)(2,1)S(1)}, bf16[256,384]{1,0:T(8,128)(2,1)S(1)}, u32[]{:S(2)}, u32[]{:S(2)}) collective-permute-start(bf16[256,384]{1,0:T(8,128)(2,1)S(1)} %get-tuple-element.265), channel_id=1, source_target_pairs={{0,1},{1,2},{2,3},{3,4},{4,5},{5,6},{6,7},{7,0},{8,9},{9,10},{10,1... | collective-permute-start | bytes 589832 | tf_op jit(solution)/shard_map/while/body/eval_jaxpr/ppermute | solution.py:194
  143.4 6.9 %collective-permute-start.22 = (bf16[256,384]{1,0:T(8,128)(2,1)S(1)}, bf16[256,384]{1,0:T(8,128)(2,1)S(1)}, u32[]{:S(2)}, u32[]{:S(2)}) collective-permute-start(bf16[256,384]{1,0:T(8,128)(2,1)S(1)} %add_convert_fusion.17), channel_id=1, source_target_pairs={{0,7},{1,0},{2,1},{3,2},{4,3},{5,4},{6,5},{7,6},{8,15},{9,8},{10,9... | collective-permute-start | bytes 589832 | tf_op jit(solution)/shard_map/while/body/eval_jaxpr/ppermute | solution.py:194
  147.1 7.0 %collective-permute-start.18 = (bf16[256,384]{1,0:T(8,128)(2,1)S(1)}, bf16[256,384]{1,0:T(8,128)(2,1)S(1)}, u32[]{:S(2)}, u32[]{:S(2)}) collective-permute-start(bf16[256,384]{1,0:T(8,128)(2,1)S(1)} %add_convert_fusion.14), channel_id=1, source_target_pairs={{0,1},{1,2},{2,3},{3,4},{4,5},{5,6},{6,7},{7,0},{8,9},{9,10},{10,1... | collective-permute-start | bytes 589832 | tf_op jit(solution)/shard_map/while/body/eval_jaxpr/ppermute | solution.py:194
  150.3 7.0 %collective-permute-start.23 = (bf16[256,384]{1,0:T(8,128)(2,1)S(1)}, bf16[256,384]{1,0:T(8,128)(2,1)S(1)}, u32[]{:S(2)}, u32[]{:S(2)}) collective-permute-start(bf16[256,384]{1,0:T(8,128)(2,1)S(1)} %add_convert_fusion.18), channel_id=1, source_target_pairs={{0,7},{1,0},{2,1},{3,2},{4,3},{5,4},{6,5},{7,6},{8,15},{9,8},{10,9... | collective-permute-start | bytes 589832 | tf_op jit(solution)/shard_map/while/body/eval_jaxpr/ppermute | solution.py:194
  154.1 7.0 %collective-permute-start.19 = (bf16[256,384]{1,0:T(8,128)(2,1)S(1)}, bf16[256,384]{1,0:T(8,128)(2,1)S(1)}, u32[]{:S(2)}, u32[]{:S(2)}) collective-permute-start(bf16[256,384]{1,0:T(8,128)(2,1)S(1)} %add_convert_fusion.15), channel_id=1, source_target_pairs={{0,1},{1,2},{2,3},{3,4},{4,5},{5,6},{6,7},{7,0},{8,9},{9,10},{10,1... | collective-permute-start | bytes 589832 | tf_op jit(solution)/shard_map/while/body/eval_jaxpr/ppermute | solution.py:194
  157.4 8.5 %collective-permute-start.24 = (bf16[256,384]{1,0:T(8,128)(2,1)S(1)}, bf16[256,384]{1,0:T(8,128)(2,1)S(1)}, u32[]{:S(2)}, u32[]{:S(2)}) collective-permute-start(bf16[256,384]{1,0:T(8,128)(2,1)S(1)} %add_convert_fusion.19), channel_id=1, source_target_pairs={{0,16},{1,17},{2,18},{3,19},{4,20},{5,21},{6,22},{7,23},{8,24},{9,... | collective-permute-start | bytes 589832 | tf_op jit(solution)/shard_map/while/body/eval_jaxpr/ppermute | solution.py:219
  161.1 10.6 %collective-permute-start.20 = (bf16[256,384]{1,0:T(8,128)(2,1)S(1)}, bf16[256,384]{1,0:T(8,128)(2,1)S(1)}, u32[]{:S(2)}, u32[]{:S(2)}) collective-permute-start(bf16[256,384]{1,0:T(8,128)(2,1)S(1)} %add_convert_fusion.16), channel_id=1, source_target_pairs={{0,17},{1,18},{2,19},{3,20},{4,21},{5,22},{6,23},{7,16},{8,25},{9,... | collective-permute-start | bytes 589832 | tf_op jit(solution)/shard_map/while/body/eval_jaxpr/ppermute | solution.py:219
  171.8 0.7 copy-start.1

commit v7 on v5

--- a/solution.py
+++ b/solution.py
@@ -40,13 +40,15 @@
         both = jnp.where(row == 0, high, jnp.where(row == 1, gain - high, 0.0))
         scaled_ref[patches : patches + EXTRA, at * width : (at + 1) * width] = both.astype(jnp.bfloat16)
 
-    @pl.loop(0, patches // ROWS)
+    height = ROWS if first else patches
+
+    @pl.loop(0, patches // height)
     def _(block):
-        part = pl.ds(pl.multiple_of(block * ROWS, ROWS), ROWS)
+        part = pl.ds(pl.multiple_of(block * height, height), height)
         if first:
             shift = jnp.sum(x_refs[0][part, :].astype(jnp.float32), axis=-1, keepdims=True) / width
-            shift_ref[part, :] = jnp.broadcast_to(shift, (ROWS, 128))
-            total = squares = jnp.zeros((ROWS, 128), jnp.float32)
+            shift_ref[part, :] = jnp.broadcast_to(shift, (height, 128))
+            total = squares = jnp.zeros((height, 128), jnp.float32)
         else:
             shift = shift_ref[part, 0:1]
             total, squares = before_ref[0, part, :], before_ref[1, part, :]

time: 172 us -> 172 us (level)
  transfers between devices with their start and end apart: 50 -> 50, of which waited for: 33 -> 33; matrix products, arithmetic and copies ran while one was open for 2% -> 2% of each run, Pallas kernels for 12% -> 11%
where the time goes in v7:
time: 172 us
  waiting for transfers between devices  81.6 us (47%)
  starting transfers between devices  62.7 us (36%)
  Pallas kernels  21.3 us (12%)
  local copies, waits for them, and re-layouts  4.74 us (3%)
    ppermute x42, waiting for transfers between devices, shifted(): lax.ppermute(block, axis, [(i, (i + by) % peers) for i in range(peers)])  58.9 us
    ppermute x42, starting transfers between devices, shifted(): lax.ppermute(block, axis, [(i, (i + by) % peers) for i in range(peers)])  53.7 us
    ppermute x6, waiting for transfers between devices, to_next_section(): return lax.ppermute(block, SECTION + (PAIR, RING), pairs)  22.7 us
    pallas_call x2, Pallas kernels, partial(): pl.pallas_call(functools.partial(partial_block, count), out_shape=[jax.Sh...  11.6 us
    ppermute x2, starting transfers between devices, across(): return lax.ppermute(block, (PAIR, RING), pairs)  7.14 us
    pallas_call x4, Pallas kernels, projection(): pl.pallas_call(functools.partial(projection_block, places), out_shape=[ja...  5 us
    pallas_call x2, Pallas kernels, attention(): pl.pallas_call(functools.partial(final_block, count, pieces), out_shape=j...  4.73 us
  transfers between devices with their start and end apart: 50, of which 33 were waited for; matrix products, arithmetic and copies ran while one was open for 2% of the time, Pallas kernels for 11%

profile of v7, /device:TPU:0, one launch (start us, length us, event | category | flops | bytes accessed | tf_op | source)
XLA Modules:
  0.0 171.8 jit_solution(7279346524994350916)
XLA Ops:
  0.0 0.9 copy.14
  1.2 169.9 %while.12 = (s32[]{:T(128)}, bf16[256,384]{1,0:T(8,128)(2,1)S(1)}, pred[]{:T(512)}, s32[12]{0:T(128)S(1)}, s32[4]{0:T(128)S(1)}, /*index=5*/f32[16,1,384]{2,1,0:...) while((s32[]{:T(128)}, bf16[256,384]{1,0:T(8,128)(2,1)S(1)}, ...), condition=%wide.region_1.2_spmd, body=%wide.region_0.1_spmd.sunk | while | flops 3047426 | bytes 45257908 | solution.py:281
  1.4 4.0 %collective-permute-start.1 = (bf16[256,384]{1,0:T(8,128)(2,1)S(1)}, bf16[256,384]{1,0:T(8,128)(2,1)S(1)}, u32[]{:S(2)}, u32[]{:S(2)}) collective-permute-start(bf16[256,384]{1,0:T(8,128)(2,1)S(1)} %get-tuple-element.283.refs_0_), channel_id=1, source_target_pairs={{0,7},{1,0},{2,1},{3,2},{4,3},{5,4},{6,5},{7,6},{8,15},{9,8},{10,9... | collective-permute-start | bytes 589832 | tf_op jit(solution)/shard_map/while/body/eval_jaxpr/ppermute | solution.py:196
  5.5 1.6 collective-permute-start.2
  7.0 1.5 constant_dynamic-slice_fusion.2
  8.6 1.7 %collective-permute-done.refs_2_ = bf16[256,384]{1,0:T(8,128)(2,1)S(1)} collective-permute-done((bf16[256,384]{1,0:T(8,128)(2,1)S(1)}, bf16[256,384]{1,0:T(8,128)(2,1)S(1)}, u32[]{:S(2)}, u32[]{:S(2)}) %collective-permute-start) | collective-permute-done | bytes 196640 | tf_op jit(solution)/shard_map/while/body/eval_jaxpr/ppermute | solution.py:196
  10.3 1.5 collective-permute-done.2.refs_1_
  11.8 1.6 collective-permute-start.16
  13.4 1.7 collective-permute-start.9
  15.4 2.9 %collective-permute-start.12 = (bf16[256,384]{1,0:T(8,128)(2,1)S(1)}, bf16[256,384]{1,0:T(8,128)(2,1)S(1)}, u32[]{:S(2)}, u32[]{:S(2)}) collective-permute-start(bf16[256,384]{1,0:T(8,128)(2,1)S(1)} %collective-permute-done.1.refs_3_), channel_id=1, source_target_pairs={{0,7},{1,0},{2,1},{3,2},{4,3},{5,4},{6,5},{7,6},{8,15},{9,8},{10,9... | collective-permute-start | bytes 589832 | tf_op jit(solution)/shard_map/while/body/eval_jaxpr/ppermute | solution.py:196
  18.3 2.9 %collective-permute-done.9.refs_7_ = bf16[256,384]{1,0:T(8,128)(2,1)S(1)} collective-permute-done((bf16[256,384]{1,0:T(8,128)(2,1)S(1)}, bf16[256,384]{1,0:T(8,128)(2,1)S(1)}, u32[]{:S(2)}, u32[]{:S(2)}) %collective-permute-start.9) | collective-permute-done | bytes 196640 | tf_op jit(solution)/shard_map/while/body/eval_jaxpr/ppermute | solution.py:196
  21.2 2.6 %collective-permute-start.10 = (bf16[256,384]{1,0:T(8,128)(2,1)S(1)}, bf16[256,384]{1,0:T(8,128)(2,1)S(1)}, u32[]{:S(2)}, u32[]{:S(2)}) collective-permute-start(bf16[256,384]{1,0:T(8,128)(2,1)S(1)} %collective-permute-done.9.refs_7_), channel_id=1, source_target_pairs={{0,7},{1,0},{2,1},{3,2},{4,3},{5,4},{6,5},{7,6},{8,15},{9,8},{10,9... | collective-permute-start | bytes 589832 | tf_op jit(solution)/shard_map/while/body/eval_jaxpr/ppermute | solution.py:196
  24.0 1.4 collective-permute-done.12.refs_5_
  25.4 2.6 %collective-permute-start.13 = (bf16[256,384]{1,0:T(8,128)(2,1)S(1)}, bf16[256,384]{1,0:T(8,128)(2,1)S(1)}, u32[]{:S(2)}, u32[]{:S(2)}) collective-permute-start(bf16[256,384]{1,0:T(8,128)(2,1)S(1)} %collective-permute-done.12.refs_5_), channel_id=1, source_target_pairs={{0,7},{1,0},{2,1},{3,2},{4,3},{5,4},{6,5},{7,6},{8,15},{9,8},{10,9... | collective-permute-start | bytes 589832 | tf_op jit(solution)/shard_map/while/body/eval_jaxpr/ppermute | solution.py:196
  28.3 1.4 collective-permute-done.10.refs_11_
  29.7 3.2 %collective-permute-start.11 = (bf16[256,384]{1,0:T(8,128)(2,1)S(1)}, bf16[256,384]{1,0:T(8,128)(2,1)S(1)}, u32[]{:S(2)}, u32[]{:S(2)}) collective-permute-start(bf16[256,384]{1,0:T(8,128)(2,1)S(1)} %collective-permute-done.10.refs_11_), channel_id=1, source_target_pairs={{0,7},{1,0},{2,1},{3,2},{4,3},{5,4},{6,5},{7,6},{8,15},{9,8},{10,9... | collective-permute-start | bytes 589832 | tf_op jit(solution)/shard_map/while/body/eval_jaxpr/ppermute | solution.py:196
  32.9 1.0 collective-permute-done.13.refs_9_
  33.9 2.7 %collective-permute-start.14 = (bf16[256,384]{1,0:T(8,128)(2,1)S(1)}, bf16[256,384]{1,0:T(8,128)(2,1)S(1)}, u32[]{:S(2)}, u32[]{:S(2)}) collective-permute-start(bf16[256,384]{1,0:T(8,128)(2,1)S(1)} %collective-permute-done.13.refs_9_), channel_id=1, source_target_pairs={{0,15},{1,8},{2,9},{3,10},{4,11},{5,12},{6,13},{7,14},{8,7},{9,0},... | collective-permute-start | bytes 589832 | tf_op jit(solution)/shard_map/while/body/eval_jaxpr/ppermute | solution.py:202
  37.2 5.8 %qkv_partial.3 = (f32[3,272,256]{2,1,0:T(8,128)S(1)}, f32[2,256,128]{2,1,0:T(8,128)S(1)}, f32[256,128]{1,0:T(8,128)S(1)}, bf16[3,1536,256]{2,1,0:T(8,128)(2,1)S(1)}) custom-call(s32[12]{0:T(128)S(1)} %get-tuple-element.297.rows_ref, s32[4]{0:T(128)S(1)} %get-tuple-element.298.late_rows_ref.rows_ref, f32[16,1,384]{2,1,0:T(1,128)S(1)} %copy-done.2, ...), custom_call_target="tpu_custom_call" | custom-call | tf_op jit(solution)/shard_map/while/body/eval_jaxpr/qkv_partial/pallas_call | solution.py:132
  43.1 1.0 collective-permute-done.5.refs_0_
  44.1 2.4 %attention_block.1.own_ref = bf16[256,256]{1,0:T(8,128)(2,1)S(1)} custom-call(s32[4]{0:T(128)S(1)} %get-tuple-element.298.late_rows_ref.rows_ref, f32[16,1,384]{2,1,0:T(1,128)S(1)} %copy-done.2, bf16[256,384]{1,0:T(8,128)(2,1)S(1)} %collective-permute-done.5.refs_0_, bf16[256,384]{1,0:T(8,128)(2,1)S(1)} %collective-permute-done.8.refs_1_, ...), custom_call_target="tpu_custom_call" | custom-call | tf_op jit(solution)/shard_map/while/body/eval_jaxpr/attention_block/pallas_call | solution.py:157
  46.5 1.4 collective-permute-start.15
  47.9 5.9 %collective-permute-done.15.other_ref = bf16[256,256]{1,0:T(8,128)(2,1)S(1)} collective-permute-done((bf16[256,256]{1,0:T(8,128)(2,1)S(1)}, bf16[256,256]{1,0:T(8,128)(2,1)S(1)}, u32[]{:S(2)}, u32[]{:S(2)}) %collective-permute-start.15) | collective-permute-done | bytes 131104 | tf_op jit(solution)/shard_map/while/body/eval_jaxpr/ppermute | solution.py:196
  53.8 0.8 projection_block.6
  54.7 1.7 projection_block.7
  56.4 3.3 %collective-permute-start.21 = (bf16[256,384]{1,0:T(8,128)(2,1)S(1)}, bf16[256,384]{1,0:T(8,128)(2,1)S(1)}, u32[]{:S(2)}, u32[]{:S(2)}) collective-permute-start(bf16[256,384]{1,0:T(8,128)(2,1)S(1)} %get-tuple-element.268), channel_id=1, source_target_pairs={{0,7},{1,0},{2,1},{3,2},{4,3},{5,4},{6,5},{7,6},{8,15},{9,8},{10,9... | collective-permute-start | bytes 589832 | tf_op jit(solution)/shard_map/while/body/eval_jaxpr/ppermute | solution.py:196
  59.9 1.7 %collective-permute-done.17 = bf16[256,384]{1,0:T(8,128)(2,1)S(1)} collective-permute-done((bf16[256,384]{1,0:T(8,128)(2,1)S(1)}, bf16[256,384]{1,0:T(8,128)(2,1)S(1)}, u32[]{:S(2)}, u32[]{:S(2)}) %collective-permute-start.17) | collective-permute-done | bytes 196640 | tf_op jit(solution)/shard_map/while/body/eval_jaxpr/ppermute | solution.py:196
  61.7 1.1 collective-permute-done.21
  62.9 3.8 %collective-permute-start.22 = (bf16[256,384]{1,0:T(8,128)(2,1)S(1)}, bf16[256,384]{1,0:T(8,128)(2,1)S(1)}, u32[]{:S(2)}, u32[]{:S(2)}) collective-permute-start(bf16[256,384]{1,0:T(8,128)(2,1)S(1)} %add_convert_fusion.17), channel_id=1, source_target_pairs={{0,7},{1,0},{2,1},{3,2},{4,3},{5,4},{6,5},{7,6},{8,15},{9,8},{10,9... | collective-permute-start | bytes 589832 | tf_op jit(solution)/shard_map/while/body/eval_jaxpr/ppermute | solution.py:196
  66.7 2.9 %collective-permute-done.18 = bf16[256,384]{1,0:T(8,128)(2,1)S(1)} collective-permute-done((bf16[256,384]{1,0:T(8,128)(2,1)S(1)}, bf16[256,384]{1,0:T(8,128)(2,1)S(1)}, u32[]{:S(2)}, u32[]{:S(2)}) %collective-permute-start.18) | collective-permute-done | bytes 196640 | tf_op jit(solution)/shard_map/while/body/eval_jaxpr/ppermute | solution.py:196
  70.0 1.5 collective-permute-start.23
  71.4 5.3 %collective-permute-done.19 = bf16[256,384]{1,0:T(8,128)(2,1)S(1)} collective-permute-done((bf16[256,384]{1,0:T(8,128)(2,1)S(1)}, bf16[256,384]{1,0:T(8,128)(2,1)S(1)}, u32[]{:S(2)}, u32[]{:S(2)}) %collective-permute-start.19) | collective-permute-done | bytes 196640 | tf_op jit(solution)/shard_map/while/body/eval_jaxpr/ppermute | solution.py:196
  76.9 4.0 %collective-permute-done.23 = bf16[256,384]{1,0:T(8,128)(2,1)S(1)} collective-permute-done((bf16[256,384]{1,0:T(8,128)(2,1)S(1)}, bf16[256,384]{1,0:T(8,128)(2,1)S(1)}, u32[]{:S(2)}, u32[]{:S(2)}) %collective-permute-start.23) | collective-permute-done | bytes 196640 | tf_op jit(solution)/shard_map/while/body/eval_jaxpr/ppermute | solution.py:221
  80.9 6.5 %collective-permute-done.20 = bf16[256,384]{1,0:T(8,128)(2,1)S(1)} collective-permute-done((bf16[256,384]{1,0:T(8,128)(2,1)S(1)}, bf16[256,384]{1,0:T(8,128)(2,1)S(1)}, u32[]{:S(2)}, u32[]{:S(2)}) %collective-permute-start.20) | collective-permute-done | bytes 196640 | tf_op jit(solution)/shard_map/while/body/eval_jaxpr/ppermute | solution.py:221
  87.6 3.2 %collective-permute-start.1 = (bf16[256,384]{1,0:T(8,128)(2,1)S(1)}, bf16[256,384]{1,0:T(8,128)(2,1)S(1)}, u32[]{:S(2)}, u32[]{:S(2)}) collective-permute-start(bf16[256,384]{1,0:T(8,128)(2,1)S(1)} %get-tuple-element.283.refs_0_), channel_id=1, source_target_pairs={{0,7},{1,0},{2,1},{3,2},{4,3},{5,4},{6,5},{7,6},{8,15},{9,8},{10,9... | collective-permute-start | bytes 589832 | tf_op jit(solution)/shard_map/while/body/eval_jaxpr/ppermute | solution.py:196
  91.2 1.5 constant_dynamic-slice_fusion.2
  92.7 1.8 %collective-permute-done.refs_2_ = bf16[256,384]{1,0:T(8,128)(2,1)S(1)} collective-permute-done((bf16[256,384]{1,0:T(8,128)(2,1)S(1)}, bf16[256,384]{1,0:T(8,128)(2,1)S(1)}, u32[]{:S(2)}, u32[]{:S(2)}) %collective-permute-start) | collective-permute-done | bytes 196640 | tf_op jit(solution)/shard_map/while/body/eval_jaxpr/ppermute | solution.py:196
  94.5 1.6 collective-permute-done.1.refs_3_
  96.1 2.5 %collective-permute-done.2.refs_1_ = bf16[256,384]{1,0:T(8,128)(2,1)S(1)} collective-permute-done((bf16[256,384]{1,0:T(8,128)(2,1)S(1)}, bf16[256,384]{1,0:T(8,128)(2,1)S(1)}, u32[]{:S(2)}, u32[]{:S(2)}) %collective-permute-start.2) | collective-permute-done | bytes 196640 | tf_op jit(solution)/shard_map/while/body/eval_jaxpr/ppermute | solution.py:196
  99.0 1.1 collective-permute-start.9
  100.2 0.9 collective-permute-start.6
  101.1 2.4 %collective-permute-start.12 = (bf16[256,384]{1,0:T(8,128)(2,1)S(1)}, bf16[256,384]{1,0:T(8,128)(2,1)S(1)}, u32[]{:S(2)}, u32[]{:S(2)}) collective-permute-start(bf16[256,384]{1,0:T(8,128)(2,1)S(1)} %collective-permute-done.1.refs_3_), channel_id=1, source_target_pairs={{0,7},{1,0},{2,1},{3,2},{4,3},{5,4},{6,5},{7,6},{8,15},{9,8},{10,9... | collective-permute-start | bytes 589832 | tf_op jit(solution)/shard_map/while/body/eval_jaxpr/ppermute | solution.py:196
  103.4 3.4 %collective-permute-done.9.refs_7_ = bf16[256,384]{1,0:T(8,128)(2,1)S(1)} collective-permute-done((bf16[256,384]{1,0:T(8,128)(2,1)S(1)}, bf16[256,384]{1,0:T(8,128)(2,1)S(1)}, u32[]{:S(2)}, u32[]{:S(2)}) %collective-permute-start.9) | collective-permute-done | bytes 196640 | tf_op jit(solution)/shard_map/while/body/eval_jaxpr/ppermute | solution.py:196
  106.8 2.2 %collective-permute-start.10 = (bf16[256,384]{1,0:T(8,128)(2,1)S(1)}, bf16[256,384]{1,0:T(8,128)(2,1)S(1)}, u32[]{:S(2)}, u32[]{:S(2)}) collective-permute-start(bf16[256,384]{1,0:T(8,128)(2,1)S(1)} %collective-permute-done.9.refs_7_), channel_id=1, source_target_pairs={{0,7},{1,0},{2,1},{3,2},{4,3},{5,4},{6,5},{7,6},{8,15},{9,8},{10,9... | collective-permute-start | bytes 589832 | tf_op jit(solution)/shard_map/while/body/eval_jaxpr/ppermute | solution.py:196
  109.0 2.0 %collective-permute-done.12.refs_5_ = bf16[256,384]{1,0:T(8,128)(2,1)S(1)} collective-permute-done((bf16[256,384]{1,0:T(8,128)(2,1)S(1)}, bf16[256,384]{1,0:T(8,128)(2,1)S(1)}, u32[]{:S(2)}, u32[]{:S(2)}) %collective-permute-start.12) | collective-permute-done | bytes 196640 | tf_op jit(solution)/shard_map/while/body/eval_jaxpr/ppermute | solution.py:196
  111.0 2.2 %collective-permute-start.13 = (bf16[256,384]{1,0:T(8,128)(2,1)S(1)}, bf16[256,384]{1,0:T(8,128)(2,1)S(1)}, u32[]{:S(2)}, u32[]{:S(2)}) collective-permute-start(bf16[256,384]{1,0:T(8,128)(2,1)S(1)} %collective-permute-done.12.refs_5_), channel_id=1, source_target_pairs={{0,7},{1,0},{2,1},{3,2},{4,3},{5,4},{6,5},{7,6},{8,15},{9,8},{10,9... | collective-permute-start | bytes 589832 | tf_op jit(solution)/shard_map/while/body/eval_jaxpr/ppermute | solution.py:196
  113.2 1.3 collective-permute-done.10.refs_11_
  114.5 3.4 %collective-permute-start.11 = (bf16[256,384]{1,0:T(8,128)(2,1)S(1)}, bf16[256,384]{1,0:T(8,128)(2,1)S(1)}, u32[]{:S(2)}, u32[]{:S(2)}) collective-permute-start(bf16[256,384]{1,0:T(8,128)(2,1)S(1)} %collective-permute-done.10.refs_11_), channel_id=1, source_target_pairs={{0,7},{1,0},{2,1},{3,2},{4,3},{5,4},{6,5},{7,6},{8,15},{9,8},{10,9... | collective-permute-start | bytes 589832 | tf_op jit(solution)/shard_map/while/body/eval_jaxpr/ppermute | solution.py:196
  117.9 4.5 %collective-permute-start.14 = (bf16[256,384]{1,0:T(8,128)(2,1)S(1)}, bf16[256,384]{1,0:T(8,128)(2,1)S(1)}, u32[]{:S(2)}, u32[]{:S(2)}) collective-permute-start(bf16[256,384]{1,0:T(8,128)(2,1)S(1)} %collective-permute-done.13.refs_9_), channel_id=1, source_target_pairs={{0,15},{1,8},{2,9},{3,10},{4,11},{5,12},{6,13},{7,14},{8,7},{9,0},... | collective-permute-start | bytes 589832 | tf_op jit(solution)/shard_map/while/body/eval_jaxpr/ppermute | solution.py:202
  122.4 5.8 %qkv_partial.3 = (f32[3,272,256]{2,1,0:T(8,128)S(1)}, f32[2,256,128]{2,1,0:T(8,128)S(1)}, f32[256,128]{1,0:T(8,128)S(1)}, bf16[3,1536,256]{2,1,0:T(8,128)(2,1)S(1)}) custom-call(s32[12]{0:T(128)S(1)} %get-tuple-element.297.rows_ref, s32[4]{0:T(128)S(1)} %get-tuple-element.298.late_rows_ref.rows_ref, f32[16,1,384]{2,1,0:T(1,128)S(1)} %copy-done.2, ...), custom_call_target="tpu_custom_call" | custom-call | tf_op jit(solution)/shard_map/while/body/eval_jaxpr/qkv_partial/pallas_call | solution.py:132
  128.3 1.0 collective-permute-done.5.refs_0_
  129.3 2.4 %attention_block.1.own_ref = bf16[256,256]{1,0:T(8,128)(2,1)S(1)} custom-call(s32[4]{0:T(128)S(1)} %get-tuple-element.298.late_rows_ref.rows_ref, f32[16,1,384]{2,1,0:T(1,128)S(1)} %copy-done.2, bf16[256,384]{1,0:T(8,128)(2,1)S(1)} %collective-permute-done.5.refs_0_, bf16[256,384]{1,0:T(8,128)(2,1)S(1)} %collective-permute-done.8.refs_1_, ...), custom_call_target="tpu_custom_call" | custom-call | tf_op jit(solution)/shard_map/while/body/eval_jaxpr/attention_block/pallas_call | solution.py:157
  132.0 4.7 %collective-permute-done.15.other_ref = bf16[256,256]{1,0:T(8,128)(2,1)S(1)} collective-permute-done((bf16[256,256]{1,0:T(8,128)(2,1)S(1)}, bf16[256,256]{1,0:T(8,128)(2,1)S(1)}, u32[]{:S(2)}, u32[]{:S(2)}) %collective-permute-start.15) | collective-permute-done | bytes 131104 | tf_op jit(solution)/shard_map/while/body/eval_jaxpr/ppermute | solution.py:196
  136.7 0.8 projection_block.6
  137.6 1.7 projection_block.7
  139.3 3.3 %collective-permute-start.21 = (bf16[256,384]{1,0:T(8,128)(2,1)S(1)}, bf16[256,384]{1,0:T(8,128)(2,1)S(1)}, u32[]{:S(2)}, u32[]{:S(2)}) collective-permute-start(bf16[256,384]{1,0:T(8,128)(2,1)S(1)} %get-tuple-element.268), channel_id=1, source_target_pairs={{0,7},{1,0},{2,1},{3,2},{4,3},{5,4},{6,5},{7,6},{8,15},{9,8},{10,9... | collective-permute-start | bytes 589832 | tf_op jit(solution)/shard_map/while/body/eval_jaxpr/ppermute | solution.py:196
  142.8 1.7 %collective-permute-done.17 = bf16[256,384]{1,0:T(8,128)(2,1)S(1)} collective-permute-done((bf16[256,384]{1,0:T(8,128)(2,1)S(1)}, bf16[256,384]{1,0:T(8,128)(2,1)S(1)}, u32[]{:S(2)}, u32[]{:S(2)}) %collective-permute-start.17) | collective-permute-done | bytes 196640 | tf_op jit(solution)/shard_map/while/body/eval_jaxpr/ppermute | solution.py:196
  144.7 2.0 %collective-permute-done.21 = bf16[256,384]{1,0:T(8,128)(2,1)S(1)} collective-permute-done((bf16[256,384]{1,0:T(8,128)(2,1)S(1)}, bf16[256,384]{1,0:T(8,128)(2,1)S(1)}, u32[]{:S(2)}, u32[]{:S(2)}) %collective-permute-start.21) | collective-permute-done | bytes 196640 | tf_op jit(solution)/shard_map/while/body/eval_jaxpr/ppermute | solution.py:196
  146.7 3.8 %collective-permute-start.22 = (bf16[256,384]{1,0:T(8,128)(2,1)S(1)}, bf16[256,384]{1,0:T(8,128)(2,1)S(1)}, u32[]{:S(2)}, u32[]{:S(2)}) collective-permute-start(bf16[256,384]{1,0:T(8,128)(2,1)S(1)} %add_convert_fusion.17), channel_id=1, source_target_pairs={{0,7},{1,0},{2,1},{3,2},{4,3},{5,4},{6,5},{7,6},{8,15},{9,8},{10,9... | collective-permute-start | bytes 589832 | tf_op jit(solution)/shard_map/while/body/eval_jaxpr/ppermute | solution.py:196
  150.5 1.1 collective-permute-done.18
  152.1 1.5 collective-permute-done.22
  153.8 4.8 %collective-permute-done.19 = bf16[256,384]{1,0:T(8,128)(2,1)S(1)} collective-permute-done((bf16[256,384]{1,0:T(8,128)(2,1)S(1)}, bf16[256,384]{1,0:T(8,128)(2,1)S(1)}, u32[]{:S(2)}, u32[]{:S(2)}) %collective-permute-start.19) | collective-permute-done | bytes 196640 | tf_op jit(solution)/shard_map/while/body/eval_jaxpr/ppermute | solution.py:196
  158.8 4.3 %collective-permute-done.23 = bf16[256,384]{1,0:T(8,128)(2,1)S(1)} collective-permute-done((bf16[256,384]{1,0:T(8,128)(2,1)S(1)}, bf16[256,384]{1,0:T(8,128)(2,1)S(1)}, u32[]{:S(2)}, u32[]{:S(2)}) %collective-permute-start.23) | collective-permute-done | bytes 196640 | tf_op jit(solution)/shard_map/while/body/eval_jaxpr/ppermute | solution.py:221
  163.1 7.9 %collective-permute-done.20 = bf16[256,384]{1,0:T(8,128)(2,1)S(1)} collective-permute-done((bf16[256,384]{1,0:T(8,128)(2,1)S(1)}, bf16[256,384]{1,0:T(8,128)(2,1)S(1)}, u32[]{:S(2)}, u32[]{:S(2)}) %collective-permute-start.20) | collective-permute-done | bytes 196640 | tf_op jit(solution)/shard_map/while/body/eval_jaxpr/ppermute | solution.py:221
  (80 shorter events, 6.2 us)
Async XLA Ops:
  1.2 36.0 %copy-start.2 = (f32[16,1,384]{2,1,0:T(1,128)S(1)}, f32[16,1,384]{2,1,0:T(1,128)}, u32[]{:S(2)}) copy-start(f32[16,1,384]{2,1,0:T(1,128)} %get-tuple-element.299.gain_ref) | copy-start | bytes 73732 | tf_op jit(solution)/shard_map/while
  1.2 9.1 %collective-permute-start = (bf16[256,384]{1,0:T(8,128)(2,1)S(1)}, bf16[256,384]{1,0:T(8,128)(2,1)S(1)}, u32[]{:S(2)}, u32[]{:S(2)}) collective-permute-start(bf16[256,384]{1,0:T(8,128)(2,1)S(1)} %get-tuple-element.283.refs_0_), channel_id=1, source_target_pairs={{0,1},{1,2},{2,3},{3,4},{4,5},{5,6},{6,7},{7,0},{8,9},{9,10},{10,1... | collective-permute-start | bytes 589832 | tf_op jit(solution)/shard_map/while/body/eval_jaxpr/ppermute | solution.py:196
  1.4 8.8 %collective-permute-start.1 = (bf16[256,384]{1,0:T(8,128)(2,1)S(1)}, bf16[256,384]{1,0:T(8,128)(2,1)S(1)}, u32[]{:S(2)}, u32[]{:S(2)}) collective-permute-start(bf16[256,384]{1,0:T(8,128)(2,1)S(1)} %get-tuple-element.283.refs_0_), channel_id=1, source_target_pairs={{0,7},{1,0},{2,1},{3,2},{4,3},{5,4},{6,5},{7,6},{8,15},{9,8},{10,9... | collective-permute-start | bytes 589832 | tf_op jit(solution)/shard_map/while/body/eval_jaxpr/ppermute | solution.py:196
  5.5 6.4 %collective-permute-start.2 = (bf16[256,384]{1,0:T(8,128)(2,1)S(1)}, bf16[256,384]{1,0:T(8,128)(2,1)S(1)}, u32[]{:S(2)}, u32[]{:S(2)}) collective-permute-start(bf16[256,384]{1,0:T(8,128)(2,1)S(1)} %get-tuple-element.283.refs_0_), channel_id=1, source_target_pairs={{0,8},{8,0},{1,9},{9,1},{2,10},{10,2},{3,11},{11,3},{4,12},{12,4},... | collective-permute-start | bytes 589832 | tf_op jit(solution)/shard_map/while/body/eval_jaxpr/ppermute | solution.py:196
  11.8 42.0 %collective-permute-start.16 = (bf16[256,3072]{1,0:T(8,128)(2,1)S(1)}, bf16[256,3072]{1,0:T(8,128)(2,1)S(1)}, u32[]{:S(2)}, u32[]{:S(2)}) collective-permute-start(bf16[256,3072]{1,0:T(8,128)(2,1)S(1)} %constant_dynamic-slice_fusion.2), channel_id=1, source_target_pairs={{0,8},{8,0},{1,9},{9,1},{2,10},{10,2},{3,11},{11,3},{4,12},{12,4},... | collective-permute-start | bytes 4718600 | tf_op jit(solution)/shard_map/while/body/eval_jaxpr/ppermute | solution.py:196
  13.4 7.8 %collective-permute-start.9 = (bf16[256,384]{1,0:T(8,128)(2,1)S(1)}, bf16[256,384]{1,0:T(8,128)(2,1)S(1)}, u32[]{:S(2)}, u32[]{:S(2)}) collective-permute-start(bf16[256,384]{1,0:T(8,128)(2,1)S(1)} %collective-permute-done.2.refs_1_), channel_id=1, source_target_pairs={{0,7},{1,0},{2,1},{3,2},{4,3},{5,4},{6,5},{7,6},{8,15},{9,8},{10,9... | collective-permute-start | bytes 589832 | tf_op jit(solution)/shard_map/while/body/eval_jaxpr/ppermute | solution.py:196
  15.1 9.0 %collective-permute-start.6 = (bf16[256,384]{1,0:T(8,128)(2,1)S(1)}, bf16[256,384]{1,0:T(8,128)(2,1)S(1)}, u32[]{:S(2)}, u32[]{:S(2)}) collective-permute-start(bf16[256,384]{1,0:T(8,128)(2,1)S(1)} %collective-permute-done.2.refs_1_), channel_id=1, source_target_pairs={{0,1},{1,2},{2,3},{3,4},{4,5},{5,6},{6,7},{7,0},{8,9},{9,10},{10,1... | collective-permute-start | bytes 589832 | tf_op jit(solution)/shard_map/while/body/eval_jaxpr/ppermute | solution.py:196
  15.4 10.0 %collective-permute-start.12 = (bf16[256,384]{1,0:T(8,128)(2,1)S(1)}, bf16[256,384]{1,0:T(8,128)(2,1)S(1)}, u32[]{:S(2)}, u32[]{:S(2)}) collective-permute-start(bf16[256,384]{1,0:T(8,128)(2,1)S(1)} %collective-permute-done.1.refs_3_), channel_id=1, source_target_pairs={{0,7},{1,0},{2,1},{3,2},{4,3},{5,4},{6,5},{7,6},{8,15},{9,8},{10,9... | collective-permute-start | bytes 589832 | tf_op jit(solution)/shard_map/while/body/eval_jaxpr/ppermute | solution.py:196
  18.3 10.0 %collective-permute-start.3 = (bf16[256,384]{1,0:T(8,128)(2,1)S(1)}, bf16[256,384]{1,0:T(8,128)(2,1)S(1)}, u32[]{:S(2)}, u32[]{:S(2)}) collective-permute-start(bf16[256,384]{1,0:T(8,128)(2,1)S(1)} %collective-permute-done.refs_2_), channel_id=1, source_target_pairs={{0,1},{1,2},{2,3},{3,4},{4,5},{5,6},{6,7},{7,0},{8,9},{9,10},{10,1... | collective-permute-start | bytes 589832 | tf_op jit(solution)/shard_map/while/body/eval_jaxpr/ppermute | solution.py:196
  21.2 8.4 %collective-permute-start.10 = (bf16[256,384]{1,0:T(8,128)(2,1)S(1)}, bf16[256,384]{1,0:T(8,128)(2,1)S(1)}, u32[]{:S(2)}, u32[]{:S(2)}) collective-permute-start(bf16[256,384]{1,0:T(8,128)(2,1)S(1)} %collective-permute-done.9.refs_7_), channel_id=1, source_target_pairs={{0,7},{1,0},{2,1},{3,2},{4,3},{5,4},{6,5},{7,6},{8,15},{9,8},{10,9... | collective-permute-start | bytes 589832 | tf_op jit(solution)/shard_map/while/body/eval_jaxpr/ppermute | solution.py:196
  24.0 8.8 %collective-permute-start.7 = (bf16[256,384]{1,0:T(8,128)(2,1)S(1)}, bf16[256,384]{1,0:T(8,128)(2,1)S(1)}, u32[]{:S(2)}, u32[]{:S(2)}) collective-permute-start(bf16[256,384]{1,0:T(8,128)(2,1)S(1)} %collective-permute-done.6.refs_6_), channel_id=1, source_target_pairs={{0,1},{1,2},{2,3},{3,4},{4,5},{5,6},{6,7},{7,0},{8,9},{9,10},{10,1... | collective-permute-start | bytes 589832 | tf_op jit(solution)/shard_map/while/body/eval_jaxpr/ppermute | solution.py:196
  25.4 8.4 %collective-permute-start.13 = (bf16[256,384]{1,0:T(8,128)(2,1)S(1)}, bf16[256,384]{1,0:T(8,128)(2,1)S(1)}, u32[]{:S(2)}, u32[]{:S(2)}) collective-permute-start(bf16[256,384]{1,0:T(8,128)(2,1)S(1)} %collective-permute-done.12.refs_5_), channel_id=1, source_target_pairs={{0,7},{1,0},{2,1},{3,2},{4,3},{5,4},{6,5},{7,6},{8,15},{9,8},{10,9... | collective-permute-start | bytes 589832 | tf_op jit(solution)/shard_map/while/body/eval_jaxpr/ppermute | solution.py:196
  28.3 9.0 %collective-permute-start.4 = (bf16[256,384]{1,0:T(8,128)(2,1)S(1)}, bf16[256,384]{1,0:T(8,128)(2,1)S(1)}, u32[]{:S(2)}, u32[]{:S(2)}) collective-permute-start(bf16[256,384]{1,0:T(8,128)(2,1)S(1)} %collective-permute-done.3.refs_4_), channel_id=1, source_target_pairs={{0,1},{1,2},{2,3},{3,4},{4,5},{5,6},{6,7},{7,0},{8,9},{9,10},{10,1... | collective-permute-start | bytes 589832 | tf_op jit(solution)/shard_map/while/body/eval_jaxpr/ppermute | solution.py:196
  29.7 13.4 %collective-permute-start.11 = (bf16[256,384]{1,0:T(8,128)(2,1)S(1)}, bf16[256,384]{1,0:T(8,128)(2,1)S(1)}, u32[]{:S(2)}, u32[]{:S(2)}) collective-permute-start(bf16[256,384]{1,0:T(8,128)(2,1)S(1)} %collective-permute-done.10.refs_11_), channel_id=1, source_target_pairs={{0,7},{1,0},{2,1},{3,2},{4,3},{5,4},{6,5},{7,6},{8,15},{9,8},{10,9... | collective-permute-start | bytes 589832 | tf_op jit(solution)/shard_map/while/body/eval_jaxpr/ppermute | solution.py:196
  32.9 10.2 %collective-permute-start.8 = (bf16[256,384]{1,0:T(8,128)(2,1)S(1)}, bf16[256,384]{1,0:T(8,128)(2,1)S(1)}, u32[]{:S(2)}, u32[]{:S(2)}) collective-permute-start(bf16[256,384]{1,0:T(8,128)(2,1)S(1)} %collective-permute-done.7.refs_10_), channel_id=1, source_target_pairs={{0,1},{1,2},{2,3},{3,4},{4,5},{5,6},{6,7},{7,0},{8,9},{9,10},{10,1... | collective-permute-start | bytes 589832 | tf_op jit(solution)/shard_map/while/body/eval_jaxpr/ppermute | solution.py:196
  33.9 9.2 %collective-permute-start.14 = (bf16[256,384]{1,0:T(8,128)(2,1)S(1)}, bf16[256,384]{1,0:T(8,128)(2,1)S(1)}, u32[]{:S(2)}, u32[]{:S(2)}) collective-permute-start(bf16[256,384]{1,0:T(8,128)(2,1)S(1)} %collective-permute-done.13.refs_9_), channel_id=1, source_target_pairs={{0,15},{1,8},{2,9},{3,10},{4,11},{5,12},{6,13},{7,14},{8,7},{9,0},... | collective-permute-start | bytes 589832 | tf_op jit(solution)/shard_map/while/body/eval_jaxpr/ppermute | solution.py:202
  37.2 6.9 %collective-permute-start.5 = (bf16[256,384]{1,0:T(8,128)(2,1)S(1)}, bf16[256,384]{1,0:T(8,128)(2,1)S(1)}, u32[]{:S(2)}, u32[]{:S(2)}) collective-permute-start(bf16[256,384]{1,0:T(8,128)(2,1)S(1)} %collective-permute-done.4.refs_8_), channel_id=1, source_target_pairs={{0,1},{1,2},{2,3},{3,4},{4,5},{5,6},{6,7},{7,0},{8,9},{9,10},{10,1... | collective-permute-start | bytes 589832 | tf_op jit(solution)/shard_map/while/body/eval_jaxpr/ppermute | solution.py:196
  37.2 6.9 %copy-start.3 = (f32[1,2,128]{2,1,0:T(2,128)S(1)}, f32[1,2,128]{2,1,0:T(2,128)}, u32[]{:S(2)}) copy-start(f32[1,2,128]{2,1,0:T(2,128)} %get-tuple-element.301) | copy-start | bytes 3076 | tf_op jit(solution)/shard_map/while
  43.1 10.7 %copy-start = (bf16[256,6144]{1,0:T(8,128)(2,1)S(1)}, bf16[256,6144]{1,0:T(8,128)(2,1)}, u32[]{:S(2)}) copy-start(bf16[256,6144]{1,0:T(8,128)(2,1)} %get-tuple-element.260.w_own_ref) | copy-start | bytes 9437188 | tf_op jit(solution)/shard_map/while
  46.5 7.3 %collective-permute-start.15 = (bf16[256,256]{1,0:T(8,128)(2,1)S(1)}, bf16[256,256]{1,0:T(8,128)(2,1)S(1)}, u32[]{:S(2)}, u32[]{:S(2)}) collective-permute-start(bf16[256,256]{1,0:T(8,128)(2,1)S(1)} %attention_block.1.own_ref), channel_id=1, source_target_pairs={{0,8},{8,0},{1,9},{9,1},{2,10},{10,2},{3,11},{11,3},{4,12},{12,4},... | collective-permute-start | bytes 393224 | tf_op jit(solution)/shard_map/while/body/eval_jaxpr/ppermute | solution.py:196
  54.6 7.0 %collective-permute-start.17 = (bf16[256,384]{1,0:T(8,128)(2,1)S(1)}, bf16[256,384]{1,0:T(8,128)(2,1)S(1)}, u32[]{:S(2)}, u32[]{:S(2)}) collective-permute-start(bf16[256,384]{1,0:T(8,128)(2,1)S(1)} %projection_block.6), channel_id=1, source_target_pairs={{0,1},{1,2},{2,3},{3,4},{4,5},{5,6},{6,7},{7,0},{8,9},{9,10},{10,1... | collective-permute-start | bytes 589832 | tf_op jit(solution)/shard_map/while/body/eval_jaxpr/ppermute | solution.py:196
  56.4 6.5 %collective-permute-start.21 = (bf16[256,384]{1,0:T(8,128)(2,1)S(1)}, bf16[256,384]{1,0:T(8,128)(2,1)S(1)}, u32[]{:S(2)}, u32[]{:S(2)}) collective-permute-start(bf16[256,384]{1,0:T(8,128)(2,1)S(1)} %get-tuple-element.268), channel_id=1, source_target_pairs={{0,7},{1,0},{2,1},{3,2},{4,3},{5,4},{6,5},{7,6},{8,15},{9,8},{10,9... | collective-permute-start | bytes 589832 | tf_op jit(solution)/shard_map/while/body/eval_jaxpr/ppermute | solution.py:196
  59.8 17.1 %collective-permute-start.24 = (bf16[256,384]{1,0:T(8,128)(2,1)S(1)}, bf16[256,384]{1,0:T(8,128)(2,1)S(1)}, u32[]{:S(2)}, u32[]{:S(2)}) collective-permute-start(bf16[256,384]{1,0:T(8,128)(2,1)S(1)} %add_convert_fusion.19), channel_id=1, source_target_pairs={{0,16},{1,17},{2,18},{3,19},{4,20},{5,21},{6,22},{7,23},{8,24},{9,... | collective-permute-start | bytes 589832 | tf_op jit(solution)/shard_map/while/body/eval_jaxpr/ppermute | solution.py:221
  61.7 8.0 %collective-permute-start.18 = (bf16[256,384]{1,0:T(8,128)(2,1)S(1)}, bf16[256,384]{1,0:T(8,128)(2,1)S(1)}, u32[]{:S(2)}, u32[]{:S(2)}) collective-permute-start(bf16[256,384]{1,0:T(8,128)(2,1)S(1)} %add_convert_fusion.14), channel_id=1, source_target_pairs={{0,1},{1,2},{2,3},{3,4},{4,5},{5,6},{6,7},{7,0},{8,9},{9,10},{10,1... | collective-permute-start | bytes 589832 | tf_op jit(solution)/shard_map/while/body/eval_jaxpr/ppermute | solution.py:196
  62.9 7.0 %collective-permute-start.22 = (bf16[256,384]{1,0:T(8,128)(2,1)S(1)}, bf16[256,384]{1,0:T(8,128)(2,1)S(1)}, u32[]{:S(2)}, u32[]{:S(2)}) collective-permute-start(bf16[256,384]{1,0:T(8,128)(2,1)S(1)} %add_convert_fusion.17), channel_id=1, source_target_pairs={{0,7},{1,0},{2,1},{3,2},{4,3},{5,4},{6,5},{7,6},{8,15},{9,8},{10,9... | collective-permute-start | bytes 589832 | tf_op jit(solution)/shard_map/while/body/eval_jaxpr/ppermute | solution.py:196
  69.7 7.1 %collective-permute-start.19 = (bf16[256,384]{1,0:T(8,128)(2,1)S(1)}, bf16[256,384]{1,0:T(8,128)(2,1)S(1)}, u32[]{:S(2)}, u32[]{:S(2)}) collective-permute-start(bf16[256,384]{1,0:T(8,128)(2,1)S(1)} %add_convert_fusion.15), channel_id=1, source_target_pairs={{0,1},{1,2},{2,3},{3,4},{4,5},{5,6},{6,7},{7,0},{8,9},{9,10},{10,1... | collective-permute-start | bytes 589832 | tf_op jit(solution)/shard_map/while/body/eval_jaxpr/ppermute | solution.py:196
  70.0 10.9 %collective-permute-start.23 = (bf16[256,384]{1,0:T(8,128)(2,1)S(1)}, bf16[256,384]{1,0:T(8,128)(2,1)S(1)}, u32[]{:S(2)}, u32[]{:S(2)}) collective-permute-start(bf16[256,384]{1,0:T(8,128)(2,1)S(1)} %add_convert_fusion.18), channel_id=1, source_target_pairs={{0,23},{1,16},{2,17},{3,18},{4,19},{5,20},{6,21},{7,22},{8,31},{9,... | collective-permute-start | bytes 589832 | tf_op jit(solution)/shard_map/while/body/eval_jaxpr/ppermute | solution.py:221
  76.8 10.6 %collective-permute-start.20 = (bf16[256,384]{1,0:T(8,128)(2,1)S(1)}, bf16[256,384]{1,0:T(8,128)(2,1)S(1)}, u32[]{:S(2)}, u32[]{:S(2)}) collective-permute-start(bf16[256,384]{1,0:T(8,128)(2,1)S(1)} %add_convert_fusion.16), channel_id=1, source_target_pairs={{0,17},{1,18},{2,19},{3,20},{4,21},{5,22},{6,23},{7,16},{8,25},{9,... | collective-permute-start | bytes 589832 | tf_op jit(solution)/shard_map/while/body/eval_jaxpr/ppermute | solution.py:221
  87.5 34.9 %copy-start.2 = (f32[16,1,384]{2,1,0:T(1,128)S(1)}, f32[16,1,384]{2,1,0:T(1,128)}, u32[]{:S(2)}) copy-start(f32[16,1,384]{2,1,0:T(1,128)} %get-tuple-element.299.gain_ref) | copy-start | bytes 73732 | tf_op jit(solution)/shard_map/while
  87.5 7.0 %collective-permute-start = (bf16[256,384]{1,0:T(8,128)(2,1)S(1)}, bf16[256,384]{1,0:T(8,128)(2,1)S(1)}, u32[]{:S(2)}, u32[]{:S(2)}) collective-permute-start(bf16[256,384]{1,0:T(8,128)(2,1)S(1)} %get-tuple-element.283.refs_0_), channel_id=1, source_target_pairs={{0,1},{1,2},{2,3},{3,4},{4,5},{5,6},{6,7},{7,0},{8,9},{9,10},{10,1... | collective-permute-start | bytes 589832 | tf_op jit(solution)/shard_map/while/body/eval_jaxpr/ppermute | solution.py:196
  87.6 8.5 %collective-permute-start.1 = (bf16[256,384]{1,0:T(8,128)(2,1)S(1)}, bf16[256,384]{1,0:T(8,128)(2,1)S(1)}, u32[]{:S(2)}, u32[]{:S(2)}) collective-permute-start(bf16[256,384]{1,0:T(8,128)(2,1)S(1)} %get-tuple-element.283.refs_0_), channel_id=1, source_target_pairs={{0,7},{1,0},{2,1},{3,2},{4,3},{5,4},{6,5},{7,6},{8,15},{9,8},{10,9... | collective-permute-start | bytes 589832 | tf_op jit(solution)/shard_map/while/body/eval_jaxpr/ppermute | solution.py:196
  90.8 7.8 %collective-permute-start.2 = (bf16[256,384]{1,0:T(8,128)(2,1)S(1)}, bf16[256,384]{1,0:T(8,128)(2,1)S(1)}, u32[]{:S(2)}, u32[]{:S(2)}) collective-permute-start(bf16[256,384]{1,0:T(8,128)(2,1)S(1)} %get-tuple-element.283.refs_0_), channel_id=1, source_target_pairs={{0,8},{8,0},{1,9},{9,1},{2,10},{10,2},{3,11},{11,3},{4,12},{12,4},... | collective-permute-start | bytes 589832 | tf_op jit(solution)/shard_map/while/body/eval_jaxpr/ppermute | solution.py:196
  98.7 38.0 %collective-permute-start.16 = (bf16[256,3072]{1,0:T(8,128)(2,1)S(1)}, bf16[256,3072]{1,0:T(8,128)(2,1)S(1)}, u32[]{:S(2)}, u32[]{:S(2)}) collective-permute-start(bf16[256,3072]{1,0:T(8,128)(2,1)S(1)} %constant_dynamic-slice_fusion.2), channel_id=1, source_target_pairs={{0,8},{8,0},{1,9},{9,1},{2,10},{10,2},{3,11},{11,3},{4,12},{12,4},... | collective-permute-start | bytes 4718600 | tf_op jit(solution)/shard_map/while/body/eval_jaxpr/ppermute | solution.py:196
  99.0 7.7 %collective-permute-start.9 = (bf16[256,384]{1,0:T(8,128)(2,1)S(1)}, bf16[256,384]{1,0:T(8,128)(2,1)S(1)}, u32[]{:S(2)}, u32[]{:S(2)}) collective-permute-start(bf16[256,384]{1,0:T(8,128)(2,1)S(1)} %collective-permute-done.2.refs_1_), channel_id=1, source_target_pairs={{0,7},{1,0},{2,1},{3,2},{4,3},{5,4},{6,5},{7,6},{8,15},{9,8},{10,9... | collective-permute-start | bytes 589832 | tf_op jit(solution)/shard_map/while/body/eval_jaxpr/ppermute | solution.py:196
  100.2 8.8 %collective-permute-start.6 = (bf16[256,384]{1,0:T(8,128)(2,1)S(1)}, bf16[256,384]{1,0:T(8,128)(2,1)S(1)}, u32[]{:S(2)}, u32[]{:S(2)}) collective-permute-start(bf16[256,384]{1,0:T(8,128)(2,1)S(1)} %collective-permute-done.2.refs_1_), channel_id=1, source_target_pairs={{0,1},{1,2},{2,3},{3,4},{4,5},{5,6},{6,7},{7,0},{8,9},{9,10},{10,1... | collective-permute-start | bytes 589832 | tf_op jit(solution)/shard_map/while/body/eval_jaxpr/ppermute | solution.py:196
  101.1 9.9 %collective-permute-start.12 = (bf16[256,384]{1,0:T(8,128)(2,1)S(1)}, bf16[256,384]{1,0:T(8,128)(2,1)S(1)}, u32[]{:S(2)}, u32[]{:S(2)}) collective-permute-start(bf16[256,384]{1,0:T(8,128)(2,1)S(1)} %collective-permute-done.1.refs_3_), channel_id=1, source_target_pairs={{0,7},{1,0},{2,1},{3,2},{4,3},{5,4},{6,5},{7,6},{8,15},{9,8},{10,9... | collective-permute-start | bytes 589832 | tf_op jit(solution)/shard_map/while/body/eval_jaxpr/ppermute | solution.py:196
  103.4 9.8 %collective-permute-start.3 = (bf16[256,384]{1,0:T(8,128)(2,1)S(1)}, bf16[256,384]{1,0:T(8,128)(2,1)S(1)}, u32[]{:S(2)}, u32[]{:S(2)}) collective-permute-start(bf16[256,384]{1,0:T(8,128)(2,1)S(1)} %collective-permute-done.refs_2_), channel_id=1, source_target_pairs={{0,1},{1,2},{2,3},{3,4},{4,5},{5,6},{6,7},{7,0},{8,9},{9,10},{10,1... | collective-permute-start | bytes 589832 | tf_op jit(solution)/shard_map/while/body/eval_jaxpr/ppermute | solution.py:196
  106.8 7.7 %collective-permute-start.10 = (bf16[256,384]{1,0:T(8,128)(2,1)S(1)}, bf16[256,384]{1,0:T(8,128)(2,1)S(1)}, u32[]{:S(2)}, u32[]{:S(2)}) collective-permute-start(bf16[256,384]{1,0:T(8,128)(2,1)S(1)} %collective-permute-done.9.refs_7_), channel_id=1, source_target_pairs={{0,7},{1,0},{2,1},{3,2},{4,3},{5,4},{6,5},{7,6},{8,15},{9,8},{10,9... | collective-permute-start | bytes 589832 | tf_op jit(solution)/shard_map/while/body/eval_jaxpr/ppermute | solution.py:196
  109.0 9.0 %collective-permute-start.7 = (bf16[256,384]{1,0:T(8,128)(2,1)S(1)}, bf16[256,384]{1,0:T(8,128)(2,1)S(1)}, u32[]{:S(2)}, u32[]{:S(2)}) collective-permute-start(bf16[256,384]{1,0:T(8,128)(2,1)S(1)} %collective-permute-done.6.refs_6_), channel_id=1, source_target_pairs={{0,1},{1,2},{2,3},{3,4},{4,5},{5,6},{6,7},{7,0},{8,9},{9,10},{10,1... | collective-permute-start | bytes 589832 | tf_op jit(solution)/shard_map/while/body/eval_jaxpr/ppermute | solution.py:196
  111.0 6.9 %collective-permute-start.13 = (bf16[256,384]{1,0:T(8,128)(2,1)S(1)}, bf16[256,384]{1,0:T(8,128)(2,1)S(1)}, u32[]{:S(2)}, u32[]{:S(2)}) collective-permute-start(bf16[256,384]{1,0:T(8,128)(2,1)S(1)} %collective-permute-done.12.refs_5_), channel_id=1, source_target_pairs={{0,7},{1,0},{2,1},{3,2},{4,3},{5,4},{6,5},{7,6},{8,15},{9,8},{10,9... | collective-permute-start | bytes 589832 | tf_op jit(solution)/shard_map/while/body/eval_jaxpr/ppermute | solution.py:196
  113.2 9.2 %collective-permute-start.4 = (bf16[256,384]{1,0:T(8,128)(2,1)S(1)}, bf16[256,384]{1,0:T(8,128)(2,1)S(1)}, u32[]{:S(2)}, u32[]{:S(2)}) collective-permute-start(bf16[256,384]{1,0:T(8,128)(2,1)S(1)} %collective-permute-done.3.refs_4_), channel_id=1, source_target_pairs={{0,1},{1,2},{2,3},{3,4},{4,5},{5,6},{6,7},{7,0},{8,9},{9,10},{10,1... | collective-permute-start | bytes 589832 | tf_op jit(solution)/shard_map/while/body/eval_jaxpr/ppermute | solution.py:196
  114.5 13.8 %collective-permute-start.11 = (bf16[256,384]{1,0:T(8,128)(2,1)S(1)}, bf16[256,384]{1,0:T(8,128)(2,1)S(1)}, u32[]{:S(2)}, u32[]{:S(2)}) collective-permute-start(bf16[256,384]{1,0:T(8,128)(2,1)S(1)} %collective-permute-done.10.refs_11_), channel_id=1, source_target_pairs={{0,7},{1,0},{2,1},{3,2},{4,3},{5,4},{6,5},{7,6},{8,15},{9,8},{10,9... | collective-permute-start | bytes 589832 | tf_op jit(solution)/shard_map/while/body/eval_jaxpr/ppermute | solution.py:196
  117.9 10.3 %collective-permute-start.8 = (bf16[256,384]{1,0:T(8,128)(2,1)S(1)}, bf16[256,384]{1,0:T(8,128)(2,1)S(1)}, u32[]{:S(2)}, u32[]{:S(2)}) collective-permute-start(bf16[256,384]{1,0:T(8,128)(2,1)S(1)} %collective-permute-done.7.refs_10_), channel_id=1, source_target_pairs={{0,1},{1,2},{2,3},{3,4},{4,5},{5,6},{6,7},{7,0},{8,9},{9,10},{10,1... | collective-permute-start | bytes 589832 | tf_op jit(solution)/shard_map/while/body/eval_jaxpr/ppermute | solution.py:196
  117.9 10.3 %collective-permute-start.14 = (bf16[256,384]{1,0:T(8,128)(2,1)S(1)}, bf16[256,384]{1,0:T(8,128)(2,1)S(1)}, u32[]{:S(2)}, u32[]{:S(2)}) collective-permute-start(bf16[256,384]{1,0:T(8,128)(2,1)S(1)} %collective-permute-done.13.refs_9_), channel_id=1, source_target_pairs={{0,15},{1,8},{2,9},{3,10},{4,11},{5,12},{6,13},{7,14},{8,7},{9,0},... | collective-permute-start | bytes 589832 | tf_op jit(solution)/shard_map/while/body/eval_jaxpr/ppermute | solution.py:202
  122.4 6.9 %collective-permute-start.5 = (bf16[256,384]{1,0:T(8,128)(2,1)S(1)}, bf16[256,384]{1,0:T(8,128)(2,1)S(1)}, u32[]{:S(2)}, u32[]{:S(2)}) collective-permute-start(bf16[256,384]{1,0:T(8,128)(2,1)S(1)} %collective-permute-done.4.refs_8_), channel_id=1, source_target_pairs={{0,1},{1,2},{2,3},{3,4},{4,5},{5,6},{6,7},{7,0},{8,9},{9,10},{10,1... | collective-permute-start | bytes 589832 | tf_op jit(solution)/shard_map/while/body/eval_jaxpr/ppermute | solution.py:196
  122.4 6.9 %copy-start.3 = (f32[1,2,128]{2,1,0:T(2,128)S(1)}, f32[1,2,128]{2,1,0:T(2,128)}, u32[]{:S(2)}) copy-start(f32[1,2,128]{2,1,0:T(2,128)} %get-tuple-element.301) | copy-start | bytes 3076 | tf_op jit(solution)/shard_map/while
  128.2 8.5 %copy-start = (bf16[256,6144]{1,0:T(8,128)(2,1)S(1)}, bf16[256,6144]{1,0:T(8,128)(2,1)}, u32[]{:S(2)}) copy-start(bf16[256,6144]{1,0:T(8,128)(2,1)} %get-tuple-element.260.w_own_ref) | copy-start | bytes 9437188 | tf_op jit(solution)/shard_map/while
  131.6 5.1 %collective-permute-start.15 = (bf16[256,256]{1,0:T(8,128)(2,1)S(1)}, bf16[256,256]{1,0:T(8,128)(2,1)S(1)}, u32[]{:S(2)}, u32[]{:S(2)}) collective-permute-start(bf16[256,256]{1,0:T(8,128)(2,1)S(1)} %attention_block.1.own_ref), channel_id=1, source_target_pairs={{0,8},{8,0},{1,9},{9,1},{2,10},{10,2},{3,11},{11,3},{4,12},{12,4},... | collective-permute-start | bytes 393224 | tf_op jit(solution)/shard_map/while/body/eval_jaxpr/ppermute | solution.py:196
  137.5 7.0 %collective-permute-start.17 = (bf16[256,384]{1,0:T(8,128)(2,1)S(1)}, bf16[256,384]{1,0:T(8,128)(2,1)S(1)}, u32[]{:S(2)}, u32[]{:S(2)}) collective-permute-start(bf16[256,384]{1,0:T(8,128)(2,1)S(1)} %projection_block.6), channel_id=1, source_target_pairs={{0,1},{1,2},{2,3},{3,4},{4,5},{5,6},{6,7},{7,0},{8,9},{9,10},{10,1... | collective-permute-start | bytes 589832 | tf_op jit(solution)/shard_map/while/body/eval_jaxpr/ppermute | solution.py:196
  139.3 7.3 %collective-permute-start.21 = (bf16[256,384]{1,0:T(8,128)(2,1)S(1)}, bf16[256,384]{1,0:T(8,128)(2,1)S(1)}, u32[]{:S(2)}, u32[]{:S(2)}) collective-permute-start(bf16[256,384]{1,0:T(8,128)(2,1)S(1)} %get-tuple-element.268), channel_id=1, source_target_pairs={{0,7},{1,0},{2,1},{3,2},{4,3},{5,4},{6,5},{7,6},{8,15},{9,8},{10,9... | collective-permute-start | bytes 589832 | tf_op jit(solution)/shard_map/while/body/eval_jaxpr/ppermute | solution.py:196
  142.7 16.1 %collective-permute-start.24 = (bf16[256,384]{1,0:T(8,128)(2,1)S(1)}, bf16[256,384]{1,0:T(8,128)(2,1)S(1)}, u32[]{:S(2)}, u32[]{:S(2)}) collective-permute-start(bf16[256,384]{1,0:T(8,128)(2,1)S(1)} %add_convert_fusion.19), channel_id=1, source_target_pairs={{0,16},{1,17},{2,18},{3,19},{4,20},{5,21},{6,22},{7,23},{8,24},{9,... | collective-permute-start | bytes 589832 | tf_op jit(solution)/shard_map/while/body/eval_jaxpr/ppermute | solution.py:221
  144.6 7.0 %collective-permute-start.18 = (bf16[256,384]{1,0:T(8,128)(2,1)S(1)}, bf16[256,384]{1,0:T(8,128)(2,1)S(1)}, u32[]{:S(2)}, u32[]{:S(2)}) collective-permute-start(bf16[256,384]{1,0:T(8,128)(2,1)S(1)} %add_convert_fusion.14), channel_id=1, source_target_pairs={{0,1},{1,2},{2,3},{3,4},{4,5},{5,6},{6,7},{7,0},{8,9},{9,10},{10,1... | collective-permute-start | bytes 589832 | tf_op jit(solution)/shard_map/while/body/eval_jaxpr/ppermute | solution.py:196
  146.7 7.0 %collective-permute-start.22 = (bf16[256,384]{1,0:T(8,128)(2,1)S(1)}, bf16[256,384]{1,0:T(8,128)(2,1)S(1)}, u32[]{:S(2)}, u32[]{:S(2)}) collective-permute-start(bf16[256,384]{1,0:T(8,128)(2,1)S(1)} %add_convert_fusion.17), channel_id=1, source_target_pairs={{0,7},{1,0},{2,1},{3,2},{4,3},{5,4},{6,5},{7,6},{8,15},{9,8},{10,9... | collective-permute-start | bytes 589832 | tf_op jit(solution)/shard_map/while/body/eval_jaxpr/ppermute | solution.py:196
  151.6 7.0 %collective-permute-start.19 = (bf16[256,384]{1,0:T(8,128)(2,1)S(1)}, bf16[256,384]{1,0:T(8,128)(2,1)S(1)}, u32[]{:S(2)}, u32[]{:S(2)}) collective-permute-start(bf16[256,384]{1,0:T(8,128)(2,1)S(1)} %add_convert_fusion.15), channel_id=1, source_target_pairs={{0,1},{1,2},{2,3},{3,4},{4,5},{5,6},{6,7},{7,0},{8,9},{9,10},{10,1... | collective-permute-start | bytes 589832 | tf_op jit(solution)/shard_map/while/body/eval_jaxpr/ppermute | solution.py:196
  153.7 9.4 %collective-permute-start.23 = (bf16[256,384]{1,0:T(8,128)(2,1)S(1)}, bf16[256,384]{1,0:T(8,128)(2,1)S(1)}, u32[]{:S(2)}, u32[]{:S(2)}) collective-permute-start(bf16[256,384]{1,0:T(8,128)(2,1)S(1)} %add_convert_fusion.18), channel_id=1, source_target_pairs={{0,23},{1,16},{2,17},{3,18},{4,19},{5,20},{6,21},{7,22},{8,31},{9,... | collective-permute-start | bytes 589832 | tf_op jit(solution)/shard_map/while/body/eval_jaxpr/ppermute | solution.py:221
  158.7 12.3 %collective-permute-start.20 = (bf16[256,384]{1,0:T(8,128)(2,1)S(1)}, bf16[256,384]{1,0:T(8,128)(2,1)S(1)}, u32[]{:S(2)}, u32[]{:S(2)}) collective-permute-start(bf16[256,384]{1,0:T(8,128)(2,1)S(1)} %add_convert_fusion.16), channel_id=1, source_target_pairs={{0,17},{1,18},{2,19},{3,20},{4,21},{5,22},{6,23},{7,16},{8,25},{9,... | collective-permute-start | bytes 589832 | tf_op jit(solution)/shard_map/while/body/eval_jaxpr/ppermute | solution.py:221
  171.1 0.7 copy-start.1
